TPU v7x, 32 devices: a whole 2x2x4 slice. The times are simulated.
32 devices in a mesh: seq: 4 (over x, core), shard: 8 (over z, y).
Axes of the slice: x: 2, y: 2, z: 4, core: 2. Of those that a mesh axis runs over, the one named last changes fastest.
Arguments:
- inputs: bfloat16 [8, 2048, 1024], P('shard', 'seq'), may hold values from -6 to 6
- attn_gain: bfloat16 [1024], P('shard'), may hold values from 0.5 to 1.5
- qkv_weight: bfloat16 [3, 1024, 1024], P(None, 'shard'), may hold values from -0.1875 to 0.1875
- out_weight: bfloat16 [1024, 1024], P('shard'), may hold values from -6 to 6
- mlp_gain: bfloat16 [1024], P('shard'), may hold values from 0.5 to 1.5
- in_weight: bfloat16 [1024, 5248], P('shard'), may hold values from -0.1875 to 0.1875
- mlp_out: bfloat16 [2624, 1024], P(None, 'shard'), may hold values from -0.125 to 0.125
- cotangent: bfloat16 [8, 2048, 1024], P('shard', 'seq'), may hold values from -6 to 6
Outputs:
- result: bfloat16 [8, 2048, 1024], P('shard', 'seq')
- input_grad: float32 [8, 2048, 1024], P('shard', 'seq')
- attn_gain_grad: float32 [1024], P(('seq', 'shard'))
- qkv_grad: float32 [3, 1024, 1024], P(None, 'shard', 'seq')
- out_grad: float32 [1024, 1024], P('seq', 'shard')
- mlp_gain_grad: float32 [1024], P(('seq', 'shard'))
- in_grad: float32 [1024, 5248], P('shard', 'seq')
- mlp_out_grad: float32 [2624, 1024], P('seq', 'shard')
All inputs are finite; a program needn't handle non-finite values.
Results may differ from a plain program's by a relative error of at most 0.017.
Values may be sent and summed in bfloat16 or wider, within the bound.
No kernel may reach another device: no remote copies, remote signals or barrier semaphores. Data moves between devices by JAX's collectives and lax.ppermute only.
A program may use at most 192 MiB of HBM per device.

v0:
```python
from functools import partial
import math

import jax
import jax.numpy as jnp
from jax import lax
from jax.sharding import PartitionSpec as P

HEADS = 16
HD = 64
FF = 2624


epsilon = 1e-05
rope_base = 160000.0
query_block = 512


def layer_norm(values, gain_vec):
    center = values - jnp.mean(values, axis=-1, keepdims=True)
    inv_scale = lax.rsqrt(jnp.mean(center * center, axis=-1, keepdims=True) + epsilon)
    return center * inv_scale * gain_vec


def rope_tables(positions, head_size):
    frequency = 1.0 / rope_base ** (jnp.arange(0, head_size, 2, dtype=jnp.float32) / head_size)
    angles = positions.astype(jnp.float32)[:, None] * frequency[None, :]
    angles = jnp.concatenate([angles, angles], axis=-1)
    return (jnp.cos(angles)[:, None, :], jnp.sin(angles)[:, None, :])


def rotate(values, cosine_table, sine_table):
    half_size = values.shape[-1] // 2
    turned = jnp.concatenate([-values[..., half_size:], values[..., :half_size]], axis=-1)
    return values * cosine_table + turned * sine_table


def unrotate(grads, cosine_table, sine_table):
    half_size = grads.shape[-1] // 2
    scaled = grads * sine_table
    turned = jnp.concatenate([scaled[..., half_size:], -scaled[..., :half_size]], axis=-1)
    return grads * cosine_table + turned


def gated_unit(gate_part, up_part):
    return jax.nn.gelu(gate_part, approximate=False) * up_part


def forward_block(query_part, keys_all, values_all, score_scale):
    scores = (
        jnp.einsum("qhd,khd->hqk", query_part, keys_all, preferred_element_type=jnp.float32)
        * score_scale
    )
    row_max = jnp.max(scores, axis=-1, keepdims=True)
    exponent = jnp.exp(scores - row_max)
    row_total = jnp.sum(exponent, axis=-1, keepdims=True)
    probs = exponent / row_total
    context = jnp.einsum(
        "hqk,khd->qhd", probs.astype(jnp.bfloat16), values_all, preferred_element_type=jnp.float32
    )
    log_total = (row_max + jnp.log(row_total))[..., 0]
    return (context.astype(jnp.bfloat16), log_total)


def attend_sequence(members, score_scale, query_rows):
    queries, keys_all, values_all = members
    full_span = queries.shape[0]
    query_parts = queries.reshape(
        full_span // query_rows, query_rows, queries.shape[1], queries.shape[2]
    )
    context, log_total = lax.map(
        lambda query_part: forward_block(query_part, keys_all, values_all, score_scale), query_parts
    )
    return (context.reshape(queries.shape), log_total)


def backward_block(totals, members, keys_all, values_all, score_scale):
    key_total, value_total = totals
    query_part, context_part, log_part = members
    scores = (
        jnp.einsum("qhd,khd->hqk", query_part, keys_all, preferred_element_type=jnp.float32)
        * score_scale
    )
    probs = jnp.exp(scores - log_part[..., None])
    probs_low = probs.astype(jnp.bfloat16)
    probs_grad = jnp.einsum(
        "qhd,khd->hqk", context_part, values_all, preferred_element_type=jnp.float32
    )
    row_inner = jnp.sum(probs * probs_grad, axis=-1, keepdims=True)
    scores_grad = (probs * (probs_grad - row_inner)).astype(jnp.bfloat16)
    query_grad = (
        jnp.einsum("hqk,khd->qhd", scores_grad, keys_all, preferred_element_type=jnp.float32)
        * score_scale
    )
    key_total = (
        key_total
        + jnp.einsum("hqk,qhd->khd", scores_grad, query_part, preferred_element_type=jnp.float32)
        * score_scale
    )
    value_total = value_total + jnp.einsum(
        "hqk,qhd->khd", probs_low, context_part, preferred_element_type=jnp.float32
    )
    return ((key_total, value_total), query_grad.astype(jnp.bfloat16))


def attend_back(members, score_scale, query_rows):
    queries, keys_all, values_all, context_grad, log_total = members
    full_span = queries.shape[0]
    block_count = full_span // query_rows
    query_parts = queries.reshape(block_count, query_rows, queries.shape[1], queries.shape[2])
    grad_parts = context_grad.reshape(block_count, query_rows, queries.shape[1], queries.shape[2])
    empty_grad = jnp.zeros(keys_all.shape, jnp.float32)
    step_fn = partial(
        backward_block, keys_all=keys_all, values_all=values_all, score_scale=score_scale
    )
    (key_total, value_total), query_grad = lax.scan(
        step_fn, (empty_grad, empty_grad), (query_parts, grad_parts, log_total)
    )
    return (
        query_grad.reshape(queries.shape),
        key_total.astype(jnp.bfloat16),
        value_total.astype(jnp.bfloat16),
    )


def per_device(inputs, attn_gain, qkv_weight, out_weight, mlp_gain, in_weight, mlp_out, cotangent):
    seq_count, row_count, feature_count = inputs.shape
    groups = lax.axis_size("seq")
    seq_place = lax.axis_index("seq")
    full_span = row_count * groups
    heads_here = HEADS // groups
    cols_here = heads_here * HD
    token_count = seq_count * row_count
    score_scale = 1.0 / math.sqrt(HD)
    query_rows = min(query_block, full_span)
    token_cos, token_sin = rope_tables(seq_place * row_count + jnp.arange(row_count), HD)
    whole_cos, whole_sin = rope_tables(jnp.arange(full_span), HD)
    qkv_full, out_full, gain_first = (
        lax.all_gather(qkv_weight, "shard", axis=1, tiled=True),
        lax.all_gather(out_weight, "shard", axis=0, tiled=True),
        lax.all_gather(attn_gain, "shard", axis=0, tiled=True),
    )
    residual = inputs.astype(jnp.float32).reshape(token_count, feature_count)
    normed_one, norm_one_back = jax.vjp(layer_norm, residual, gain_first.astype(jnp.float32))
    first_low = normed_one.astype(jnp.bfloat16)
    projected = jnp.einsum("td,cde->cte", first_low, qkv_full, preferred_element_type=jnp.float32)
    projected = projected.reshape(3, seq_count, row_count, HEADS, HD)
    query_tok = rotate(projected[0], token_cos, token_sin).astype(jnp.bfloat16)
    key_tok = rotate(projected[1], token_cos, token_sin).astype(jnp.bfloat16)
    value_tok = projected[2].astype(jnp.bfloat16)
    packed = jnp.stack([query_tok, key_tok, value_tok], axis=2).reshape(
        seq_count, row_count, 3, groups, cols_here
    )
    spread = lax.all_to_all(packed, "seq", split_axis=3, concat_axis=1, tiled=True)
    spread = spread.reshape(seq_count, full_span, 3, heads_here, HD)
    queries = spread[:, :, 0]
    keys_all = spread[:, :, 1]
    values_all = spread[:, :, 2]
    context, log_total = lax.map(
        partial(attend_sequence, score_scale=score_scale, query_rows=query_rows),
        (queries, keys_all, values_all),
    )
    context_heads = context.reshape(seq_count, groups, row_count, 1, cols_here)
    merged = lax.all_to_all(context_heads, "seq", split_axis=1, concat_axis=3, tiled=True).reshape(
        token_count, feature_count
    )
    after_attn = residual + jnp.dot(merged, out_full, preferred_element_type=jnp.float32)
    wide_full, down_full, gain_second = (
        lax.all_gather(in_weight, "shard", axis=0, tiled=True),
        lax.all_gather(mlp_out, "shard", axis=1, tiled=True),
        lax.all_gather(mlp_gain, "shard", axis=0, tiled=True),
    )
    normed_two, norm_two_back = jax.vjp(layer_norm, after_attn, gain_second.astype(jnp.float32))
    second_low = normed_two.astype(jnp.bfloat16)
    gate_up = jnp.dot(second_low, wide_full, preferred_element_type=jnp.float32)
    hidden_value, glu_back = jax.vjp(gated_unit, gate_up[:, :FF], gate_up[:, FF:])
    hidden_low = hidden_value.astype(jnp.bfloat16)
    result = after_attn + jnp.dot(hidden_low, down_full, preferred_element_type=jnp.float32)
    result_out = result.astype(jnp.bfloat16).reshape(seq_count, row_count, feature_count)
    wide_again, down_again = (
        lax.all_gather(in_weight, "shard", axis=0, tiled=True),
        lax.all_gather(mlp_out, "shard", axis=1, tiled=True),
    )
    result_grad = cotangent.reshape(token_count, feature_count)
    hidden_grad = jnp.einsum(
        "te,fe->tf", result_grad, down_again, preferred_element_type=jnp.float32
    )
    gate_grad, up_grad = glu_back(hidden_grad)
    gate_up_grad = jnp.concatenate([gate_grad, up_grad], axis=1).astype(jnp.bfloat16)
    second_grad = jnp.einsum(
        "tf,df->td", gate_up_grad, wide_again, preferred_element_type=jnp.float32
    )
    norm_two_grad, gain_two_grad = norm_two_back(second_grad)
    attn_res_grad = result_grad.astype(jnp.float32) + norm_two_grad
    attn_res_low = attn_res_grad.astype(jnp.bfloat16)
    qkv_again, out_again = (
        lax.all_gather(qkv_weight, "shard", axis=1, tiled=True),
        lax.all_gather(out_weight, "shard", axis=0, tiled=True),
    )
    context_tok = jnp.einsum(
        "te,ie->ti", attn_res_low, out_again, preferred_element_type=jnp.float32
    ).astype(jnp.bfloat16)
    context_tok = context_tok.reshape(seq_count, 1, row_count, groups, cols_here)
    context_grad = lax.all_to_all(context_tok, "seq", split_axis=3, concat_axis=1, tiled=True)
    context_grad = context_grad.reshape(seq_count, full_span, heads_here, HD)
    query_grad, key_grad, value_grad = lax.map(
        partial(attend_back, score_scale=score_scale, query_rows=query_rows),
        (queries, keys_all, values_all, context_grad, log_total),
    )
    raw_heads = jnp.stack(
        [
            unrotate(query_grad.astype(jnp.float32), whole_cos, whole_sin).astype(jnp.bfloat16),
            unrotate(key_grad.astype(jnp.float32), whole_cos, whole_sin).astype(jnp.bfloat16),
            value_grad,
        ],
        axis=2,
    )
    back_moved = raw_heads.reshape(seq_count, groups, row_count, 3, 1, cols_here)
    raw_grad = lax.all_to_all(back_moved, "seq", split_axis=1, concat_axis=4, tiled=True).reshape(
        token_count, 3, feature_count
    )
    first_grad = jnp.einsum("tce,cde->td", raw_grad, qkv_again, preferred_element_type=jnp.float32)
    norm_one_grad, gain_one_grad = norm_one_back(first_grad)
    input_grad = (attn_res_grad + norm_one_grad).reshape(seq_count, row_count, feature_count)
    qkv_term = jnp.einsum("td,tce->cde", first_low, raw_grad, preferred_element_type=jnp.float32)
    out_term = jnp.einsum("ti,te->ie", merged, attn_res_low, preferred_element_type=jnp.float32)
    wide_term = jnp.einsum(
        "td,tf->df", second_low, gate_up_grad, preferred_element_type=jnp.float32
    )
    down_term = jnp.einsum("tf,te->fe", hidden_low, result_grad, preferred_element_type=jnp.float32)
    partial_sums = (
        lax.psum_scatter(
            qkv_term.astype(jnp.bfloat16), "seq", scatter_dimension=2, tiled=True
        ).astype(jnp.float32),
        lax.psum_scatter(
            out_term.astype(jnp.bfloat16), "seq", scatter_dimension=0, tiled=True
        ).astype(jnp.float32),
        lax.psum_scatter(
            wide_term.astype(jnp.bfloat16), "seq", scatter_dimension=1, tiled=True
        ).astype(jnp.float32),
        lax.psum_scatter(
            down_term.astype(jnp.bfloat16), "seq", scatter_dimension=0, tiled=True
        ).astype(jnp.float32),
        lax.psum_scatter(
            gain_one_grad.astype(jnp.bfloat16), "seq", scatter_dimension=0, tiled=True
        ).astype(jnp.float32),
        lax.psum_scatter(
            gain_two_grad.astype(jnp.bfloat16), "seq", scatter_dimension=0, tiled=True
        ).astype(jnp.float32),
    )
    summed = (
        lax.psum_scatter(partial_sums[0], "shard", scatter_dimension=1, tiled=True),
        lax.psum_scatter(partial_sums[1], "shard", scatter_dimension=1, tiled=True),
        lax.psum_scatter(partial_sums[2], "shard", scatter_dimension=0, tiled=True),
        lax.psum_scatter(partial_sums[3], "shard", scatter_dimension=1, tiled=True),
        lax.psum_scatter(partial_sums[4], "shard", scatter_dimension=0, tiled=True),
        lax.psum_scatter(partial_sums[5], "shard", scatter_dimension=0, tiled=True),
    )
    return (
        result_out,
        input_grad,
        summed[4],
        summed[0],
        summed[1],
        summed[5],
        summed[2],
        summed[3],
    )


def solution(mesh):
    placed = (
        P("shard", "seq", None),
        P("shard"),
        P(None, "shard", None),
        P("shard", None),
        P("shard"),
        P("shard", None),
        P(None, "shard"),
        P("shard", "seq", None),
    )
    return jax.shard_map(
        per_device,
        mesh=mesh,
        in_specs=placed,
        out_specs=(
            P("shard", "seq", None),
            P("shard", "seq", None),
            P(("seq", "shard")),
            P(None, "shard", "seq"),
            P("seq", "shard"),
            P(("seq", "shard")),
            P("shard", "seq"),
            P("seq", "shard"),
        ),
        check_vma=False,
    )
```

profile of v0, /device:TPU:0, one launch (start us, length us, event | category | flops | bytes accessed | tf_op | source)
XLA Modules:
  0.0 1312.8 jit_solution(17249475839369998332)
XLA Ops:
  9.4 22.5 %all-gather = bf16[8,1,128]{2,1,0:T(2,128)(2,1)S(1)} all-gather(bf16[1,1,128]{2,1,0:T(2,128)(2,1)} %bitcast.278), channel_id=1, replica_groups=mesh['seq'=4,'shard'=8] {'shard'}, dimensions={0}, use_global_device_ids=true | all-gather | bytes 2304 | tf_op jit(solution)/shard_map/all_gather | solution.py:141
  33.4 78.6 %all-gather.7.cloned.1.call-done = bf16[3,1024,1024]{2,1,0:T(8,128)(2,1)} async-done(((bf16[3,128,1024]{2,1,0:T(8,128)(2,1)}), bf16[3,1024,1024]{2,1,0:T(8,128)(2,1)}) %all-gather.7.cloned.1.call-update) | async-done | bytes 6291472 | tf_op jit(solution)/shard_map/all_gather | solution.py:139
  112.0 5.7 convolution_bitcast_fusion
  137.9 36.3 %all-to-all-done = bf16[1,512,3,4,256]{1,4,2,0,3:T(8,128)(2,1)S(1)} async-done(((bf16[1,512,3,4,256]{1,4,2,0,3:T(8,128)(2,1)}), bf16[1,512,3,4,256]{1,4,2,0,3:T(8,128)(2,1)S(1)}, u32[]{:S(2)}, u32[]{:S(2)}) %all-to-all-start) | async-done | bytes 3145760 | tf_op jit(solution)/shard_map/all_to_all | solution.py:154
  178.4 6.2 reshape.536
  190.8 43.5 %while.47 = (s32[]{:T(128)}, bf16[4,512,4,64]{1,3,2,0:T(8,128)(2,1)}, f32[4,4,512]{2,1,0:T(4,128)S(1)}, bf16[4,512,4,64]{1,3,2,0:T(8,128)(2,1)S(1)}, bf16[2048,4...) while((s32[]{:T(128)}, bf16[4,512,4,64]{1,3,2,0:T(8,128)(2,1)}, ...), condition=%wide.region_5.0_spmd, body=%wide.region_2.5_spmd.sunk | while | flops 1111619584 | bytes 53019220 | solution.py:71
  240.0 17.8 %all-gather.1 = bf16[8,1,128]{2,1,0:T(2,128)(2,1)S(1)} all-gather(bf16[1,1,128]{2,1,0:T(2,128)(2,1)S(1)} %bitcast.279), channel_id=1, replica_groups=mesh['seq'=4,'shard'=8] {'shard'}, dimensions={0}, use_global_device_ids=true | all-gather | bytes 2304 | tf_op jit(solution)/shard_map/all_gather | solution.py:171
  263.0 53.5 %all-gather.11.cloned.1.call-done = bf16[1024,5248]{1,0:T(8,128)(2,1)} async-done(((bf16[128,5248]{1,0:T(8,128)(2,1)}), bf16[1024,5248]{1,0:T(8,128)(2,1)}) %all-gather.11.cloned.1.call-update) | async-done | bytes 10747920 | tf_op jit(solution)/shard_map/all_gather | solution.py:169
  316.5 13.4 %fusion.99 = f32[512,5248]{1,0:T(8,128)} fusion(bf16[1024,5248]{1,0:T(8,128)(2,1)} %all-gather.11.cloned.1.call-done, f32[512,1024]{1,0:T(8,128)} %copy-done.11, f32[1024]{0:T(1024)S(1)} %bitcast.274, f32[512]{0:T(512)S(1)} %fusion.95, f32[512]{0:T(512)S(1)} %broadcast_multiply_fusion.3), kind=kOutput, calls=%fused_computation.174 | convolution fusion | flops 5505024000 | bytes 23601152 | tf_op jit(solution)/shard_map/dot_general | solution.py:175
  329.9 75.5 %all-gather.13.cloned.1.call-done = bf16[2624,1024]{1,0:T(8,128)(2,1)} async-done(((bf16[2624,128]{1,0:T(8,128)(2,1)}), bf16[2624,1024]{1,0:T(8,128)(2,1)}) %all-gather.13.cloned.1.call-update) | async-done | bytes 5373968 | tf_op jit(solution)/shard_map/all_gather | solution.py:170
  405.4 20.4 %add_convert_fusion = (bf16[512,2624]{1,0:T(8,128)(2,1)}, f32[512,2624]{1,0:T(8,128)S(1)}, f32[512,2624]{1,0:T(8,128)}) fusion(f32[512,5248]{1,0:T(8,128)} %fusion.99, bf16[2624,1024]{1,0:T(8,128)(2,1)} %all-gather.13.cloned.1.call-done, bf16[1,512,1024]{2,1,0:T(8,128)(2,1)} %param.19), kind=kOutput, calls=%fused_computation.52 | convolution fusion | flops 2849538048 | bytes 30605312 | tf_op jit(solution)/shard_map/te,fe->tf/dot_general | solution.py:185
  431.0 13.0 multiply_reduce_fusion.2
  469.5 5.7 all-to-all-done.2
  478.6 176.0 %while.48 = (s32[]{:T(128)}, f32[2048,4,64]{0,2,1:T(8,128)S(1)}, f32[2048,4,64]{0,2,1:T(8,128)}, bf16[4,512,4,64]{1,3,2,0:T(8,128)(2,1)}, bf16[4,512,4,64]{1,3,2...) while((s32[]{:T(128)}, f32[2048,4,64]{0,2,1:T(8,128)S(1)}, ...), condition=%wide.region_12.13_spmd.clone, body=%wide.region_10.12_spmd.clone.sunk | while | flops 2737567744 | bytes 272952000 | solution.py:116
  481.9 10.7 multiply_reduce_fusion.8
  493.0 10.5 multiply_convert_fusion.7
  503.5 5.4 fusion.158
  508.9 7.5 fusion.160
  516.4 5.5 fusion.159
  525.3 10.7 multiply_reduce_fusion.8
  536.3 10.5 multiply_convert_fusion.7
  552.2 7.5 fusion.160
  559.7 6.3 fusion.159
  569.4 10.7 multiply_reduce_fusion.8
  580.4 10.5 multiply_convert_fusion.7
  596.3 7.5 fusion.160
  603.8 6.3 fusion.159
  613.5 10.7 multiply_reduce_fusion.8
  624.5 10.5 multiply_convert_fusion.7
  640.4 7.5 fusion.160
  647.9 6.3 fusion.159
  682.9 39.4 %all_to_all.60 = bf16[1,4,512,3,1,256]{2,5,4,3,0,1:T(8,128)(2,1)S(1)} all-to-all(bf16[1,4,512,3,1,256]{2,5,4,3,0,1:T(8,128)(2,1)S(1)} %copy.92), channel_id=1, replica_groups=mesh['seq'=4,'shard'=8] {'seq'}, dimensions={1} | all-to-all | bytes 6291456 | tf_op jit(solution)/shard_map/all_to_all | solution.py:219
  726.0 6.2 reshape.544
  732.2 7.5 convert_bitcast_fusion
  744.9 7.5 convolution_convert_fusion.1
  754.0 15.7 %convolution_convert_fusion = bf16[1024,5248]{0,1:T(8,128)(2,1)} fusion(bf16[512,2624]{1,0:T(8,128)(2,1)} %get-tuple-element.316, bf16[512,2624]{1,0:T(8,128)(2,1)} %get-tuple-element.310, f32[512,1024]{1,0:T(8,128)S(1)} %copy-done.13, f32[1024]{0:T(1024)S(1)} %bitcast.277, f32[512]{0:T(512)S(1)} %copy-done.43, f32[512]{0:T(512)S(1)} %copy-done.39), kind=kOutput, calls=%fused_computation.46 | convolution fusion | flops 5521145856 | bytes 18227200 | tf_op jit(solution)/shard_map/td,tf->df/dot_general | solution.py:227
  769.8 25.8 %reduce-scatter.9.cloned.1.call-done = bf16[3,1024,256]{1,2,0:T(8,128)(2,1)} async-done(((bf16[3,1024,1024]{1,2,0:T(8,128)(2,1)}), bf16[3,1024,256]{1,2,0:T(8,128)(2,1)}) %reduce-scatter.9.cloned.1.call-update) | async-done | bytes 1572880 | tf_op jit(solution)/shard_map/reduce_scatter | solution.py:232
  799.2 30.4 %reduce-scatter.13.cloned.1.call-done = bf16[256,1024]{1,0:T(8,128)(2,1)} async-done(((bf16[1024,1024]{1,0:T(8,128)(2,1)}), bf16[256,1024]{1,0:T(8,128)(2,1)}) %reduce-scatter.13.cloned.1.call-update) | async-done | bytes 524304 | tf_op jit(solution)/shard_map/reduce_scatter | solution.py:235
  831.8 52.6 %reduce-scatter.21.cloned.1.call-done = bf16[656,1024]{1,0:T(8,128)(2,1)} async-done(((bf16[2624,1024]{1,0:T(8,128)(2,1)}), bf16[656,1024]{1,0:T(8,128)(2,1)}) %reduce-scatter.21.cloned.1.call-update) | async-done | bytes 1343504 | tf_op jit(solution)/shard_map/reduce_scatter | solution.py:241
  887.6 86.7 %reduce-scatter.17.cloned.1.call-done = bf16[1024,1312]{0,1:T(8,128)(2,1)} async-done(((bf16[1024,5248]{0,1:T(8,128)(2,1)}), bf16[1024,1312]{0,1:T(8,128)(2,1)}) %reduce-scatter.17.cloned.1.call-update) | async-done | bytes 2686992 | tf_op jit(solution)/shard_map/reduce_scatter | solution.py:238
  982.3 7.7 fusion.71
  990.0 6.0 fusion.63
  998.3 6.1 all-reduce.5
  1004.6 21.5 %all-reduce.4 = (f32[256]{0:T(256)S(1)}, f32[256]{0:T(256)S(1)}) all-reduce(f32[256]{0:T(256)S(1)} %dynamic-slice_convert_fusion.1, f32[256]{0:T(256)S(1)} %dynamic-slice_convert_fusion), channel_id=3, replica_groups=mesh['seq'=4,'shard'=8] {'shard'}, use_global_device_ids=true, to_apply=%region_17.18.clone | all-reduce | flops 512 | bytes 4096
  1031.4 22.3 %reduce-scatter.11.cloned.1.call-done = f32[3,128,256]{1,2,0:T(8,128)} async-done(((f32[3,1024,256]{1,2,0:T(8,128)}), f32[3,128,256]{1,2,0:T(8,128)}) %reduce-scatter.11.cloned.1.call-update) | async-done | bytes 393232 | tf_op jit(solution)/shard_map/reduce_scatter | solution.py:252
  1055.6 65.4 %reduce-scatter.15.cloned.1.call-done = f32[256,128]{1,0:T(8,128)} async-done(((f32[256,1024]{1,0:T(8,128)}), f32[256,128]{1,0:T(8,128)}) %reduce-scatter.15.cloned.1.call-update) | async-done | bytes 131088 | tf_op jit(solution)/shard_map/reduce_scatter | solution.py:253
  1121.0 76.5 %reduce-scatter.23.cloned.1.call-done = f32[656,128]{1,0:T(8,128)} async-done(((f32[656,1024]{1,0:T(8,128)}), f32[656,128]{1,0:T(8,128)}) %reduce-scatter.23.cloned.1.call-update) | async-done | bytes 335888 | tf_op jit(solution)/shard_map/reduce_scatter | solution.py:255
  1197.5 108.2 %reduce-scatter.19.cloned.1.call-done = f32[128,1312]{0,1:T(8,128)} async-done(((f32[1024,1312]{0,1:T(8,128)}), f32[128,1312]{0,1:T(8,128)}) %reduce-scatter.19.cloned.1.call-update) | async-done | bytes 671760 | tf_op jit(solution)/shard_map/reduce_scatter | solution.py:254
  (250 shorter events, 216.9 us)
Async XLA Ops:
  7.2 25.5 %copy-start.4 = (bf16[1,512,1024]{2,1,0:T(8,128)(2,1)S(1)}, bf16[1,512,1024]{2,1,0:T(8,128)(2,1)}, u32[]{:S(2)}) copy-start(bf16[1,512,1024]{2,1,0:T(8,128)(2,1)} %param.12) | copy-start | bytes 3145732
  7.2 104.8 %all-gather.7.cloned.1.call-start = ((), (), s32[]{:S(2)}) async-start(), calls=%async_computation.12 | async-start | bytes 7077888 | tf_op jit(solution)/shard_map/all_gather | solution.py:139
  7.9 249.9 %all-gather.9.cloned.1.call-start = ((), (), s32[]{:S(2)}) async-start(), calls=%async_computation.13 | async-start | bytes 2359296 | tf_op jit(solution)/shard_map/all_gather | solution.py:140
  8.7 307.9 %all-gather.11.cloned.1.call-start = ((), (), s32[]{:S(2)}) async-start(), calls=%async_computation.14 | async-start | bytes 12091392 | tf_op jit(solution)/shard_map/all_gather | solution.py:169
  31.9 85.8 %copy-start.28 = (f32[8,1,128]{2,1,0:T(1,128)}, f32[8,1,128]{2,1,0:T(1,128)S(1)}, u32[]{:S(2)}) copy-start(f32[8,1,128]{2,1,0:T(1,128)S(1)} %convert_element_type.250) | copy-start | bytes 12292
  32.9 84.8 %copy-start.30 = (f32[512]{0:T(512)}, f32[512]{0:T(512)S(1)}, u32[]{:S(2)}) copy-start(f32[512]{0:T(512)S(1)} %broadcast_multiply_fusion.4) | copy-start | bytes 6148
  33.4 84.4 %copy-start.34 = (f32[512]{0:T(512)}, f32[512]{0:T(512)S(1)}, u32[]{:S(2)}) copy-start(f32[512]{0:T(512)S(1)} %fusion.62) | copy-start | bytes 6148
  33.4 84.4 %copy-start.36 = (f32[512]{0:T(512)}, f32[512]{0:T(512)S(1)}, u32[]{:S(2)}) copy-start(f32[512]{0:T(512)S(1)} %fusion.94) | copy-start | bytes 6148
  133.6 40.6 %all-to-all-start = ((bf16[1,512,3,4,256]{1,4,2,0,3:T(8,128)(2,1)}), bf16[1,512,3,4,256]{1,4,2,0,3:T(8,128)(2,1)S(1)}, u32[]{:S(2)}, u32[]{:S(2)}) async-start(bf16[1,512,3,4,256]{1,4,2,0,3:T(8,128)(2,1)} %copy.82), calls=%async_computation | async-start | bytes 6291456 | tf_op jit(solution)/shard_map/all_to_all | solution.py:154
  137.4 268.1 %all-gather.13.cloned.1.call-start = ((), (), s32[]{:S(2)}) async-start(), calls=%async_computation.15 | async-start | bytes 6045696 | tf_op jit(solution)/shard_map/all_gather | solution.py:170
  190.8 49.2 %copy-start.47 = (bf16[128]{0:T(256)(128)(2,1)S(1)}, bf16[128]{0:T(256)(128)(2,1)}, u32[]{:S(2)}) copy-start(bf16[128]{0:T(256)(128)(2,1)} %param.16) | copy-start | bytes 772
  235.7 22.1 %all-to-all-start.1 = ((bf16[1,4,512,1,256]{2,4,3,0,1:T(8,128)(2,1)}), bf16[1,4,512,1,256]{2,4,3,0,1:T(8,128)(2,1)}, u32[]{:S(2)}, u32[]{:S(2)}) async-start(bf16[1,4,512,1,256]{2,4,3,0,1:T(8,128)(2,1)} %bitcast.26), calls=%async_computation.1 | async-start | bytes 2097152 | tf_op jit(solution)/shard_map/all_to_all | solution.py:164
  257.8 186.3 %copy-start.40 = (f32[8,1,128]{2,1,0:T(1,128)}, f32[8,1,128]{2,1,0:T(1,128)S(1)}, u32[]{:S(2)}) copy-start(f32[8,1,128]{2,1,0:T(1,128)S(1)} %convert_element_type.251) | copy-start | bytes 12292
  261.4 182.7 %copy-start.38 = (f32[512]{0:T(512)}, f32[512]{0:T(512)S(1)}, u32[]{:S(2)}) copy-start(f32[512]{0:T(512)S(1)} %broadcast_multiply_fusion.3) | copy-start | bytes 6148
  263.0 181.1 %copy-start.42 = (f32[512]{0:T(512)}, f32[512]{0:T(512)S(1)}, u32[]{:S(2)}) copy-start(f32[512]{0:T(512)S(1)} %fusion.95) | copy-start | bytes 6148
  405.4 20.4 %copy-start.14 = (f32[512,5248]{1,0:T(8,128)S(1)}, f32[512,5248]{1,0:T(8,128)}, u32[]{:S(2)}) copy-start(f32[512,5248]{1,0:T(8,128)} %fusion.99) | copy-start | bytes 32243716
  425.9 5.2 copy-start.12
  444.1 3.8 copy-start.19
  446.5 4.9 copy-start.32
  451.5 9.3 copy-start.45
  456.4 18.8 %all-to-all-start.2 = ((bf16[1,1,512,4,256]{4,2,1,0,3:T(8,128)(2,1)}), bf16[1,1,512,4,256]{4,2,1,0,3:T(8,128)(2,1)}, u32[]{:S(2)}, u32[]{:S(2)}) async-start(bf16[1,1,512,4,256]{4,2,1,0,3:T(8,128)(2,1)} %copy.87), calls=%async_computation.2 | async-start | bytes 2097152 | tf_op jit(solution)/shard_map/all_to_all | solution.py:204
  460.7 334.9 %reduce-scatter.9.cloned.1.call-start = ((), (), s32[]{:S(2)}) async-start(), calls=%async_computation.16 | async-start | bytes 7864320 | tf_op jit(solution)/shard_map/reduce_scatter | solution.py:232
  481.9 11.1 copy-start
  503.5 12.9 copy-start.1
  525.2 11.1 copy-start
  546.8 12.9 copy-start.1
  569.3 11.1 copy-start
  590.9 12.9 copy-start.1
  613.4 11.1 copy-start
  635.0 12.9 copy-start.1
  654.6 7.1 copy-start.16
  676.3 3.2 copy-start.23
  726.0 6.2 copy-start.5
  726.0 6.2 copy-start.29
  726.0 6.2 copy-start.31
  726.0 6.2 copy-start.37
  739.8 5.1 copy-start.20
  739.8 89.8 %reduce-scatter.13.cloned.1.call-start = ((), (), s32[]{:S(2)}) async-start(), calls=%async_computation.18 | async-start | bytes 2621440 | tf_op jit(solution)/shard_map/reduce_scatter | solution.py:235
  744.8 139.6 %reduce-scatter.21.cloned.1.call-start = ((), (), s32[]{:S(2)}) async-start(), calls=%async_computation.22 | async-start | bytes 6717440 | tf_op jit(solution)/shard_map/reduce_scatter | solution.py:241
  752.4 221.9 %reduce-scatter.17.cloned.1.call-start = ((), (), s32[]{:S(2)}) async-start(), calls=%async_computation.20 | async-start | bytes 13434880 | tf_op jit(solution)/shard_map/reduce_scatter | solution.py:238
  769.7 283.9 %reduce-scatter.11.cloned.1.call-start = ((), (), s32[]{:S(2)}) async-start(), calls=%async_computation.17 | async-start | bytes 3538944 | tf_op jit(solution)/shard_map/reduce_scatter | solution.py:252
  799.1 321.8 %reduce-scatter.15.cloned.1.call-start = ((), (), s32[]{:S(2)}) async-start(), calls=%async_computation.19 | async-start | bytes 1179648 | tf_op jit(solution)/shard_map/reduce_scatter | solution.py:253
  831.8 365.7 %reduce-scatter.23.cloned.1.call-start = ((), (), s32[]{:S(2)}) async-start(), calls=%async_computation.23 | async-start | bytes 3022848 | tf_op jit(solution)/shard_map/reduce_scatter | solution.py:255
  887.6 418.1 %reduce-scatter.19.cloned.1.call-start = ((), (), s32[]{:S(2)}) async-start(), calls=%async_computation.21 | async-start | bytes 6045696 | tf_op jit(solution)/shard_map/reduce_scatter | solution.py:254
  982.2 7.7 copy-start.24
  990.0 6.0 copy-start.35
  996.0 31.2 %copy-start.8 = (f32[512,1024]{1,0:T(8,128)S(1)}, f32[512,1024]{1,0:T(8,128)}, u32[]{:S(2)}) copy-start(f32[512,1024]{1,0:T(8,128)} %copy-done.7) | copy-start | bytes 6291460
  996.0 31.2 %copy-start.33 = (f32[512]{0:T(512)S(1)}, f32[512]{0:T(512)}, u32[]{:S(2)}) copy-start(f32[512]{0:T(512)} %copy-done.32) | copy-start | bytes 6148
  (23 other events, 35.3 us)
Sparse Core Ops, SparseCore 0:
  10.2 101.7 all-gather.6
  114.1 47.4 all-gather.8
  163.8 152.6 all-gather.10
  318.4 86.9 all-gather.12
  739.9 55.6 reduce-scatter.8
  798.1 31.4 reduce-scatter.12
  832.1 52.2 reduce-scatter.20
  887.2 87.0 reduce-scatter.16
  978.4 75.2 reduce-scatter.10
  1057.9 63.0 reduce-scatter.14
  1125.0 72.4 reduce-scatter.22
  1202.0 103.6 reduce-scatter.18
where the time goes:
time: 1320 us; the launch traced here: 1310 us
  waiting for transfers between devices  720 us (55%)
  matrix products  269 us (20%)
  blocking collectives  107 us (8%)
  other arithmetic  101 us (8%)
  local copies, waits for them, and re-layouts  85.7 us (6%)
  between operations  16.4 us (1%)
    reduce_scatter x1, waiting for transfers between devices, per_device(): lax.psum_scatter(partial_sums[2], 'shard', scatter_dimension=0, tiled=True)  108 us
    reduce_scatter x1, waiting for transfers between devices, per_device(): lax.psum_scatter(wide_term.astype(jnp.bfloat16), 'seq', scatter_dimension...  86.7 us
    all_gather x1, waiting for transfers between devices, per_device(): lax.all_gather(qkv_weight, 'shard', axis=1, tiled=True)  78.6 us
    reduce_scatter x1, waiting for transfers between devices, per_device(): lax.psum_scatter(partial_sums[3], 'shard', scatter_dimension=1, tiled=True)  76.5 us
    all_gather x1, waiting for transfers between devices, per_device(): lax.all_gather(mlp_out, 'shard', axis=1, tiled=True)  75.5 us
    reduce_scatter x1, waiting for transfers between devices, per_device(): lax.psum_scatter(partial_sums[1], 'shard', scatter_dimension=1, tiled=True)  65.4 us
    all_gather x1, waiting for transfers between devices, per_device(): lax.all_gather(in_weight, 'shard', axis=0, tiled=True)  53.5 us
    reduce_scatter x1, waiting for transfers between devices, per_device(): lax.psum_scatter(down_term.astype(jnp.bfloat16), 'seq', scatter_dimension...  52.6 us
  transfers between devices with their start and end apart: 15, of which 13 were waited for; matrix products, arithmetic and copies ran while one was open for 13% of the time, Pallas kernels for 0%

commit v1 on v0

v1 whole, which is shorter than its diff:
```python
from functools import partial
import math

import jax
import jax.numpy as jnp
from jax import lax
from jax.experimental import pallas as pl
from jax.experimental.pallas import tpu as pltpu
from jax.sharding import PartitionSpec as P

HEADS = 16
HD = 64
FF = 2624

epsilon = 1e-05
rope_base = 160000.0

f32 = jnp.float32
bf16 = jnp.bfloat16

WIDTH = 1024
HALF = FF // 2
PADDED = 1408
BLOCK = FF // 4
COLS = 256
EXTRA = 16
ROWS_BY_COLS = (((0,), (0,)), ((), ()))
COLS_BY_COLS = (((1,), (1,)), ((), ()))
VMEM_LIMIT = 58 * 1024 * 1024

ANY = pl.BlockSpec(memory_space=pl.ANY)
SMEM = pl.BlockSpec(memory_space=pltpu.SMEM)


def params():
    return pltpu.CompilerParams(vmem_limit_bytes=VMEM_LIMIT)


def sds(shape, dtype=bf16):
    return jax.ShapeDtypeStruct(shape, dtype)


def aligned(index, size):
    return pl.ds(pl.multiple_of(index * size, size), size)


def normalize(values):
    center = values - jnp.mean(values, axis=-1, keepdims=True)
    inv_scale = lax.rsqrt(jnp.mean(center * center, axis=-1, keepdims=True) + epsilon)
    return center * inv_scale, inv_scale


def norm_back(grads, xhat, inv_scale):
    mean_grad = jnp.mean(grads, axis=-1, keepdims=True)
    mean_both = jnp.mean(grads * xhat, axis=-1, keepdims=True)
    return inv_scale * (grads - mean_grad - xhat * mean_both)


def turned(values):
    lane = lax.broadcasted_iota(jnp.int32, values.shape, 1)
    width = values.shape[1]
    return jnp.where(
        lane % HD < HD // 2, pltpu.roll(values, width - HD // 2, 1), pltpu.roll(values, HD // 2, 1)
    )


def twice(table):
    return jnp.concatenate([table, table], axis=1)


def qkv_kernel(count, idx, *refs):
    x_refs, refs = refs[:4], refs[4:]
    w_refs, refs = refs[:count], refs[count:]
    if count == 1:
        gain_ref, refs = refs[0], refs[1:]
    cos_ref, sin_ref, fn_o, q_o, k_o, v_o, w_o, g_o, xs, gs, semx, semw, semg = refs
    step = pl.program_id(0)
    shard = idx[0]
    size = WIDTH // count

    def x_copy(r):
        return pltpu.make_async_copy(x_refs[r], xs.at[r], semx.at[r])

    def w_copy(r):
        return pltpu.make_async_copy(
            w_refs[r].at[pl.ds(0, size)], w_o.at[aligned(jnp.bitwise_xor(shard, r), size)], semw.at[r]
        )

    def g_copy(r):
        return pltpu.make_async_copy(
            w_refs[r].at[pl.ds(size, EXTRA)], gs.at[jnp.bitwise_xor(shard, r)], semg.at[r]
        )

    @pl.when(step == 0)
    def _():
        if count == 1:
            w_all = pltpu.make_async_copy(w_refs[0], w_o, semw.at[0])
            w_all.start()
        else:
            for r in range(count):
                w_copy(r).start()
                g_copy(r).start()
        for r in range(4):
            x_copy(r).start()
        if count == 1:
            w_all.wait()
            g_o[0:1] = gain_ref[0:1].astype(f32)
            g_o[1:2] = gain_ref[1:2].astype(f32)
        else:
            for r in range(count):
                w_copy(r).wait()
                g_copy(r).wait()
            for r in range(count):
                part = gs[r].astype(f32)
                g_o[0:1, r * size : (r + 1) * size] = part[0:1, 0:size]
                g_o[1:2, r * size : (r + 1) * size] = part[0:1, size : 2 * size]

    for r in range(4):

        @pl.when(step == r)
        def _():
            x_copy(r).wait()

    xhat, _ = normalize(xs[step].astype(f32))
    first_low = (xhat * g_o[0:1]).astype(bf16)
    fn_o[...] = first_low
    cosine, sine = twice(cos_ref[...]), twice(sin_ref[...])
    outs = (q_o, k_o, v_o)
    for part in range(3):
        value = jnp.dot(first_low, w_o[:, part * COLS : (part + 1) * COLS], preferred_element_type=f32)
        if part < 2:
            value = value * cosine + turned(value) * sine
        value = value.astype(bf16)
        if part == 0:
            value = value * jnp.asarray(1.0 / math.sqrt(HD), bf16)
        outs[part][...] = value


def qkv_call(count, idx, chunks, pieces, gains, cosine, sine):
    rows = chunks[0].shape[0]
    by_step = lambda width: pl.BlockSpec((rows, width), lambda r: (r, 0))
    whole = lambda shape: pl.BlockSpec(shape, lambda r: (0, 0))
    extra = [] if count > 1 else [gains]
    return pl.pallas_call(
        partial(qkv_kernel, count),
        grid=(4,),
        in_specs=[SMEM]
        + [ANY] * (4 + count)
        + ([] if count > 1 else [whole((2, WIDTH))])
        + [by_step(128), by_step(128)],
        out_specs=[
            by_step(WIDTH),
            by_step(COLS),
            by_step(COLS),
            by_step(COLS),
            whole((WIDTH, 3 * COLS)),
            whole((8, WIDTH)),
        ],
        out_shape=[
            sds((4 * rows, WIDTH)),
            sds((4 * rows, COLS)),
            sds((4 * rows, COLS)),
            sds((4 * rows, COLS)),
            sds((WIDTH, 3 * COLS)),
            sds((8, WIDTH), f32),
        ],
        scratch_shapes=[
            pltpu.VMEM((4, rows, WIDTH), bf16),
            pltpu.VMEM((8, EXTRA, 3 * COLS), bf16),
            pltpu.SemaphoreType.DMA((4,)),
            pltpu.SemaphoreType.DMA((count,)),
            pltpu.SemaphoreType.DMA((count,)),
        ],
        compiler_params=params(),
        name="project",
    )(idx, *chunks, *pieces, *extra, cosine, sine)


def head_of(shape):
    return lax.broadcasted_iota(jnp.int32, shape, len(shape) - 1) // HD


def attend_kernel(q_ref, k_ref, v_ref, o_ref, lse_ref):
    q, k, v = q_ref[...], k_ref[...], v_ref[...]
    heads = head_of(q.shape)
    total = jnp.zeros(q.shape, f32)
    lses = jnp.zeros((q.shape[0], 128), f32)
    lane = lax.broadcasted_iota(jnp.int32, lses.shape, 1)
    for h in range(COLS // HD):
        q_h = jnp.where(heads == h, q, jnp.zeros_like(q))
        scores = lax.dot_general(q_h, k, COLS_BY_COLS, preferred_element_type=f32)
        row_max = jnp.max(scores, axis=1, keepdims=True)
        exponent = jnp.exp(scores - row_max)
        row_total = jnp.sum(exponent, axis=1, keepdims=True)
        context = jnp.dot(exponent.astype(bf16), v, preferred_element_type=f32)
        total = jnp.where(heads == h, context * (1.0 / row_total), total)
        lses = jnp.where(lane == h, row_max + jnp.log(row_total), lses)
    o_ref[...] = total.astype(bf16)
    lse_ref[...] = lses.T[:8]


def attend(q, k, v, part, tile=512):
    span = k.shape[0]
    rows = span // 2
    steps = rows // tile
    kept = pl.BlockSpec((span, COLS), lambda i: (0, 0))
    return pl.pallas_call(
        attend_kernel,
        grid=(steps,),
        in_specs=[pl.BlockSpec((tile, COLS), lambda i: (i + part * steps, 0)), kept, kept],
        out_specs=[
            pl.BlockSpec((tile, COLS), lambda i: (i, 0)),
            pl.BlockSpec((8, tile), lambda i: (0, i)),
        ],
        out_shape=[sds((rows, COLS)), sds((8, rows), f32)],
        compiler_params=params(),
        name="attend",
    )(q, k, v)


def attend_back_kernel(last, *refs):
    q_ref, do_ref, o_ref, lse_ref, k_ref, v_ref, qcos, qsin, refs = *refs[:8], refs[8:]
    if last:
        dk_i, dv_i, kcos, ksin, refs = *refs[:4], refs[4:]
    dq_ref, dk_ref, dv_ref, do_s, inner_s, dq_s = refs
    step = pl.program_id(0)
    n_heads = COLS // HD

    @pl.when(step == 0)
    def _():
        do = do_ref[...]
        product = do.astype(f32) * o_ref[...].astype(f32)
        high = product.astype(bf16)
        rest = (product - high.astype(f32)).astype(bf16)
        chosen = (
            head_of((8, COLS)) == lax.broadcasted_iota(jnp.int32, (8, COLS), 0)
        ).astype(bf16)
        inner_s[...] = lax.dot_general(
            chosen, high, COLS_BY_COLS, preferred_element_type=f32
        ) + lax.dot_general(chosen, rest, COLS_BY_COLS, preferred_element_type=f32)
        heads = head_of(do.shape)
        for h in range(n_heads):
            do_s[h] = jnp.where(heads == h, do, jnp.zeros_like(do))
        dq_s[...] = jnp.zeros_like(dq_s)

    q, k, v = q_ref[...], k_ref[...], v_ref[...]
    heads = head_of(k.shape)
    dk = jnp.zeros(k.shape, f32)
    dv = jnp.zeros(k.shape, f32)
    dq = dq_s[...]
    for h in range(n_heads):
        k_h = jnp.where(heads == h, k, jnp.zeros_like(k))
        scores = lax.dot_general(k_h, q, COLS_BY_COLS, preferred_element_type=f32)
        probs = jnp.exp(scores - lse_ref[h : h + 1, :])
        probs_grad = lax.dot_general(v, do_s[h], COLS_BY_COLS, preferred_element_type=f32)
        scores_grad = (probs * (probs_grad - inner_s[h : h + 1, :])).astype(bf16)
        dv = dv + jnp.dot(probs.astype(bf16), do_s[h], preferred_element_type=f32)
        dk = jnp.where(heads == h, jnp.dot(scores_grad, q, preferred_element_type=f32), dk)
        dq = dq + lax.dot_general(scores_grad, k_h, ROWS_BY_COLS, preferred_element_type=f32)
    dq_s[...] = dq
    if last:
        dk = dk + dk_i[...]
        dv = dv + dv_i[...]
        dk_ref[...] = (dk * twice(kcos[...]) - turned(dk) * twice(ksin[...])).astype(bf16)
        dv_ref[...] = dv.astype(bf16)
    else:
        dk_ref[...] = dk
        dv_ref[...] = dv

    @pl.when(step == pl.num_programs(0) - 1)
    def _():
        dq = dq_s[...] * (1.0 / math.sqrt(HD))
        dq_ref[...] = (dq * twice(qcos[...]) - turned(dq) * twice(qsin[...])).astype(bf16)


def attend_back(part, q, do, o, lse, k, v, cosine, sine, earlier=None, tile=512):
    span = k.shape[0]
    rows = do.shape[0]
    last = earlier is not None
    rows_at = lambda at, width: pl.BlockSpec((rows, width), lambda i: (at, 0))
    keys = lambda width: pl.BlockSpec((tile, width), lambda i: (i, 0))
    grads = bf16 if last else f32
    return pl.pallas_call(
        partial(attend_back_kernel, last),
        grid=(span // tile,),
        in_specs=[
            rows_at(part, COLS),
            rows_at(0, COLS),
            rows_at(0, COLS),
            pl.BlockSpec((8, rows), lambda i: (0, 0)),
            keys(COLS),
            keys(COLS),
            rows_at(part, 128),
            rows_at(part, 128),
        ]
        + ([keys(COLS), keys(COLS), keys(128), keys(128)] if last else []),
        out_specs=[rows_at(0, COLS), keys(COLS), keys(COLS)],
        out_shape=[sds((rows, COLS)), sds((span, COLS), grads), sds((span, COLS), grads)],
        scratch_shapes=[
            pltpu.VMEM((COLS // HD, rows, COLS), bf16),
            pltpu.VMEM((8, rows), f32),
            pltpu.VMEM((rows, COLS), f32),
        ],
        compiler_params=params(),
        name="attend_back",
    )(q, do, o, lse, k, v, cosine, sine, *((*earlier, cosine, sine) if last else ()))


def fetch_rows(count, shard, piece_refs, target, sem):
    size = target.shape[0] // count
    copies = []
    for r in range(count):
        place = aligned(jnp.bitwise_xor(shard, r), size) if count > 1 else pl.ds(0, size)
        copies.append(pltpu.make_async_copy(piece_refs[r], target.at[place], sem.at[r]))
    return copies


def out_kernel(count, idx, mine_ref, other_ref, *refs):
    w_refs, (o_ref, wsel_ref, w_s, sem) = refs[:count], refs[count:]
    copies = fetch_rows(count, idx[0], w_refs, w_s, sem)
    for copy in copies:
        copy.start()
    for copy in copies:
        copy.wait()
    seq = idx[1]
    wsel_ref[0:COLS] = w_s[aligned(seq, COLS)]
    wsel_ref[COLS:] = w_s[aligned(jnp.bitwise_xor(seq, 2), COLS)]
    value = jnp.dot(mine_ref[...], wsel_ref[0:COLS], preferred_element_type=f32)
    value = value + jnp.dot(other_ref[...], wsel_ref[COLS:], preferred_element_type=f32)
    o_ref[...] = value.astype(bf16)


def out_call(count, idx, mine, other, pieces):
    vmem = pl.BlockSpec(memory_space=pltpu.VMEM)
    return pl.pallas_call(
        partial(out_kernel, count),
        in_specs=[SMEM, vmem, vmem] + [ANY] * count,
        out_specs=[vmem, vmem],
        out_shape=[sds((mine.shape[0], WIDTH)), sds((2 * COLS, WIDTH))],
        scratch_shapes=[pltpu.VMEM((WIDTH, WIDTH), bf16), pltpu.SemaphoreType.DMA((count,))],
        compiler_params=params(),
        name="out_project",
    )(idx, mine, other, *pieces)


def mlp_kernel(count, idx, *refs):
    x0, x1, po, pr, c0, c1, g_ref, refs = *refs[:7], refs[7:]
    win_refs, wd_refs, refs = refs[:count], refs[count : 2 * count], refs[2 * count :]
    sn_o, hid_o, gug_o, sgp_o, wd_o, refs = *refs[:5], refs[5:]
    xs, pos, prs, cs, wi, wd, sn_s, hid_s, gug_s, sgp_s, sem_a, sem_i, sem_d, sem_o = refs
    shard = idx[0]
    rows = xs.shape[1]
    loads = [
        pltpu.make_async_copy(x0, xs.at[0], sem_a.at[0]),
        pltpu.make_async_copy(x1, xs.at[1], sem_a.at[1]),
        pltpu.make_async_copy(po, pos, sem_a.at[2]),
        pltpu.make_async_copy(pr, prs, sem_a.at[3]),
        pltpu.make_async_copy(c0, cs.at[pl.ds(0, rows)], sem_a.at[4]),
        pltpu.make_async_copy(c1, cs.at[pl.ds(rows, rows)], sem_a.at[5]),
    ]
    wi_loads = fetch_rows(count, shard, win_refs, wi, sem_i)
    wd_loads = []
    width = WIDTH // count
    for r in range(count):
        place = aligned(jnp.bitwise_xor(shard, r), width) if count > 1 else pl.ds(0, width)
        wd_loads.append(
            pltpu.make_async_copy(wd_refs[r], wd.at[pl.ds(0, HALF), place], sem_d.at[r])
        )
    for copy in loads[:4] + wi_loads + loads[4:] + wd_loads:
        copy.start()
    wd[HALF:] = jnp.zeros((PADDED - HALF, WIDTH), bf16)
    for copy in loads[:4]:
        copy.wait()
    for r in range(2):
        here, there = pl.ds(r * rows, rows), pl.ds((1 - r) * rows, rows)
        after = xs[r].astype(f32) + pos[here].astype(f32) + prs[there].astype(f32)
        xhat, _ = normalize(after)
        sn_s[here] = (xhat * g_ref[1:2]).astype(bf16)
    stores = []

    def store(source, target, k):
        copy = pltpu.make_async_copy(source, target, sem_o.at[k])
        copy.start()
        stores.append(copy)

    store(sn_s, sn_o, 0)
    for copy in wi_loads + loads[4:] + wd_loads:
        copy.wait()
    store(wd, wd_o, 1)
    start = 0
    while start < PADDED:
        size = min(256, PADDED - start)
        here = pl.ds(start, size)
        gate = jnp.dot(sn_s[...], wi[:, here], preferred_element_type=f32)
        up = jnp.dot(sn_s[...], wi[:, pl.ds(PADDED + start, size)], preferred_element_type=f32)
        back = lax.dot_general(cs[...], wd[here], COLS_BY_COLS, preferred_element_type=f32)
        below = 0.5 * (1.0 + lax.erf(gate * math.sqrt(0.5)))
        density = jnp.exp(-0.5 * gate * gate) * (1.0 / math.sqrt(2.0 * math.pi))
        unit = gate * below
        hid_s[:, here] = (unit * up).astype(bf16)
        gug_s[0, :, here] = (back * up * (below + gate * density)).astype(bf16)
        gug_s[1, :, here] = (back * unit).astype(bf16)
        start += size
    store(hid_s, hid_o, 2)
    store(gug_s, gug_o, 3)
    value = lax.dot_general(gug_s[0], wi[:, :PADDED], COLS_BY_COLS, preferred_element_type=f32)
    value = value + lax.dot_general(gug_s[1], wi[:, PADDED:], COLS_BY_COLS, preferred_element_type=f32)
    sgp_s[...] = value.astype(bf16)
    store(sgp_s, sgp_o, 4)
    for copy in stores:
        copy.wait()


def mlp_call(count, idx, x0, x1, po, pr, c0, c1, gains, win, wd):
    rows = x0.shape[0]
    return pl.pallas_call(
        partial(mlp_kernel, count),
        in_specs=[SMEM] + [ANY] * 6 + [pl.BlockSpec(memory_space=pltpu.VMEM)] + [ANY] * (2 * count),
        out_specs=[ANY] * 5,
        out_shape=[
            sds((2 * rows, WIDTH)),
            sds((2 * rows, PADDED)),
            sds((2, 2 * rows, PADDED)),
            sds((2 * rows, WIDTH)),
            sds((PADDED, WIDTH)),
        ],
        scratch_shapes=[
            pltpu.VMEM((2, rows, WIDTH), bf16),
            pltpu.VMEM((2 * rows, WIDTH), bf16),
            pltpu.VMEM((2 * rows, WIDTH), bf16),
            pltpu.VMEM((2 * rows, WIDTH), bf16),
            pltpu.VMEM((WIDTH, 2 * PADDED), bf16),
            pltpu.VMEM((PADDED, WIDTH), bf16),
            pltpu.VMEM((2 * rows, WIDTH), bf16),
            pltpu.VMEM((2 * rows, PADDED), bf16),
            pltpu.VMEM((2, 2 * rows, PADDED), bf16),
            pltpu.VMEM((2 * rows, WIDTH), bf16),
            pltpu.SemaphoreType.DMA((6,)),
            pltpu.SemaphoreType.DMA((count,)),
            pltpu.SemaphoreType.DMA((count,)),
            pltpu.SemaphoreType.DMA((5,)),
        ],
        compiler_params=params(),
        name="feed_forward",
    )(idx, x0, x1, po, pr, c0, c1, gains, *win, *wd)


def down_kernel(count, idx, hid_ref, wd_ref, c0, c1, other_o, mine_o, keep_o, send_o, acc):
    shard, x_place = idx[0], idx[2]
    rows = c0.shape[0]
    for r, target in ((1, other_o), (0, mine_o)):
        target[...] = jnp.dot(
            hid_ref[r * rows : (r + 1) * rows], wd_ref[...], preferred_element_type=f32
        ).astype(bf16)
    acc[...] = lax.dot_general(
        hid_ref[0:rows], c0[...], ROWS_BY_COLS, preferred_element_type=f32
    ) + lax.dot_general(hid_ref[rows:], c1[...], ROWS_BY_COLS, preferred_element_type=f32)
    width = WIDTH // count
    for part, target in ((1, send_o), (0, keep_o)):
        here = pl.ds(pl.multiple_of(jnp.bitwise_xor(x_place, part) * BLOCK, 8), BLOCK)
        for r in range(count):
            place = aligned(jnp.bitwise_xor(shard, r), width) if count > 1 else pl.ds(0, width)
            target[r] = acc[here, place].astype(bf16)


def down_call(count, idx, hidden, wd, c0, c1):
    rows = c0.shape[0]
    vmem = pl.BlockSpec(memory_space=pltpu.VMEM)
    return pl.pallas_call(
        partial(down_kernel, count),
        in_specs=[SMEM] + [vmem] * 4,
        out_specs=[vmem] * 4,
        out_shape=[
            sds((rows, WIDTH)),
            sds((rows, WIDTH)),
            sds((count, BLOCK, WIDTH // count)),
            sds((count, BLOCK, WIDTH // count)),
        ],
        scratch_shapes=[pltpu.VMEM((PADDED, WIDTH), f32)],
        compiler_params=params(),
        name="down_project",
    )(idx, hidden, wd, c0, c1)


def norm_two_kernel(x0, x1, po, pr, so, sr, c0, c1, g_ref, wsel, res_o, low_o, mine_o, other_o, gain_o):
    rows = x0.shape[0]
    gain = g_ref[1:2]
    for r, (x_ref, c_ref) in enumerate(((x0, c0), (x1, c1))):
        here, there = pl.ds(r * rows, rows), pl.ds((1 - r) * rows, rows)
        after = x_ref[...].astype(f32) + po[here].astype(f32) + pr[there].astype(f32)
        xhat, inv_scale = normalize(after)
        second = so[here].astype(f32) + sr[there].astype(f32)
        res = c_ref[...].astype(f32) + norm_back(second * gain, xhat, inv_scale)
        if r == 0:
            res_o[...] = res
            total = jnp.sum(second * xhat, axis=0, keepdims=True)
            gain_o[...] = jnp.broadcast_to(total, gain_o.shape)
        low = res.astype(bf16)
        low_o[here] = low
        value = lax.dot_general(low, wsel[...], COLS_BY_COLS, preferred_element_type=f32).astype(bf16)
        mine_o[here] = value[:, :COLS]
        other_o[here] = value[:, COLS:]


def norm_two_call(x0, x1, po, pr, so, sr, c0, c1, gains, wsel):
    rows = x0.shape[0]
    vmem = pl.BlockSpec(memory_space=pltpu.VMEM)
    return pl.pallas_call(
        norm_two_kernel,
        in_specs=[vmem] * 10,
        out_specs=[vmem] * 5,
        out_shape=[
            sds((rows, WIDTH), f32),
            sds((2 * rows, WIDTH)),
            sds((2 * rows, COLS)),
            sds((2 * rows, COLS)),
            sds((8, WIDTH), f32),
        ],
        compiler_params=params(),
        name="norm_two_back",
    )(x0, x1, po, pr, so, sr, c0, c1, gains, wsel)


def wide_kernel(count, idx, sn_ref, gug_ref, *refs):
    outs, acc = refs[:-1], refs[-1]
    part = pl.program_id(0)
    shard = idx[0]
    acc[...] = lax.dot_general(sn_ref[...], gug_ref[0], ROWS_BY_COLS, preferred_element_type=f32)
    size = WIDTH // count
    for r in range(count):
        place = aligned(jnp.bitwise_xor(shard, r), size) if count > 1 else pl.ds(0, size)
        outs[r % len(outs)][0, r // len(outs)] = acc[place].astype(bf16)


def wide_call(count, idx, sn, gug):
    tokens = sn.shape[0]
    split = 2 if count > 1 else 1
    size = WIDTH // count
    spec = lambda shape, at: pl.BlockSpec(shape, at)
    grid_spec = pltpu.PrefetchScalarGridSpec(
        num_scalar_prefetch=1,
        grid=(2,),
        in_specs=[
            spec((tokens, WIDTH), lambda p, s: (0, 0)),
            spec((1, tokens, PADDED), lambda p, s: (jnp.bitwise_xor(p, s[2]), 0, 0)),
        ],
        out_specs=[spec((1, count // split, size, PADDED), lambda p, s: (p, 0, 0, 0))] * split,
        scratch_shapes=[pltpu.VMEM((WIDTH, PADDED), f32)],
    )
    return pl.pallas_call(
        partial(wide_kernel, count),
        grid_spec=grid_spec,
        out_shape=[sds((2, count // split, size, PADDED))] * split,
        compiler_params=params(),
        name="wide_grad",
    )(idx, sn, gug)


def out_grad_kernel(count, idx, mine, other, low, keep_o, send_o, acc):
    shard = idx[0]
    width = WIDTH // count
    for source, target in ((other, send_o), (mine, keep_o)):
        acc[...] = lax.dot_general(source[...], low[...], ROWS_BY_COLS, preferred_element_type=f32)
        for r in range(count):
            place = aligned(jnp.bitwise_xor(shard, r), width) if count > 1 else pl.ds(0, width)
            target[r] = acc[:, place].astype(bf16)


def out_grad_call(count, idx, mine, other, low):
    vmem = pl.BlockSpec(memory_space=pltpu.VMEM)
    return pl.pallas_call(
        partial(out_grad_kernel, count),
        in_specs=[SMEM] + [vmem] * 3,
        out_specs=[vmem] * 2,
        out_shape=[sds((count, COLS, WIDTH // count))] * 2,
        scratch_shapes=[pltpu.VMEM((COLS, WIDTH), f32)],
        compiler_params=params(),
        name="out_grad",
    )(idx, mine, other, low)


def first_kernel(q_ref, k0, v0, k1, v1, w_ref, far_o, near_o):
    pass


def back_project_kernel(q_ref, k_ref, v_ref, w_ref, o_ref):
    value = lax.dot_general(q_ref[...], w_ref[:, :COLS], COLS_BY_COLS, preferred_element_type=f32)
    value += lax.dot_general(k_ref[...], w_ref[:, COLS : 2 * COLS], COLS_BY_COLS, preferred_element_type=f32)
    value += lax.dot_general(v_ref[...], w_ref[:, 2 * COLS :], COLS_BY_COLS, preferred_element_type=f32)
    o_ref[0] = value.astype(bf16)


def back_project(q_near, q_far, k, v, w, chunk):
    rows = q_near.shape[0] // 2
    outs = []
    at = lambda where: pl.BlockSpec((rows, COLS), lambda i: (where, 0))
    for half, q in ((1, q_far), (0, q_near)):
        where = 2 * half + chunk
        outs.append(
            pl.pallas_call(
                back_project_kernel,
                grid=(1,),
                in_specs=[at(chunk), at(where), at(where), pl.BlockSpec((WIDTH, 3 * COLS), lambda i: (0, 0))],
                out_specs=pl.BlockSpec((1, rows, WIDTH), lambda i: (0, 0, 0)),
                out_shape=sds((1, rows, WIDTH)),
                compiler_params=params(),
                name="back_project",
            )(q, k, v, w)
        )
    return outs


def qkv_grad_kernel(count, idx, fn_ref, qn, qf, k_ref, v_ref, w_ref, g_ref, keep_o, *refs):
    if count > 1:
        send_o, gain_o, acc = refs
    else:
        gain_o, acc = refs
    rows = qn.shape[0]
    near, far = fn_ref[:rows], fn_ref[rows:]
    acc[:, :COLS] = lax.dot_general(
        near, qn[...], ROWS_BY_COLS, preferred_element_type=f32
    ) + lax.dot_general(far, qf[...], ROWS_BY_COLS, preferred_element_type=f32)
    acc[:, COLS : 2 * COLS] = lax.dot_general(
        fn_ref[...], k_ref[...], ROWS_BY_COLS, preferred_element_type=f32
    )
    acc[:, 2 * COLS :] = lax.dot_general(
        fn_ref[...], v_ref[...], ROWS_BY_COLS, preferred_element_type=f32
    )
    shard = idx[0]
    size = WIDTH // count
    for r in range(count):
        place = aligned(jnp.bitwise_xor(shard, r), size) if count > 1 else pl.ds(0, size)
        target = (keep_o, send_o)[r % 2] if count > 1 else keep_o
        target[r // 2 if count > 1 else r] = acc[place].astype(bf16)
    both = acc[...] * w_ref[...].astype(f32)
    high = both.astype(bf16)
    rest = (both - high.astype(f32)).astype(bf16)
    ones = jnp.ones((8, 3 * COLS), bf16)
    total = lax.dot_general(ones, high, COLS_BY_COLS, preferred_element_type=f32)
    total += lax.dot_general(ones, rest, COLS_BY_COLS, preferred_element_type=f32)
    gain_o[...] = total / g_ref[0:1]


def qkv_grad_call(count, idx, first_low, q_near, q_far, k, v, w, gains):
    vmem = pl.BlockSpec(memory_space=pltpu.VMEM)
    split = 2 if count > 1 else 1
    size = WIDTH // count
    return pl.pallas_call(
        partial(qkv_grad_kernel, count),
        in_specs=[SMEM] + [vmem] * 7,
        out_specs=[vmem] * (split + 1),
        out_shape=[sds((count // split, size, 3 * COLS))] * split + [sds((8, WIDTH), f32)],
        scratch_shapes=[pltpu.VMEM((WIDTH, 3 * COLS), f32)],
        compiler_params=params(),
        name="project_grad",
    )(idx, first_low, q_near, q_far, k, v, w, gains)


def norm_one_kernel(x_ref, res_ref, own, core, far, g_ref, o_ref):
    xhat, inv_scale = normalize(x_ref[...].astype(f32))
    first = own[0].astype(f32) + core[0].astype(f32) + far[0].astype(f32)
    o_ref[...] = res_ref[...] + norm_back(first * g_ref[0:1], xhat, inv_scale)


def norm_one_call(x, res, own, core, far, gains):
    vmem = pl.BlockSpec(memory_space=pltpu.VMEM)
    return pl.pallas_call(
        norm_one_kernel,
        in_specs=[vmem] * 6,
        out_specs=vmem,
        out_shape=sds(res.shape, f32),
        compiler_params=params(),
        name="norm_one_back",
    )(x, res, own, core, far, gains)


def swap(value, axis, bits):
    size = lax.axis_size(axis)
    return lax.ppermute(value, axis, [(place, place ^ bits) for place in range(size)])


def gather_eight(value):
    p = [value] + [None] * 7
    p[4] = swap(value, "shard", 4)
    p[2] = swap(value, "shard", 2)
    p[1] = swap(value, "shard", 1)
    p[6] = swap(p[4], "shard", 2)
    p[3] = swap(p[2], "shard", 1)
    p[5] = swap(p[4], "shard", 1)
    p[7] = swap(p[6], "shard", 1)
    return p


def plus(left, right):
    return (left.astype(f32) + right.astype(f32)).astype(bf16)


def reduce_z(parts):
    there = plus(parts[2], swap(parts[3], "shard", 2))
    near = swap(parts[1], "shard", 2)
    far = swap(there, "shard", 4)
    return parts[0].astype(f32) + near.astype(f32) + far.astype(f32)


def tie(values, after):
    values, _ = lax.optimization_barrier((values, after))
    return values


def per_device(inputs, attn_gain, qkv_weight, out_weight, mlp_gain, in_weight, mlp_out, cotangent):
    _, rows, width = inputs.shape
    shards = lax.axis_size("shard")
    eight = shards == 8
    count = 8 if eight else 1
    piece = width // shards
    seq, shard = lax.axis_index("seq"), lax.axis_index("shard")
    x_place, core = seq // 2, seq % 2
    idx = jnp.stack([shard, seq, x_place, core]).astype(jnp.int32)

    order = jnp.bitwise_xor(seq, jnp.arange(4))
    places = (order[:, None] * rows + jnp.arange(rows)[None, :]).reshape(-1)
    frequency = 1.0 / rope_base ** (jnp.arange(0, HD, 2, dtype=f32) / HD)
    angles = places.astype(f32)[:, None] * jnp.tile(frequency, 4)[None, :]
    sign = jnp.where(jnp.arange(128) % HD < HD // 2, -1.0, 1.0)
    cosine, sine = jnp.cos(angles), jnp.sin(angles) * sign

    x0 = inputs[0]
    c0 = cotangent[0]
    w_qkv = lax.dynamic_slice_in_dim(qkv_weight, seq * COLS, COLS, 2)
    w_qkv = jnp.transpose(w_qkv, (1, 0, 2)).reshape(piece, 3 * COLS)
    w_in = in_weight.reshape(piece, 2, 2, HALF)
    w_in = lax.dynamic_index_in_dim(w_in, core, 2, keepdims=False)
    w_in = jnp.pad(w_in, ((0, 0), (0, 0), (0, PADDED - HALF))).reshape(piece, 2 * PADDED)
    w_down = lax.dynamic_slice_in_dim(mlp_out, core * HALF, HALF, 0)

    x2 = swap(x0, "seq", 2)
    x1 = swap(x0, "seq", 1)
    x3 = swap(x2, "seq", 1)
    if eight:
        gain_rows = jnp.concatenate([attn_gain, mlp_gain, jnp.zeros(3 * COLS - 2 * piece, bf16)])[None]
        w_qkv = jnp.concatenate([w_qkv, jnp.pad(gain_rows, ((0, EXTRA - 1), (0, 0)))], axis=0)
        qkv_pieces = gather_eight(w_qkv)
        both_gains = None
        later = tie((out_weight, w_in, w_down), (qkv_pieces[7], x2))
        out_pieces = gather_eight(later[0])
        later = tie(later[1:], (out_pieces[7],))
        in_pieces = gather_eight(later[0])
        later = tie(later[1:], (in_pieces[7],))
        down_pieces = gather_eight(later[0])
    else:
        both_gains = jnp.stack(
            [
                lax.all_gather(attn_gain, "shard", axis=0, tiled=True),
                lax.all_gather(mlp_gain, "shard", axis=0, tiled=True),
            ]
        )
        qkv_pieces = [lax.all_gather(w_qkv, "shard", axis=0, tiled=True)]
        out_pieces = [lax.all_gather(out_weight, "shard", axis=0, tiled=True)]
        in_pieces = [lax.all_gather(w_in, "shard", axis=0, tiled=True)]
        down_pieces = [lax.all_gather(w_down, "shard", axis=1, tiled=True)]
    c1 = swap(c0, "seq", 1)

    first_low, q, k, v, w_full, gains = qkv_call(
        count, idx, (x0, x1, x2, x3), qkv_pieces, both_gains, cosine, sine
    )
    ctx_far, lse_far = attend(q, k, v, 1)
    ctx_other = swap(ctx_far, "seq", 2)
    ctx_near, lse_near = attend(tie(q, ctx_far), k, v, 0)
    out_own, w_sel = out_call(count, idx, ctx_near, ctx_other, out_pieces)
    out_core = swap(out_own, "seq", 1)
    second_low, hidden, gate_up_grad, second_own, w_down_full = mlp_call(
        count, idx, x0, x1, out_own, out_core, c0, c1, gains, in_pieces, down_pieces
    )
    second_core = swap(second_own, "seq", 1)
    down_other, down_mine, down_keep, down_send = down_call(
        count, idx, hidden, w_down_full, c0, c1
    )
    down_core = swap(down_other, "seq", 1)
    res, res_low, grad_near, grad_other, gain_two = norm_two_call(
        x0, x1, out_own, out_core, second_own, second_core, c0, c1, gains, w_sel
    )
    grad_far = swap(grad_other, "seq", 2)
    result = (
        x0.astype(f32)
        + out_own[:rows].astype(f32)
        + out_core[rows:].astype(f32)
        + down_mine.astype(f32)
        + down_core.astype(f32)
    ).astype(bf16)[None]
    wide = wide_call(count, idx, second_low, gate_up_grad)
    out_keep, out_send = out_grad_call(count, idx, ctx_near, ctx_other, res_low)

    raw_q_near, dk, dv = attend_back(0, q, grad_near, ctx_near, lse_near, k, v, cosine, sine)
    raw_q_far, raw_k, raw_v = attend_back(
        1, q, grad_far, ctx_far, lse_far, k, v, cosine, sine, (dk, dv)
    )

    far_core, near_core = back_project(raw_q_near, raw_q_far, raw_k, raw_v, w_full, 1)
    far_got, near_got = swap(far_core, "seq", 1), swap(near_core, "seq", 1)
    far_own, near_own = back_project(raw_q_near, raw_q_far, raw_k, raw_v, w_full, 0)
    first_far = swap(plus(far_own, far_got), "seq", 2)
    *qkv_terms, gain_one = qkv_grad_call(
        count, idx, first_low, raw_q_near, raw_q_far, raw_k, raw_v, w_full, gains
    )
    input_grad = norm_one_call(x0, res, near_own, near_got, first_far, gains)[None]

    down_sum = plus(down_keep, swap(down_send, "seq", 2))
    out_sum = plus(out_keep, swap(out_send, "seq", 2))
    gain_terms = jnp.concatenate([gain_one[:1], gain_two[:1]], axis=0)
    if eight:
        wide_keep, wide_send = wide
        wide_sum = plus(wide_keep, swap(wide_send, "shard", 1))
        wide_sum = plus(wide_sum[0], swap(wide_sum[1], "seq", 2))
        wide_total = reduce_z([wide_sum[r] for r in range(4)])
        down_sum, out_sum = (
            plus(t[0::2], swap(t[1::2], "shard", 1)) for t in (down_sum, out_sum)
        )
        down_total = reduce_z([down_sum[r] for r in range(4)])
        out_total = reduce_z([out_sum[r] for r in range(4)])
        qkv_keep, qkv_send = qkv_terms
        qkv_sum = plus(qkv_keep, swap(qkv_send, "shard", 1))
        qkv_total = reduce_z([qkv_sum[r] for r in range(4)])
        for axis, bits in (("seq", 1), ("shard", 1), ("shard", 2), ("seq", 2), ("shard", 4)):
            gain_terms = gain_terms + swap(gain_terms, axis, bits)
    else:
        wide_sum = plus(wide[0][0, 0], swap(wide[0][1, 0], "seq", 2))
        scatter = lambda value, dim: lax.psum_scatter(
            value, "shard", scatter_dimension=dim, tiled=True
        ).astype(f32)
        wide_total = scatter(wide_sum, 0)
        down_total = scatter(down_sum[0], 1)
        out_total = scatter(out_sum[0], 1)
        qkv_total = scatter(qkv_terms[0][0], 0)
        gain_terms = lax.psum(gain_terms, ("seq", "shard"))
    moved = lax.ppermute(down_total.astype(bf16), "seq", [(1, 2), (2, 1)]).astype(f32)
    down_total = jnp.where((seq == 1) | (seq == 2), moved, down_total)
    take = width // (4 * shards)
    gain_out = lax.dynamic_slice_in_dim(gain_terms, (seq * shards + shard) * take, take, 1)
    qkv_out = jnp.transpose(qkv_total.reshape(piece, 3, COLS), (1, 0, 2))
    return (
        result,
        input_grad,
        gain_out[0],
        qkv_out,
        out_total,
        gain_out[1],
        wide_total[:, :HALF],
        down_total,
    )


def solution(mesh):
    placed = (
        P("shard", "seq", None),
        P("shard"),
        P(None, "shard", None),
        P("shard", None),
        P("shard"),
        P("shard", None),
        P(None, "shard"),
        P("shard", "seq", None),
    )
    return jax.shard_map(
        per_device,
        mesh=mesh,
        in_specs=placed,
        out_specs=(
            P("shard", "seq", None),
            P("shard", "seq", None),
            P(("seq", "shard")),
            P(None, "shard", "seq"),
            P("seq", "shard"),
            P(("seq", "shard")),
            P("shard", "seq"),
            P("seq", "shard"),
        ),
        check_vma=False,
    )
```

time: 1320 us -> 536 us (0.41)
  waiting for transfers between devices: 720 us -> 213 us
  matrix products: 269 us -> 0 us
  Pallas kernels: 0 us -> 214 us
  blocking collectives: 107 us -> 0 us
  other arithmetic: 101 us -> 22.1 us
  local copies, waits for them, and re-layouts: 85.7 us -> 13.5 us
  starting transfers between devices: 12.9 us -> 69.5 us
  between operations: 16.4 us -> 1.48 us
    reduce_scatter x8 -> x0, waiting for transfers between devices: 468 us -> none  [the longest x1 108 us: per_device(): lax.psum_scatter(partial_sums[2], 'shard', scatter_dimension=0, tiled=True)]
    dot_general x40 -> x0, matrix products: 269 us -> none  [the longest x4 42.9 us: backward_block(): jnp.einsum('qhd,khd->hqk', context_part, values_all, preferred_element_ty...]
    pallas_call x0 -> x17, Pallas kernels: none -> 214 us  [the longest x2 59.3 us: attend_back(): pl.pallas_call(partial(attend_back_kernel, last), grid=(span // tile,), i...]
    ppermute x0 -> x65, waiting for transfers between devices: none -> 213 us  [the longest x64 213 us: swap(): lax.ppermute(value, axis, [(place, place ^ bits) for place in range(size)])]
    all_gather x4 -> x0, waiting for transfers between devices: 208 us -> none  [the longest x1 78.6 us: per_device(): lax.all_gather(qkv_weight, 'shard', axis=1, tiled=True)]
    ppermute x0 -> x65, starting transfers between devices: none -> 69.5 us  [the longest x64 68.6 us: swap(): lax.ppermute(value, axis, [(place, place ^ bits) for place in range(size)])]
    convert_element_type x19 -> x13, other arithmetic: 62.5 us -> 9.53 us  [the longest x12 9.46 us: plus(): return (left.astype(f32) + right.astype(f32)).astype(bf16)]
    all_to_all x3 -> x0, waiting for transfers between devices: 42.1 us -> none  [the longest x1 36.3 us: per_device(): lax.all_to_all(packed, 'seq', split_axis=3, concat_axis=1, tiled=True)]
  transfers between devices with their start and end apart: 15 -> 65, of which waited for: 13 -> 30; matrix products, arithmetic and copies ran while one was open for 13% -> 6% of each run, Pallas kernels for 0% -> 33%
where the time goes in v1:
time: 536 us; the launch traced here: 534 us
  Pallas kernels  214 us (40%)
  waiting for transfers between devices  213 us (40%)
  starting transfers between devices  69.5 us (13%)
  other arithmetic  22.1 us (4%)
  local copies, waits for them, and re-layouts  13.5 us (3%)
    ppermute x64, waiting for transfers between devices, swap(): lax.ppermute(value, axis, [(place, place ^ bits) for place in range(size)])  213 us
    ppermute x64, starting transfers between devices, swap(): lax.ppermute(value, axis, [(place, place ^ bits) for place in range(size)])  68.6 us
    pallas_call x2, Pallas kernels, attend_back(): pl.pallas_call(partial(attend_back_kernel, last), grid=(span // tile,), i...  59.3 us
    pallas_call x2, Pallas kernels, attend(): pl.pallas_call(attend_kernel, grid=(steps,), in_specs=[pl.BlockSpec((tile...  42.6 us
    pallas_call x1, Pallas kernels, mlp_call(): pl.pallas_call(partial(mlp_kernel, count), in_specs=[SMEM] + [ANY] * 6 +...  25.9 us
    pallas_call x4, Pallas kernels, back_project(): pl.pallas_call(back_project_kernel, grid=(1,), in_specs=[at(chunk), at(wh...  14.8 us
    pallas_call x1, Pallas kernels, wide_call(): pl.pallas_call(partial(wide_kernel, count), grid_spec=grid_spec, out_shap...  12.2 us
    pallas_call x1, Pallas kernels, down_call(): pl.pallas_call(partial(down_kernel, count), in_specs=[SMEM] + [vmem] * 4,...  11.7 us
  transfers between devices with their start and end apart: 65, of which 30 were waited for; matrix products, arithmetic and copies ran while one was open for 6% of the time, Pallas kernels for 33%

profile of v1, /device:TPU:0, one launch (start us, length us, event | category | flops | bytes accessed | tf_op | source)
XLA Modules:
  0.0 533.7 jit_solution(15726552636981790825)
XLA Ops:
  0.6 3.0 collective-permute-start.1
  4.8 2.7 collective-permute-start.6
  9.5 8.0 %collective-permute-done.6.refs_8_ = bf16[144,768]{1,0:T(8,128)(2,1)} collective-permute-done((bf16[144,768]{1,0:T(8,128)(2,1)S(1)}, bf16[144,768]{1,0:T(8,128)(2,1)}, u32[]{:S(2)}, u32[]{:S(2)}) %collective-permute-start.6) | collective-permute-done | bytes 221216 | tf_op jit(solution)/shard_map/ppermute | solution.py:679
  18.4 5.6 %collective-permute-done.8.refs_10_ = bf16[144,768]{1,0:T(8,128)(2,1)} collective-permute-done((bf16[144,768]{1,0:T(8,128)(2,1)}, bf16[144,768]{1,0:T(8,128)(2,1)}, u32[]{:S(2)}, u32[]{:S(2)}) %collective-permute-start.8) | collective-permute-done | bytes 221216 | tf_op jit(solution)/shard_map/ppermute | solution.py:679
  27.3 2.9 collective-permute-done.9.refs_11_
  30.2 4.3 collective-permute-start.14
  34.5 10.9 %collective-permute-done.14.refs_4_ = bf16[128,1024]{1,0:T(8,128)(2,1)S(1)} collective-permute-done((bf16[128,1024]{1,0:T(8,128)(2,1)}, bf16[128,1024]{1,0:T(8,128)(2,1)S(1)}, u32[]{:S(2)}, u32[]{:S(2)}) %collective-permute-start.14) | collective-permute-done | bytes 262176 | tf_op jit(solution)/shard_map/ppermute | solution.py:679
  49.4 5.3 collective-permute-done.16.refs_6_
  59.3 4.3 collective-permute-done.17.refs_7_
  65.6 5.6 %fusion.1 = (f32[2048,128]{1,0:T(8,128)}, f32[2048,128]{1,0:T(8,128)}) fusion(f32[128]{0:T(128)S(1)} %compare_select_fusion, f32[128]{0:T(128)S(1)} %mul.49, f32[2048]{0:T(1024)S(1)} %bitcast.105), kind=kLoop, calls=%fused_computation.12 | loop fusion | flops 524288 | bytes 2106368 | tf_op jit(solution)/shard_map/mul | solution.py:725
  71.8 2.8 collective-permute-start.12
  75.6 11.5 %project.1 = (bf16[2048,1024]{1,0:T(8,128)(2,1)}, bf16[2048,256]{1,0:T(8,128)(2,1)}, bf16[2048,256]{1,0:T(8,128)(2,1)}, bf16[2048,256]{1,0:T(8,128)(2,1)}, bf16[1024,768]{1,0:T(8,128)(2,1)}, /*index=5*/f32[8,1024]{1,0:T(8,128)}) custom-call(s32[4]{0:T(128)} %pad_add_fusion.idx, bf16[512,1024]{1,0:T(8,128)(2,1)} %bitcast.91, bf16[512,1024]{1,0:T(8,128)(2,1)} %copy-done.8, ...), custom_call_target="tpu_custom_call" | custom-call | tf_op jit(solution)/shard_map/project/pallas_call | solution.py:144
  87.1 15.1 %attend.2 = (bf16[1024,256]{1,0:T(8,128)(2,1)}, f32[8,1024]{1,0:T(8,128)}) custom-call(bf16[2048,256]{1,0:T(8,128)(2,1)} %get-tuple-element.58.q_ref.refs_0_, bf16[2048,256]{1,0:T(8,128)(2,1)} %get-tuple-element.55.k_ref.refs_4_, bf16[2048,256]{1,0:T(8,128)(2,1)} %get-tuple-element.56.v_ref.refs_5_), custom_call_target="tpu_custom_call" | custom-call | tf_op jit(solution)/shard_map/attend/pallas_call | solution.py:207
  105.4 27.5 %attend.3 = (bf16[1024,256]{1,0:T(8,128)(2,1)}, f32[8,1024]{1,0:T(8,128)}) custom-call(bf16[2048,256]{1,0:T(8,128)(2,1)} %get-tuple-element.58.q_ref.refs_0_, bf16[2048,256]{1,0:T(8,128)(2,1)} %get-tuple-element.55.k_ref.refs_4_, bf16[2048,256]{1,0:T(8,128)(2,1)} %get-tuple-element.56.v_ref.refs_5_), custom_call_target="tpu_custom_call" | custom-call | tf_op jit(solution)/shard_map/attend/pallas_call | solution.py:207
  134.0 5.4 %out_project.1 = (bf16[1024,1024]{1,0:T(8,128)(2,1)}, bf16[512,1024]{1,0:T(8,128)(2,1)}) custom-call(s32[4]{0:T(128)} %pad_add_fusion.idx, bf16[1024,256]{1,0:T(8,128)(2,1)} %get-tuple-element.59.mine_ref.refs_2_.mine, bf16[1024,256]{1,0:T(8,128)(2,1)} %copy-done.14, bf16[128,1024]{1,0:T(8,128)(2,1)} %refs_0_, bf16[128,1024]{1,0:T(8,128)(2,1)} %copy-done.37, ...), custom_call_target="tpu_custom_call" | custom-call | tf_op jit(solution)/shard_map/out_project/pallas_call | solution.py:335
  144.0 14.3 %collective-permute-done.21.refs_9_ = bf16[128,2816]{1,0:T(8,128)(2,1)S(1)} collective-permute-done((bf16[128,2816]{1,0:T(8,128)(2,1)S(1)}, bf16[128,2816]{1,0:T(8,128)(2,1)S(1)}, u32[]{:S(2)}, u32[]{:S(2)}) %collective-permute-start.21) | collective-permute-done | bytes 720928 | tf_op jit(solution)/shard_map/ppermute | solution.py:679
  162.6 13.8 %collective-permute-done.20.refs_8_ = bf16[128,2816]{1,0:T(8,128)(2,1)S(1)} collective-permute-done((bf16[128,2816]{1,0:T(8,128)(2,1)S(1)}, bf16[128,2816]{1,0:T(8,128)(2,1)S(1)}, u32[]{:S(2)}, u32[]{:S(2)}) %collective-permute-start.20) | collective-permute-done | bytes 720928 | tf_op jit(solution)/shard_map/ppermute | solution.py:679
  178.5 13.4 %collective-permute-done.24.refs_12_ = bf16[128,2816]{1,0:T(8,128)(2,1)S(1)} collective-permute-done((bf16[128,2816]{1,0:T(8,128)(2,1)}, bf16[128,2816]{1,0:T(8,128)(2,1)S(1)}, u32[]{:S(2)}, u32[]{:S(2)}) %collective-permute-start.24) | collective-permute-done | bytes 720928 | tf_op jit(solution)/shard_map/ppermute | solution.py:679
  193.4 13.9 %collective-permute-done.22.refs_10_ = bf16[128,2816]{1,0:T(8,128)(2,1)S(1)} collective-permute-done((bf16[128,2816]{1,0:T(8,128)(2,1)S(1)}, bf16[128,2816]{1,0:T(8,128)(2,1)S(1)}, u32[]{:S(2)}, u32[]{:S(2)}) %collective-permute-start.22) | collective-permute-done | bytes 720928 | tf_op jit(solution)/shard_map/ppermute | solution.py:679
  210.9 3.6 collective-permute-done.27.refs_16_
  214.6 7.2 %collective-permute-done.31.refs_20_ = bf16[1312,128]{1,0:T(8,128)(2,1)S(1)} collective-permute-done((bf16[1312,128]{1,0:T(8,128)(2,1)S(1)}, bf16[1312,128]{1,0:T(8,128)(2,1)S(1)}, u32[]{:S(2)}, u32[]{:S(2)}) %collective-permute-start.31) | collective-permute-done | bytes 335904 | tf_op jit(solution)/shard_map/ppermute | solution.py:679
  221.8 7.2 %collective-permute-done.29.refs_18_ = bf16[1312,128]{1,0:T(8,128)(2,1)S(1)} collective-permute-done((bf16[1312,128]{1,0:T(8,128)(2,1)S(1)}, bf16[1312,128]{1,0:T(8,128)(2,1)S(1)}, u32[]{:S(2)}, u32[]{:S(2)}) %collective-permute-start.29) | collective-permute-done | bytes 335904 | tf_op jit(solution)/shard_map/ppermute | solution.py:679
  229.0 6.0 %collective-permute-done.33.refs_22_ = bf16[1312,128]{1,0:T(8,128)(2,1)S(1)} collective-permute-done((bf16[1312,128]{1,0:T(8,128)(2,1)S(1)}, bf16[1312,128]{1,0:T(8,128)(2,1)S(1)}, u32[]{:S(2)}, u32[]{:S(2)}) %collective-permute-start.33) | collective-permute-done | bytes 335904 | tf_op jit(solution)/shard_map/ppermute | solution.py:679
  235.8 25.9 %feed_forward.1 = (bf16[1024,1024]{1,0:T(8,128)(2,1)}, bf16[1024,1408]{1,0:T(8,128)(2,1)}, bf16[2,1024,1408]{2,1,0:T(8,128)(2,1)}, bf16[1024,1024]{1,0:T(8,128)(2,1)}, bf16[1408,1024]{1,0:T(8,128)(2,1)}) custom-call(s32[4]{0:T(128)} %pad_add_fusion.idx, bf16[512,1024]{1,0:T(8,128)(2,1)} %bitcast.92, bf16[512,1024]{1,0:T(8,128)(2,1)} %copy-done.8, ...), custom_call_target="tpu_custom_call" | custom-call | tf_op jit(solution)/shard_map/feed_forward/pallas_call | solution.py:416
  261.7 11.7 %down_project.1 = (bf16[512,1024]{1,0:T(8,128)(2,1)}, bf16[512,1024]{1,0:T(8,128)(2,1)}, bf16[8,656,128]{2,1,0:T(8,128)(2,1)}, bf16[8,656,128]{2,1,0:T(8,128)(2,1)}) custom-call(s32[4]{0:T(128)} %pad_add_fusion.idx, bf16[1024,1408]{1,0:T(8,128)(2,1)} %get-tuple-element.68.hid_ref, bf16[1408,1024]{1,0:T(8,128)(2,1)} %get-tuple-element.69.wd_ref, ...), custom_call_target="tpu_custom_call" | custom-call | tf_op jit(solution)/shard_map/down_project/pallas_call | solution.py:469
  274.8 29.1 %collective-permute-done.59 = bf16[8,656,128]{2,1,0:T(8,128)(2,1)S(1)} collective-permute-done((bf16[8,656,128]{2,1,0:T(8,128)(2,1)}, bf16[8,656,128]{2,1,0:T(8,128)(2,1)S(1)}, u32[]{:S(2)}, u32[]{:S(2)}) %collective-permute-start.59) | collective-permute-done | bytes 1343520 | tf_op jit(solution)/shard_map/ppermute | solution.py:679
  307.3 12.2 %wide_grad.1 = (bf16[2,4,128,1408]{3,2,1,0:T(8,128)(2,1)}, bf16[2,4,128,1408]{3,2,1,0:T(8,128)(2,1)}) custom-call(s32[4]{0:T(128)} %pad_add_fusion.idx, bf16[1024,1024]{1,0:T(8,128)(2,1)} %get-tuple-element.94.sn_ref, bf16[2,1024,1408]{2,1,0:T(8,128)(2,1)} %get-tuple-element.95.gug_ref), custom_call_target="tpu_custom_call" | custom-call | tf_op jit(solution)/shard_map/wide_grad/pallas_call | solution.py:550
  320.0 10.7 %norm_two_back.1 = (f32[512,1024]{1,0:T(8,128)}, bf16[1024,1024]{1,0:T(8,128)(2,1)}, bf16[1024,256]{1,0:T(8,128)(2,1)}, bf16[1024,256]{1,0:T(8,128)(2,1)}, f32[8,1024]{1,0:T(8,128)}) custom-call(bf16[512,1024]{1,0:T(8,128)(2,1)} %bitcast.93, bf16[512,1024]{1,0:T(8,128)(2,1)} %copy-done.8, bf16[1024,1024]{1,0:T(8,128)(2,1)} %get-tuple-element.61.refs_2_.po, ...), custom_call_target="tpu_custom_call" | custom-call | tf_op jit(solution)/shard_map/norm_two_back/pallas_call | solution.py:508
  335.8 29.2 %attend_back.2 = (bf16[1024,256]{1,0:T(8,128)(2,1)}, f32[2048,256]{1,0:T(8,128)}, f32[2048,256]{1,0:T(8,128)}) custom-call(bf16[2048,256]{1,0:T(8,128)(2,1)} %get-tuple-element.58.q_ref.refs_0_, bf16[1024,256]{1,0:T(8,128)(2,1)} %get-tuple-element.75.refs_1_, bf16[1024,256]{1,0:T(8,128)(2,1)} %get-tuple-element.59.mine_ref.refs_2_.mine, ...), custom_call_target="tpu_custom_call" | custom-call | tf_op jit(solution)/shard_map/attend_back/pallas_call | solution.py:283
  365.0 4.3 out_grad.1
  370.2 30.1 %attend_back.3 = (bf16[1024,256]{1,0:T(8,128)(2,1)}, bf16[2048,256]{1,0:T(8,128)(2,1)}, bf16[2048,256]{1,0:T(8,128)(2,1)}) custom-call(bf16[2048,256]{1,0:T(8,128)(2,1)} %get-tuple-element.58.q_ref.refs_0_, bf16[1024,256]{1,0:T(8,128)(2,1)} %copy-done.26, bf16[1024,256]{1,0:T(8,128)(2,1)} %get-tuple-element.57.refs_2_, f32[8,1024]{1,0:T(8,128)} %get-tuple-element.79.refs_3_, ...), custom_call_target="tpu_custom_call" | custom-call | tf_op jit(solution)/shard_map/attend_back/pallas_call | solution.py:283
  400.3 9.9 %project_grad.1 = (bf16[4,128,768]{2,1,0:T(8,128)(2,1)}, bf16[4,128,768]{2,1,0:T(8,128)(2,1)}, f32[8,1024]{1,0:T(8,128)}) custom-call(s32[4]{0:T(128)} %pad_add_fusion.idx, bf16[2048,1024]{1,0:T(8,128)(2,1)} %get-tuple-element.86.fn_ref, bf16[1024,256]{1,0:T(8,128)(2,1)} %get-tuple-element.77.q_ref.qn, bf16[1024,256]{1,0:T(8,128)(2,1)} %get-tuple-element.85.q_ref.qf, ...), custom_call_target="tpu_custom_call" | custom-call | tf_op jit(solution)/shard_map/project_grad/pallas_call | solution.py:648
  414.0 9.3 %collective-permute-done.63 = bf16[656,128]{1,0:T(8,128)(2,1)S(1)} collective-permute-done((bf16[656,128]{1,0:T(8,128)(2,1)S(1)}, bf16[656,128]{1,0:T(8,128)(2,1)S(1)}, u32[]{:S(2)}, u32[]{:S(2)}) %collective-permute-start.63) | collective-permute-done | bytes 167968 | tf_op jit(solution)/shard_map/ppermute | solution.py:679
  424.4 3.7 fusion.2
  428.2 2.8 collective-permute-start.43
  435.5 3.6 back_project.7
  439.2 3.6 back_project.6
  442.8 3.6 back_project.5
  446.5 3.9 back_project.4.own
  460.5 3.5 collective-permute-done.52
  464.3 11.4 %collective-permute-done.45 = bf16[4,128,768]{2,1,0:T(8,128)(2,1)S(1)} collective-permute-done((bf16[4,128,768]{2,1,0:T(8,128)(2,1)S(1)}, bf16[4,128,768]{2,1,0:T(8,128)(2,1)S(1)}, u32[]{:S(2)}, u32[]{:S(2)}) %collective-permute-start.45) | collective-permute-done | bytes 786464 | tf_op jit(solution)/shard_map/ppermute | solution.py:679
  477.4 12.2 %collective-permute-done.55 = bf16[4,128,1408]{2,1,0:T(8,128)(2,1)S(1)} collective-permute-done((bf16[4,128,1408]{2,1,0:T(8,128)(2,1)S(1)}, bf16[4,128,1408]{2,1,0:T(8,128)(2,1)S(1)}, u32[]{:S(2)}, u32[]{:S(2)}) %collective-permute-start.55) | collective-permute-done | bytes 1441824 | tf_op jit(solution)/shard_map/ppermute | solution.py:679
  494.2 3.2 collective-permute-done.47
  499.2 4.4 collective-permute-done.57
  504.8 2.9 collective-permute-start.48
  508.0 8.4 %collective-permute-done.46 = bf16[128,768]{1,0:T(8,128)(2,1)S(1)} collective-permute-done((bf16[128,768]{1,0:T(8,128)(2,1)S(1)}, bf16[128,768]{1,0:T(8,128)(2,1)S(1)}, u32[]{:S(2)}, u32[]{:S(2)}) %collective-permute-start.46) | collective-permute-done | bytes 196640 | tf_op jit(solution)/shard_map/ppermute | solution.py:679
  519.9 5.9 %norm_one_back.1 = f32[512,1024]{1,0:T(8,128)} custom-call(bf16[512,1024]{1,0:T(8,128)(2,1)} %bitcast.94, f32[512,1024]{1,0:T(8,128)} %get-tuple-element.74.res_ref, bf16[1,512,1024]{2,1,0:T(8,128)(2,1)} %back_project.4.own, bf16[1,512,1024]{2,1,0:T(8,128)(2,1)} %collective-permute-done.37.core, bf16[1,512,1024]{2,1,0:T(8,128)(2,1)} %collective-permute-done.39.far, ...), custom_call_target="tpu_custom_call" | custom-call | tf_op jit(solution)/shard_map/norm_one_back/pallas_call | solution.py:667
  526.7 5.6 %collective-permute-done.58 = bf16[128,1408]{1,0:T(8,128)(2,1)S(1)} collective-permute-done((bf16[128,1408]{1,0:T(8,128)(2,1)}, bf16[128,1408]{1,0:T(8,128)(2,1)S(1)}, u32[]{:S(2)}, u32[]{:S(2)}) %collective-permute-start.58) | collective-permute-done | bytes 360480 | tf_op jit(solution)/shard_map/ppermute | solution.py:679
  (241 shorter events, 86.6 us)
Async XLA Ops:
  0.6 29.5 %collective-permute-start.1 = (bf16[512,1024]{1,0:T(8,128)(2,1)}, bf16[512,1024]{1,0:T(8,128)(2,1)}, u32[]{:S(2)}, u32[]{:S(2)}) collective-permute-start(bf16[512,1024]{1,0:T(8,128)(2,1)} %bitcast.90), channel_id=1, source_target_pairs={{0,16},{8,24},{16,0},{24,8},{1,17},{9,25},{17,1},{25,9},{2,18},{10... | collective-permute-start | bytes 3145736 | tf_op jit(solution)/shard_map/ppermute | solution.py:679
  4.8 12.7 %collective-permute-start.6 = (bf16[144,768]{1,0:T(8,128)(2,1)S(1)}, bf16[144,768]{1,0:T(8,128)(2,1)}, u32[]{:S(2)}, u32[]{:S(2)}) collective-permute-start(bf16[144,768]{1,0:T(8,128)(2,1)S(1)} %fusion.10.refs_4_), channel_id=1, source_target_pairs={{0,4},{1,5},{2,6},{3,7},{4,0},{5,1},{6,2},{7,3},{8,12},{9,13},{10,... | collective-permute-start | bytes 663560 | tf_op jit(solution)/shard_map/ppermute | solution.py:679
  30.2 15.1 %collective-permute-start.14 = (bf16[128,1024]{1,0:T(8,128)(2,1)}, bf16[128,1024]{1,0:T(8,128)(2,1)S(1)}, u32[]{:S(2)}, u32[]{:S(2)}) collective-permute-start(bf16[128,1024]{1,0:T(8,128)(2,1)} %refs_0_), channel_id=1, source_target_pairs={{0,4},{1,5},{2,6},{3,7},{4,0},{5,1},{6,2},{7,3},{8,12},{9,13},{10,... | collective-permute-start | bytes 786440 | tf_op jit(solution)/shard_map/ppermute | solution.py:679
  47.4 17.8 %collective-permute-start.3 = (bf16[144,768]{1,0:T(8,128)(2,1)S(1)}, bf16[144,768]{1,0:T(8,128)(2,1)}, u32[]{:S(2)}, u32[]{:S(2)}) collective-permute-start(bf16[144,768]{1,0:T(8,128)(2,1)S(1)} %fusion.10.refs_4_), channel_id=1, source_target_pairs={{0,1},{1,0},{2,3},{3,2},{4,5},{5,4},{6,7},{7,6},{8,9},{9,8},{10,11... | collective-permute-start | bytes 663560 | tf_op jit(solution)/shard_map/ppermute | solution.py:679
  48.9 25.7 %collective-permute-start = (bf16[512,1024]{1,0:T(8,128)(2,1)S(1)}, bf16[512,1024]{1,0:T(8,128)(2,1)S(1)}, u32[]{:S(2)}, u32[]{:S(2)}) collective-permute-start(bf16[512,1024]{1,0:T(8,128)(2,1)S(1)} %bitcast.95), channel_id=1, source_target_pairs={{0,8},{8,0},{16,24},{24,16},{1,9},{9,1},{17,25},{25,17},{2,10},{10... | collective-permute-start | bytes 3145736 | tf_op jit(solution)/shard_map/ppermute | solution.py:679
  48.9 25.7 %collective-permute-start.2 = (bf16[512,1024]{1,0:T(8,128)(2,1)}, bf16[512,1024]{1,0:T(8,128)(2,1)}, u32[]{:S(2)}, u32[]{:S(2)}) collective-permute-start(bf16[512,1024]{1,0:T(8,128)(2,1)} %collective-permute-done.1.refs_2_), channel_id=1, source_target_pairs={{0,8},{8,0},{16,24},{24,16},{1,9},{9,1},{17,25},{25,17},{2,10},{10... | collective-permute-start | bytes 3145736 | tf_op jit(solution)/shard_map/ppermute | solution.py:679
  57.8 14.0 %collective-permute-start.7 = (bf16[144,768]{1,0:T(8,128)(2,1)}, bf16[144,768]{1,0:T(8,128)(2,1)}, u32[]{:S(2)}, u32[]{:S(2)}) collective-permute-start(bf16[144,768]{1,0:T(8,128)(2,1)} %collective-permute-done.6.refs_8_), channel_id=1, source_target_pairs={{0,1},{1,0},{2,3},{3,2},{4,5},{5,4},{6,7},{7,6},{8,9},{9,8},{10,11... | collective-permute-start | bytes 663560 | tf_op jit(solution)/shard_map/ppermute | solution.py:679
  65.1 37.7 %collective-permute-start.23 = (bf16[128,2816]{1,0:T(8,128)(2,1)S(1)}, bf16[128,2816]{1,0:T(8,128)(2,1)}, u32[]{:S(2)}, u32[]{:S(2)}) collective-permute-start(bf16[128,2816]{1,0:T(8,128)(2,1)S(1)} %copy.26.refs_7_), channel_id=1, source_target_pairs={{0,4},{1,5},{2,6},{3,7},{4,0},{5,1},{6,2},{7,3},{8,12},{9,13},{10,... | collective-permute-start | bytes 2162696 | tf_op jit(solution)/shard_map/ppermute | solution.py:679
  71.8 33.1 %collective-permute-start.12 = (bf16[128,1024]{1,0:T(8,128)(2,1)}, bf16[128,1024]{1,0:T(8,128)(2,1)S(1)}, u32[]{:S(2)}, u32[]{:S(2)}) collective-permute-start(bf16[128,1024]{1,0:T(8,128)(2,1)} %refs_0_), channel_id=1, source_target_pairs={{0,2},{1,3},{2,0},{3,1},{4,6},{5,7},{6,4},{7,5},{8,10},{9,11},{10,... | collective-permute-start | bytes 786440 | tf_op jit(solution)/shard_map/ppermute | solution.py:679
  102.2 30.8 %collective-permute-start.10 = (bf16[1024,256]{1,0:T(8,128)(2,1)}, bf16[1024,256]{1,0:T(8,128)(2,1)S(1)}, u32[]{:S(2)}, u32[]{:S(2)}) collective-permute-start(bf16[1024,256]{1,0:T(8,128)(2,1)} %get-tuple-element.57.refs_2_), channel_id=1, source_target_pairs={{0,16},{8,24},{16,0},{24,8},{1,17},{9,25},{17,1},{25,9},{2,18},{10... | collective-permute-start | bytes 1572872 | tf_op jit(solution)/shard_map/ppermute | solution.py:679
  102.9 39.1 %collective-permute-start.25 = (bf16[128,2816]{1,0:T(8,128)(2,1)}, bf16[128,2816]{1,0:T(8,128)(2,1)S(1)}, u32[]{:S(2)}, u32[]{:S(2)}) collective-permute-start(bf16[128,2816]{1,0:T(8,128)(2,1)} %collective-permute-done.23.refs_11_), channel_id=1, source_target_pairs={{0,2},{1,3},{2,0},{3,1},{4,6},{5,7},{6,4},{7,5},{8,10},{9,11},{10,... | collective-permute-start | bytes 2162696 | tf_op jit(solution)/shard_map/ppermute | solution.py:679
  102.9 30.1 %collective-permute-start.11 = (bf16[128,1024]{1,0:T(8,128)(2,1)}, bf16[128,1024]{1,0:T(8,128)(2,1)S(1)}, u32[]{:S(2)}, u32[]{:S(2)}) collective-permute-start(bf16[128,1024]{1,0:T(8,128)(2,1)} %refs_0_), channel_id=1, source_target_pairs={{0,1},{1,0},{2,3},{3,2},{4,5},{5,4},{6,7},{7,6},{8,9},{9,8},{10,11... | collective-permute-start | bytes 786440 | tf_op jit(solution)/shard_map/ppermute | solution.py:679
  103.4 29.6 %collective-permute-start.15 = (bf16[128,1024]{1,0:T(8,128)(2,1)S(1)}, bf16[128,1024]{1,0:T(8,128)(2,1)S(1)}, u32[]{:S(2)}, u32[]{:S(2)}) collective-permute-start(bf16[128,1024]{1,0:T(8,128)(2,1)S(1)} %copy-done.35), channel_id=1, source_target_pairs={{0,1},{1,0},{2,3},{3,2},{4,5},{5,4},{6,7},{7,6},{8,9},{9,8},{10,11... | collective-permute-start | bytes 786440 | tf_op jit(solution)/shard_map/ppermute | solution.py:679
  104.9 28.1 %collective-permute-start.13 = (bf16[128,1024]{1,0:T(8,128)(2,1)S(1)}, bf16[128,1024]{1,0:T(8,128)(2,1)S(1)}, u32[]{:S(2)}, u32[]{:S(2)}) collective-permute-start(bf16[128,1024]{1,0:T(8,128)(2,1)S(1)} %collective-permute-done.12.refs_2_), channel_id=1, source_target_pairs={{0,1},{1,0},{2,3},{3,2},{4,5},{5,4},{6,7},{7,6},{8,9},{9,8},{10,11... | collective-permute-start | bytes 786440 | tf_op jit(solution)/shard_map/ppermute | solution.py:679
  139.4 89.6 %collective-permute-start.18 = (bf16[1024,1024]{1,0:T(8,128)(2,1)}, bf16[1024,1024]{1,0:T(8,128)(2,1)S(1)}, u32[]{:S(2)}, u32[]{:S(2)}) collective-permute-start(bf16[1024,1024]{1,0:T(8,128)(2,1)} %get-tuple-element.61.refs_2_.po), channel_id=1, source_target_pairs={{0,8},{8,0},{16,24},{24,16},{1,9},{9,1},{17,25},{25,17},{2,10},{10... | collective-permute-start | bytes 6291464 | tf_op jit(solution)/shard_map/ppermute | solution.py:679
  139.5 23.1 %collective-permute-start.19 = (bf16[512,1024]{1,0:T(8,128)(2,1)S(1)}, bf16[512,1024]{1,0:T(8,128)(2,1)S(1)}, u32[]{:S(2)}, u32[]{:S(2)}) collective-permute-start(bf16[512,1024]{1,0:T(8,128)(2,1)S(1)} %bitcast.99), channel_id=1, source_target_pairs={{0,8},{8,0},{16,24},{24,16},{1,9},{9,1},{17,25},{25,17},{2,10},{10... | collective-permute-start | bytes 3145736 | tf_op jit(solution)/shard_map/ppermute | solution.py:679
  140.0 18.4 %collective-permute-start.21 = (bf16[128,2816]{1,0:T(8,128)(2,1)S(1)}, bf16[128,2816]{1,0:T(8,128)(2,1)S(1)}, u32[]{:S(2)}, u32[]{:S(2)}) collective-permute-start(bf16[128,2816]{1,0:T(8,128)(2,1)S(1)} %copy.26.refs_7_), channel_id=1, source_target_pairs={{0,2},{1,3},{2,0},{3,1},{4,6},{5,7},{6,4},{7,5},{8,10},{9,11},{10,... | collective-permute-start | bytes 2162696 | tf_op jit(solution)/shard_map/ppermute | solution.py:679
  142.0 19.0 %collective-permute-start.26 = (bf16[128,2816]{1,0:T(8,128)(2,1)S(1)}, bf16[128,2816]{1,0:T(8,128)(2,1)S(1)}, u32[]{:S(2)}, u32[]{:S(2)}) collective-permute-start(bf16[128,2816]{1,0:T(8,128)(2,1)S(1)} %collective-permute-done.25.refs_13_), channel_id=1, source_target_pairs={{0,1},{1,0},{2,3},{3,2},{4,5},{5,4},{6,7},{7,6},{8,9},{9,8},{10,11... | collective-permute-start | bytes 2162696 | tf_op jit(solution)/shard_map/ppermute | solution.py:679
  143.5 33.0 %collective-permute-start.20 = (bf16[128,2816]{1,0:T(8,128)(2,1)S(1)}, bf16[128,2816]{1,0:T(8,128)(2,1)S(1)}, u32[]{:S(2)}, u32[]{:S(2)}) collective-permute-start(bf16[128,2816]{1,0:T(8,128)(2,1)S(1)} %copy.26.refs_7_), channel_id=1, source_target_pairs={{0,1},{1,0},{2,3},{3,2},{4,5},{5,4},{6,7},{7,6},{8,9},{9,8},{10,11... | collective-permute-start | bytes 2162696 | tf_op jit(solution)/shard_map/ppermute | solution.py:679
  158.4 33.5 %collective-permute-start.24 = (bf16[128,2816]{1,0:T(8,128)(2,1)}, bf16[128,2816]{1,0:T(8,128)(2,1)S(1)}, u32[]{:S(2)}, u32[]{:S(2)}) collective-permute-start(bf16[128,2816]{1,0:T(8,128)(2,1)} %collective-permute-done.23.refs_11_), channel_id=1, source_target_pairs={{0,1},{1,0},{2,3},{3,2},{4,5},{5,4},{6,7},{7,6},{8,9},{9,8},{10,11... | collective-permute-start | bytes 2162696 | tf_op jit(solution)/shard_map/ppermute | solution.py:679
  161.0 46.3 %collective-permute-start.22 = (bf16[128,2816]{1,0:T(8,128)(2,1)S(1)}, bf16[128,2816]{1,0:T(8,128)(2,1)S(1)}, u32[]{:S(2)}, u32[]{:S(2)}) collective-permute-start(bf16[128,2816]{1,0:T(8,128)(2,1)S(1)} %collective-permute-done.21.refs_9_), channel_id=1, source_target_pairs={{0,1},{1,0},{2,3},{3,2},{4,5},{5,4},{6,7},{7,6},{8,9},{9,8},{10,11... | collective-permute-start | bytes 2162696 | tf_op jit(solution)/shard_map/ppermute | solution.py:679
  162.5 15.5 %collective-permute-start.30 = (bf16[1312,128]{1,0:T(8,128)(2,1)S(1)}, bf16[1312,128]{1,0:T(8,128)(2,1)S(1)}, u32[]{:S(2)}, u32[]{:S(2)}) collective-permute-start(bf16[1312,128]{1,0:T(8,128)(2,1)S(1)} %copy-done.15), channel_id=1, source_target_pairs={{0,4},{1,5},{2,6},{3,7},{4,0},{5,1},{6,2},{7,3},{8,12},{9,13},{10,... | collective-permute-start | bytes 1007624 | tf_op jit(solution)/shard_map/ppermute | solution.py:679
  176.5 32.4 %collective-permute-start.28 = (bf16[1312,128]{1,0:T(8,128)(2,1)S(1)}, bf16[1312,128]{1,0:T(8,128)(2,1)S(1)}, u32[]{:S(2)}, u32[]{:S(2)}) collective-permute-start(bf16[1312,128]{1,0:T(8,128)(2,1)S(1)} %copy-done.15), channel_id=1, source_target_pairs={{0,2},{1,3},{2,0},{3,1},{4,6},{5,7},{6,4},{7,5},{8,10},{9,11},{10,... | collective-permute-start | bytes 1007624 | tf_op jit(solution)/shard_map/ppermute | solution.py:679
  178.1 31.3 %collective-permute-start.32 = (bf16[1312,128]{1,0:T(8,128)(2,1)S(1)}, bf16[1312,128]{1,0:T(8,128)(2,1)S(1)}, u32[]{:S(2)}, u32[]{:S(2)}) collective-permute-start(bf16[1312,128]{1,0:T(8,128)(2,1)S(1)} %collective-permute-done.30.refs_19_), channel_id=1, source_target_pairs={{0,2},{1,3},{2,0},{3,1},{4,6},{5,7},{6,4},{7,5},{8,10},{9,11},{10,... | collective-permute-start | bytes 1007624 | tf_op jit(solution)/shard_map/ppermute | solution.py:679
  191.9 22.6 %collective-permute-start.27 = (bf16[1312,128]{1,0:T(8,128)(2,1)S(1)}, bf16[1312,128]{1,0:T(8,128)(2,1)S(1)}, u32[]{:S(2)}, u32[]{:S(2)}) collective-permute-start(bf16[1312,128]{1,0:T(8,128)(2,1)S(1)} %copy-done.15), channel_id=1, source_target_pairs={{0,1},{1,0},{2,3},{3,2},{4,5},{5,4},{6,7},{7,6},{8,9},{9,8},{10,11... | collective-permute-start | bytes 1007624 | tf_op jit(solution)/shard_map/ppermute | solution.py:679
  207.4 14.4 %collective-permute-start.31 = (bf16[1312,128]{1,0:T(8,128)(2,1)S(1)}, bf16[1312,128]{1,0:T(8,128)(2,1)S(1)}, u32[]{:S(2)}, u32[]{:S(2)}) collective-permute-start(bf16[1312,128]{1,0:T(8,128)(2,1)S(1)} %collective-permute-done.30.refs_19_), channel_id=1, source_target_pairs={{0,1},{1,0},{2,3},{3,2},{4,5},{5,4},{6,7},{7,6},{8,9},{9,8},{10,11... | collective-permute-start | bytes 1007624 | tf_op jit(solution)/shard_map/ppermute | solution.py:679
  208.9 20.1 %collective-permute-start.29 = (bf16[1312,128]{1,0:T(8,128)(2,1)S(1)}, bf16[1312,128]{1,0:T(8,128)(2,1)S(1)}, u32[]{:S(2)}, u32[]{:S(2)}) collective-permute-start(bf16[1312,128]{1,0:T(8,128)(2,1)S(1)} %collective-permute-done.28.refs_17_), channel_id=1, source_target_pairs={{0,1},{1,0},{2,3},{3,2},{4,5},{5,4},{6,7},{7,6},{8,9},{9,8},{10,11... | collective-permute-start | bytes 1007624 | tf_op jit(solution)/shard_map/ppermute | solution.py:679
  209.4 25.6 %collective-permute-start.33 = (bf16[1312,128]{1,0:T(8,128)(2,1)S(1)}, bf16[1312,128]{1,0:T(8,128)(2,1)S(1)}, u32[]{:S(2)}, u32[]{:S(2)}) collective-permute-start(bf16[1312,128]{1,0:T(8,128)(2,1)S(1)} %collective-permute-done.32.refs_21_), channel_id=1, source_target_pairs={{0,1},{1,0},{2,3},{3,2},{4,5},{5,4},{6,7},{7,6},{8,9},{9,8},{10,11... | collective-permute-start | bytes 1007624 | tf_op jit(solution)/shard_map/ppermute | solution.py:679
  273.4 30.5 %collective-permute-start.59 = (bf16[8,656,128]{2,1,0:T(8,128)(2,1)}, bf16[8,656,128]{2,1,0:T(8,128)(2,1)S(1)}, u32[]{:S(2)}, u32[]{:S(2)}) collective-permute-start(bf16[8,656,128]{2,1,0:T(8,128)(2,1)} %get-tuple-element.99), channel_id=1, source_target_pairs={{0,16},{8,24},{16,0},{24,8},{1,17},{9,25},{17,1},{25,9},{2,18},{10... | collective-permute-start | bytes 4030472 | tf_op jit(solution)/shard_map/ppermute | solution.py:679
  274.8 45.2 %collective-permute-start.35 = (bf16[1024,1024]{1,0:T(8,128)(2,1)S(1)}, bf16[1024,1024]{1,0:T(8,128)(2,1)}, u32[]{:S(2)}, u32[]{:S(2)}) collective-permute-start(bf16[1024,1024]{1,0:T(8,128)(2,1)S(1)} %copy-done.13), channel_id=1, source_target_pairs={{0,8},{8,0},{16,24},{24,16},{1,9},{9,1},{17,25},{25,17},{2,10},{10... | collective-permute-start | bytes 6291464 | tf_op jit(solution)/shard_map/ppermute | solution.py:679
  305.7 26.4 %collective-permute-start.60 = (bf16[4,656,128]{2,1,0:T(8,128)(2,1)S(1)}, bf16[4,656,128]{2,1,0:T(8,128)(2,1)S(1)}, u32[]{:S(2)}, u32[]{:S(2)}) collective-permute-start(bf16[4,656,128]{2,1,0:T(8,128)(2,1)S(1)} %slice.111), channel_id=1, source_target_pairs={{0,1},{1,0},{2,3},{3,2},{4,5},{5,4},{6,7},{7,6},{8,9},{9,8},{10,11... | collective-permute-start | bytes 2015240 | tf_op jit(solution)/shard_map/ppermute | solution.py:679
  319.5 133.5 %collective-permute-start.54 = (bf16[2,4,128,1408]{3,2,1,0:T(8,128)(2,1)}, bf16[2,4,128,1408]{3,2,1,0:T(8,128)(2,1)}, u32[]{:S(2)}, u32[]{:S(2)}) collective-permute-start(bf16[2,4,128,1408]{3,2,1,0:T(8,128)(2,1)} %get-tuple-element.97), channel_id=1, source_target_pairs={{0,1},{1,0},{2,3},{3,2},{4,5},{5,4},{6,7},{7,6},{8,9},{9,8},{10,11... | collective-permute-start | bytes 8650760 | tf_op jit(solution)/shard_map/ppermute | solution.py:679
  330.7 38.7 %collective-permute-start.36 = (bf16[1024,256]{1,0:T(8,128)(2,1)}, bf16[1024,256]{1,0:T(8,128)(2,1)S(1)}, u32[]{:S(2)}, u32[]{:S(2)}) collective-permute-start(bf16[1024,256]{1,0:T(8,128)(2,1)} %get-tuple-element.78), channel_id=1, source_target_pairs={{0,16},{8,24},{16,0},{24,8},{1,17},{9,25},{17,1},{25,9},{2,18},{10... | collective-permute-start | bytes 1572872 | tf_op jit(solution)/shard_map/ppermute | solution.py:679
  333.0 78.0 %collective-permute-start.62 = (bf16[656,128]{1,0:T(8,128)(2,1)}, bf16[656,128]{1,0:T(8,128)(2,1)}, u32[]{:S(2)}, u32[]{:S(2)}) collective-permute-start(bf16[656,128]{1,0:T(8,128)(2,1)} %get-tuple-element.122), channel_id=1, source_target_pairs={{0,2},{1,3},{2,0},{3,1},{4,6},{5,7},{6,4},{7,5},{8,10},{9,11},{10,... | collective-permute-start | bytes 503816 | tf_op jit(solution)/shard_map/ppermute | solution.py:679
  333.7 90.7 %collective-permute-start.34 = (bf16[512,1024]{1,0:T(8,128)(2,1)}, bf16[512,1024]{1,0:T(8,128)(2,1)}, u32[]{:S(2)}, u32[]{:S(2)}) collective-permute-start(bf16[512,1024]{1,0:T(8,128)(2,1)} %get-tuple-element.71), channel_id=1, source_target_pairs={{0,8},{8,0},{16,24},{24,16},{1,9},{9,1},{17,25},{25,17},{2,10},{10... | collective-permute-start | bytes 3145736 | tf_op jit(solution)/shard_map/ppermute | solution.py:679
  333.7 78.7 %collective-permute-start.61 = (bf16[656,128]{1,0:T(8,128)(2,1)}, bf16[656,128]{1,0:T(8,128)(2,1)S(1)}, u32[]{:S(2)}, u32[]{:S(2)}) collective-permute-start(bf16[656,128]{1,0:T(8,128)(2,1)} %get-tuple-element.121), channel_id=1, source_target_pairs={{0,2},{1,3},{2,0},{3,1},{4,6},{5,7},{6,4},{7,5},{8,10},{9,11},{10,... | collective-permute-start | bytes 503816 | tf_op jit(solution)/shard_map/ppermute | solution.py:679
  369.4 65.0 %collective-permute-start.49 = (bf16[8,256,128]{2,1,0:T(8,128)(2,1)}, bf16[8,256,128]{2,1,0:T(8,128)(2,1)}, u32[]{:S(2)}, u32[]{:S(2)}) collective-permute-start(bf16[8,256,128]{2,1,0:T(8,128)(2,1)} %get-tuple-element.93), channel_id=1, source_target_pairs={{0,16},{8,24},{16,0},{24,8},{1,17},{9,25},{17,1},{25,9},{2,18},{10... | collective-permute-start | bytes 1572872 | tf_op jit(solution)/shard_map/ppermute | solution.py:679
  432.6 19.8 %collective-permute-start.44 = (f32[2,1024]{1,0:T(2,128)S(1)}, f32[2,1024]{1,0:T(2,128)S(1)}, u32[]{:S(2)}, u32[]{:S(2)}) collective-permute-start(f32[2,1024]{1,0:T(2,128)S(1)} %add.157), channel_id=1, source_target_pairs={{0,4},{1,5},{2,6},{3,7},{4,0},{5,1},{6,2},{7,3},{8,12},{9,13},{10,... | collective-permute-start | bytes 24584 | tf_op jit(solution)/shard_map/ppermute | solution.py:679
  451.9 23.7 %collective-permute-start.45 = (bf16[4,128,768]{2,1,0:T(8,128)(2,1)S(1)}, bf16[4,128,768]{2,1,0:T(8,128)(2,1)S(1)}, u32[]{:S(2)}, u32[]{:S(2)}) collective-permute-start(bf16[4,128,768]{2,1,0:T(8,128)(2,1)S(1)} %copy-done.41), channel_id=1, source_target_pairs={{0,1},{1,0},{2,3},{3,2},{4,5},{5,4},{6,7},{7,6},{8,9},{9,8},{10,11... | collective-permute-start | bytes 2359304 | tf_op jit(solution)/shard_map/ppermute | solution.py:679
  452.4 65.8 %collective-permute-start.37 = (bf16[1,512,1024]{2,1,0:T(8,128)(2,1)S(1)}, bf16[1,512,1024]{2,1,0:T(8,128)(2,1)}, u32[]{:S(2)}, u32[]{:S(2)}) collective-permute-start(bf16[1,512,1024]{2,1,0:T(8,128)(2,1)S(1)} %copy-done.16), channel_id=1, source_target_pairs={{0,8},{8,0},{16,24},{24,16},{1,9},{9,1},{17,25},{25,17},{2,10},{10... | collective-permute-start | bytes 3145736 | tf_op jit(solution)/shard_map/ppermute | solution.py:679
  452.4 38.6 %collective-permute-start.38 = (bf16[1,512,1024]{2,1,0:T(8,128)(2,1)}, bf16[1,512,1024]{2,1,0:T(8,128)(2,1)S(1)}, u32[]{:S(2)}, u32[]{:S(2)}) collective-permute-start(bf16[1,512,1024]{2,1,0:T(8,128)(2,1)} %back_project.7), channel_id=1, source_target_pairs={{0,8},{8,0},{16,24},{24,16},{1,9},{9,1},{17,25},{25,17},{2,10},{10... | collective-permute-start | bytes 3145736 | tf_op jit(solution)/shard_map/ppermute | solution.py:679
  455.7 33.9 %collective-permute-start.55 = (bf16[4,128,1408]{2,1,0:T(8,128)(2,1)S(1)}, bf16[4,128,1408]{2,1,0:T(8,128)(2,1)S(1)}, u32[]{:S(2)}, u32[]{:S(2)}) collective-permute-start(bf16[4,128,1408]{2,1,0:T(8,128)(2,1)S(1)} %slice_bitcast_fusion), channel_id=1, source_target_pairs={{0,16},{8,24},{16,0},{24,8},{1,17},{9,25},{17,1},{25,9},{2,18},{10... | collective-permute-start | bytes 4325384 | tf_op jit(solution)/shard_map/ppermute | solution.py:679
  464.0 40.8 %collective-permute-start.51 = (bf16[256,128]{1,0:T(8,128)(2,1)S(1)}, bf16[256,128]{1,0:T(8,128)(2,1)S(1)}, u32[]{:S(2)}, u32[]{:S(2)}) collective-permute-start(bf16[256,128]{1,0:T(8,128)(2,1)S(1)} %get-tuple-element.123), channel_id=1, source_target_pairs={{0,2},{1,3},{2,0},{3,1},{4,6},{5,7},{6,4},{7,5},{8,10},{9,11},{10,... | collective-permute-start | bytes 196616 | tf_op jit(solution)/shard_map/ppermute | solution.py:679
  475.6 32.1 %collective-permute-start.53 = (bf16[256,128]{1,0:T(8,128)(2,1)S(1)}, bf16[256,128]{1,0:T(8,128)(2,1)S(1)}, u32[]{:S(2)}, u32[]{:S(2)}) collective-permute-start(bf16[256,128]{1,0:T(8,128)(2,1)S(1)} %fusion.12), channel_id=1, source_target_pairs={{0,4},{1,5},{2,6},{3,7},{4,0},{5,1},{6,2},{7,3},{8,12},{9,13},{10,... | collective-permute-start | bytes 196616 | tf_op jit(solution)/shard_map/ppermute | solution.py:679
  497.4 22.5 %collective-permute-start.39 = (bf16[1,512,1024]{2,1,0:T(8,128)(2,1)}, bf16[1,512,1024]{2,1,0:T(8,128)(2,1)}, u32[]{:S(2)}, u32[]{:S(2)}) collective-permute-start(bf16[1,512,1024]{2,1,0:T(8,128)(2,1)} %add_convert_fusion.2), channel_id=1, source_target_pairs={{0,16},{8,24},{16,0},{24,8},{1,17},{9,25},{17,1},{25,9},{2,18},{10... | collective-permute-start | bytes 3145736 | tf_op jit(solution)/shard_map/ppermute | solution.py:679
  503.6 12.7 %collective-permute-start.46 = (bf16[128,768]{1,0:T(8,128)(2,1)S(1)}, bf16[128,768]{1,0:T(8,128)(2,1)S(1)}, u32[]{:S(2)}, u32[]{:S(2)}) collective-permute-start(bf16[128,768]{1,0:T(8,128)(2,1)S(1)} %get-tuple-element.119), channel_id=1, source_target_pairs={{0,2},{1,3},{2,0},{3,1},{4,6},{5,7},{6,4},{7,5},{8,10},{9,11},{10,... | collective-permute-start | bytes 589832 | tf_op jit(solution)/shard_map/ppermute | solution.py:679
  507.7 19.0 %collective-permute-start.56 = (bf16[128,1408]{1,0:T(8,128)(2,1)}, bf16[128,1408]{1,0:T(8,128)(2,1)S(1)}, u32[]{:S(2)}, u32[]{:S(2)}) collective-permute-start(bf16[128,1408]{1,0:T(8,128)(2,1)} %get-tuple-element.116), channel_id=1, source_target_pairs={{0,2},{1,3},{2,0},{3,1},{4,6},{5,7},{6,4},{7,5},{8,10},{9,11},{10,... | collective-permute-start | bytes 1081352 | tf_op jit(solution)/shard_map/ppermute | solution.py:679
  516.4 15.9 %collective-permute-start.58 = (bf16[128,1408]{1,0:T(8,128)(2,1)}, bf16[128,1408]{1,0:T(8,128)(2,1)S(1)}, u32[]{:S(2)}, u32[]{:S(2)}) collective-permute-start(bf16[128,1408]{1,0:T(8,128)(2,1)} %fusion.3), channel_id=1, source_target_pairs={{0,4},{1,5},{2,6},{3,7},{4,0},{5,1},{6,2},{7,3},{8,12},{9,13},{10,... | collective-permute-start | bytes 1081352 | tf_op jit(solution)/shard_map/ppermute | solution.py:679
  (59 other events, 1238.6 us)

commit v2 on v1

v2 whole, which is shorter than its diff:
```python
from functools import partial
import math

import jax
import jax.numpy as jnp
from jax import lax
from jax.experimental import pallas as pl
from jax.experimental.pallas import tpu as pltpu
from jax.sharding import PartitionSpec as P

HEADS = 16
HD = 64
FF = 2624

epsilon = 1e-05
rope_base = 160000.0

f32 = jnp.float32
bf16 = jnp.bfloat16

WIDTH = 1024
HALF = FF // 2
PADDED = 1408
BLOCK = FF // 4
COLS = 256
CHUNKS = (0, 4, 2, 6, 1, 5, 3, 7)
EXTRA = 16
ROWS_BY_COLS = (((0,), (0,)), ((), ()))
COLS_BY_COLS = (((1,), (1,)), ((), ()))
VMEM_LIMIT = 58 * 1024 * 1024

ANY = pl.BlockSpec(memory_space=pl.ANY)
SMEM = pl.BlockSpec(memory_space=pltpu.SMEM)


def cost(micros):
    return pl.CostEstimate(flops=int(micros), transcendentals=0, bytes_accessed=int(micros))


def params():
    return pltpu.CompilerParams(vmem_limit_bytes=VMEM_LIMIT)


def sds(shape, dtype=bf16):
    return jax.ShapeDtypeStruct(shape, dtype)


def aligned(index, size):
    return pl.ds(pl.multiple_of(index * size, size), size)


def normalize(values):
    center = values - jnp.mean(values, axis=-1, keepdims=True)
    inv_scale = lax.rsqrt(jnp.mean(center * center, axis=-1, keepdims=True) + epsilon)
    return center * inv_scale, inv_scale


def norm_back(grads, xhat, inv_scale):
    mean_grad = jnp.mean(grads, axis=-1, keepdims=True)
    mean_both = jnp.mean(grads * xhat, axis=-1, keepdims=True)
    return inv_scale * (grads - mean_grad - xhat * mean_both)


def turned(values):
    lane = lax.broadcasted_iota(jnp.int32, values.shape, 1)
    width = values.shape[1]
    return jnp.where(
        lane % HD < HD // 2, pltpu.roll(values, width - HD // 2, 1), pltpu.roll(values, HD // 2, 1)
    )


def twice(table):
    return jnp.concatenate([table, table], axis=1)


def piece_of(refs, place, rows=None, width=None):
    array, lead, column = place
    index = () if lead is None else (lead,)
    rows = slice(None) if rows is None else rows
    cols = slice(None) if width is None else pl.ds(column, width)
    return refs[array].at[(*index, rows, cols)]


def fetch_rows(count, shard, refs, places, width, target, sem):
    size = target.shape[0] // count
    copies = []
    for r in range(count):
        rows = aligned(jnp.bitwise_xor(shard, r), size) if count > 1 else pl.ds(0, size)
        copies.append(
            pltpu.make_async_copy(piece_of(refs, places[r], width=width), target.at[rows], sem.at[r])
        )
    return copies


def qkv_kernel(count, places, idx, *refs):
    x_refs, refs = refs[:4], refs[4:]
    n_arrays = 1 + max(array for array, _, _ in places)
    w_refs, refs = refs[:n_arrays], refs[n_arrays:]
    if count == 1:
        gain_ref, refs = refs[0], refs[1:]
    cos_ref, sin_ref, fn_o, q_o, k_o, v_o, w_o, g_o, xs, gs, semx, semw, semg = refs
    step = pl.program_id(0)
    shard = idx[0]
    size = WIDTH // count

    def x_copy(r):
        return pltpu.make_async_copy(x_refs[r], xs.at[r], semx.at[r])

    def w_copy(r):
        return pltpu.make_async_copy(
            piece_of(w_refs, places[r], rows=pl.ds(0, size)), w_o.at[aligned(jnp.bitwise_xor(shard, r), size)], semw.at[r]
        )

    def g_copy(r):
        return pltpu.make_async_copy(
            piece_of(w_refs, places[r], rows=pl.ds(size, EXTRA)), gs.at[jnp.bitwise_xor(shard, r)], semg.at[r]
        )

    @pl.when(step == 0)
    def _():
        if count == 1:
            w_all = pltpu.make_async_copy(w_refs[0], w_o, semw.at[0])
            w_all.start()
        else:
            for r in range(count):
                w_copy(r).start()
                g_copy(r).start()
        for r in range(4):
            x_copy(r).start()
        if count == 1:
            w_all.wait()
            g_o[0:1] = gain_ref[0:1].astype(f32)
            g_o[1:2] = gain_ref[1:2].astype(f32)
        else:
            for r in range(count):
                w_copy(r).wait()
                g_copy(r).wait()
            for r in range(count):
                part = gs[r].astype(f32)
                g_o[0:1, r * size : (r + 1) * size] = part[0:1, 0:size]
                g_o[1:2, r * size : (r + 1) * size] = part[0:1, size : 2 * size]

    for r in range(4):

        @pl.when(step == r)
        def _():
            x_copy(r).wait()

    xhat, _ = normalize(xs[step].astype(f32))
    first_low = (xhat * g_o[0:1]).astype(bf16)
    fn_o[...] = first_low
    cosine, sine = twice(cos_ref[...]), twice(sin_ref[...])
    outs = (q_o, k_o, v_o)
    for part in range(3):
        value = jnp.dot(first_low, w_o[:, part * COLS : (part + 1) * COLS], preferred_element_type=f32)
        if part < 2:
            value = value * cosine + turned(value) * sine
        value = value.astype(bf16)
        if part == 0:
            value = value * jnp.asarray(1.0 / math.sqrt(HD), bf16)
        outs[part][...] = value


def qkv_call(count, idx, chunks, pieces, gains, cosine, sine):
    arrays, where = pieces
    rows = chunks[0].shape[0]
    by_step = lambda width: pl.BlockSpec((rows, width), lambda r: (r, 0))
    whole = lambda shape: pl.BlockSpec(shape, lambda r: (0, 0))
    extra = [] if count > 1 else [gains]
    return pl.pallas_call(
        partial(qkv_kernel, count, where),
        grid=(4,),
        in_specs=[SMEM]
        + [ANY] * (4 + len(arrays))
        + ([] if count > 1 else [whole((2, WIDTH))])
        + [by_step(128), by_step(128)],
        out_specs=[
            by_step(WIDTH),
            by_step(COLS),
            by_step(COLS),
            by_step(COLS),
            whole((WIDTH, 3 * COLS)),
            whole((8, WIDTH)),
        ],
        out_shape=[
            sds((4 * rows, WIDTH)),
            sds((4 * rows, COLS)),
            sds((4 * rows, COLS)),
            sds((4 * rows, COLS)),
            sds((WIDTH, 3 * COLS)),
            sds((8, WIDTH), f32),
        ],
        scratch_shapes=[
            pltpu.VMEM((4, rows, WIDTH), bf16),
            pltpu.VMEM((8, EXTRA, 3 * COLS), bf16),
            pltpu.SemaphoreType.DMA((4,)),
            pltpu.SemaphoreType.DMA((count,)),
            pltpu.SemaphoreType.DMA((count,)),
        ],
        compiler_params=params(),
        cost_estimate=cost(11),
        name="project",
    )(idx, *chunks, *arrays, *extra, cosine, sine)


def head_of(shape):
    return lax.broadcasted_iota(jnp.int32, shape, len(shape) - 1) // HD


def attend_kernel(q_ref, k_ref, v_ref, o_ref, lse_ref):
    q, k, v = q_ref[...], k_ref[...], v_ref[...]
    heads = head_of(q.shape)
    total = jnp.zeros(q.shape, f32)
    lses = jnp.zeros((q.shape[0], 128), f32)
    lane = lax.broadcasted_iota(jnp.int32, lses.shape, 1)
    for h in range(COLS // HD):
        q_h = jnp.where(heads == h, q, jnp.zeros_like(q))
        scores = lax.dot_general(q_h, k, COLS_BY_COLS, preferred_element_type=f32)
        row_max = jnp.max(scores, axis=1, keepdims=True)
        exponent = jnp.exp(scores - row_max)
        row_total = jnp.sum(exponent, axis=1, keepdims=True)
        context = jnp.dot(exponent.astype(bf16), v, preferred_element_type=f32)
        total = jnp.where(heads == h, context * (1.0 / row_total), total)
        lses = jnp.where(lane == h, row_max + jnp.log(row_total), lses)
    o_ref[...] = total.astype(bf16)
    lse_ref[...] = lses.T[:8]


def attend(q, k, v, chunk, after=()):
    span = k.shape[0]
    rows = span // 4
    kept = pl.BlockSpec((span, COLS), lambda i: (0, 0))
    return pl.pallas_call(
        lambda *refs: attend_kernel(*refs[:3], *refs[3 + len(after) :]),
        grid=(1,),
        in_specs=[pl.BlockSpec((rows, COLS), lambda i: (chunk, 0)), kept, kept] + [ANY] * len(after),
        out_specs=[
            pl.BlockSpec((rows, COLS), lambda i: (0, 0)),
            pl.BlockSpec((8, rows), lambda i: (0, 0)),
        ],
        out_shape=[sds((rows, COLS)), sds((8, rows), f32)],
        compiler_params=params(),
        cost_estimate=cost(8),
        name="attend",
    )(q, k, v, *after)


def attend_back_kernel(last, pair, *refs):
    q_ref, do_ref, oa_ref, ob_ref, la_ref, lb_ref, k_ref, v_ref, qcos, qsin, refs = *refs[:10], refs[10:]
    if last:
        dk_i, dv_i, kcos, ksin, refs = *refs[:4], refs[4:]
    dq_ref, dk_ref, dv_ref, do_s, inner_s, lse_s, dq_s = refs
    step = pl.program_id(0)
    width = q_ref.shape[1]
    n_heads = width // HD

    @pl.when(step == 0)
    def _():
        do = do_ref[...]
        context = jnp.concatenate([oa_ref[...], ob_ref[...]], axis=0)
        product = do.astype(f32) * context.astype(f32)
        high = product.astype(bf16)
        rest = (product - high.astype(f32)).astype(bf16)
        chosen = (
            head_of((8, width)) == lax.broadcasted_iota(jnp.int32, (8, width), 0)
        ).astype(bf16)
        inner_s[...] = lax.dot_general(
            chosen, high, COLS_BY_COLS, preferred_element_type=f32
        ) + lax.dot_general(chosen, rest, COLS_BY_COLS, preferred_element_type=f32)
        lse_s[...] = jnp.concatenate([la_ref[...], lb_ref[...]], axis=1)
        heads = head_of(do.shape)
        for h in range(n_heads):
            do_s[h] = jnp.where(heads == h, do, jnp.zeros_like(do))
        dq_s[...] = jnp.zeros_like(dq_s)

    q, k, v = q_ref[...], k_ref[...], v_ref[...]
    heads = head_of(k.shape)
    dk = jnp.zeros(k.shape, f32)
    dv = jnp.zeros(k.shape, f32)
    dq = dq_s[...]
    for h in range(n_heads):
        at = n_heads * pair + h
        k_h = jnp.where(heads == h, k, jnp.zeros_like(k))
        scores = lax.dot_general(k_h, q, COLS_BY_COLS, preferred_element_type=f32)
        probs = jnp.exp(scores - lse_s[at : at + 1, :])
        probs_grad = lax.dot_general(v, do_s[h], COLS_BY_COLS, preferred_element_type=f32)
        scores_grad = (probs * (probs_grad - inner_s[h : h + 1, :])).astype(bf16)
        dv = dv + jnp.dot(probs.astype(bf16), do_s[h], preferred_element_type=f32)
        dk = jnp.where(heads == h, jnp.dot(scores_grad, q, preferred_element_type=f32), dk)
        dq = dq + lax.dot_general(scores_grad, k_h, ROWS_BY_COLS, preferred_element_type=f32)
    dq_s[...] = dq
    if last:
        dk = dk + dk_i[...]
        dv = dv + dv_i[...]
        dk_ref[...] = (dk * kcos[...] - turned(dk) * ksin[...]).astype(bf16)
        dv_ref[...] = dv.astype(bf16)
    else:
        dk_ref[...] = dk
        dv_ref[...] = dv

    @pl.when(step == pl.num_programs(0) - 1)
    def _():
        dq = dq_s[...] * (1.0 / math.sqrt(HD))
        dq_ref[...] = (dq * qcos[...] - turned(dq) * qsin[...]).astype(bf16)


def attend_back(part, pair, q, do, contexts, lses, k, v, cosine, sine, earlier=None, after=(), tile=512):
    span = k.shape[0]
    rows = do.shape[0]
    last = earlier is not None
    rows_at = lambda at, col, count=rows, width=128: pl.BlockSpec((count, width), lambda i: (at, col))
    keys = lambda col: pl.BlockSpec((tile, 128), lambda i: (i, col))
    grads = bf16 if last else f32
    n_in = 10 + (4 if last else 0)
    return pl.pallas_call(
        lambda *refs: attend_back_kernel(last, pair, *refs[:n_in], *refs[n_in + len(after) :]),
        grid=(span // tile,),
        in_specs=[
            rows_at(part, pair),
            rows_at(0, pair),
            rows_at(0, pair, rows // 2),
            rows_at(0, pair, rows // 2),
            rows_at(0, 0, 8, rows // 2),
            rows_at(0, 0, 8, rows // 2),
            keys(pair),
            keys(pair),
            rows_at(part, 0),
            rows_at(part, 0),
        ]
        + ([keys(0), keys(0), keys(0), keys(0)] if last else [])
        + [ANY] * len(after),
        out_specs=[rows_at(0, 0), keys(0), keys(0)],
        out_shape=[sds((rows, 128)), sds((span, 128), grads), sds((span, 128), grads)],
        scratch_shapes=[
            pltpu.VMEM((128 // HD, rows, 128), bf16),
            pltpu.VMEM((8, rows), f32),
            pltpu.VMEM((8, rows), f32),
            pltpu.VMEM((rows, 128), f32),
        ],
        compiler_params=params(),
        cost_estimate=cost(15),
        name="attend_back",
    )(q, do, *contexts, *lses, k, v, cosine, sine, *((*earlier, cosine, sine) if last else ()), *after)


def out_kernel(count, places, idx, ma_ref, mb_ref, other_ref, *refs):
    w_refs, (o_ref, wsel_ref, w_s, sem) = refs[:-4], refs[-4:]
    copies = fetch_rows(count, idx[0], w_refs, places, WIDTH, w_s, sem)
    for copy in copies:
        copy.start()
    for copy in copies:
        copy.wait()
    seq = idx[1]
    wsel_ref[0:COLS] = w_s[aligned(seq, COLS)]
    wsel_ref[COLS:] = w_s[aligned(jnp.bitwise_xor(seq, 2), COLS)]
    rows = ma_ref.shape[0]
    for r, mine in enumerate((ma_ref, mb_ref)):
        both = jnp.concatenate([mine[...], other_ref[r * rows : (r + 1) * rows]], axis=1)
        value = jnp.dot(both, wsel_ref[...], preferred_element_type=f32)
        o_ref[r * rows : (r + 1) * rows] = value.astype(bf16)


def out_call(count, idx, mine, other, pieces):
    vmem = pl.BlockSpec(memory_space=pltpu.VMEM)
    arrays, where = pieces
    return pl.pallas_call(
        partial(out_kernel, count, where),
        in_specs=[SMEM] + [vmem] * 3 + [ANY] * len(arrays),
        out_specs=[vmem, vmem],
        out_shape=[sds((2 * mine[0].shape[0], WIDTH)), sds((2 * COLS, WIDTH))],
        scratch_shapes=[pltpu.VMEM((WIDTH, WIDTH), bf16), pltpu.SemaphoreType.DMA((count,))],
        compiler_params=params(),
        cost_estimate=cost(5),
        name="out_project",
    )(idx, *mine, other, *arrays)


def mlp_kernel(count, n_arrays, mine, other, down, idx, *refs):
    x0, x1, po, pr, c0, c1, g_ref, refs = *refs[:7], refs[7:]
    w_refs, refs = refs[:n_arrays], refs[n_arrays:]
    sn_o, hid_o, gug_o, sgp_o, wd_o, refs = *refs[:5], refs[5:]
    xs, pos, prs, cs, wi, wd, sn_s, hid_s, gug_s, sgp_s, sem_a, sem_m, sem_i, sem_d, sem_o = refs
    shard, x_place = idx[0], idx[2]
    rows = xs.shape[1]
    loads = [
        pltpu.make_async_copy(x0, xs.at[0], sem_a.at[0]),
        pltpu.make_async_copy(x1, xs.at[1], sem_a.at[1]),
        pltpu.make_async_copy(po, pos, sem_a.at[2]),
        pltpu.make_async_copy(pr, prs, sem_a.at[3]),
        pltpu.make_async_copy(c0, cs.at[pl.ds(0, rows)], sem_a.at[4]),
        pltpu.make_async_copy(c1, cs.at[pl.ds(rows, rows)], sem_a.at[5]),
    ]
    here = wi.at[:, aligned(x_place, PADDED)]
    there = wi.at[:, aligned(1 - x_place, PADDED)]
    wi_loads = fetch_rows(count, shard, w_refs, mine, PADDED, here, sem_m)
    wi_loads += fetch_rows(count, shard, w_refs, other, PADDED, there, sem_i)
    wd_loads = fetch_rows(count, shard, w_refs, down, PADDED, wd, sem_d)
    for copy in loads[:4] + wi_loads + loads[4:] + wd_loads:
        copy.start()
    for copy in loads[:4]:
        copy.wait()
    for r in range(2):
        here, there = pl.ds(r * rows, rows), pl.ds((1 - r) * rows, rows)
        after = xs[r].astype(f32) + pos[here].astype(f32) + prs[there].astype(f32)
        xhat, _ = normalize(after)
        sn_s[here] = (xhat * g_ref[1:2]).astype(bf16)
    stores = []

    def store(source, target, k):
        copy = pltpu.make_async_copy(source, target, sem_o.at[k])
        copy.start()
        stores.append(copy)

    store(sn_s, sn_o, 0)
    for copy in wi_loads + loads[4:] + wd_loads:
        copy.wait()
    store(wd, wd_o, 1)
    start = 0
    while start < PADDED:
        size = min(256, PADDED - start)
        here = pl.ds(start, size)
        gate = jnp.dot(sn_s[...], wi[:, here], preferred_element_type=f32)
        up = jnp.dot(sn_s[...], wi[:, pl.ds(PADDED + start, size)], preferred_element_type=f32)
        back = jnp.dot(cs[...], wd[:, here], preferred_element_type=f32)
        below = 0.5 * (1.0 + lax.erf(gate * math.sqrt(0.5)))
        density = jnp.exp(-0.5 * gate * gate) * (1.0 / math.sqrt(2.0 * math.pi))
        unit = gate * below
        hid_s[:, here] = (unit * up).astype(bf16)
        gug_s[0, :, here] = (back * up * (below + gate * density)).astype(bf16)
        gug_s[1, :, here] = (back * unit).astype(bf16)
        start += size
    store(hid_s, hid_o, 2)
    store(gug_s, gug_o, 3)
    value = lax.dot_general(gug_s[0], wi[:, :PADDED], COLS_BY_COLS, preferred_element_type=f32)
    value = value + lax.dot_general(gug_s[1], wi[:, PADDED:], COLS_BY_COLS, preferred_element_type=f32)
    sgp_s[...] = value.astype(bf16)
    store(sgp_s, sgp_o, 4)
    for copy in stores:
        copy.wait()


def mlp_call(count, idx, x0, x1, po, pr, c0, c1, gains, arrays, mine, other, down):
    rows = x0.shape[0]
    return pl.pallas_call(
        partial(mlp_kernel, count, len(arrays), mine, other, down),
        in_specs=[SMEM] + [ANY] * 6 + [pl.BlockSpec(memory_space=pltpu.VMEM)] + [ANY] * len(arrays),
        out_specs=[ANY] * 5,
        out_shape=[
            sds((2 * rows, WIDTH)),
            sds((2 * rows, PADDED)),
            sds((2, 2 * rows, PADDED)),
            sds((2 * rows, WIDTH)),
            sds((WIDTH, PADDED)),
        ],
        scratch_shapes=[
            pltpu.VMEM((2, rows, WIDTH), bf16),
            pltpu.VMEM((2 * rows, WIDTH), bf16),
            pltpu.VMEM((2 * rows, WIDTH), bf16),
            pltpu.VMEM((2 * rows, WIDTH), bf16),
            pltpu.VMEM((WIDTH, 2 * PADDED), bf16),
            pltpu.VMEM((WIDTH, PADDED), bf16),
            pltpu.VMEM((2 * rows, WIDTH), bf16),
            pltpu.VMEM((2 * rows, PADDED), bf16),
            pltpu.VMEM((2, 2 * rows, PADDED), bf16),
            pltpu.VMEM((2 * rows, WIDTH), bf16),
            pltpu.SemaphoreType.DMA((6,)),
            pltpu.SemaphoreType.DMA((count,)),
            pltpu.SemaphoreType.DMA((count,)),
            pltpu.SemaphoreType.DMA((count,)),
            pltpu.SemaphoreType.DMA((5,)),
        ],
        compiler_params=params(),
        cost_estimate=cost(25),
        name="feed_forward",
    )(idx, x0, x1, po, pr, c0, c1, gains, *arrays)


def down_kernel(count, idx, hid_ref, wd_ref, c0, c1, ma, mb, other, low, res_other, res_mine, keep_o, send_o, acc):
    shard, x_place = idx[0], idx[2]
    rows = c0.shape[0]
    width = WIDTH // count
    places = [
        aligned(jnp.bitwise_xor(shard, r), width) if count > 1 else pl.ds(0, width) for r in CHUNKS[:count]
    ]
    acc[...] = lax.dot_general(
        hid_ref[0:rows], c0[...], ROWS_BY_COLS, preferred_element_type=f32
    ) + lax.dot_general(hid_ref[rows:], c1[...], ROWS_BY_COLS, preferred_element_type=f32)
    for part, target in ((1, send_o), (0, keep_o)):
        here = pl.ds(pl.multiple_of(jnp.bitwise_xor(x_place, part) * BLOCK, 8), BLOCK)
        for r in range(count):
            target[r, 0:BLOCK] = acc[here, places[r]].astype(bf16)
    mine = jnp.concatenate([ma[...], mb[...]], axis=0)
    for context, target in ((other[...], send_o), (mine, keep_o)):
        acc[0:COLS] = lax.dot_general(context, low[...], ROWS_BY_COLS, preferred_element_type=f32)
        for r in range(count):
            target[r, BLOCK:] = acc[0:COLS, places[r]].astype(bf16)
    for r, target in ((1, res_other), (0, res_mine)):
        target[...] = lax.dot_general(
            hid_ref[r * rows : (r + 1) * rows], wd_ref[...], COLS_BY_COLS, preferred_element_type=f32
        ).astype(bf16)


def down_call(count, idx, hidden, wd, c0, c1, mine, other, low):
    rows = c0.shape[0]
    vmem = pl.BlockSpec(memory_space=pltpu.VMEM)
    return pl.pallas_call(
        partial(down_kernel, count),
        in_specs=[SMEM] + [vmem] * 8,
        out_specs=[vmem] * 4,
        out_shape=[
            sds((rows, WIDTH)),
            sds((rows, WIDTH)),
            sds((count, BLOCK + COLS, WIDTH // count)),
            sds((count, BLOCK + COLS, WIDTH // count)),
        ],
        scratch_shapes=[pltpu.VMEM((PADDED, WIDTH), f32)],
        compiler_params=params(),
        cost_estimate=cost(15),
        name="down_project",
    )(idx, hidden, wd, c0, c1, *mine, other, low)


def norm_two_kernel(x0, x1, po, pr, so, sr, c0, c1, g_ref, wsel, res_o, low_o, mine_o, other_o, gain_o):
    step = pl.program_id(0)
    half = pl.num_programs(0) // 2
    first = step < half
    gain = g_ref[1:2]
    x = jnp.where(first, x0[...], x1[...])
    c = jnp.where(first, c0[...], c1[...])
    after = x.astype(f32) + po[...].astype(f32) + pr[...].astype(f32)
    xhat, inv_scale = normalize(after)
    second = so[...].astype(f32) + sr[...].astype(f32)
    res = c.astype(f32) + norm_back(second * gain, xhat, inv_scale)

    @pl.when(step == 0)
    def _():
        gain_o[...] = jnp.zeros_like(gain_o)

    @pl.when(first)
    def _():
        res_o[...] = res
        gain_o[...] += jnp.sum(second * xhat, axis=0, keepdims=True)

    low = res.astype(bf16)
    low_o[...] = low
    value = lax.dot_general(low, wsel[...], COLS_BY_COLS, preferred_element_type=f32).astype(bf16)
    mine_o[...] = value[:, :COLS]
    other_o[...] = value[:, COLS:]


def norm_two_call(x0, x1, po, pr, so, sr, c0, c1, gains, wsel, half=2):
    rows = x0.shape[0]
    size = rows // half
    spec = lambda width, at: pl.BlockSpec((size, width), lambda s: (at(s), 0))
    lower = lambda s: jnp.minimum(s, half - 1)
    upper = lambda s: jnp.maximum(s - half, 0)
    same = lambda s: s
    other = lambda s: lax.rem(s + half, 2 * half)
    whole = lambda shape: pl.BlockSpec(shape, lambda s: (0, 0))
    return pl.pallas_call(
        norm_two_kernel,
        grid=(2 * half,),
        in_specs=[
            spec(WIDTH, lower),
            spec(WIDTH, upper),
            spec(WIDTH, same),
            spec(WIDTH, other),
            spec(WIDTH, same),
            spec(WIDTH, other),
            spec(WIDTH, lower),
            spec(WIDTH, upper),
            whole((8, WIDTH)),
            whole((2 * COLS, WIDTH)),
        ],
        out_specs=[
            spec(WIDTH, lower),
            spec(WIDTH, same),
            spec(COLS, same),
            spec(COLS, same),
            whole((8, WIDTH)),
        ],
        out_shape=[
            sds((rows, WIDTH), f32),
            sds((2 * rows, WIDTH)),
            sds((2 * rows, COLS)),
            sds((2 * rows, COLS)),
            sds((8, WIDTH), f32),
        ],
        compiler_params=params(),
        cost_estimate=cost(8),
        name="norm_two_back",
    )(x0, x1, po, pr, so, sr, c0, c1, gains, wsel)


def wide_kernel(count, idx, sn_ref, gug_ref, *refs):
    outs, acc = refs[:-1], refs[-1]
    part = pl.program_id(0)
    shard = idx[0]
    acc[...] = lax.dot_general(sn_ref[...], gug_ref[0], ROWS_BY_COLS, preferred_element_type=f32)
    size = WIDTH // count
    per_array = count // len(outs)
    for k, r in enumerate(CHUNKS[:count]):
        place = aligned(jnp.bitwise_xor(shard, r), size) if count > 1 else pl.ds(0, size)
        outs[k // per_array][0, k % per_array] = acc[place].astype(bf16)


def wide_call(count, idx, sn, gug):
    tokens = sn.shape[0]
    split = 2 if count > 1 else 1
    size = WIDTH // count
    spec = lambda shape, at: pl.BlockSpec(shape, at)
    grid_spec = pltpu.PrefetchScalarGridSpec(
        num_scalar_prefetch=1,
        grid=(2,),
        in_specs=[
            spec((tokens, WIDTH), lambda p, s: (0, 0)),
            spec((1, tokens, PADDED), lambda p, s: (jnp.bitwise_xor(p, s[2]), 0, 0)),
        ],
        out_specs=[spec((1, count // split, size, PADDED), lambda p, s: (p, 0, 0, 0))] * split,
        scratch_shapes=[pltpu.VMEM((WIDTH, PADDED), f32)],
    )
    return pl.pallas_call(
        partial(wide_kernel, count),
        grid_spec=grid_spec,
        out_shape=[sds((2, count // split, size, PADDED))] * split,
        compiler_params=params(),
        cost_estimate=cost(12),
        name="wide_grad",
    )(idx, sn, gug)


def back_project_kernel(q0, q1, f0, f1, k0n, k1n, k0f, k1f, v0n, v1n, v0f, v1f, w_ref, both_o):
    for half, parts in (
        (1, (f0, f1, k0f, k1f, v0f, v1f)),
        (0, (q0, q1, k0n, k1n, v0n, v1n)),
    ):
        raw = jnp.concatenate([part[...] for part in parts], axis=1)
        both_o[half] = lax.dot_general(
            raw, w_ref[...], COLS_BY_COLS, preferred_element_type=f32
        ).astype(bf16)


def back_project(raw_pairs, w, chunk):
    rows = raw_pairs[0][0].shape[0] // 2
    at = lambda where: pl.BlockSpec((rows, 128), lambda i: (where, 0))
    q0, f0, k0, v0 = raw_pairs[0]
    q1, f1, k1, v1 = raw_pairs[1]
    return pl.pallas_call(
        back_project_kernel,
        grid=(1,),
        in_specs=[at(chunk)] * 6
        + [at(chunk + 2)] * 2
        + [at(chunk)] * 2
        + [at(chunk + 2)] * 2
        + [pl.BlockSpec((WIDTH, 3 * COLS), lambda i: (0, 0))],
        out_specs=pl.BlockSpec((2, rows, WIDTH), lambda i: (0, 0, 0)),
        out_shape=sds((2, rows, WIDTH)),
        compiler_params=params(),
        cost_estimate=cost(5),
        name="back_project",
    )(q0, q1, f0, f1, k0, k1, k0, k1, v0, v1, v0, v1, w)


def qkv_grad_kernel(count, idx, fn_ref, qn, qf, k_ref, v_ref, wq, wk, wv, g_ref, keep_o, *refs):
    if count > 1:
        send_o, gain_o, acc = refs
    else:
        gain_o, acc = refs
    rows = qn.shape[0]
    q = jnp.concatenate([qn[...], qf[...]], axis=0)
    raw = jnp.concatenate([q, k_ref[...], v_ref[...]], axis=1)
    acc[...] = lax.dot_general(fn_ref[...], raw, ROWS_BY_COLS, preferred_element_type=f32)
    shard = idx[0]
    size = WIDTH // count
    for k, r in enumerate(CHUNKS[:count]):
        place = aligned(jnp.bitwise_xor(shard, r), size) if count > 1 else pl.ds(0, size)
        target = (keep_o, send_o)[k // 4] if count > 1 else keep_o
        target[k % 4] = acc[place].astype(bf16)
    w = jnp.concatenate([wq[...], wk[...], wv[...]], axis=1)
    both = acc[...] * w.astype(f32)
    high = both.astype(bf16)
    rest = (both - high.astype(f32)).astype(bf16)
    ones = jnp.ones((8, w.shape[1]), bf16)
    total = lax.dot_general(ones, high, COLS_BY_COLS, preferred_element_type=f32)
    total += lax.dot_general(ones, rest, COLS_BY_COLS, preferred_element_type=f32)
    gain_o[...] = total / g_ref[0:1]


def qkv_grad_call(count, idx, first_low, raw, w, gains, pair):
    vmem = pl.BlockSpec(memory_space=pltpu.VMEM)
    split = 2 if count > 1 else 1
    size = WIDTH // count
    width = 3 * 128
    whole = lambda shape: pl.BlockSpec(shape, lambda i: (0,) * len(shape))
    weight = lambda part: pl.BlockSpec((WIDTH, 128), lambda i: (0, 2 * part + pair))
    grads = [(count // split, size, width)] * split + [(8, WIDTH)]
    return pl.pallas_call(
        partial(qkv_grad_kernel, count),
        grid=(1,),
        in_specs=[SMEM, whole(first_low.shape)]
        + [whole(value.shape) for value in raw]
        + [weight(0), weight(1), weight(2), whole(gains.shape)],
        out_specs=[whole(shape) for shape in grads],
        out_shape=[sds(shape) for shape in grads[:-1]] + [sds(grads[-1], f32)],
        scratch_shapes=[pltpu.VMEM((WIDTH, width), f32)],
        compiler_params=params(),
        cost_estimate=cost(6),
        name="project_grad",
    )(idx, first_low, *raw, w, w, w, gains)


def norm_one_kernel(x_ref, res_ref, own, core, far, g_ref, o_ref):
    xhat, inv_scale = normalize(x_ref[...].astype(f32))
    first = own[0].astype(f32) + core[0].astype(f32) + far[...].astype(f32)
    o_ref[...] = res_ref[...] + norm_back(first * g_ref[0:1], xhat, inv_scale)


def norm_one_call(x, res, own, core, far, gains, steps=4):
    rows = x.shape[0]
    block = pl.BlockSpec((rows // steps, WIDTH), lambda i: (i, 0))
    return pl.pallas_call(
        norm_one_kernel,
        grid=(steps,),
        in_specs=[
            block,
            block,
            pl.BlockSpec((1, rows // steps, WIDTH), lambda i: (0, i, 0)),
            pl.BlockSpec((1, rows // steps, WIDTH), lambda i: (0, i, 0)),
            block,
            pl.BlockSpec((8, WIDTH), lambda i: (0, 0)),
        ],
        out_specs=block,
        out_shape=sds(res.shape, f32),
        compiler_params=params(),
        cost_estimate=cost(3),
        name="norm_one_back",
    )(x, res, own, core, far, gains)


def swap(value, axis, bits):
    size = lax.axis_size(axis)
    return lax.ppermute(value, axis, [(place, place ^ bits) for place in range(size)])


def plus(left, right):
    return (left.astype(f32) + right.astype(f32)).astype(bf16)


def together(*values):
    return lax.optimization_barrier(values)


def per_device(inputs, attn_gain, qkv_weight, out_weight, mlp_gain, in_weight, mlp_out, cotangent):
    _, rows, width = inputs.shape
    shards = lax.axis_size("shard")
    eight = shards == 8
    count = 8 if eight else 1
    piece = width // shards
    seq, shard = lax.axis_index("seq"), lax.axis_index("shard")
    x_place, core = seq // 2, seq % 2
    idx = jnp.stack([shard, seq, x_place, core]).astype(jnp.int32)

    order = jnp.bitwise_xor(seq, jnp.arange(4))
    places = (order[:, None] * rows + jnp.arange(rows)[None, :]).reshape(-1)
    frequency = 1.0 / rope_base ** (jnp.arange(0, HD, 2, dtype=f32) / HD)
    angles = places.astype(f32)[:, None] * jnp.tile(frequency, 4)[None, :]
    sign = jnp.where(jnp.arange(128) % HD < HD // 2, -1.0, 1.0)
    cosine, sine = jnp.cos(angles), jnp.sin(angles) * sign

    x0 = inputs[0]
    c0 = cotangent[0]
    w_qkv = lax.dynamic_slice_in_dim(qkv_weight, seq * COLS, COLS, 2)
    w_qkv = jnp.transpose(w_qkv, (1, 0, 2)).reshape(piece, 3 * COLS)
    w_in = in_weight.reshape(piece, 2, 2, HALF)
    w_in = lax.dynamic_index_in_dim(w_in, core, 2, keepdims=False)
    w_in = jnp.pad(w_in, ((0, 0), (0, 0), (0, PADDED - HALF)))
    w_mine = lax.dynamic_index_in_dim(w_in, x_place, 1, keepdims=False)
    w_other = lax.dynamic_index_in_dim(w_in, 1 - x_place, 1, keepdims=False)
    w_down = lax.dynamic_slice_in_dim(mlp_out, core * HALF, HALF, 0).T
    w_down = jnp.pad(w_down, ((0, 0), (0, PADDED - HALF)))

    x2 = swap(x0, "seq", 2)
    by_y = lambda value: swap(value, "shard", 1)
    by_z = lambda value: swap(value, "shard", 2)
    by_zz = lambda value: swap(value, "shard", 4)
    by_x = lambda value: swap(value, "seq", 2)
    by_core = lambda value: swap(value, "seq", 1)
    if eight:
        gain_rows = jnp.concatenate([attn_gain, mlp_gain, jnp.zeros(3 * COLS - 2 * piece, bf16)])[None]
        a0 = jnp.concatenate([w_qkv, jnp.pad(gain_rows, ((0, EXTRA - 1), (0, 0)))], axis=0)
        f0 = jnp.concatenate([w_mine, out_weight, w_down], axis=1)
        a4, a2, a1, f1 = by_zz(a0), by_z(a0), by_y(a0), by_y(f0)
        a4, a2, a1, x0, cosine, sine, idx = together(a4, a2, a1, x0, cosine, sine, idx)
        a6, a35 = by_z(a4), by_y(jnp.stack([a2, a4]))
        x1 = by_core(x0)
        a6, a35, x2, f1 = together(a6, a35, x2, f1)
        a7 = by_y(a6)
        x3 = by_core(x2)
        g0, h0 = f0[:, : PADDED + WIDTH], f0[:, PADDED + WIDTH :]
        g0, h0, a6 = together(g0, h0, a6)
        g4, g2 = by_zz(g0), by_z(g0)
        first_low, q, k, v, w_full, gains = qkv_call(
            count,
            idx,
            (x0, x1, x2, x3),
            (
                (a0, a1, a2, a4, a35, a6, a7),
                tuple((array, lead, 0) for array, lead in
                    ((0, None), (1, None), (2, None), (4, 0), (3, None), (4, 1), (5, None), (6, None))),
            ),
            None,
            cosine,
            sine,
        )
        q, g4, g2, h0, x1 = together(q, g4, g2, h0, x1)
        g6, g35 = by_z(g4), by_y(jnp.stack([g2, g4]))
        e124 = by_x(jnp.stack([f1[:, :PADDED], g2[:, :PADDED], g4[:, :PADDED]]))
        ctx_fa, lse_fa = attend(q, k, v, 2)
        ctx_fa, q, h0 = together(ctx_fa, q, h0)
        h4, h2 = by_zz(h0), by_z(h0)
        ctx_fb, lse_fb = attend(q, k, v, 3)
        ctx_fa, ctx_fb, q, g6 = together(ctx_fa, ctx_fb, q, g6)
        other = by_x(jnp.concatenate([ctx_fa, ctx_fb], axis=0))
        ctx_na, lse_na = attend(q, k, v, 0)
        ctx_na, q, e124, g6 = together(ctx_na, q, e124, g6)
        g7 = by_y(g6)
        ctx_nb, lse_nb = attend(q, k, v, 1)
        ctx_nb, g35, h4, h2, other = together(ctx_nb, g35, h4, h2, other)
        h6, h35 = by_z(h4), by_y(jnp.stack([h2, h4]))
        e356 = by_x(jnp.concatenate([g35[:, :, :PADDED], g6[None, :, :PADDED]], axis=0))
        ctx_nb, g7, h6 = together(ctx_nb, g7, h6)
        e7 = by_x(g7[:, :PADDED])
        h6, h35, e356, ctx_nb = together(h6, h35, e356, ctx_nb)
        h7 = by_y(h6)
        arrays = (f0, f1, g2, g4, g35, g6, g7, h2, h4, h35, h6, h7, w_other, e124, e356, e7)
        wide_at = ((0, None), (1, None), (2, None), (4, 0), (3, None), (4, 1), (5, None), (6, None))
        mine_at = tuple((array, lead, 0) for array, lead in wide_at)
        out_pieces = (arrays[:7], tuple((array, lead, PADDED) for array, lead in wide_at))
        down_at = ((0, None, PADDED + WIDTH), (1, None, PADDED + WIDTH)) + tuple(
            (array, lead, 0) for array, lead in ((7, None), (9, 0), (8, None), (9, 1), (10, None), (11, None))
        )
        other_at = tuple(
            (array, lead, 0)
            for array, lead in
            ((12, None), (13, 0), (13, 1), (14, 0), (13, 2), (14, 1), (14, 2), (15, None))
        )
    else:
        x1, x3 = by_core(x0), by_core(x2)
        gather = lambda value: lax.all_gather(value, "shard", axis=0, tiled=True)
        alone = ((0, None, 0),)
        first_low, q, k, v, w_full, gains = qkv_call(
            count,
            idx,
            (x0, x1, x2, x3),
            ((gather(w_qkv),), alone),
            jnp.stack([gather(attn_gain), gather(mlp_gain)]),
            cosine,
            sine,
        )
        arrays = (gather(w_mine), gather(w_down))
        arrays += (by_x(arrays[0]),)
        out_pieces = ((gather(out_weight),), alone)
        mine_at, down_at, other_at = alone, ((1, None, 0),), ((2, None, 0),)
        (ctx_fa, lse_fa), (ctx_fb, lse_fb) = attend(q, k, v, 2), attend(q, k, v, 3)
        other = by_x(jnp.concatenate([ctx_fa, ctx_fb], axis=0))
        (ctx_na, lse_na), (ctx_nb, lse_nb) = attend(q, k, v, 0), attend(q, k, v, 1)
    c1 = by_core(c0)

    near, far = (ctx_na, ctx_nb), (ctx_fa, ctx_fb)
    lse_near, lse_far = (lse_na, lse_nb), (lse_fa, lse_fb)
    out_own, w_sel = out_call(count, idx, near, other, out_pieces)
    out_core = by_core(out_own)
    second_low, hidden, gate_up_grad, second_own, w_down_full = mlp_call(
        count, idx, x0, x1, out_own, out_core, c0, c1, gains, arrays, mine_at, other_at, down_at
    )
    second_core = by_core(second_own)
    wide = list(wide_call(count, idx, second_low, gate_up_grad))
    wide[-1], second_core = together(wide[-1], second_core)
    res, res_low, grad_near, grad_other, gain_two = norm_two_call(
        x0, x1, out_own, out_core, second_own, second_core, c0, c1, gains, w_sel
    )
    grad_far = by_x(grad_other)
    down_other, down_mine, late_keep, late_send = down_call(
        count, idx, hidden, w_down_full, c0, c1, near, other, res_low
    )
    if eight:
        wide_keep, wide_send = wide
        wide_got = by_y(wide_send)
    part = lambda half, pair, grads, earlier=None: attend_back(
        half, pair, q, grads, (near, far)[half], (lse_near, lse_far)[half], k, v, cosine, sine, earlier
    )
    late_send, down_mine, grad_near, grad_far = together(late_send, down_mine, grad_near, grad_far)
    down_core = by_core(down_other)
    late_got = by_x(late_send)
    q_n0, dk0, dv0 = part(0, 0, grad_near)
    q_n0, grad_near, down_core = together(q_n0, grad_near, down_core)
    q_n1, dk1, dv1 = part(0, 1, grad_near)
    q_n1, grad_far = together(q_n1, grad_far)
    q_f0, k0, v0 = part(1, 0, grad_far, (dk0, dv0))
    if eight:
        q_f0, late_got, wide_got, grad_far = together(q_f0, late_got, wide_got, grad_far)
        late_mine = plus(late_keep[:4], late_got[:4])
        late_got = by_y(plus(late_keep[4:], late_got[4:]))
        wide_mine = plus(wide_keep[0], wide_got[0])
        wide_got = by_x(plus(wide_keep[1], wide_got[1]))
    raw0 = (q_n0, q_f0, k0, v0)
    *terms0, gain_a = qkv_grad_call(count, idx, first_low, raw0, w_full, gains, 0)
    if eight:
        terms0[0], terms0[1], grad_far = together(terms0[0], terms0[1], grad_far)
        terms0_got = by_y(terms0[1])
    q_f1, k1, v1 = part(1, 1, grad_far, (dk1, dv1))
    raw1 = (q_n1, q_f1, k1, v1)
    first_core = back_project((raw0, raw1), w_full, 1)
    if eight:
        first_core, q_f1, late_got, terms0_got, wide_got = together(
            first_core, q_f1, late_got, terms0_got, wide_got
        )
        first_got = by_core(first_core)
        late_next = by_z(plus(late_mine[2:], late_got[2:]))
        terms0_next = by_z(plus(terms0[0][2:], terms0_got[2:]))
        wide_next = by_z(plus(wide_mine[2:], wide_got[2:]))
    else:
        first_got = by_core(first_core)
    raw1 = (q_n1, q_f1, k1, v1)
    *terms1, gain_b = qkv_grad_call(count, idx, first_low, raw1, w_full, gains, 1)
    if eight:
        terms1[0], terms1[1], first_got, q_f1 = together(terms1[0], terms1[1], first_got, q_f1)
        terms1_got = by_y(terms1[1])
        raw1 = (q_n1, q_f1, k1, v1)
    first_own = back_project((raw0, raw1), w_full, 0)
    gain_terms = jnp.concatenate([gain_a[:1] + gain_b[:1], gain_two[:1]], axis=0)
    final = lambda mine, got: mine.astype(f32) + got.astype(f32)
    if eight:
        first_own, late_next, terms0_next, gain_terms = together(
            first_own, late_next, terms0_next, gain_terms
        )
        first_far = by_x(plus(first_own[1], first_got[1]))
        late_mine = plus(late_mine[:2], late_got[:2])
        terms0_mine = plus(terms0[0][:2], terms0_got[:2])
        late_last = by_zz(plus(late_mine[1], late_next[1]))
        terms0_last = by_zz(plus(terms0_mine[1], terms0_next[1]))
        gain_terms = gain_terms + by_core(gain_terms)
        terms1_got, wide_next, gain_terms = together(terms1_got, wide_next, gain_terms)
        terms1_next = by_z(plus(terms1[0][2:], terms1_got[2:]))
        terms1_mine = plus(terms1[0][:2], terms1_got[:2])
        wide_mine = plus(wide_mine[:2], wide_got[:2])
        wide_last = by_zz(plus(wide_mine[1], wide_next[1]))
        gain_terms = gain_terms + by_y(gain_terms)
        late_total = final(plus(late_mine[0], late_next[0]), late_last)
        terms1_next, late_total, terms0_last, gain_terms, down_core = together(
            terms1_next, late_total, terms0_last, gain_terms, down_core
        )
        gain_terms = gain_terms + by_z(gain_terms)
        terms1_last = by_zz(plus(terms1_mine[1], terms1_next[1]))
        gain_terms, first_far = together(gain_terms, first_far)
        gain_terms = gain_terms + by_x(gain_terms)
        gain_terms = gain_terms + by_zz(gain_terms)
        wide_total = final(plus(wide_mine[0], wide_next[0]), wide_last)
        totals = [
            final(plus(terms0_mine[0], terms0_next[0]), terms0_last),
            final(plus(terms1_mine[0], terms1_next[0]), terms1_last),
        ]
    else:
        first_far = by_x(plus(first_own[1], first_got[1]))
        wide_sum = plus(wide[0][0, 0], by_x(wide[0][1, 0]))
        scatter = lambda value, dim: lax.psum_scatter(
            value, "shard", scatter_dimension=dim, tiled=True
        ).astype(f32)
        wide_total = scatter(wide_sum, 0)
        late_total = scatter(plus(late_keep, late_got)[0], 1)
        totals = [scatter(terms[0][0], 0) for terms in (terms0, terms1)]
        gain_terms = lax.psum(gain_terms, ("seq", "shard"))
    result = (
        x0.astype(f32)
        + out_own[:rows].astype(f32)
        + out_core[rows:].astype(f32)
        + down_mine.astype(f32)
        + down_core.astype(f32)
    ).astype(bf16)[None]
    input_grad = norm_one_call(x0, res, first_own, first_got, first_far, gains)[None]
    down_total, out_total = late_total[:BLOCK], late_total[BLOCK:]
    moved = lax.ppermute(down_total.astype(bf16), "seq", [(1, 2), (2, 1)]).astype(f32)
    down_total = jnp.where((seq == 1) | (seq == 2), moved, down_total)
    take = width // (4 * shards)
    gain_out = lax.dynamic_slice_in_dim(gain_terms, (seq * shards + shard) * take, take, 1)
    qkv_out = jnp.stack(
        [
            jnp.concatenate([total[:, at * 128 : (at + 1) * 128] for total in totals], axis=1)
            for at in range(3)
        ]
    )
    return (
        result,
        input_grad,
        gain_out[0],
        qkv_out,
        out_total,
        gain_out[1],
        wide_total[:, :HALF],
        down_total,
    )


def solution(mesh):
    placed = (
        P("shard", "seq", None),
        P("shard"),
        P(None, "shard", None),
        P("shard", None),
        P("shard"),
        P("shard", None),
        P(None, "shard"),
        P("shard", "seq", None),
    )
    return jax.shard_map(
        per_device,
        mesh=mesh,
        in_specs=placed,
        out_specs=(
            P("shard", "seq", None),
            P("shard", "seq", None),
            P(("seq", "shard")),
            P(None, "shard", "seq"),
            P("seq", "shard"),
            P(("seq", "shard")),
            P("shard", "seq"),
            P("seq", "shard"),
        ),
        check_vma=False,
    )
```

time: 536 us -> 419 us (0.78)
  waiting for transfers between devices: 213 us -> 107 us
  starting transfers between devices: 69.5 us -> 49.9 us
  other arithmetic: 22.1 us -> 32.2 us
  Pallas kernels: 214 us -> 207 us
    ppermute x64 -> x50, waiting for transfers between devices: 213 us -> 107 us  [swap(): lax.ppermute(value, axis, [(place, place ^ bits) for place in range(size)])]
    ppermute x64 -> x50, starting transfers between devices: 68.6 us -> 49.3 us  [swap(): lax.ppermute(value, axis, [(place, place ^ bits) for place in range(size)])]
    pallas_call x16 -> x18, Pallas kernels: 202 us -> 195 us  [the longest x4 62.2 us: attend_back(): pl.pallas_call(lambda *refs: attend_back_kernel(last, pair, *refs[:n_in],...]
    convert_element_type x12 -> x11, other arithmetic: 9.46 us -> 13.9 us  [plus(): return (left.astype(f32) + right.astype(f32)).astype(bf16)]
  transfers between devices with their start and end apart: 65 -> 51, of which waited for: 30 -> 16; matrix products, arithmetic and copies ran while one was open for 6% -> 9% of each run, Pallas kernels for 33% -> 42%
where the time goes in v2:
time: 419 us; the launch traced here: 414 us
  Pallas kernels  207 us (49%)
  waiting for transfers between devices  107 us (26%)
  starting transfers between devices  49.9 us (12%)
  other arithmetic  32.2 us (8%)
  local copies, waits for them, and re-layouts  15.6 us (4%)
    ppermute x50, waiting for transfers between devices, swap(): lax.ppermute(value, axis, [(place, place ^ bits) for place in range(size)])  107 us
    pallas_call x4, Pallas kernels, attend_back(): pl.pallas_call(lambda *refs: attend_back_kernel(last, pair, *refs[:n_in],...  62.2 us
    ppermute x50, starting transfers between devices, swap(): lax.ppermute(value, axis, [(place, place ^ bits) for place in range(size)])  49.3 us
    pallas_call x4, Pallas kernels, attend(): pl.pallas_call(lambda *refs: attend_kernel(*refs[:3], *refs[3 + len(after...  35.2 us
    pallas_call x1, Pallas kernels, mlp_call(): pl.pallas_call(partial(mlp_kernel, count, len(arrays), mine, other, down)...  26.4 us
    pallas_call x1, Pallas kernels, down_call(): pl.pallas_call(partial(down_kernel, count), in_specs=[SMEM] + [vmem] * 8,...  14.3 us
    convert_element_type x11, other arithmetic, plus(): return (left.astype(f32) + right.astype(f32)).astype(bf16)  13.9 us
    pallas_call x2, Pallas kernels, qkv_grad_call(): pl.pallas_call(partial(qkv_grad_kernel, count), grid=(1,), in_specs=[SMEM...  12.6 us
  transfers between devices with their start and end apart: 51, of which 16 were waited for; matrix products, arithmetic and copies ran while one was open for 9% of the time, Pallas kernels for 42%

profile of v2, /device:TPU:0, one launch (start us, length us, event | category | flops | bytes accessed | tf_op | source)
XLA Modules:
  0.0 413.7 jit_solution(8506001803757606930)
XLA Ops:
  2.9 3.0 collective-permute-start.2
  7.4 2.6 collective-permute-start
  15.7 5.5 %fusion.3 = (f32[2048,128]{1,0:T(8,128)}, f32[2048,128]{1,0:T(8,128)}) fusion(f32[128]{0:T(128)S(1)} %compare_select_fusion, f32[128]{0:T(128)S(1)} %mul.49, f32[2048]{0:T(1024)S(1)} %bitcast.108), kind=kLoop, calls=%fused_computation.16 | loop fusion | flops 524288 | bytes 2106368 | tf_op jit(solution)/shard_map/mul | solution.py:768
  25.1 5.7 %collective-permute-done.4.refs_9_ = bf16[144,768]{1,0:T(8,128)(2,1)S(1)} collective-permute-done((bf16[144,768]{1,0:T(8,128)(2,1)}, bf16[144,768]{1,0:T(8,128)(2,1)S(1)}, u32[]{:S(2)}, u32[]{:S(2)}) %collective-permute-start.4) | collective-permute-done | bytes 221216 | tf_op jit(solution)/shard_map/ppermute | solution.py:742
  30.8 16.3 %collective-permute-done.5.refs_8_ = bf16[2,144,768]{2,1,0:T(8,128)(2,1)S(1)} collective-permute-done((bf16[2,144,768]{2,1,0:T(8,128)(2,1)S(1)}, bf16[2,144,768]{2,1,0:T(8,128)(2,1)S(1)}, u32[]{:S(2)}, u32[]{:S(2)}) %collective-permute-start.5) | collective-permute-done | bytes 442400 | tf_op jit(solution)/shard_map/ppermute | solution.py:742
  50.3 5.8 %collective-permute-done.9.refs_10_ = bf16[144,768]{1,0:T(8,128)(2,1)S(1)} collective-permute-done((bf16[144,768]{1,0:T(8,128)(2,1)S(1)}, bf16[144,768]{1,0:T(8,128)(2,1)S(1)}, u32[]{:S(2)}, u32[]{:S(2)}) %collective-permute-start.9) | collective-permute-done | bytes 221216 | tf_op jit(solution)/shard_map/ppermute | solution.py:742
  57.1 12.0 %project.1 = (bf16[2048,1024]{1,0:T(8,128)(2,1)}, bf16[2048,256]{1,0:T(8,128)(2,1)}, bf16[2048,256]{1,0:T(8,128)(2,1)}, bf16[2048,256]{1,0:T(8,128)(2,1)}, bf16[1024,768]{1,0:T(8,128)(2,1)}, /*index=5*/f32[8,1024]{1,0:T(8,128)}) custom-call(s32[4]{0:T(128)} %pad_add_fusion.idx, bf16[512,1024]{1,0:T(8,128)(2,1)} %bitcast.86, bf16[512,1024]{1,0:T(8,128)(2,1)} %copy-done.7, ...), custom_call_target="tpu_custom_call" | custom-call | flops 11 | bytes 11 | tf_op jit(solution)/shard_map/project/pallas_call | solution.py:170
  69.1 7.4 %collective-permute-done.11.refs_2_.refs_9_ = bf16[128,2432]{1,0:T(8,128)(2,1)S(1)} collective-permute-done((bf16[128,2432]{1,0:T(8,128)(2,1)S(1)}, bf16[128,2432]{1,0:T(8,128)(2,1)S(1)}, u32[]{:S(2)}, u32[]{:S(2)}) %collective-permute-start.11) | collective-permute-done | bytes 622624 | tf_op jit(solution)/shard_map/ppermute | solution.py:742
  76.5 2.4 collective-permute-done.10.refs_3_.refs_10_
  81.4 8.7 %attend.4 = (bf16[512,256]{1,0:T(8,128)(2,1)}, f32[8,512]{1,0:T(8,128)}) custom-call(bf16[2048,256]{1,0:T(8,128)(2,1)} %get-tuple-element.170.refs_0_, bf16[2048,256]{1,0:T(8,128)(2,1)} %get-tuple-element.156.refs_1_.refs_6_, bf16[2048,256]{1,0:T(8,128)(2,1)} %get-tuple-element.157.refs_2_.refs_7_), custom_call_target="tpu_custom_call" | custom-call | flops 8 | bytes 8 | tf_op jit(solution)/shard_map/attend/pallas_call | solution.py:233
  90.0 8.9 %attend.5 = (bf16[512,256]{1,0:T(8,128)(2,1)}, f32[8,512]{1,0:T(8,128)}) custom-call(bf16[2048,256]{1,0:T(8,128)(2,1)} %get-tuple-element.170.refs_0_, bf16[2048,256]{1,0:T(8,128)(2,1)} %get-tuple-element.156.refs_1_.refs_6_, bf16[2048,256]{1,0:T(8,128)(2,1)} %get-tuple-element.157.refs_2_.refs_7_), custom_call_target="tpu_custom_call" | custom-call | flops 8 | bytes 8 | tf_op jit(solution)/shard_map/attend/pallas_call | solution.py:233
  101.7 2.0 collective-permute-start.16
  104.0 8.7 %attend.6 = (bf16[512,256]{1,0:T(8,128)(2,1)}, f32[8,512]{1,0:T(8,128)}) custom-call(bf16[2048,256]{1,0:T(8,128)(2,1)} %get-tuple-element.170.refs_0_, bf16[2048,256]{1,0:T(8,128)(2,1)} %get-tuple-element.156.refs_1_.refs_6_, bf16[2048,256]{1,0:T(8,128)(2,1)} %get-tuple-element.157.refs_2_.refs_7_), custom_call_target="tpu_custom_call" | custom-call | flops 8 | bytes 8 | tf_op jit(solution)/shard_map/attend/pallas_call | solution.py:233
  112.7 8.9 %attend.7 = (bf16[512,256]{1,0:T(8,128)(2,1)}, f32[8,512]{1,0:T(8,128)}) custom-call(bf16[2048,256]{1,0:T(8,128)(2,1)} %get-tuple-element.170.refs_0_, bf16[2048,256]{1,0:T(8,128)(2,1)} %get-tuple-element.156.refs_1_.refs_6_, bf16[2048,256]{1,0:T(8,128)(2,1)} %get-tuple-element.157.refs_2_.refs_7_), custom_call_target="tpu_custom_call" | custom-call | flops 8 | bytes 8 | tf_op jit(solution)/shard_map/attend/pallas_call | solution.py:233
  126.7 6.3 %collective-permute-done.19.refs_17_ = bf16[128,1408]{1,0:T(8,128)(2,1)} collective-permute-done((bf16[128,1408]{1,0:T(8,128)(2,1)S(1)}, bf16[128,1408]{1,0:T(8,128)(2,1)}, u32[]{:S(2)}, u32[]{:S(2)}) %collective-permute-start.19) | collective-permute-done | bytes 360480 | tf_op jit(solution)/shard_map/ppermute | solution.py:742
  132.9 19.5 %collective-permute-done.18.refs_6_.refs_13_ = bf16[128,2432]{1,0:T(8,128)(2,1)S(1)} collective-permute-done((bf16[128,2432]{1,0:T(8,128)(2,1)S(1)}, bf16[128,2432]{1,0:T(8,128)(2,1)S(1)}, u32[]{:S(2)}, u32[]{:S(2)}) %collective-permute-start.18) | collective-permute-done | bytes 622624 | tf_op jit(solution)/shard_map/ppermute | solution.py:742
  153.2 5.4 %out_project.1 = (bf16[1024,1024]{1,0:T(8,128)(2,1)}, bf16[512,1024]{1,0:T(8,128)(2,1)}) custom-call(s32[4]{0:T(128)} %pad_add_fusion.idx, bf16[512,256]{1,0:T(8,128)(2,1)} %get-tuple-element.169.ma_ref.ma.refs_2_, bf16[512,256]{1,0:T(8,128)(2,1)} %get-tuple-element.182.mb_ref.mb.refs_3_, bf16[1024,256]{1,0:T(8,128)(2,1)} %copy-done.19, ...), custom_call_target="tpu_custom_call" | custom-call | flops 5 | bytes 5 | tf_op jit(solution)/shard_map/out_project/pallas_call | solution.py:366
  159.2 1.8 slice.203
  164.3 7.4 %collective-permute-done.25.refs_22_ = bf16[128,1408]{1,0:T(8,128)(2,1)} collective-permute-done((bf16[128,1408]{1,0:T(8,128)(2,1)}, bf16[128,1408]{1,0:T(8,128)(2,1)}, u32[]{:S(2)}, u32[]{:S(2)}) %collective-permute-start.25) | collective-permute-done | bytes 360480 | tf_op jit(solution)/shard_map/ppermute | solution.py:742
  173.7 26.4 %feed_forward.1 = (bf16[1024,1024]{1,0:T(8,128)(2,1)}, bf16[1024,1408]{1,0:T(8,128)(2,1)}, bf16[2,1024,1408]{2,1,0:T(8,128)(2,1)}, bf16[1024,1024]{1,0:T(8,128)(2,1)}, bf16[1024,1408]{1,0:T(8,128)(2,1)}) custom-call(s32[4]{0:T(128)} %pad_add_fusion.idx, bf16[512,1024]{1,0:T(8,128)(2,1)} %bitcast.87, bf16[512,1024]{1,0:T(8,128)(2,1)} %copy-done.7, ...), custom_call_target="tpu_custom_call" | custom-call | flops 25 | bytes 25 | tf_op jit(solution)/shard_map/feed_forward/pallas_call | solution.py:444
  200.2 12.1 %wide_grad.1 = (bf16[2,4,128,1408]{3,2,1,0:T(8,128)(2,1)}, bf16[2,4,128,1408]{3,2,1,0:T(8,128)(2,1)}) custom-call(s32[4]{0:T(128)} %pad_add_fusion.idx, bf16[1024,1024]{1,0:T(8,128)(2,1)} %get-tuple-element.195.sn_ref, bf16[2,1024,1408]{2,1,0:T(8,128)(2,1)} %get-tuple-element.196.gug_ref), custom_call_target="tpu_custom_call" | custom-call | flops 12 | bytes 12 | tf_op jit(solution)/shard_map/wide_grad/pallas_call | solution.py:622
  213.8 10.6 %norm_two_back.1 = (f32[512,1024]{1,0:T(8,128)}, bf16[1024,1024]{1,0:T(8,128)(2,1)}, bf16[1024,256]{1,0:T(8,128)(2,1)}, bf16[1024,256]{1,0:T(8,128)(2,1)}, f32[8,1024]{1,0:T(8,128)}) custom-call(bf16[512,1024]{1,0:T(8,128)(2,1)} %bitcast.88, bf16[512,1024]{1,0:T(8,128)(2,1)} %copy-done.7, bf16[1024,1024]{1,0:T(8,128)(2,1)} %get-tuple-element.185.refs_2_.po, ...), custom_call_target="tpu_custom_call" | custom-call | flops 8 | bytes 8 | tf_op jit(solution)/shard_map/norm_two_back/pallas_call | solution.py:560
  225.6 14.3 %down_project.1 = (bf16[512,1024]{1,0:T(8,128)(2,1)}, bf16[512,1024]{1,0:T(8,128)(2,1)}, bf16[8,912,128]{2,1,0:T(8,128)(2,1)}, bf16[8,912,128]{2,1,0:T(8,128)(2,1)}) custom-call(s32[4]{0:T(128)} %pad_add_fusion.idx, bf16[1024,1408]{1,0:T(8,128)(2,1)} %get-tuple-element.192.hid_ref, bf16[1024,1408]{1,0:T(8,128)(2,1)} %get-tuple-element.193.wd_ref, ...), custom_call_target="tpu_custom_call" | custom-call | flops 15 | bytes 15 | tf_op jit(solution)/shard_map/down_project/pallas_call | solution.py:506
  240.8 15.1 %attend_back.4 = (bf16[1024,128]{1,0:T(8,128)(2,1)}, f32[2048,128]{1,0:T(8,128)}, f32[2048,128]{1,0:T(8,128)}) custom-call(bf16[2048,256]{1,0:T(8,128)(2,1)} %get-tuple-element.170.refs_0_, bf16[1024,256]{1,0:T(8,128)(2,1)} %get-tuple-element.212.refs_1_, bf16[512,256]{1,0:T(8,128)(2,1)} %get-tuple-element.169.ma_ref.ma.refs_2_, ...), custom_call_target="tpu_custom_call" | custom-call | flops 15 | bytes 15 | tf_op jit(solution)/shard_map/attend_back/pallas_call | solution.py:315
  255.9 15.4 %attend_back.5 = (bf16[1024,128]{1,0:T(8,128)(2,1)}, f32[2048,128]{1,0:T(8,128)}, f32[2048,128]{1,0:T(8,128)}) custom-call(bf16[2048,256]{1,0:T(8,128)(2,1)} %get-tuple-element.170.refs_0_, bf16[1024,256]{1,0:T(8,128)(2,1)} %get-tuple-element.212.refs_1_, bf16[512,256]{1,0:T(8,128)(2,1)} %get-tuple-element.169.ma_ref.ma.refs_2_, ...), custom_call_target="tpu_custom_call" | custom-call | flops 15 | bytes 15 | tf_op jit(solution)/shard_map/attend_back/pallas_call | solution.py:315
  271.3 15.8 %attend_back.6 = (bf16[1024,128]{1,0:T(8,128)(2,1)}, bf16[2048,128]{1,0:T(8,128)(2,1)}, bf16[2048,128]{1,0:T(8,128)(2,1)}) custom-call(bf16[2048,256]{1,0:T(8,128)(2,1)} %get-tuple-element.170.refs_0_, bf16[1024,256]{1,0:T(8,128)(2,1)} %copy-done.17, bf16[512,256]{1,0:T(8,128)(2,1)} %get-tuple-element.173.refs_2_, ...), custom_call_target="tpu_custom_call" | custom-call | flops 15 | bytes 15 | tf_op jit(solution)/shard_map/attend_back/pallas_call | solution.py:315
  287.1 3.5 add_convert_fusion
  291.8 1.9 add_convert_fusion.4
  294.9 6.2 %project_grad.2 = (bf16[4,128,384]{2,1,0:T(8,128)(2,1)}, bf16[4,128,384]{2,1,0:T(8,128)(2,1)}, f32[8,1024]{1,0:T(8,128)}) custom-call(s32[4]{0:T(128)} %pad_add_fusion.idx, bf16[2048,1024]{1,0:T(8,128)(2,1)} %get-tuple-element.206.fn_ref, bf16[1024,128]{1,0:T(8,128)(2,1)} %get-tuple-element.216.qn.q0, bf16[1024,128]{1,0:T(8,128)(2,1)} %get-tuple-element.225.qf.f0, ...), custom_call_target="tpu_custom_call" | custom-call | flops 6 | bytes 6 | tf_op jit(solution)/shard_map/project_grad/pallas_call | solution.py:697
  301.9 16.0 %attend_back.7 = (bf16[1024,128]{1,0:T(8,128)(2,1)}, bf16[2048,128]{1,0:T(8,128)(2,1)}, bf16[2048,128]{1,0:T(8,128)(2,1)}) custom-call(bf16[2048,256]{1,0:T(8,128)(2,1)} %get-tuple-element.170.refs_0_, bf16[1024,256]{1,0:T(8,128)(2,1)} %copy-done.17, bf16[512,256]{1,0:T(8,128)(2,1)} %get-tuple-element.173.refs_2_, ...), custom_call_target="tpu_custom_call" | custom-call | flops 15 | bytes 15 | tf_op jit(solution)/shard_map/attend_back/pallas_call | solution.py:315
  317.9 5.1 %back_project.2 = bf16[2,512,1024]{2,1,0:T(8,128)(2,1)} custom-call(bf16[1024,128]{1,0:T(8,128)(2,1)} %get-tuple-element.216.qn.q0, bf16[1024,128]{1,0:T(8,128)(2,1)} %get-tuple-element.215.q1.qn, bf16[1024,128]{1,0:T(8,128)(2,1)} %get-tuple-element.225.qf.f0, bf16[1024,128]{1,0:T(8,128)(2,1)} %get-tuple-element.250.f1.qf, ...), custom_call_target="tpu_custom_call" | custom-call | flops 5 | bytes 5 | tf_op jit(solution)/shard_map/back_project/pallas_call | solution.py:648
  323.0 2.2 collective-permute-done.32
  326.9 6.4 %project_grad.3 = (bf16[4,128,384]{2,1,0:T(8,128)(2,1)}, bf16[4,128,384]{2,1,0:T(8,128)(2,1)}, f32[8,1024]{1,0:T(8,128)}) custom-call(s32[4]{0:T(128)} %pad_add_fusion.idx, bf16[2048,1024]{1,0:T(8,128)(2,1)} %get-tuple-element.206.fn_ref, bf16[1024,128]{1,0:T(8,128)(2,1)} %get-tuple-element.215.q1.qn, bf16[1024,128]{1,0:T(8,128)(2,1)} %get-tuple-element.250.f1.qf, ...), custom_call_target="tpu_custom_call" | custom-call | flops 6 | bytes 6 | tf_op jit(solution)/shard_map/project_grad/pallas_call | solution.py:697
  333.3 1.8 add_convert_fusion.13
  338.2 2.5 fusion.1
  341.8 5.9 %back_project.3.own = bf16[2,512,1024]{2,1,0:T(8,128)(2,1)} custom-call(bf16[1024,128]{1,0:T(8,128)(2,1)} %get-tuple-element.216.qn.q0, bf16[1024,128]{1,0:T(8,128)(2,1)} %get-tuple-element.215.q1.qn, bf16[1024,128]{1,0:T(8,128)(2,1)} %get-tuple-element.225.qf.f0, bf16[1024,128]{1,0:T(8,128)(2,1)} %get-tuple-element.250.f1.qf, ...), custom_call_target="tpu_custom_call" | custom-call | flops 5 | bytes 5 | tf_op jit(solution)/shard_map/back_project/pallas_call | solution.py:648
  347.7 5.3 %collective-permute-done.37 = bf16[2,912,128]{2,1,0:T(8,128)(2,1)S(1)} collective-permute-done((bf16[2,912,128]{2,1,0:T(8,128)(2,1)}, bf16[2,912,128]{2,1,0:T(8,128)(2,1)S(1)}, u32[]{:S(2)}, u32[]{:S(2)}) %collective-permute-start.37) | collective-permute-done | bytes 466976 | tf_op jit(solution)/shard_map/ppermute | solution.py:742
  354.0 2.4 collective-permute-start.42
  358.4 1.8 fusion.5
  361.1 11.9 %collective-permute-done.41 = bf16[912,128]{1,0:T(8,128)(2,1)S(1)} collective-permute-done((bf16[912,128]{1,0:T(8,128)(2,1)S(1)}, bf16[912,128]{1,0:T(8,128)(2,1)S(1)}, u32[]{:S(2)}, u32[]{:S(2)}) %collective-permute-start.41) | collective-permute-done | bytes 233504 | tf_op jit(solution)/shard_map/ppermute | solution.py:742
  373.1 2.1 collective-permute-done.36
  376.5 2.6 collective-permute-start.40
  379.5 5.7 %collective-permute-done.40 = bf16[2,128,384]{2,1,0:T(8,128)(2,1)S(1)} collective-permute-done((bf16[2,128,384]{2,1,0:T(8,128)(2,1)S(1)}, bf16[2,128,384]{2,1,0:T(8,128)(2,1)S(1)}, u32[]{:S(2)}, u32[]{:S(2)}) %collective-permute-start.40) | collective-permute-done | bytes 196640 | tf_op jit(solution)/shard_map/ppermute | solution.py:742
  386.2 1.8 collective-permute-start.44
  388.0 3.4 collective-permute-start.48
  391.4 2.1 fusion.4
  395.0 6.7 %collective-permute-done.48 = bf16[128,384]{1,0:T(8,128)(2,1)S(1)} collective-permute-done((bf16[128,384]{1,0:T(8,128)(2,1)S(1)}, bf16[128,384]{1,0:T(8,128)(2,1)S(1)}, u32[]{:S(2)}, u32[]{:S(2)}) %collective-permute-start.48) | collective-permute-done | bytes 98336 | tf_op jit(solution)/shard_map/ppermute | solution.py:742
  407.0 5.6 %norm_one_back.1 = f32[512,1024]{1,0:T(8,128)} custom-call(bf16[512,1024]{1,0:T(8,128)(2,1)} %bitcast.89, f32[512,1024]{1,0:T(8,128)} %get-tuple-element.264.res_ref, bf16[2,512,1024]{2,1,0:T(8,128)(2,1)} %back_project.3.own, bf16[2,512,1024]{2,1,0:T(8,128)(2,1)} %copy-done.12, bf16[512,1024]{1,0:T(8,128)(2,1)} %copy-done.27, ...), custom_call_target="tpu_custom_call" | custom-call | flops 3 | bytes 3 | tf_op jit(solution)/shard_map/norm_one_back/pallas_call | solution.py:721
  (233 shorter events, 61.4 us)
Async XLA Ops:
  2.9 19.1 %collective-permute-start.2 = (bf16[144,768]{1,0:T(8,128)(2,1)}, bf16[144,768]{1,0:T(8,128)(2,1)}, u32[]{:S(2)}, u32[]{:S(2)}) collective-permute-start(bf16[144,768]{1,0:T(8,128)(2,1)} %fusion.11.refs_4_), channel_id=1, source_target_pairs={{0,1},{1,0},{2,3},{3,2},{4,5},{5,4},{6,7},{7,6},{8,9},{9,8},{10,11... | collective-permute-start | bytes 663560 | tf_op jit(solution)/shard_map/ppermute | solution.py:742
  5.8 16.1 %collective-permute-start.1 = (bf16[144,768]{1,0:T(8,128)(2,1)}, bf16[144,768]{1,0:T(8,128)(2,1)S(1)}, u32[]{:S(2)}, u32[]{:S(2)}) collective-permute-start(bf16[144,768]{1,0:T(8,128)(2,1)} %fusion.11.refs_4_), channel_id=1, source_target_pairs={{0,2},{1,3},{2,0},{3,1},{4,6},{5,7},{6,4},{7,5},{8,10},{9,11},{10,... | collective-permute-start | bytes 663560 | tf_op jit(solution)/shard_map/ppermute | solution.py:742
  7.4 14.6 %collective-permute-start = (bf16[144,768]{1,0:T(8,128)(2,1)}, bf16[144,768]{1,0:T(8,128)(2,1)}, u32[]{:S(2)}, u32[]{:S(2)}) collective-permute-start(bf16[144,768]{1,0:T(8,128)(2,1)} %fusion.11.refs_4_), channel_id=1, source_target_pairs={{0,4},{1,5},{2,6},{3,7},{4,0},{5,1},{6,2},{7,3},{8,12},{9,13},{10,... | collective-permute-start | bytes 663560 | tf_op jit(solution)/shard_map/ppermute | solution.py:742
  10.0 37.1 %collective-permute-start.6 = (bf16[512,1024]{1,0:T(8,128)(2,1)}, bf16[512,1024]{1,0:T(8,128)(2,1)}, u32[]{:S(2)}, u32[]{:S(2)}) collective-permute-start(bf16[512,1024]{1,0:T(8,128)(2,1)} %bitcast.85), channel_id=1, source_target_pairs={{0,16},{8,24},{16,0},{24,8},{1,17},{9,25},{17,1},{25,9},{2,18},{10... | collective-permute-start | bytes 3145736 | tf_op jit(solution)/shard_map/ppermute | solution.py:742
  15.0 32.1 %collective-permute-start.7 = (bf16[128,3840]{1,0:T(8,128)(2,1)}, bf16[128,3840]{1,0:T(8,128)(2,1)}, u32[]{:S(2)}, u32[]{:S(2)}) collective-permute-start(bf16[128,3840]{1,0:T(8,128)(2,1)} %pad_maximum_fusion.3.refs_0_.refs_7_), channel_id=1, source_target_pairs={{0,1},{1,0},{2,3},{3,2},{4,5},{5,4},{6,7},{7,6},{8,9},{9,8},{10,11... | collective-permute-start | bytes 2949128 | tf_op jit(solution)/shard_map/ppermute | solution.py:742
  23.0 24.1 %collective-permute-start.5 = (bf16[2,144,768]{2,1,0:T(8,128)(2,1)S(1)}, bf16[2,144,768]{2,1,0:T(8,128)(2,1)S(1)}, u32[]{:S(2)}, u32[]{:S(2)}) collective-permute-start(bf16[2,144,768]{2,1,0:T(8,128)(2,1)S(1)} %pad_maximum_fusion.7), channel_id=1, source_target_pairs={{0,1},{1,0},{2,3},{3,2},{4,5},{5,4},{6,7},{7,6},{8,9},{9,8},{10,11... | collective-permute-start | bytes 1327112 | tf_op jit(solution)/shard_map/ppermute | solution.py:742
  24.6 6.1 %collective-permute-start.4 = (bf16[144,768]{1,0:T(8,128)(2,1)}, bf16[144,768]{1,0:T(8,128)(2,1)S(1)}, u32[]{:S(2)}, u32[]{:S(2)}) collective-permute-start(bf16[144,768]{1,0:T(8,128)(2,1)} %collective-permute-done.refs_7_), channel_id=1, source_target_pairs={{0,2},{1,3},{2,0},{3,1},{4,6},{5,7},{6,4},{7,5},{8,10},{9,11},{10,... | collective-permute-start | bytes 663560 | tf_op jit(solution)/shard_map/ppermute | solution.py:742
  25.1 31.0 %collective-permute-start.3 = (bf16[512,1024]{1,0:T(8,128)(2,1)S(1)}, bf16[512,1024]{1,0:T(8,128)(2,1)S(1)}, u32[]{:S(2)}, u32[]{:S(2)}) collective-permute-start(bf16[512,1024]{1,0:T(8,128)(2,1)S(1)} %bitcast.90), channel_id=1, source_target_pairs={{0,8},{8,0},{16,24},{24,16},{1,9},{9,1},{17,25},{25,17},{2,10},{10... | collective-permute-start | bytes 3145736 | tf_op jit(solution)/shard_map/ppermute | solution.py:742
  47.9 8.2 %collective-permute-start.8 = (bf16[512,1024]{1,0:T(8,128)(2,1)}, bf16[512,1024]{1,0:T(8,128)(2,1)}, u32[]{:S(2)}, u32[]{:S(2)}) collective-permute-start(bf16[512,1024]{1,0:T(8,128)(2,1)} %collective-permute-done.6.refs_2_), channel_id=1, source_target_pairs={{0,8},{8,0},{16,24},{24,16},{1,9},{9,1},{17,25},{25,17},{2,10},{10... | collective-permute-start | bytes 3145736 | tf_op jit(solution)/shard_map/ppermute | solution.py:742
  47.9 28.6 %collective-permute-start.11 = (bf16[128,2432]{1,0:T(8,128)(2,1)S(1)}, bf16[128,2432]{1,0:T(8,128)(2,1)S(1)}, u32[]{:S(2)}, u32[]{:S(2)}) collective-permute-start(bf16[128,2432]{1,0:T(8,128)(2,1)S(1)} %pad_maximum_fusion.5), channel_id=1, source_target_pairs={{0,2},{1,3},{2,0},{3,1},{4,6},{5,7},{6,4},{7,5},{8,10},{9,11},{10,... | collective-permute-start | bytes 1867784 | tf_op jit(solution)/shard_map/ppermute | solution.py:742
  48.4 30.4 %collective-permute-start.10 = (bf16[128,2432]{1,0:T(8,128)(2,1)S(1)}, bf16[128,2432]{1,0:T(8,128)(2,1)S(1)}, u32[]{:S(2)}, u32[]{:S(2)}) collective-permute-start(bf16[128,2432]{1,0:T(8,128)(2,1)S(1)} %pad_maximum_fusion.5), channel_id=1, source_target_pairs={{0,4},{1,5},{2,6},{3,7},{4,0},{5,1},{6,2},{7,3},{8,12},{9,13},{10,... | collective-permute-start | bytes 1867784 | tf_op jit(solution)/shard_map/ppermute | solution.py:742
  48.8 7.3 %collective-permute-start.9 = (bf16[144,768]{1,0:T(8,128)(2,1)S(1)}, bf16[144,768]{1,0:T(8,128)(2,1)S(1)}, u32[]{:S(2)}, u32[]{:S(2)}) collective-permute-start(bf16[144,768]{1,0:T(8,128)(2,1)S(1)} %collective-permute-done.4.refs_9_), channel_id=1, source_target_pairs={{0,1},{1,0},{2,3},{3,2},{4,5},{5,4},{6,7},{7,6},{8,9},{9,8},{10,11... | collective-permute-start | bytes 663560 | tf_op jit(solution)/shard_map/ppermute | solution.py:742
  78.9 20.1 %collective-permute-start.12 = (bf16[128,2432]{1,0:T(8,128)(2,1)S(1)}, bf16[128,2432]{1,0:T(8,128)(2,1)S(1)}, u32[]{:S(2)}, u32[]{:S(2)}) collective-permute-start(bf16[128,2432]{1,0:T(8,128)(2,1)S(1)} %collective-permute-done.10.refs_3_.refs_10_), channel_id=1, source_target_pairs={{0,2},{1,3},{2,0},{3,1},{4,6},{5,7},{6,4},{7,5},{8,10},{9,11},{10,... | collective-permute-start | bytes 1867784 | tf_op jit(solution)/shard_map/ppermute | solution.py:742
  80.1 32.6 %collective-permute-start.13 = (bf16[3,128,1408]{2,1,0:T(8,128)(2,1)}, bf16[3,128,1408]{2,1,0:T(8,128)(2,1)}, u32[]{:S(2)}, u32[]{:S(2)}) collective-permute-start(bf16[3,128,1408]{2,1,0:T(8,128)(2,1)} %pad_maximum_fusion.1), channel_id=1, source_target_pairs={{0,16},{8,24},{16,0},{24,8},{1,17},{9,25},{17,1},{25,9},{2,18},{10... | collective-permute-start | bytes 3244040 | tf_op jit(solution)/shard_map/ppermute | solution.py:742
  80.8 40.9 %collective-permute-start.14 = (bf16[2,128,2432]{2,1,0:T(8,128)(2,1)S(1)}, bf16[2,128,2432]{2,1,0:T(8,128)(2,1)S(1)}, u32[]{:S(2)}, u32[]{:S(2)}) collective-permute-start(bf16[2,128,2432]{2,1,0:T(8,128)(2,1)S(1)} %pad_maximum_fusion), channel_id=1, source_target_pairs={{0,1},{1,0},{2,3},{3,2},{4,5},{5,4},{6,7},{7,6},{8,9},{9,8},{10,11... | collective-permute-start | bytes 3735560 | tf_op jit(solution)/shard_map/ppermute | solution.py:742
  100.1 21.5 %collective-permute-start.17 = (bf16[1024,256]{1,0:T(8,128)(2,1)S(1)}, bf16[1024,256]{1,0:T(8,128)(2,1)S(1)}, u32[]{:S(2)}, u32[]{:S(2)}) collective-permute-start(bf16[1024,256]{1,0:T(8,128)(2,1)S(1)} %pad_maximum_fusion.6), channel_id=1, source_target_pairs={{0,16},{8,24},{16,0},{24,8},{1,17},{9,25},{17,1},{25,9},{2,18},{10... | collective-permute-start | bytes 1572872 | tf_op jit(solution)/shard_map/ppermute | solution.py:742
  101.7 19.9 %collective-permute-start.16 = (bf16[128,1408]{1,0:T(8,128)(2,1)S(1)}, bf16[128,1408]{1,0:T(8,128)(2,1)S(1)}, u32[]{:S(2)}, u32[]{:S(2)}) collective-permute-start(bf16[128,1408]{1,0:T(8,128)(2,1)S(1)} %copy-done.23), channel_id=1, source_target_pairs={{0,2},{1,3},{2,0},{3,1},{4,6},{5,7},{6,4},{7,5},{8,10},{9,11},{10,... | collective-permute-start | bytes 1081352 | tf_op jit(solution)/shard_map/ppermute | solution.py:742
  103.7 18.0 %collective-permute-start.15 = (bf16[128,1408]{1,0:T(8,128)(2,1)S(1)}, bf16[128,1408]{1,0:T(8,128)(2,1)S(1)}, u32[]{:S(2)}, u32[]{:S(2)}) collective-permute-start(bf16[128,1408]{1,0:T(8,128)(2,1)S(1)} %copy-done.23), channel_id=1, source_target_pairs={{0,4},{1,5},{2,6},{3,7},{4,0},{5,1},{6,2},{7,3},{8,12},{9,13},{10,... | collective-permute-start | bytes 1081352 | tf_op jit(solution)/shard_map/ppermute | solution.py:742
  121.9 30.6 %collective-permute-start.21 = (bf16[3,128,1408]{2,1,0:T(8,128)(2,1)S(1)}, bf16[3,128,1408]{2,1,0:T(8,128)(2,1)}, u32[]{:S(2)}, u32[]{:S(2)}) collective-permute-start(bf16[3,128,1408]{2,1,0:T(8,128)(2,1)S(1)} %pad_maximum_fusion.2), channel_id=1, source_target_pairs={{0,16},{8,24},{16,0},{24,8},{1,17},{9,25},{17,1},{25,9},{2,18},{10... | collective-permute-start | bytes 3244040 | tf_op jit(solution)/shard_map/ppermute | solution.py:742
  123.1 29.4 %collective-permute-start.20 = (bf16[2,128,1408]{2,1,0:T(8,128)(2,1)S(1)}, bf16[2,128,1408]{2,1,0:T(8,128)(2,1)S(1)}, u32[]{:S(2)}, u32[]{:S(2)}) collective-permute-start(bf16[2,128,1408]{2,1,0:T(8,128)(2,1)S(1)} %pad_maximum_fusion.4), channel_id=1, source_target_pairs={{0,1},{1,0},{2,3},{3,2},{4,5},{5,4},{6,7},{7,6},{8,9},{9,8},{10,11... | collective-permute-start | bytes 2162696 | tf_op jit(solution)/shard_map/ppermute | solution.py:742
  124.6 27.8 %collective-permute-start.18 = (bf16[128,2432]{1,0:T(8,128)(2,1)S(1)}, bf16[128,2432]{1,0:T(8,128)(2,1)S(1)}, u32[]{:S(2)}, u32[]{:S(2)}) collective-permute-start(bf16[128,2432]{1,0:T(8,128)(2,1)S(1)} %collective-permute-done.12.refs_5_.refs_12_), channel_id=1, source_target_pairs={{0,1},{1,0},{2,3},{3,2},{4,5},{5,4},{6,7},{7,6},{8,9},{9,8},{10,11... | collective-permute-start | bytes 1867784 | tf_op jit(solution)/shard_map/ppermute | solution.py:742
  125.1 7.9 %collective-permute-start.19 = (bf16[128,1408]{1,0:T(8,128)(2,1)S(1)}, bf16[128,1408]{1,0:T(8,128)(2,1)}, u32[]{:S(2)}, u32[]{:S(2)}) collective-permute-start(bf16[128,1408]{1,0:T(8,128)(2,1)S(1)} %collective-permute-done.15.refs_15_), channel_id=1, source_target_pairs={{0,2},{1,3},{2,0},{3,1},{4,6},{5,7},{6,4},{7,5},{8,10},{9,11},{10,... | collective-permute-start | bytes 1081352 | tf_op jit(solution)/shard_map/ppermute | solution.py:742
  158.6 13.6 %collective-permute-start.22 = (bf16[1024,1024]{1,0:T(8,128)(2,1)}, bf16[1024,1024]{1,0:T(8,128)(2,1)S(1)}, u32[]{:S(2)}, u32[]{:S(2)}) collective-permute-start(bf16[1024,1024]{1,0:T(8,128)(2,1)} %get-tuple-element.185.refs_2_.po), channel_id=1, source_target_pairs={{0,8},{8,0},{16,24},{24,16},{1,9},{9,1},{17,25},{25,17},{2,10},{10... | collective-permute-start | bytes 6291464 | tf_op jit(solution)/shard_map/ppermute | solution.py:742
  161.0 10.7 %collective-permute-start.25 = (bf16[128,1408]{1,0:T(8,128)(2,1)}, bf16[128,1408]{1,0:T(8,128)(2,1)}, u32[]{:S(2)}, u32[]{:S(2)}) collective-permute-start(bf16[128,1408]{1,0:T(8,128)(2,1)} %slice.203), channel_id=1, source_target_pairs={{0,16},{8,24},{16,0},{24,8},{1,17},{9,25},{17,1},{25,9},{2,18},{10... | collective-permute-start | bytes 1081352 | tf_op jit(solution)/shard_map/ppermute | solution.py:742
  161.8 10.4 %collective-permute-start.24 = (bf16[128,1408]{1,0:T(8,128)(2,1)}, bf16[128,1408]{1,0:T(8,128)(2,1)}, u32[]{:S(2)}, u32[]{:S(2)}) collective-permute-start(bf16[128,1408]{1,0:T(8,128)(2,1)} %collective-permute-done.19.refs_17_), channel_id=1, source_target_pairs={{0,1},{1,0},{2,3},{3,2},{4,5},{5,4},{6,7},{7,6},{8,9},{9,8},{10,11... | collective-permute-start | bytes 1081352 | tf_op jit(solution)/shard_map/ppermute | solution.py:742
  200.1 12.1 %collective-permute-start.26 = (bf16[1024,1024]{1,0:T(8,128)(2,1)}, bf16[1024,1024]{1,0:T(8,128)(2,1)S(1)}, u32[]{:S(2)}, u32[]{:S(2)}) collective-permute-start(bf16[1024,1024]{1,0:T(8,128)(2,1)} %get-tuple-element.194.so), channel_id=1, source_target_pairs={{0,8},{8,0},{16,24},{24,16},{1,9},{9,1},{17,25},{25,17},{2,10},{10... | collective-permute-start | bytes 6291464 | tf_op jit(solution)/shard_map/ppermute | solution.py:742
  212.2 74.8 %collective-permute-start.30 = (bf16[2,4,128,1408]{3,2,1,0:T(8,128)(2,1)}, bf16[2,4,128,1408]{3,2,1,0:T(8,128)(2,1)}, u32[]{:S(2)}, u32[]{:S(2)}) collective-permute-start(bf16[2,4,128,1408]{3,2,1,0:T(8,128)(2,1)} %get-tuple-element.224), channel_id=1, source_target_pairs={{0,1},{1,0},{2,3},{3,2},{4,5},{5,4},{6,7},{7,6},{8,9},{9,8},{10,11... | collective-permute-start | bytes 8650760 | tf_op jit(solution)/shard_map/ppermute | solution.py:742
  224.4 15.5 %collective-permute-start.27 = (bf16[1024,256]{1,0:T(8,128)(2,1)}, bf16[1024,256]{1,0:T(8,128)(2,1)S(1)}, u32[]{:S(2)}, u32[]{:S(2)}) collective-permute-start(bf16[1024,256]{1,0:T(8,128)(2,1)} %get-tuple-element.204), channel_id=1, source_target_pairs={{0,16},{8,24},{16,0},{24,8},{1,17},{9,25},{17,1},{25,9},{2,18},{10... | collective-permute-start | bytes 1572872 | tf_op jit(solution)/shard_map/ppermute | solution.py:742
  239.9 47.1 %collective-permute-start.29 = (bf16[8,912,128]{2,1,0:T(8,128)(2,1)}, bf16[8,912,128]{2,1,0:T(8,128)(2,1)S(1)}, u32[]{:S(2)}, u32[]{:S(2)}) collective-permute-start(bf16[8,912,128]{2,1,0:T(8,128)(2,1)} %get-tuple-element.223), channel_id=1, source_target_pairs={{0,16},{8,24},{16,0},{24,8},{1,17},{9,25},{17,1},{25,9},{2,18},{10... | collective-permute-start | bytes 5603336 | tf_op jit(solution)/shard_map/ppermute | solution.py:742
  240.8 15.1 %collective-permute-start.28 = (bf16[512,1024]{1,0:T(8,128)(2,1)}, bf16[512,1024]{1,0:T(8,128)(2,1)S(1)}, u32[]{:S(2)}, u32[]{:S(2)}) collective-permute-start(bf16[512,1024]{1,0:T(8,128)(2,1)} %get-tuple-element.211), channel_id=1, source_target_pairs={{0,8},{8,0},{16,24},{24,16},{1,9},{9,1},{17,25},{25,17},{2,10},{10... | collective-permute-start | bytes 3145736 | tf_op jit(solution)/shard_map/ppermute | solution.py:742
  290.6 34.7 %collective-permute-start.33 = (bf16[4,128,1408]{2,1,0:T(8,128)(2,1)S(1)}, bf16[4,128,1408]{2,1,0:T(8,128)(2,1)}, u32[]{:S(2)}, u32[]{:S(2)}) collective-permute-start(bf16[4,128,1408]{2,1,0:T(8,128)(2,1)S(1)} %get-tuple-element.299), channel_id=1, source_target_pairs={{0,16},{8,24},{16,0},{24,8},{1,17},{9,25},{17,1},{25,9},{2,18},{10... | collective-permute-start | bytes 4325384 | tf_op jit(solution)/shard_map/ppermute | solution.py:742
  293.7 31.6 %collective-permute-start.31 = (bf16[4,912,128]{2,1,0:T(8,128)(2,1)}, bf16[4,912,128]{2,1,0:T(8,128)(2,1)S(1)}, u32[]{:S(2)}, u32[]{:S(2)}) collective-permute-start(bf16[4,912,128]{2,1,0:T(8,128)(2,1)} %get-tuple-element.301), channel_id=1, source_target_pairs={{0,1},{1,0},{2,3},{3,2},{4,5},{5,4},{6,7},{7,6},{8,9},{9,8},{10,11... | collective-permute-start | bytes 2801672 | tf_op jit(solution)/shard_map/ppermute | solution.py:742
  301.1 24.1 %collective-permute-start.32 = (bf16[4,128,384]{2,1,0:T(8,128)(2,1)}, bf16[4,128,384]{2,1,0:T(8,128)(2,1)}, u32[]{:S(2)}, u32[]{:S(2)}) collective-permute-start(bf16[4,128,384]{2,1,0:T(8,128)(2,1)} %get-tuple-element.240), channel_id=1, source_target_pairs={{0,1},{1,0},{2,3},{3,2},{4,5},{5,4},{6,7},{7,6},{8,9},{9,8},{10,11... | collective-permute-start | bytes 1179656 | tf_op jit(solution)/shard_map/ppermute | solution.py:742
  326.1 15.7 %collective-permute-start.34 = (bf16[2,512,1024]{2,1,0:T(8,128)(2,1)}, bf16[2,512,1024]{2,1,0:T(8,128)(2,1)S(1)}, u32[]{:S(2)}, u32[]{:S(2)}) collective-permute-start(bf16[2,512,1024]{2,1,0:T(8,128)(2,1)} %back_project.2), channel_id=1, source_target_pairs={{0,8},{8,0},{16,24},{24,16},{1,9},{9,1},{17,25},{25,17},{2,10},{10... | collective-permute-start | bytes 6291464 | tf_op jit(solution)/shard_map/ppermute | solution.py:742
  335.1 12.6 %collective-permute-start.38 = (bf16[2,128,384]{2,1,0:T(8,128)(2,1)}, bf16[2,128,384]{2,1,0:T(8,128)(2,1)}, u32[]{:S(2)}, u32[]{:S(2)}) collective-permute-start(bf16[2,128,384]{2,1,0:T(8,128)(2,1)} %get-tuple-element.311), channel_id=1, source_target_pairs={{0,2},{1,3},{2,0},{3,1},{4,6},{5,7},{6,4},{7,5},{8,10},{9,11},{10,... | collective-permute-start | bytes 589832 | tf_op jit(solution)/shard_map/ppermute | solution.py:742
  336.5 16.5 %collective-permute-start.37 = (bf16[2,912,128]{2,1,0:T(8,128)(2,1)}, bf16[2,912,128]{2,1,0:T(8,128)(2,1)S(1)}, u32[]{:S(2)}, u32[]{:S(2)}) collective-permute-start(bf16[2,912,128]{2,1,0:T(8,128)(2,1)} %get-tuple-element.305), channel_id=1, source_target_pairs={{0,2},{1,3},{2,0},{3,1},{4,6},{5,7},{6,4},{7,5},{8,10},{9,11},{10,... | collective-permute-start | bytes 1400840 | tf_op jit(solution)/shard_map/ppermute | solution.py:742
  340.7 34.4 %collective-permute-start.36 = (bf16[2,128,1408]{2,1,0:T(8,128)(2,1)}, bf16[2,128,1408]{2,1,0:T(8,128)(2,1)S(1)}, u32[]{:S(2)}, u32[]{:S(2)}) collective-permute-start(bf16[2,128,1408]{2,1,0:T(8,128)(2,1)} %get-tuple-element.303), channel_id=1, source_target_pairs={{0,2},{1,3},{2,0},{3,1},{4,6},{5,7},{6,4},{7,5},{8,10},{9,11},{10,... | collective-permute-start | bytes 2162696 | tf_op jit(solution)/shard_map/ppermute | solution.py:742
  353.0 7.2 %collective-permute-start.39 = (f32[2,1024]{1,0:T(2,128)S(1)}, f32[2,1024]{1,0:T(2,128)S(1)}, u32[]{:S(2)}, u32[]{:S(2)}) collective-permute-start(f32[2,1024]{1,0:T(2,128)S(1)} %pad_maximum_fusion.9), channel_id=1, source_target_pairs={{0,8},{8,0},{16,24},{24,16},{1,9},{9,1},{17,25},{25,17},{2,10},{10... | collective-permute-start | bytes 24584 | tf_op jit(solution)/shard_map/ppermute | solution.py:742
  354.0 25.5 %collective-permute-start.42 = (bf16[128,384]{1,0:T(8,128)(2,1)S(1)}, bf16[128,384]{1,0:T(8,128)(2,1)S(1)}, u32[]{:S(2)}, u32[]{:S(2)}) collective-permute-start(bf16[128,384]{1,0:T(8,128)(2,1)S(1)} %fusion.12), channel_id=1, source_target_pairs={{0,4},{1,5},{2,6},{3,7},{4,0},{5,1},{6,2},{7,3},{8,12},{9,13},{10,... | collective-permute-start | bytes 294920 | tf_op jit(solution)/shard_map/ppermute | solution.py:742
  356.5 16.5 %collective-permute-start.41 = (bf16[912,128]{1,0:T(8,128)(2,1)S(1)}, bf16[912,128]{1,0:T(8,128)(2,1)S(1)}, u32[]{:S(2)}, u32[]{:S(2)}) collective-permute-start(bf16[912,128]{1,0:T(8,128)(2,1)S(1)} %fusion.10), channel_id=1, source_target_pairs={{0,4},{1,5},{2,6},{3,7},{4,0},{5,1},{6,2},{7,3},{8,12},{9,13},{10,... | collective-permute-start | bytes 700424 | tf_op jit(solution)/shard_map/ppermute | solution.py:742
  357.2 18.0 %collective-permute-start.35 = (bf16[4,128,384]{2,1,0:T(8,128)(2,1)}, bf16[4,128,384]{2,1,0:T(8,128)(2,1)S(1)}, u32[]{:S(2)}, u32[]{:S(2)}) collective-permute-start(bf16[4,128,384]{2,1,0:T(8,128)(2,1)} %get-tuple-element.248), channel_id=1, source_target_pairs={{0,1},{1,0},{2,3},{3,2},{4,5},{5,4},{6,7},{7,6},{8,9},{9,8},{10,11... | collective-permute-start | bytes 1179656 | tf_op jit(solution)/shard_map/ppermute | solution.py:742
  360.2 42.4 %collective-permute-start.45 = (bf16[512,1024]{1,0:T(8,128)(2,1)S(1)}, bf16[512,1024]{1,0:T(8,128)(2,1)S(1)}, u32[]{:S(2)}, u32[]{:S(2)}) collective-permute-start(bf16[512,1024]{1,0:T(8,128)(2,1)S(1)} %fusion.5), channel_id=1, source_target_pairs={{0,16},{8,24},{16,0},{24,8},{1,17},{9,25},{17,1},{25,9},{2,18},{10... | collective-permute-start | bytes 3145736 | tf_op jit(solution)/shard_map/ppermute | solution.py:742
  376.5 8.7 %collective-permute-start.40 = (bf16[2,128,384]{2,1,0:T(8,128)(2,1)S(1)}, bf16[2,128,384]{2,1,0:T(8,128)(2,1)S(1)}, u32[]{:S(2)}, u32[]{:S(2)}) collective-permute-start(bf16[2,128,384]{2,1,0:T(8,128)(2,1)S(1)} %get-tuple-element.309), channel_id=1, source_target_pairs={{0,2},{1,3},{2,0},{3,1},{4,6},{5,7},{6,4},{7,5},{8,10},{9,11},{10,... | collective-permute-start | bytes 589832 | tf_op jit(solution)/shard_map/ppermute | solution.py:742
  379.3 24.1 %collective-permute-start.49 = (bf16[128,1408]{1,0:T(8,128)(2,1)S(1)}, bf16[128,1408]{1,0:T(8,128)(2,1)S(1)}, u32[]{:S(2)}, u32[]{:S(2)}) collective-permute-start(bf16[128,1408]{1,0:T(8,128)(2,1)S(1)} %get-tuple-element.306), channel_id=1, source_target_pairs={{0,4},{1,5},{2,6},{3,7},{4,0},{5,1},{6,2},{7,3},{8,12},{9,13},{10,... | collective-permute-start | bytes 1081352 | tf_op jit(solution)/shard_map/ppermute | solution.py:742
  386.2 8.8 %collective-permute-start.44 = (f32[2,1024]{1,0:T(2,128)S(1)}, f32[2,1024]{1,0:T(2,128)S(1)}, u32[]{:S(2)}, u32[]{:S(2)}) collective-permute-start(f32[2,1024]{1,0:T(2,128)S(1)} %add.209), channel_id=1, source_target_pairs={{0,2},{1,3},{2,0},{3,1},{4,6},{5,7},{6,4},{7,5},{8,10},{9,11},{10,... | collective-permute-start | bytes 24584 | tf_op jit(solution)/shard_map/ppermute | solution.py:742
  388.0 13.7 %collective-permute-start.48 = (bf16[128,384]{1,0:T(8,128)(2,1)S(1)}, bf16[128,384]{1,0:T(8,128)(2,1)S(1)}, u32[]{:S(2)}, u32[]{:S(2)}) collective-permute-start(bf16[128,384]{1,0:T(8,128)(2,1)S(1)} %fusion.15), channel_id=1, source_target_pairs={{0,4},{1,5},{2,6},{3,7},{4,0},{5,1},{6,2},{7,3},{8,12},{9,13},{10,... | collective-permute-start | bytes 294920 | tf_op jit(solution)/shard_map/ppermute | solution.py:742
  394.3 12.0 %collective-permute-start.50 = (bf16[656,128]{1,0:T(8,128)(2,1)S(1)}, bf16[656,128]{1,0:T(8,128)(2,1)S(1)}, u32[]{:S(2)}, u32[]{:S(2)}) collective-permute-start(bf16[656,128]{1,0:T(8,128)(2,1)S(1)} %slice.341), channel_id=1, source_target_pairs={{8,16},{16,8},{9,17},{17,9},{10,18},{18,10},{11,19},{19,11},{12,20... | collective-permute-start | bytes 503816 | tf_op jit(solution)/shard_map/ppermute | solution.py:982
  406.3 6.4 %collective-permute-start.47 = (f32[2,1024]{1,0:T(2,128)S(1)}, f32[2,1024]{1,0:T(2,128)S(1)}, u32[]{:S(2)}, u32[]{:S(2)}) collective-permute-start(f32[2,1024]{1,0:T(2,128)S(1)} %add.213), channel_id=1, source_target_pairs={{0,4},{1,5},{2,6},{3,7},{4,0},{5,1},{6,2},{7,3},{8,12},{9,13},{10,... | collective-permute-start | bytes 24584 | tf_op jit(solution)/shard_map/ppermute | solution.py:742
  (47 other events, 503.0 us)

commit v3 on v2

--- a/solution.py
+++ b/solution.py
@@ -24,6 +24,7 @@
 BLOCK = FF // 4
 COLS = 256
 CHUNKS = (0, 4, 2, 6, 1, 5, 3, 7)
+SPLIT = 768
 EXTRA = 16
 ROWS_BY_COLS = (((0,), (0,)), ((), ()))
 COLS_BY_COLS = (((1,), (1,)), ((), ()))
@@ -81,11 +82,11 @@
     return refs[array].at[(*index, rows, cols)]
 
 
-def fetch_rows(count, shard, refs, places, width, target, sem):
+def fetch_rows(count, idx, refs, places, width, target, sem):
     size = target.shape[0] // count
     copies = []
     for r in range(count):
-        rows = aligned(jnp.bitwise_xor(shard, r), size) if count > 1 else pl.ds(0, size)
+        rows = aligned(idx[4 + r], size) if count > 1 else pl.ds(0, size)
         copies.append(
             pltpu.make_async_copy(piece_of(refs, places[r], width=width), target.at[rows], sem.at[r])
         )
@@ -345,7 +346,7 @@
 
 def out_kernel(count, places, idx, ma_ref, mb_ref, other_ref, *refs):
     w_refs, (o_ref, wsel_ref, w_s, sem) = refs[:-4], refs[-4:]
-    copies = fetch_rows(count, idx[0], w_refs, places, WIDTH, w_s, sem)
+    copies = fetch_rows(count, idx, w_refs, places, WIDTH, w_s, sem)
     for copy in copies:
         copy.start()
     for copy in copies:
@@ -380,7 +381,7 @@
     w_refs, refs = refs[:n_arrays], refs[n_arrays:]
     sn_o, hid_o, gug_o, sgp_o, wd_o, refs = *refs[:5], refs[5:]
     xs, pos, prs, cs, wi, wd, sn_s, hid_s, gug_s, sgp_s, sem_a, sem_m, sem_i, sem_d, sem_o = refs
-    shard, x_place = idx[0], idx[2]
+    x_place = idx[2]
     rows = xs.shape[1]
     loads = [
         pltpu.make_async_copy(x0, xs.at[0], sem_a.at[0]),
@@ -392,9 +393,9 @@
     ]
     here = wi.at[:, aligned(x_place, PADDED)]
     there = wi.at[:, aligned(1 - x_place, PADDED)]
-    wi_loads = fetch_rows(count, shard, w_refs, mine, PADDED, here, sem_m)
-    wi_loads += fetch_rows(count, shard, w_refs, other, PADDED, there, sem_i)
-    wd_loads = fetch_rows(count, shard, w_refs, down, PADDED, wd, sem_d)
+    wi_loads = fetch_rows(count, idx, w_refs, mine, PADDED, here, sem_m)
+    wi_loads += fetch_rows(count, idx, w_refs, other, PADDED, there, sem_i)
+    wd_loads = fetch_rows(count, idx, w_refs, down, PADDED, wd, sem_d)
     for copy in loads[:4] + wi_loads + loads[4:] + wd_loads:
         copy.start()
     for copy in loads[:4]:
@@ -475,7 +476,8 @@
     )(idx, x0, x1, po, pr, c0, c1, gains, *arrays)
 
 
-def down_kernel(count, idx, hid_ref, wd_ref, c0, c1, ma, mb, other, low, res_other, res_mine, keep_o, send_o, acc):
+def down_kernel(count, idx, hid_ref, wd_ref, c0, c1, ma, mb, other, low, res_other, res_mine, *refs):
+    outs, downs, acc = refs[:2], refs[2:-1], refs[-1]
     shard, x_place = idx[0], idx[2]
     rows = c0.shape[0]
     width = WIDTH // count
@@ -485,15 +487,15 @@
     acc[...] = lax.dot_general(
         hid_ref[0:rows], c0[...], ROWS_BY_COLS, preferred_element_type=f32
     ) + lax.dot_general(hid_ref[rows:], c1[...], ROWS_BY_COLS, preferred_element_type=f32)
-    for part, target in ((1, send_o), (0, keep_o)):
+    for part in range(2):
         here = pl.ds(pl.multiple_of(jnp.bitwise_xor(x_place, part) * BLOCK, 8), BLOCK)
         for r in range(count):
-            target[r, 0:BLOCK] = acc[here, places[r]].astype(bf16)
+            downs[r // 4][part, r % 4] = acc[here, places[r]].astype(bf16)
     mine = jnp.concatenate([ma[...], mb[...]], axis=0)
-    for context, target in ((other[...], send_o), (mine, keep_o)):
+    for part, context in enumerate((mine, other[...])):
         acc[0:COLS] = lax.dot_general(context, low[...], ROWS_BY_COLS, preferred_element_type=f32)
         for r in range(count):
-            target[r, BLOCK:] = acc[0:COLS, places[r]].astype(bf16)
+            outs[part][r] = acc[0:COLS, places[r]].astype(bf16)
     for r, target in ((1, res_other), (0, res_mine)):
         target[...] = lax.dot_general(
             hid_ref[r * rows : (r + 1) * rows], wd_ref[...], COLS_BY_COLS, preferred_element_type=f32
@@ -502,17 +504,15 @@
 
 def down_call(count, idx, hidden, wd, c0, c1, mine, other, low):
     rows = c0.shape[0]
+    split = 2 if count > 1 else 1
     vmem = pl.BlockSpec(memory_space=pltpu.VMEM)
     return pl.pallas_call(
         partial(down_kernel, count),
         in_specs=[SMEM] + [vmem] * 8,
-        out_specs=[vmem] * 4,
-        out_shape=[
-            sds((rows, WIDTH)),
-            sds((rows, WIDTH)),
-            sds((count, BLOCK + COLS, WIDTH // count)),
-            sds((count, BLOCK + COLS, WIDTH // count)),
-        ],
+        out_specs=[vmem] * (4 + split),
+        out_shape=[sds((rows, WIDTH))] * 2
+        + [sds((count, COLS, WIDTH // count))] * 2
+        + [sds((2, count // split, BLOCK, WIDTH // count))] * split,
         scratch_shapes=[pltpu.VMEM((PADDED, WIDTH), f32)],
         compiler_params=params(),
         cost_estimate=cost(15),
@@ -593,22 +593,42 @@
 
 
 def wide_kernel(count, idx, sn_ref, gug_ref, *refs):
-    outs, acc = refs[:-1], refs[-1]
+    shard = idx[0]
     part = pl.program_id(0)
-    shard = idx[0]
+    size = WIDTH // count
+    if count == 1:
+        out, acc = refs
+        acc[...] = lax.dot_general(sn_ref[...], gug_ref[0], ROWS_BY_COLS, preferred_element_type=f32)
+        out[0, 0] = acc[...].astype(bf16)
+        return
+    keep_a, send_a, keep_b, send_b, acc = refs
     acc[...] = lax.dot_general(sn_ref[...], gug_ref[0], ROWS_BY_COLS, preferred_element_type=f32)
-    size = WIDTH // count
-    per_array = count // len(outs)
-    for k, r in enumerate(CHUNKS[:count]):
-        place = aligned(jnp.bitwise_xor(shard, r), size) if count > 1 else pl.ds(0, size)
-        outs[k // per_array][0, k % per_array] = acc[place].astype(bf16)
+    for k, r in enumerate(CHUNKS):
+        place = aligned(jnp.bitwise_xor(shard, r), size)
+        (keep_a, send_a)[k // 4][0, k % 4] = acc[place, :SPLIT].astype(bf16)
+
+    def store(target):
+        for k, r in enumerate(CHUNKS):
+            place = aligned(jnp.bitwise_xor(shard, r), size)
+            target[k] = acc[place, SPLIT:].astype(bf16)
+
+    @pl.when(part == 0)
+    def _():
+        store(keep_b)
+
+    @pl.when(part == 1)
+    def _():
+        store(send_b)
 
 
 def wide_call(count, idx, sn, gug):
     tokens = sn.shape[0]
-    split = 2 if count > 1 else 1
     size = WIDTH // count
     spec = lambda shape, at: pl.BlockSpec(shape, at)
+    whole = lambda shape: pl.BlockSpec(shape, lambda p, s: (0,) * len(shape))
+    by_part = lambda shape: pl.BlockSpec((1, *shape[1:]), lambda p, s: (p, 0, 0, 0))
+    first, second = (2, 4, size, SPLIT), (8, size, PADDED - SPLIT)
+    alone = (2, 1, WIDTH, PADDED)
     grid_spec = pltpu.PrefetchScalarGridSpec(
         num_scalar_prefetch=1,
         grid=(2,),
@@ -616,13 +636,13 @@
             spec((tokens, WIDTH), lambda p, s: (0, 0)),
             spec((1, tokens, PADDED), lambda p, s: (jnp.bitwise_xor(p, s[2]), 0, 0)),
         ],
-        out_specs=[spec((1, count // split, size, PADDED), lambda p, s: (p, 0, 0, 0))] * split,
+        out_specs=[by_part(first)] * 2 + [whole(second)] * 2 if count > 1 else [by_part(alone)],
         scratch_shapes=[pltpu.VMEM((WIDTH, PADDED), f32)],
     )
     return pl.pallas_call(
         partial(wide_kernel, count),
         grid_spec=grid_spec,
-        out_shape=[sds((2, count // split, size, PADDED))] * split,
+        out_shape=[sds(first)] * 2 + [sds(second)] * 2 if count > 1 else [sds(alone)],
         compiler_params=params(),
         cost_estimate=cost(12),
         name="wide_grad",
@@ -675,7 +695,9 @@
     for k, r in enumerate(CHUNKS[:count]):
         place = aligned(jnp.bitwise_xor(shard, r), size) if count > 1 else pl.ds(0, size)
         target = (keep_o, send_o)[k // 4] if count > 1 else keep_o
-        target[k % 4] = acc[place].astype(bf16)
+        for part in range(3):
+            value = acc[place, part * 128 : (part + 1) * 128]
+            target[k % 4, part * size : (part + 1) * size] = value.astype(bf16)
     w = jnp.concatenate([wq[...], wk[...], wv[...]], axis=1)
     both = acc[...] * w.astype(f32)
     high = both.astype(bf16)
@@ -693,7 +715,7 @@
     width = 3 * 128
     whole = lambda shape: pl.BlockSpec(shape, lambda i: (0,) * len(shape))
     weight = lambda part: pl.BlockSpec((WIDTH, 128), lambda i: (0, 2 * part + pair))
-    grads = [(count // split, size, width)] * split + [(8, WIDTH)]
+    grads = [(count // split, 3 * size, 128)] * split + [(8, WIDTH)]
     return pl.pallas_call(
         partial(qkv_grad_kernel, count),
         grid=(1,),
@@ -758,7 +780,8 @@
     piece = width // shards
     seq, shard = lax.axis_index("seq"), lax.axis_index("shard")
     x_place, core = seq // 2, seq % 2
-    idx = jnp.stack([shard, seq, x_place, core]).astype(jnp.int32)
+    owners = [jnp.bitwise_xor(lax.rem(shard + 8 - 2 * (r % 4), 8), r // 4) for r in range(8)]
+    idx = jnp.stack([shard, seq, x_place, core, *owners]).astype(jnp.int32)
 
     order = jnp.bitwise_xor(seq, jnp.arange(4))
     places = (order[:, None] * rows + jnp.arange(rows)[None, :]).reshape(-1)
@@ -789,16 +812,22 @@
         gain_rows = jnp.concatenate([attn_gain, mlp_gain, jnp.zeros(3 * COLS - 2 * piece, bf16)])[None]
         a0 = jnp.concatenate([w_qkv, jnp.pad(gain_rows, ((0, EXTRA - 1), (0, 0)))], axis=0)
         f0 = jnp.concatenate([w_mine, out_weight, w_down], axis=1)
-        a4, a2, a1, f1 = by_zz(a0), by_z(a0), by_y(a0), by_y(f0)
-        a4, a2, a1, x0, cosine, sine, idx = together(a4, a2, a1, x0, cosine, sine, idx)
+        g0, h0 = f0[:, : PADDED + WIDTH], f0[:, PADDED + WIDTH :]
+        narrow = lambda value: value[..., :PADDED]
+        ring = lambda value: lax.ppermute(
+            value, "shard", [(place, (place + 2) % 8) for place in range(8)]
+        )
+        a4, a2, a1 = by_zz(a0), by_z(a0), by_y(a0)
+        a4, a2, a1, x0, cosine, sine, idx, f0, g0, h0, w_other = together(
+            a4, a2, a1, x0, cosine, sine, idx, f0, g0, h0, w_other
+        )
         a6, a35 = by_z(a4), by_y(jnp.stack([a2, a4]))
         x1 = by_core(x0)
-        a6, a35, x2, f1 = together(a6, a35, x2, f1)
+        a6, a35, x2 = together(a6, a35, x2)
         a7 = by_y(a6)
         x3 = by_core(x2)
-        g0, h0 = f0[:, : PADDED + WIDTH], f0[:, PADDED + WIDTH :]
-        g0, h0, a6 = together(g0, h0, a6)
-        g4, g2 = by_zz(g0), by_z(g0)
+        x3, x1, a7, f0, g0, h0 = together(x3, x1, a7, f0, g0, h0)
+        g1, h1, f4 = ring(g0), ring(h0), by_y(f0)
         first_low, q, k, v, w_full, gains = qkv_call(
             count,
             idx,
@@ -812,37 +841,41 @@
             cosine,
             sine,
         )
-        q, g4, g2, h0, x1 = together(q, g4, g2, h0, x1)
-        g6, g35 = by_z(g4), by_y(jnp.stack([g2, g4]))
-        e124 = by_x(jnp.stack([f1[:, :PADDED], g2[:, :PADDED], g4[:, :PADDED]]))
+        q, g1, h1, f4 = together(q, g1, h1, f4)
+        g2, g5, h2, h5 = ring(g1), by_y(g1), ring(h1), by_y(h1)
+        e14 = by_x(jnp.stack([narrow(g1), narrow(f4)]))
         ctx_fa, lse_fa = attend(q, k, v, 2)
-        ctx_fa, q, h0 = together(ctx_fa, q, h0)
-        h4, h2 = by_zz(h0), by_z(h0)
+        ctx_fa, q = together(ctx_fa, q)
         ctx_fb, lse_fb = attend(q, k, v, 3)
-        ctx_fa, ctx_fb, q, g6 = together(ctx_fa, ctx_fb, q, g6)
+        ctx_fa, ctx_fb, q, g2, g5, h2, h5, e14 = together(ctx_fa, ctx_fb, q, g2, g5, h2, h5, e14)
         other = by_x(jnp.concatenate([ctx_fa, ctx_fb], axis=0))
+        g3, g6 = ring(g2), by_y(g2)
+        e25 = by_x(jnp.stack([narrow(g2), narrow(g5)]))
         ctx_na, lse_na = attend(q, k, v, 0)
-        ctx_na, q, e124, g6 = together(ctx_na, q, e124, g6)
-        g7 = by_y(g6)
+        ctx_na, q = together(ctx_na, q)
         ctx_nb, lse_nb = attend(q, k, v, 1)
-        ctx_nb, g35, h4, h2, other = together(ctx_nb, g35, h4, h2, other)
-        h6, h35 = by_z(h4), by_y(jnp.stack([h2, h4]))
-        e356 = by_x(jnp.concatenate([g35[:, :, :PADDED], g6[None, :, :PADDED]], axis=0))
-        ctx_nb, g7, h6 = together(ctx_nb, g7, h6)
-        e7 = by_x(g7[:, :PADDED])
-        h6, h35, e356, ctx_nb = together(h6, h35, e356, ctx_nb)
-        h7 = by_y(h6)
-        arrays = (f0, f1, g2, g4, g35, g6, g7, h2, h4, h35, h6, h7, w_other, e124, e356, e7)
-        wide_at = ((0, None), (1, None), (2, None), (4, 0), (3, None), (4, 1), (5, None), (6, None))
+        ctx_nb, g3, g6, e25, h2, h5 = together(ctx_nb, g3, g6, e25, h2, h5)
+        g7 = by_y(g3)
+        h3 = ring(h2)
+        e36 = by_x(jnp.stack([narrow(g3), narrow(g6)]))
+        ctx_nb, h3, g7, other = together(ctx_nb, h3, g7, other)
+        h67 = by_y(jnp.stack([h2, h3]))
+        e7 = by_x(narrow(g7))
+        arrays = (f0, g1, g2, g3, f4, g5, g6, g7, h1, h2, h3, h5, h67, w_other, e14, e25, e36, e7)
+        wide_at = tuple((array, None) for array in range(8))
         mine_at = tuple((array, lead, 0) for array, lead in wide_at)
-        out_pieces = (arrays[:7], tuple((array, lead, PADDED) for array, lead in wide_at))
-        down_at = ((0, None, PADDED + WIDTH), (1, None, PADDED + WIDTH)) + tuple(
-            (array, lead, 0) for array, lead in ((7, None), (9, 0), (8, None), (9, 1), (10, None), (11, None))
+        out_pieces = (arrays[:8], tuple((array, lead, PADDED) for array, lead in wide_at))
+        late = PADDED + WIDTH
+        down_at = tuple(
+            (array, lead, column)
+            for array, lead, column in
+            ((0, None, late), (8, None, 0), (9, None, 0), (10, None, 0))
+            + ((4, None, late), (11, None, 0), (12, 0, 0), (12, 1, 0))
         )
         other_at = tuple(
             (array, lead, 0)
             for array, lead in
-            ((12, None), (13, 0), (13, 1), (14, 0), (13, 2), (14, 1), (14, 2), (15, None))
+            ((13, None), (14, 0), (15, 0), (16, 0), (14, 1), (15, 1), (16, 1), (17, None))
         )
     else:
         x1, x3 = by_core(x0), by_core(x2)
@@ -869,6 +902,9 @@
     near, far = (ctx_na, ctx_nb), (ctx_fa, ctx_fb)
     lse_near, lse_far = (lse_na, lse_nb), (lse_fa, lse_fb)
     out_own, w_sel = out_call(count, idx, near, other, out_pieces)
+    if eight:
+        out_own, *last = together(out_own, *arrays)
+        arrays = tuple(last)
     out_core = by_core(out_own)
     second_low, hidden, gate_up_grad, second_own, w_down_full = mlp_call(
         count, idx, x0, x1, out_own, out_core, c0, c1, gains, arrays, mine_at, other_at, down_at
@@ -880,86 +916,99 @@
         x0, x1, out_own, out_core, second_own, second_core, c0, c1, gains, w_sel
     )
     grad_far = by_x(grad_other)
-    down_other, down_mine, late_keep, late_send = down_call(
+    down_other, down_mine, out_keep, out_send, *down = down_call(
         count, idx, hidden, w_down_full, c0, c1, near, other, res_low
     )
-    if eight:
-        wide_keep, wide_send = wide
-        wide_got = by_y(wide_send)
     part = lambda half, pair, grads, earlier=None: attend_back(
         half, pair, q, grads, (near, far)[half], (lse_near, lse_far)[half], k, v, cosine, sine, earlier
     )
-    late_send, down_mine, grad_near, grad_far = together(late_send, down_mine, grad_near, grad_far)
-    down_core = by_core(down_other)
-    late_got = by_x(late_send)
+    if eight:
+        a_keep, a_send, b_keep, b_send = wide
+        a_got, b_got = by_y(a_send), by_x(b_send)
+        out_send, grad_near, down[1] = together(out_send, grad_near, down[1])
+        out_got, down_got = by_x(out_send), by_y(down[1])
+        down_core = by_core(down_other)
+    else:
+        down_core = by_core(down_other)
     q_n0, dk0, dv0 = part(0, 0, grad_near)
-    q_n0, grad_near, down_core = together(q_n0, grad_near, down_core)
+    if eight:
+        q_n0, grad_near, grad_far, down_core, a_got, b_got = together(
+            q_n0, grad_near, grad_far, down_core, a_got, b_got
+        )
+        a_keep, a_got = plus(a_keep[0], a_got[0]), by_x(plus(a_keep[1], a_got[1]))
+        b_keep, b_got = plus(b_keep[:4], b_got[:4]), by_y(plus(b_keep[4:], b_got[4:]))
     q_n1, dk1, dv1 = part(0, 1, grad_near)
     q_n1, grad_far = together(q_n1, grad_far)
     q_f0, k0, v0 = part(1, 0, grad_far, (dk0, dv0))
     if eight:
-        q_f0, late_got, wide_got, grad_far = together(q_f0, late_got, wide_got, grad_far)
-        late_mine = plus(late_keep[:4], late_got[:4])
-        late_got = by_y(plus(late_keep[4:], late_got[4:]))
-        wide_mine = plus(wide_keep[0], wide_got[0])
-        wide_got = by_x(plus(wide_keep[1], wide_got[1]))
+        q_f0, out_got, down_got, grad_far = together(q_f0, out_got, down_got, grad_far)
+        down_keep, down_got = plus(down[0][0], down_got[0]), by_x(plus(down[0][1], down_got[1]))
     raw0 = (q_n0, q_f0, k0, v0)
     *terms0, gain_a = qkv_grad_call(count, idx, first_low, raw0, w_full, gains, 0)
     if eight:
-        terms0[0], terms0[1], grad_far = together(terms0[0], terms0[1], grad_far)
-        terms0_got = by_y(terms0[1])
+        terms0[0], terms0[1], a_got, b_got, grad_far = together(
+            terms0[0], terms0[1], a_got, b_got, grad_far
+        )
+        both = lambda lo, hi: jnp.concatenate(
+            [plus(a_keep[lo:hi], a_got[lo:hi]), plus(b_keep[lo:hi], b_got[lo:hi])], axis=-1
+        )
+        wide_next, wide_keep = by_z(both(2, 4)), both(0, 2)
+        out_next = by_y(jnp.concatenate([plus(out_keep[4:], out_got[4:]), terms0[1]], axis=1))
+        out_keep = plus(out_keep[:4], out_got[:4])
     q_f1, k1, v1 = part(1, 1, grad_far, (dk1, dv1))
     raw1 = (q_n1, q_f1, k1, v1)
     first_core = back_project((raw0, raw1), w_full, 1)
+    first_got = by_core(first_core)
     if eight:
-        first_core, q_f1, late_got, terms0_got, wide_got = together(
-            first_core, q_f1, late_got, terms0_got, wide_got
-        )
-        first_got = by_core(first_core)
-        late_next = by_z(plus(late_mine[2:], late_got[2:]))
-        terms0_next = by_z(plus(terms0[0][2:], terms0_got[2:]))
-        wide_next = by_z(plus(wide_mine[2:], wide_got[2:]))
-    else:
-        first_got = by_core(first_core)
+        first_core, q_f1, wide_next, out_next, down_got = together(
+            first_core, q_f1, wide_next, out_next, down_got
+        )
+        wide_last, wide_keep = by_zz(plus(wide_keep[1], wide_next[1])), plus(wide_keep[0], wide_next[0])
+        rest = lambda lo, hi: jnp.concatenate(
+            [
+                plus(down_keep[lo:hi], down_got[lo:hi]),
+                plus(out_keep[lo:hi], out_next[lo:hi, :COLS]),
+                plus(terms0[0][lo:hi], out_next[lo:hi, COLS:]),
+            ],
+            axis=1,
+        )
+        rest_next, rest_keep = by_z(rest(2, 4)), rest(0, 2)
     raw1 = (q_n1, q_f1, k1, v1)
     *terms1, gain_b = qkv_grad_call(count, idx, first_low, raw1, w_full, gains, 1)
+    gain_terms = jnp.concatenate([gain_a[:1] + gain_b[:1], gain_two[:1]], axis=0)
     if eight:
-        terms1[0], terms1[1], first_got, q_f1 = together(terms1[0], terms1[1], first_got, q_f1)
+        terms1[0], terms1[1], gain_terms, first_got, q_f1 = together(
+            terms1[0], terms1[1], gain_terms, first_got, q_f1
+        )
         terms1_got = by_y(terms1[1])
+        gain_got = by_core(gain_terms)
         raw1 = (q_n1, q_f1, k1, v1)
     first_own = back_project((raw0, raw1), w_full, 0)
-    gain_terms = jnp.concatenate([gain_a[:1] + gain_b[:1], gain_two[:1]], axis=0)
     final = lambda mine, got: mine.astype(f32) + got.astype(f32)
     if eight:
-        first_own, late_next, terms0_next, gain_terms = together(
-            first_own, late_next, terms0_next, gain_terms
-        )
+        first_own, first_got, gain_got = together(first_own, first_got, gain_got)
         first_far = by_x(plus(first_own[1], first_got[1]))
-        late_mine = plus(late_mine[:2], late_got[:2])
-        terms0_mine = plus(terms0[0][:2], terms0_got[:2])
-        late_last = by_zz(plus(late_mine[1], late_next[1]))
-        terms0_last = by_zz(plus(terms0_mine[1], terms0_next[1]))
-        gain_terms = gain_terms + by_core(gain_terms)
-        terms1_got, wide_next, gain_terms = together(terms1_got, wide_next, gain_terms)
+        gain_terms = gain_terms + gain_got
+        gain_got = by_y(gain_terms)
+        first_own, terms1_got, wide_last = together(first_own, terms1_got, wide_last)
         terms1_next = by_z(plus(terms1[0][2:], terms1_got[2:]))
-        terms1_mine = plus(terms1[0][:2], terms1_got[:2])
-        wide_mine = plus(wide_mine[:2], wide_got[:2])
-        wide_last = by_zz(plus(wide_mine[1], wide_next[1]))
-        gain_terms = gain_terms + by_y(gain_terms)
-        late_total = final(plus(late_mine[0], late_next[0]), late_last)
-        terms1_next, late_total, terms0_last, gain_terms, down_core = together(
-            terms1_next, late_total, terms0_last, gain_terms, down_core
-        )
-        gain_terms = gain_terms + by_z(gain_terms)
-        terms1_last = by_zz(plus(terms1_mine[1], terms1_next[1]))
-        gain_terms, first_far = together(gain_terms, first_far)
+        terms1_keep = plus(terms1[0][:2], terms1_got[:2])
+        first_own, rest_next, gain_got = together(first_own, rest_next, gain_got)
+        rest_last, rest_keep = by_zz(plus(rest_keep[1], rest_next[1])), plus(rest_keep[0], rest_next[0])
+        gain_terms = gain_terms + gain_got
+        gain_got = by_z(gain_terms)
+        terms1_next, gain_got = together(terms1_next, gain_got)
+        terms1_last = by_zz(plus(terms1_keep[1], terms1_next[1]))
+        terms1_keep = plus(terms1_keep[0], terms1_next[0])
+        gain_terms = gain_terms + gain_got
+        gain_got = by_zz(gain_terms)
+        first_far, gain_got = together(first_far, gain_got)
+        gain_terms = gain_terms + gain_got
         gain_terms = gain_terms + by_x(gain_terms)
-        gain_terms = gain_terms + by_zz(gain_terms)
-        wide_total = final(plus(wide_mine[0], wide_next[0]), wide_last)
-        totals = [
-            final(plus(terms0_mine[0], terms0_next[0]), terms0_last),
-            final(plus(terms1_mine[0], terms1_next[0]), terms1_last),
-        ]
+        wide_total = final(wide_keep, wide_last)
+        rest_total = final(rest_keep, rest_last)
+        down_total, out_total = rest_total[:BLOCK], rest_total[BLOCK : BLOCK + COLS]
+        totals = [rest_total[BLOCK + COLS :], final(terms1_keep, terms1_last)]
     else:
         first_far = by_x(plus(first_own[1], first_got[1]))
         wide_sum = plus(wide[0][0, 0], by_x(wide[0][1, 0]))
@@ -967,8 +1016,9 @@
             value, "shard", scatter_dimension=dim, tiled=True
         ).astype(f32)
         wide_total = scatter(wide_sum, 0)
-        late_total = scatter(plus(late_keep, late_got)[0], 1)
-        totals = [scatter(terms[0][0], 0) for terms in (terms0, terms1)]
+        down_total = scatter(plus(down[0][0, 0], by_x(down[0][1, 0])), 1)
+        out_total = scatter(plus(out_keep, by_x(out_send))[0], 1)
+        totals = [scatter(terms[0].reshape(3, width, 128), 1) for terms in (terms0, terms1)]
         gain_terms = lax.psum(gain_terms, ("seq", "shard"))
     result = (
         x0.astype(f32)
@@ -978,17 +1028,13 @@
         + down_core.astype(f32)
     ).astype(bf16)[None]
     input_grad = norm_one_call(x0, res, first_own, first_got, first_far, gains)[None]
-    down_total, out_total = late_total[:BLOCK], late_total[BLOCK:]
+    if eight:
+        down_total, first_own = together(down_total, first_own)
     moved = lax.ppermute(down_total.astype(bf16), "seq", [(1, 2), (2, 1)]).astype(f32)
     down_total = jnp.where((seq == 1) | (seq == 2), moved, down_total)
     take = width // (4 * shards)
     gain_out = lax.dynamic_slice_in_dim(gain_terms, (seq * shards + shard) * take, take, 1)
-    qkv_out = jnp.stack(
-        [
-            jnp.concatenate([total[:, at * 128 : (at + 1) * 128] for total in totals], axis=1)
-            for at in range(3)
-        ]
-    )
+    qkv_out = jnp.concatenate([total.reshape(3, piece, 128) for total in totals], axis=2)
     return (
         result,
         input_grad,

time: 419 us -> 404 us (0.964)
  waiting for transfers between devices: 107 us -> 88.8 us
  other arithmetic: 32.2 us -> 41 us
    ppermute x50 -> x47, waiting for transfers between devices: 107 us -> 73.7 us  [swap(): lax.ppermute(value, axis, [(place, place ^ bits) for place in range(size)])]
    ppermute x0 -> x6, waiting for transfers between devices: none -> 15.2 us  [per_device(): lax.ppermute(value, 'shard', [(place, (place + 2) % 8) for place in range...]
    ppermute x50 -> x47, starting transfers between devices: 49.3 us -> 45.3 us  [swap(): lax.ppermute(value, axis, [(place, place ^ bits) for place in range(size)])]
    convert_element_type x11 -> x13, other arithmetic: 13.9 us -> 16.3 us  [plus(): return (left.astype(f32) + right.astype(f32)).astype(bf16)]
    unnamed x93 -> x113, local copies, waits for them, and re-layouts: 8.42 us -> 7.78 us
  transfers between devices with their start and end apart: 51 -> 54, of which waited for: 16 -> 16; matrix products, arithmetic and copies ran while one was open for 9% -> 11% of each run, Pallas kernels for 42% -> 45%
where the time goes in v3:
time: 404 us; the launch traced here: 398 us
  Pallas kernels  207 us (51%)
  waiting for transfers between devices  88.8 us (22%)
  starting transfers between devices  47.4 us (12%)
  other arithmetic  41 us (10%)
  local copies, waits for them, and re-layouts  12.3 us (3%)
    ppermute x47, waiting for transfers between devices, swap(): lax.ppermute(value, axis, [(place, place ^ bits) for place in range(size)])  73.7 us
    pallas_call x4, Pallas kernels, attend_back(): pl.pallas_call(lambda *refs: attend_back_kernel(last, pair, *refs[:n_in],...  62.4 us
    ppermute x47, starting transfers between devices, swap(): lax.ppermute(value, axis, [(place, place ^ bits) for place in range(size)])  45.3 us
    pallas_call x4, Pallas kernels, attend(): pl.pallas_call(lambda *refs: attend_kernel(*refs[:3], *refs[3 + len(after...  35.3 us
    pallas_call x1, Pallas kernels, mlp_call(): pl.pallas_call(partial(mlp_kernel, count, len(arrays), mine, other, down)...  26.2 us
    convert_element_type x13, other arithmetic, plus(): return (left.astype(f32) + right.astype(f32)).astype(bf16)  16.3 us
    ppermute x6, waiting for transfers between devices, per_device(): lax.ppermute(value, 'shard', [(place, (place + 2) % 8) for place in range...  15.2 us
    pallas_call x1, Pallas kernels, down_call(): pl.pallas_call(partial(down_kernel, count), in_specs=[SMEM] + [vmem] * 8,...  13.8 us
  transfers between devices with their start and end apart: 54, of which 16 were waited for; matrix products, arithmetic and copies ran while one was open for 11% of the time, Pallas kernels for 45%

profile of v3, /device:TPU:0, one launch (start us, length us, event | category | flops | bytes accessed | tf_op | source)
XLA Modules:
  0.0 398.1 jit_solution(15115942897779219143)
XLA Ops:
  2.9 3.0 collective-permute-start.2
  5.8 1.6 collective-permute-start.1
  7.4 2.6 collective-permute-start
  12.0 2.0 copy.27
  14.4 5.6 %fusion = (f32[2048,128]{1,0:T(8,128)}, f32[2048,128]{1,0:T(8,128)}) fusion(f32[128]{0:T(128)S(1)} %compare_select_fusion, f32[128]{0:T(128)S(1)} %mul.49, f32[2048]{0:T(1024)S(1)} %bitcast.118), kind=kLoop, calls=%fused_computation.10 | loop fusion | flops 524288 | bytes 2106368 | tf_op jit(solution)/shard_map/mul | solution.py:791
  24.8 5.7 %collective-permute-done.3.refs_9_ = bf16[144,768]{1,0:T(8,128)(2,1)S(1)} collective-permute-done((bf16[144,768]{1,0:T(8,128)(2,1)}, bf16[144,768]{1,0:T(8,128)(2,1)S(1)}, u32[]{:S(2)}, u32[]{:S(2)}) %collective-permute-start.3) | collective-permute-done | bytes 221216 | tf_op jit(solution)/shard_map/ppermute | solution.py:764
  30.5 4.1 %collective-permute-done.4.refs_8_ = bf16[2,144,768]{2,1,0:T(8,128)(2,1)S(1)} collective-permute-done((bf16[2,144,768]{2,1,0:T(8,128)(2,1)S(1)}, bf16[2,144,768]{2,1,0:T(8,128)(2,1)S(1)}, u32[]{:S(2)}, u32[]{:S(2)}) %collective-permute-start.4) | collective-permute-done | bytes 442400 | tf_op jit(solution)/shard_map/ppermute | solution.py:764
  35.9 7.3 %collective-permute-done.8.refs_10_ = bf16[144,768]{1,0:T(8,128)(2,1)S(1)} collective-permute-done((bf16[144,768]{1,0:T(8,128)(2,1)S(1)}, bf16[144,768]{1,0:T(8,128)(2,1)S(1)}, u32[]{:S(2)}, u32[]{:S(2)}) %collective-permute-start.8) | collective-permute-done | bytes 221216 | tf_op jit(solution)/shard_map/ppermute | solution.py:764
  44.8 11.7 %project.1 = (bf16[2048,1024]{1,0:T(8,128)(2,1)}, bf16[2048,256]{1,0:T(8,128)(2,1)}, bf16[2048,256]{1,0:T(8,128)(2,1)}, bf16[2048,256]{1,0:T(8,128)(2,1)}, bf16[1024,768]{1,0:T(8,128)(2,1)}, /*index=5*/f32[8,1024]{1,0:T(8,128)}) custom-call(s32[12]{0:T(128)} %stack.96.idx, bf16[512,1024]{1,0:T(8,128)(2,1)} %bitcast.96, bf16[512,1024]{1,0:T(8,128)(2,1)} %copy-done.7, ...), custom_call_target="tpu_custom_call" | custom-call | flops 11 | bytes 11 | tf_op jit(solution)/shard_map/project/pallas_call | solution.py:171
  56.5 12.8 %collective-permute-done.10.refs_15_ = bf16[128,1408]{1,0:T(8,128)(2,1)S(1)} collective-permute-done((bf16[128,1408]{1,0:T(8,128)(2,1)S(1)}, bf16[128,1408]{1,0:T(8,128)(2,1)S(1)}, u32[]{:S(2)}, u32[]{:S(2)}) %collective-permute-start.10) | collective-permute-done | bytes 360480 | tf_op jit(solution)/shard_map/ppermute | solution.py:817
  72.9 8.7 %attend.4 = (bf16[512,256]{1,0:T(8,128)(2,1)}, f32[8,512]{1,0:T(8,128)}) custom-call(bf16[2048,256]{1,0:T(8,128)(2,1)} %get-tuple-element.205.refs_0_, bf16[2048,256]{1,0:T(8,128)(2,1)} %get-tuple-element.193.refs_1_.refs_6_, bf16[2048,256]{1,0:T(8,128)(2,1)} %get-tuple-element.194.refs_2_.refs_7_), custom_call_target="tpu_custom_call" | custom-call | flops 8 | bytes 8 | tf_op jit(solution)/shard_map/attend/pallas_call | solution.py:234
  81.6 9.1 %attend.5 = (bf16[512,256]{1,0:T(8,128)(2,1)}, f32[8,512]{1,0:T(8,128)}) custom-call(bf16[2048,256]{1,0:T(8,128)(2,1)} %get-tuple-element.205.refs_0_, bf16[2048,256]{1,0:T(8,128)(2,1)} %get-tuple-element.193.refs_1_.refs_6_, bf16[2048,256]{1,0:T(8,128)(2,1)} %get-tuple-element.194.refs_2_.refs_7_), custom_call_target="tpu_custom_call" | custom-call | flops 8 | bytes 8 | tf_op jit(solution)/shard_map/attend/pallas_call | solution.py:234
  90.7 2.3 collective-permute-done.15.refs_18_
  92.9 2.4 collective-permute-done.14.refs_16_
  99.2 8.7 %attend.6 = (bf16[512,256]{1,0:T(8,128)(2,1)}, f32[8,512]{1,0:T(8,128)}) custom-call(bf16[2048,256]{1,0:T(8,128)(2,1)} %get-tuple-element.205.refs_0_, bf16[2048,256]{1,0:T(8,128)(2,1)} %get-tuple-element.193.refs_1_.refs_6_, bf16[2048,256]{1,0:T(8,128)(2,1)} %get-tuple-element.194.refs_2_.refs_7_), custom_call_target="tpu_custom_call" | custom-call | flops 8 | bytes 8 | tf_op jit(solution)/shard_map/attend/pallas_call | solution.py:234
  107.9 8.9 %attend.7 = (bf16[512,256]{1,0:T(8,128)(2,1)}, f32[8,512]{1,0:T(8,128)}) custom-call(bf16[2048,256]{1,0:T(8,128)(2,1)} %get-tuple-element.205.refs_0_, bf16[2048,256]{1,0:T(8,128)(2,1)} %get-tuple-element.193.refs_1_.refs_6_, bf16[2048,256]{1,0:T(8,128)(2,1)} %get-tuple-element.194.refs_2_.refs_7_), custom_call_target="tpu_custom_call" | custom-call | flops 8 | bytes 8 | tf_op jit(solution)/shard_map/attend/pallas_call | solution.py:234
  121.3 10.5 %collective-permute-done.22.other_ref.other = bf16[1024,256]{1,0:T(8,128)(2,1)S(1)} collective-permute-done((bf16[1024,256]{1,0:T(8,128)(2,1)S(1)}, bf16[1024,256]{1,0:T(8,128)(2,1)S(1)}, u32[]{:S(2)}, u32[]{:S(2)}) %collective-permute-start.22) | collective-permute-done | bytes 524320 | tf_op jit(solution)/shard_map/ppermute | solution.py:764
  134.4 5.4 %out_project.1 = (bf16[1024,1024]{1,0:T(8,128)(2,1)}, bf16[512,1024]{1,0:T(8,128)(2,1)}) custom-call(s32[12]{0:T(128)} %stack.96.idx, bf16[512,256]{1,0:T(8,128)(2,1)} %get-tuple-element.204.ma_ref.ma.refs_2_, bf16[512,256]{1,0:T(8,128)(2,1)} %get-tuple-element.216.mb_ref.mb.refs_3_, bf16[1024,256]{1,0:T(8,128)(2,1)} %copy-done.23, ...), custom_call_target="tpu_custom_call" | custom-call | flops 5 | bytes 5 | tf_op jit(solution)/shard_map/out_project/pallas_call | solution.py:367
  139.8 7.0 %collective-permute-done.24.refs_23_ = bf16[2,128,1408]{2,1,0:T(8,128)(2,1)S(1)} collective-permute-done((bf16[2,128,1408]{2,1,0:T(8,128)(2,1)}, bf16[2,128,1408]{2,1,0:T(8,128)(2,1)S(1)}, u32[]{:S(2)}, u32[]{:S(2)}) %collective-permute-start.24) | collective-permute-done | bytes 720928 | tf_op jit(solution)/shard_map/ppermute | solution.py:764
  146.8 3.9 collective-permute-done.25.refs_24_
  151.3 4.8 %collective-permute-done.27.refs_5_.c1 = bf16[512,1024]{1,0:T(8,128)(2,1)S(1)} collective-permute-done((bf16[512,1024]{1,0:T(8,128)(2,1)S(1)}, bf16[512,1024]{1,0:T(8,128)(2,1)S(1)}, u32[]{:S(2)}, u32[]{:S(2)}) %collective-permute-start.27) | collective-permute-done | bytes 1048608 | tf_op jit(solution)/shard_map/ppermute | solution.py:764
  158.0 26.2 %feed_forward.1 = (bf16[1024,1024]{1,0:T(8,128)(2,1)}, bf16[1024,1408]{1,0:T(8,128)(2,1)}, bf16[2,1024,1408]{2,1,0:T(8,128)(2,1)}, bf16[1024,1024]{1,0:T(8,128)(2,1)}, bf16[1024,1408]{1,0:T(8,128)(2,1)}) custom-call(s32[12]{0:T(128)} %stack.96.idx, bf16[512,1024]{1,0:T(8,128)(2,1)} %bitcast.97, bf16[512,1024]{1,0:T(8,128)(2,1)} %copy-done.7, ...), custom_call_target="tpu_custom_call" | custom-call | flops 25 | bytes 25 | tf_op jit(solution)/shard_map/feed_forward/pallas_call | solution.py:445
  184.4 12.7 %wide_grad.1 = (bf16[2,4,128,768]{3,2,1,0:T(8,128)(2,1)}, bf16[2,4,128,768]{3,2,1,0:T(8,128)(2,1)}, bf16[8,128,640]{2,1,0:T(8,128)(2,1)}, bf16[8,128,640]{2,1,0:T(8,128)(2,1)}) custom-call(s32[12]{0:T(128)} %stack.96.idx, bf16[1024,1024]{1,0:T(8,128)(2,1)} %get-tuple-element.249.sn_ref, bf16[2,1024,1408]{2,1,0:T(8,128)(2,1)} %get-tuple-element.250.gug_ref), custom_call_target="tpu_custom_call" | custom-call | flops 12 | bytes 12 | tf_op jit(solution)/shard_map/wide_grad/pallas_call | solution.py:642
  199.0 10.4 %norm_two_back.1 = (f32[512,1024]{1,0:T(8,128)}, bf16[1024,1024]{1,0:T(8,128)(2,1)}, bf16[1024,256]{1,0:T(8,128)(2,1)}, bf16[1024,256]{1,0:T(8,128)(2,1)}, f32[8,1024]{1,0:T(8,128)}) custom-call(bf16[512,1024]{1,0:T(8,128)(2,1)} %bitcast.98, bf16[512,1024]{1,0:T(8,128)(2,1)} %copy-done.7, bf16[1024,1024]{1,0:T(8,128)(2,1)} %get-tuple-element.226.refs_2_.po, ...), custom_call_target="tpu_custom_call" | custom-call | flops 8 | bytes 8 | tf_op jit(solution)/shard_map/norm_two_back/pallas_call | solution.py:560
  209.5 13.8 %down_project.1 = (bf16[512,1024]{1,0:T(8,128)(2,1)}, bf16[512,1024]{1,0:T(8,128)(2,1)}, bf16[8,256,128]{2,1,0:T(8,128)(2,1)}, bf16[8,256,128]{2,1,0:T(8,128)(2,...) custom-call(s32[12]{0:T(128)} %stack.96.idx, bf16[1024,1408]{1,0:T(8,128)(2,1)} %get-tuple-element.246.hid_ref, ...), custom_call_target="tpu_custom_call" | custom-call | flops 15 | bytes 15 | tf_op jit(solution)/shard_map/down_project/pallas_call | solution.py:509
  225.6 15.3 %attend_back.4 = (bf16[1024,128]{1,0:T(8,128)(2,1)}, f32[2048,128]{1,0:T(8,128)}, f32[2048,128]{1,0:T(8,128)}) custom-call(bf16[2048,256]{1,0:T(8,128)(2,1)} %get-tuple-element.205.refs_0_, bf16[1024,256]{1,0:T(8,128)(2,1)} %get-tuple-element.270.refs_1_, bf16[512,256]{1,0:T(8,128)(2,1)} %get-tuple-element.204.ma_ref.ma.refs_2_, ...), custom_call_target="tpu_custom_call" | custom-call | flops 15 | bytes 15 | tf_op jit(solution)/shard_map/attend_back/pallas_call | solution.py:316
  244.5 1.6 add_convert_fusion.6
  246.7 15.1 %attend_back.5 = (bf16[1024,128]{1,0:T(8,128)(2,1)}, f32[2048,128]{1,0:T(8,128)}, f32[2048,128]{1,0:T(8,128)}) custom-call(bf16[2048,256]{1,0:T(8,128)(2,1)} %get-tuple-element.205.refs_0_, bf16[1024,256]{1,0:T(8,128)(2,1)} %get-tuple-element.270.refs_1_, bf16[512,256]{1,0:T(8,128)(2,1)} %get-tuple-element.204.ma_ref.ma.refs_2_, ...), custom_call_target="tpu_custom_call" | custom-call | flops 15 | bytes 15 | tf_op jit(solution)/shard_map/attend_back/pallas_call | solution.py:316
  261.8 16.0 %attend_back.6 = (bf16[1024,128]{1,0:T(8,128)(2,1)}, bf16[2048,128]{1,0:T(8,128)(2,1)}, bf16[2048,128]{1,0:T(8,128)(2,1)}) custom-call(bf16[2048,256]{1,0:T(8,128)(2,1)} %get-tuple-element.205.refs_0_, bf16[1024,256]{1,0:T(8,128)(2,1)} %copy-done.21, bf16[512,256]{1,0:T(8,128)(2,1)} %get-tuple-element.214.refs_2_, ...), custom_call_target="tpu_custom_call" | custom-call | flops 15 | bytes 15 | tf_op jit(solution)/shard_map/attend_back/pallas_call | solution.py:316
  277.9 2.7 add_convert_fusion.4
  281.8 6.3 %project_grad.2 = (bf16[4,384,128]{2,1,0:T(8,128)(2,1)}, bf16[4,384,128]{2,1,0:T(8,128)(2,1)}, f32[8,1024]{1,0:T(8,128)}) custom-call(s32[12]{0:T(128)} %stack.96.idx, bf16[2048,1024]{1,0:T(8,128)(2,1)} %get-tuple-element.283.fn_ref, bf16[1024,128]{1,0:T(8,128)(2,1)} %get-tuple-element.269.qn.q0, bf16[1024,128]{1,0:T(8,128)(2,1)} %get-tuple-element.282.qf.f0, ...), custom_call_target="tpu_custom_call" | custom-call | flops 6 | bytes 6 | tf_op jit(solution)/shard_map/project_grad/pallas_call | solution.py:719
  294.8 16.0 %attend_back.7 = (bf16[1024,128]{1,0:T(8,128)(2,1)}, bf16[2048,128]{1,0:T(8,128)(2,1)}, bf16[2048,128]{1,0:T(8,128)(2,1)}) custom-call(bf16[2048,256]{1,0:T(8,128)(2,1)} %get-tuple-element.205.refs_0_, bf16[1024,256]{1,0:T(8,128)(2,1)} %copy-done.21, bf16[512,256]{1,0:T(8,128)(2,1)} %get-tuple-element.214.refs_2_, ...), custom_call_target="tpu_custom_call" | custom-call | flops 15 | bytes 15 | tf_op jit(solution)/shard_map/attend_back/pallas_call | solution.py:316
  310.8 5.3 %back_project.2 = bf16[2,512,1024]{2,1,0:T(8,128)(2,1)} custom-call(bf16[1024,128]{1,0:T(8,128)(2,1)} %get-tuple-element.269.qn.q0, bf16[1024,128]{1,0:T(8,128)(2,1)} %get-tuple-element.273.q1.qn, bf16[1024,128]{1,0:T(8,128)(2,1)} %get-tuple-element.282.qf.f0, bf16[1024,128]{1,0:T(8,128)(2,1)} %get-tuple-element.313.f1.qf, ...), custom_call_target="tpu_custom_call" | custom-call | flops 5 | bytes 5 | tf_op jit(solution)/shard_map/back_project/pallas_call | solution.py:668
  316.2 3.7 fusion.1
  319.9 6.5 %project_grad.3 = (bf16[4,384,128]{2,1,0:T(8,128)(2,1)}, bf16[4,384,128]{2,1,0:T(8,128)(2,1)}, f32[8,1024]{1,0:T(8,128)}) custom-call(s32[12]{0:T(128)} %stack.96.idx, bf16[2048,1024]{1,0:T(8,128)(2,1)} %get-tuple-element.283.fn_ref, bf16[1024,128]{1,0:T(8,128)(2,1)} %get-tuple-element.273.q1.qn, bf16[1024,128]{1,0:T(8,128)(2,1)} %get-tuple-element.313.f1.qf, ...), custom_call_target="tpu_custom_call" | custom-call | flops 6 | bytes 6 | tf_op jit(solution)/shard_map/project_grad/pallas_call | solution.py:719
  326.4 2.1 fusion.11
  328.5 4.1 %collective-permute-start.43 = (bf16[128,1408]{1,0:T(8,128)(2,1)}, bf16[128,1408]{1,0:T(8,128)(2,1)S(1)}, u32[]{:S(2)}, u32[]{:S(2)}) collective-permute-start(bf16[128,1408]{1,0:T(8,128)(2,1)} %get-tuple-element.369), channel_id=1, source_target_pairs={{0,4},{1,5},{2,6},{3,7},{4,0},{5,1},{6,2},{7,3},{8,12},{9,13},{10,... | collective-permute-start | bytes 1081352 | tf_op jit(solution)/shard_map/ppermute | solution.py:764
  337.9 5.2 %back_project.3.own = bf16[2,512,1024]{2,1,0:T(8,128)(2,1)} custom-call(bf16[1024,128]{1,0:T(8,128)(2,1)} %get-tuple-element.269.qn.q0, bf16[1024,128]{1,0:T(8,128)(2,1)} %get-tuple-element.273.q1.qn, bf16[1024,128]{1,0:T(8,128)(2,1)} %get-tuple-element.282.qf.f0, bf16[1024,128]{1,0:T(8,128)(2,1)} %get-tuple-element.313.f1.qf, ...), custom_call_target="tpu_custom_call" | custom-call | flops 5 | bytes 5 | tf_op jit(solution)/shard_map/back_project/pallas_call | solution.py:668
  343.1 1.5 collective-permute-start.45
  344.6 1.9 fusion.2
  347.4 2.3 collective-permute-done.43
  349.7 11.1 %collective-permute-done.44 = bf16[2,1296,128]{2,1,0:T(8,128)(2,1)S(1)} collective-permute-done((bf16[2,1296,128]{2,1,0:T(8,128)(2,1)S(1)}, bf16[2,1296,128]{2,1,0:T(8,128)(2,1)S(1)}, u32[]{:S(2)}, u32[]{:S(2)}) %collective-permute-start.44) | collective-permute-done | bytes 663584 | tf_op jit(solution)/shard_map/ppermute | solution.py:764
  361.8 2.0 collective-permute-start.47
  365.8 3.7 collective-permute-done.47
  370.5 3.0 collective-permute-start.52
  373.4 10.1 %collective-permute-done.51 = bf16[1296,128]{1,0:T(8,128)(2,1)} collective-permute-done((bf16[1296,128]{1,0:T(8,128)(2,1)}, bf16[1296,128]{1,0:T(8,128)(2,1)}, u32[]{:S(2)}, u32[]{:S(2)}) %collective-permute-start.51) | collective-permute-done | bytes 331808 | tf_op jit(solution)/shard_map/ppermute | solution.py:764
  388.1 2.7 collective-permute-start.50
  391.6 5.6 %norm_one_back.1 = f32[512,1024]{1,0:T(8,128)} custom-call(bf16[512,1024]{1,0:T(8,128)(2,1)} %bitcast.99, f32[512,1024]{1,0:T(8,128)} %get-tuple-element.268.res_ref, bf16[2,512,1024]{2,1,0:T(8,128)(2,1)} %back_project.3.own, bf16[2,512,1024]{2,1,0:T(8,128)(2,1)} %collective-permute-done.40.core, bf16[512,1024]{1,0:T(8,128)(2,1)} %copy-done.31, ...), custom_call_target="tpu_custom_call" | custom-call | flops 3 | bytes 3 | tf_op jit(solution)/shard_map/norm_one_back/pallas_call | solution.py:743
  (263 shorter events, 61.4 us)
Async XLA Ops:
  2.9 19.8 %collective-permute-start.2 = (bf16[144,768]{1,0:T(8,128)(2,1)}, bf16[144,768]{1,0:T(8,128)(2,1)}, u32[]{:S(2)}, u32[]{:S(2)}) collective-permute-start(bf16[144,768]{1,0:T(8,128)(2,1)} %fusion.15.refs_4_), channel_id=1, source_target_pairs={{0,1},{1,0},{2,3},{3,2},{4,5},{5,4},{6,7},{7,6},{8,9},{9,8},{10,11... | collective-permute-start | bytes 663560 | tf_op jit(solution)/shard_map/ppermute | solution.py:764
  5.8 16.8 %collective-permute-start.1 = (bf16[144,768]{1,0:T(8,128)(2,1)}, bf16[144,768]{1,0:T(8,128)(2,1)}, u32[]{:S(2)}, u32[]{:S(2)}) collective-permute-start(bf16[144,768]{1,0:T(8,128)(2,1)} %fusion.15.refs_4_), channel_id=1, source_target_pairs={{0,2},{1,3},{2,0},{3,1},{4,6},{5,7},{6,4},{7,5},{8,10},{9,11},{10,... | collective-permute-start | bytes 663560 | tf_op jit(solution)/shard_map/ppermute | solution.py:764
  7.4 15.3 %collective-permute-start = (bf16[144,768]{1,0:T(8,128)(2,1)}, bf16[144,768]{1,0:T(8,128)(2,1)}, u32[]{:S(2)}, u32[]{:S(2)}) collective-permute-start(bf16[144,768]{1,0:T(8,128)(2,1)} %fusion.15.refs_4_), channel_id=1, source_target_pairs={{0,4},{1,5},{2,6},{3,7},{4,0},{5,1},{6,2},{7,3},{8,12},{9,13},{10,... | collective-permute-start | bytes 663560 | tf_op jit(solution)/shard_map/ppermute | solution.py:764
  10.0 25.4 %collective-permute-start.5 = (bf16[512,1024]{1,0:T(8,128)(2,1)S(1)}, bf16[512,1024]{1,0:T(8,128)(2,1)}, u32[]{:S(2)}, u32[]{:S(2)}) collective-permute-start(bf16[512,1024]{1,0:T(8,128)(2,1)S(1)} %bitcast.100), channel_id=1, source_target_pairs={{0,16},{8,24},{16,0},{24,8},{1,17},{9,25},{17,1},{25,9},{2,18},{10... | collective-permute-start | bytes 3145736 | tf_op jit(solution)/shard_map/ppermute | solution.py:764
  23.8 10.9 %collective-permute-start.4 = (bf16[2,144,768]{2,1,0:T(8,128)(2,1)S(1)}, bf16[2,144,768]{2,1,0:T(8,128)(2,1)S(1)}, u32[]{:S(2)}, u32[]{:S(2)}) collective-permute-start(bf16[2,144,768]{2,1,0:T(8,128)(2,1)S(1)} %pad_maximum_fusion.11), channel_id=1, source_target_pairs={{0,1},{1,0},{2,3},{3,2},{4,5},{5,4},{6,7},{7,6},{8,9},{9,8},{10,11... | collective-permute-start | bytes 1327112 | tf_op jit(solution)/shard_map/ppermute | solution.py:764
  24.8 18.5 %collective-permute-start.7 = (bf16[512,1024]{1,0:T(8,128)(2,1)S(1)}, bf16[512,1024]{1,0:T(8,128)(2,1)S(1)}, u32[]{:S(2)}, u32[]{:S(2)}) collective-permute-start(bf16[512,1024]{1,0:T(8,128)(2,1)S(1)} %bitcast.101), channel_id=1, source_target_pairs={{0,8},{8,0},{16,24},{24,16},{1,9},{9,1},{17,25},{25,17},{2,10},{10... | collective-permute-start | bytes 3145736 | tf_op jit(solution)/shard_map/ppermute | solution.py:764
  35.4 7.9 %collective-permute-start.6 = (bf16[512,1024]{1,0:T(8,128)(2,1)}, bf16[512,1024]{1,0:T(8,128)(2,1)S(1)}, u32[]{:S(2)}, u32[]{:S(2)}) collective-permute-start(bf16[512,1024]{1,0:T(8,128)(2,1)} %collective-permute-done.5.refs_2_), channel_id=1, source_target_pairs={{0,8},{8,0},{16,24},{24,16},{1,9},{9,1},{17,25},{25,17},{2,10},{10... | collective-permute-start | bytes 3145736 | tf_op jit(solution)/shard_map/ppermute | solution.py:764
  35.4 7.8 %collective-permute-start.8 = (bf16[144,768]{1,0:T(8,128)(2,1)S(1)}, bf16[144,768]{1,0:T(8,128)(2,1)S(1)}, u32[]{:S(2)}, u32[]{:S(2)}) collective-permute-start(bf16[144,768]{1,0:T(8,128)(2,1)S(1)} %collective-permute-done.3.refs_9_), channel_id=1, source_target_pairs={{0,1},{1,0},{2,3},{3,2},{4,5},{5,4},{6,7},{7,6},{8,9},{9,8},{10,11... | collective-permute-start | bytes 663560 | tf_op jit(solution)/shard_map/ppermute | solution.py:764
  43.3 26.0 %collective-permute-start.11 = (bf16[128,3840]{1,0:T(8,128)(2,1)S(1)}, bf16[128,3840]{1,0:T(8,128)(2,1)S(1)}, u32[]{:S(2)}, u32[]{:S(2)}) collective-permute-start(bf16[128,3840]{1,0:T(8,128)(2,1)S(1)} %pad_maximum_fusion.refs_0_.refs_7_), channel_id=1, source_target_pairs={{0,1},{1,0},{2,3},{3,2},{4,5},{5,4},{6,7},{7,6},{8,9},{9,8},{10,11... | collective-permute-start | bytes 2949128 | tf_op jit(solution)/shard_map/ppermute | solution.py:764
  43.9 25.4 %collective-permute-start.9 = (bf16[128,2432]{1,0:T(8,128)(2,1)}, bf16[128,2432]{1,0:T(8,128)(2,1)S(1)}, u32[]{:S(2)}, u32[]{:S(2)}) collective-permute-start(bf16[128,2432]{1,0:T(8,128)(2,1)} %pad_maximum_fusion.9), channel_id=1, source_target_pairs={{0,2},{1,3},{2,4},{3,5},{4,6},{5,7},{6,0},{7,1},{8,10},{9,11},{10,... | collective-permute-start | bytes 1867784 | tf_op jit(solution)/shard_map/ppermute | solution.py:817
  44.4 24.9 %collective-permute-start.10 = (bf16[128,1408]{1,0:T(8,128)(2,1)S(1)}, bf16[128,1408]{1,0:T(8,128)(2,1)S(1)}, u32[]{:S(2)}, u32[]{:S(2)}) collective-permute-start(bf16[128,1408]{1,0:T(8,128)(2,1)S(1)} %pad.14), channel_id=1, source_target_pairs={{0,2},{1,3},{2,4},{3,5},{4,6},{5,7},{6,0},{7,1},{8,10},{9,11},{10,... | collective-permute-start | bytes 1081352 | tf_op jit(solution)/shard_map/ppermute | solution.py:817
  70.1 25.2 %collective-permute-start.16 = (bf16[2,128,1408]{2,1,0:T(8,128)(2,1)S(1)}, bf16[2,128,1408]{2,1,0:T(8,128)(2,1)S(1)}, u32[]{:S(2)}, u32[]{:S(2)}) collective-permute-start(bf16[2,128,1408]{2,1,0:T(8,128)(2,1)S(1)} %pad_maximum_fusion.1), channel_id=1, source_target_pairs={{0,16},{8,24},{16,0},{24,8},{1,17},{9,25},{17,1},{25,9},{2,18},{10... | collective-permute-start | bytes 2162696 | tf_op jit(solution)/shard_map/ppermute | solution.py:764
  70.7 24.6 %collective-permute-start.13 = (bf16[128,2432]{1,0:T(8,128)(2,1)S(1)}, bf16[128,2432]{1,0:T(8,128)(2,1)S(1)}, u32[]{:S(2)}, u32[]{:S(2)}) collective-permute-start(bf16[128,2432]{1,0:T(8,128)(2,1)S(1)} %collective-permute-done.9.refs_1_.refs_8_), channel_id=1, source_target_pairs={{0,1},{1,0},{2,3},{3,2},{4,5},{5,4},{6,7},{7,6},{8,9},{9,8},{10,11... | collective-permute-start | bytes 1867784 | tf_op jit(solution)/shard_map/ppermute | solution.py:764
  71.9 23.4 %collective-permute-start.12 = (bf16[128,2432]{1,0:T(8,128)(2,1)S(1)}, bf16[128,2432]{1,0:T(8,128)(2,1)S(1)}, u32[]{:S(2)}, u32[]{:S(2)}) collective-permute-start(bf16[128,2432]{1,0:T(8,128)(2,1)S(1)} %collective-permute-done.9.refs_1_.refs_8_), channel_id=1, source_target_pairs={{0,2},{1,3},{2,4},{3,5},{4,6},{5,7},{6,0},{7,1},{8,10},{9,11},{10,... | collective-permute-start | bytes 1867784 | tf_op jit(solution)/shard_map/ppermute | solution.py:817
  71.9 21.0 %collective-permute-start.15 = (bf16[128,1408]{1,0:T(8,128)(2,1)}, bf16[128,1408]{1,0:T(8,128)(2,1)S(1)}, u32[]{:S(2)}, u32[]{:S(2)}) collective-permute-start(bf16[128,1408]{1,0:T(8,128)(2,1)} %copy-done.47), channel_id=1, source_target_pairs={{0,1},{1,0},{2,3},{3,2},{4,5},{5,4},{6,7},{7,6},{8,9},{9,8},{10,11... | collective-permute-start | bytes 1081352 | tf_op jit(solution)/shard_map/ppermute | solution.py:764
  72.7 22.6 %collective-permute-start.14 = (bf16[128,1408]{1,0:T(8,128)(2,1)}, bf16[128,1408]{1,0:T(8,128)(2,1)S(1)}, u32[]{:S(2)}, u32[]{:S(2)}) collective-permute-start(bf16[128,1408]{1,0:T(8,128)(2,1)} %copy-done.47), channel_id=1, source_target_pairs={{0,2},{1,3},{2,4},{3,5},{4,6},{5,7},{6,0},{7,1},{8,10},{9,11},{10,... | collective-permute-start | bytes 1081352 | tf_op jit(solution)/shard_map/ppermute | solution.py:817
  96.5 21.0 %collective-permute-start.19 = (bf16[2,128,1408]{2,1,0:T(8,128)(2,1)}, bf16[2,128,1408]{2,1,0:T(8,128)(2,1)S(1)}, u32[]{:S(2)}, u32[]{:S(2)}) collective-permute-start(bf16[2,128,1408]{2,1,0:T(8,128)(2,1)} %pad_maximum_fusion.2), channel_id=1, source_target_pairs={{0,16},{8,24},{16,0},{24,8},{1,17},{9,25},{17,1},{25,9},{2,18},{10... | collective-permute-start | bytes 2162696 | tf_op jit(solution)/shard_map/ppermute | solution.py:764
  98.0 19.4 %collective-permute-start.18 = (bf16[128,2432]{1,0:T(8,128)(2,1)S(1)}, bf16[128,2432]{1,0:T(8,128)(2,1)S(1)}, u32[]{:S(2)}, u32[]{:S(2)}) collective-permute-start(bf16[128,2432]{1,0:T(8,128)(2,1)S(1)} %collective-permute-done.12.refs_2_.refs_9_), channel_id=1, source_target_pairs={{0,1},{1,0},{2,3},{3,2},{4,5},{5,4},{6,7},{7,6},{8,9},{9,8},{10,11... | collective-permute-start | bytes 1867784 | tf_op jit(solution)/shard_map/ppermute | solution.py:764
  99.2 18.3 %collective-permute-start.17 = (bf16[128,2432]{1,0:T(8,128)(2,1)S(1)}, bf16[128,2432]{1,0:T(8,128)(2,1)S(1)}, u32[]{:S(2)}, u32[]{:S(2)}) collective-permute-start(bf16[128,2432]{1,0:T(8,128)(2,1)S(1)} %collective-permute-done.12.refs_2_.refs_9_), channel_id=1, source_target_pairs={{0,2},{1,3},{2,4},{3,5},{4,6},{5,7},{6,0},{7,1},{8,10},{9,11},{10,... | collective-permute-start | bytes 1867784 | tf_op jit(solution)/shard_map/ppermute | solution.py:817
  116.8 14.9 %collective-permute-start.22 = (bf16[1024,256]{1,0:T(8,128)(2,1)S(1)}, bf16[1024,256]{1,0:T(8,128)(2,1)S(1)}, u32[]{:S(2)}, u32[]{:S(2)}) collective-permute-start(bf16[1024,256]{1,0:T(8,128)(2,1)S(1)} %pad_maximum_fusion.10), channel_id=1, source_target_pairs={{0,16},{8,24},{16,0},{24,8},{1,17},{9,25},{17,1},{25,9},{2,18},{10... | collective-permute-start | bytes 1572872 | tf_op jit(solution)/shard_map/ppermute | solution.py:764
  117.5 14.3 %collective-permute-start.21 = (bf16[128,2432]{1,0:T(8,128)(2,1)S(1)}, bf16[128,2432]{1,0:T(8,128)(2,1)S(1)}, u32[]{:S(2)}, u32[]{:S(2)}) collective-permute-start(bf16[128,2432]{1,0:T(8,128)(2,1)S(1)} %collective-permute-done.17.refs_3_.refs_10_), channel_id=1, source_target_pairs={{0,1},{1,0},{2,3},{3,2},{4,5},{5,4},{6,7},{7,6},{8,9},{9,8},{10,11... | collective-permute-start | bytes 1867784 | tf_op jit(solution)/shard_map/ppermute | solution.py:764
  118.4 13.3 %collective-permute-start.20 = (bf16[128,1408]{1,0:T(8,128)(2,1)S(1)}, bf16[128,1408]{1,0:T(8,128)(2,1)S(1)}, u32[]{:S(2)}, u32[]{:S(2)}) collective-permute-start(bf16[128,1408]{1,0:T(8,128)(2,1)S(1)} %collective-permute-done.14.refs_16_), channel_id=1, source_target_pairs={{0,2},{1,3},{2,4},{3,5},{4,6},{5,7},{6,0},{7,1},{8,10},{9,11},{10,... | collective-permute-start | bytes 1081352 | tf_op jit(solution)/shard_map/ppermute | solution.py:817
  119.8 27.1 %collective-permute-start.24 = (bf16[2,128,1408]{2,1,0:T(8,128)(2,1)}, bf16[2,128,1408]{2,1,0:T(8,128)(2,1)S(1)}, u32[]{:S(2)}, u32[]{:S(2)}) collective-permute-start(bf16[2,128,1408]{2,1,0:T(8,128)(2,1)} %pad_maximum_fusion.4), channel_id=1, source_target_pairs={{0,16},{8,24},{16,0},{24,8},{1,17},{9,25},{17,1},{25,9},{2,18},{10... | collective-permute-start | bytes 2162696 | tf_op jit(solution)/shard_map/ppermute | solution.py:764
  132.9 17.8 %collective-permute-start.23 = (bf16[2,128,1408]{2,1,0:T(8,128)(2,1)}, bf16[2,128,1408]{2,1,0:T(8,128)(2,1)}, u32[]{:S(2)}, u32[]{:S(2)}) collective-permute-start(bf16[2,128,1408]{2,1,0:T(8,128)(2,1)} %pad_maximum_fusion.3), channel_id=1, source_target_pairs={{0,1},{1,0},{2,3},{3,2},{4,5},{5,4},{6,7},{7,6},{8,9},{9,8},{10,11... | collective-permute-start | bytes 2162696 | tf_op jit(solution)/shard_map/ppermute | solution.py:764
  133.8 16.9 %collective-permute-start.25 = (bf16[128,1408]{1,0:T(8,128)(2,1)S(1)}, bf16[128,1408]{1,0:T(8,128)(2,1)S(1)}, u32[]{:S(2)}, u32[]{:S(2)}) collective-permute-start(bf16[128,1408]{1,0:T(8,128)(2,1)S(1)} %slice.228), channel_id=1, source_target_pairs={{0,16},{8,24},{16,0},{24,8},{1,17},{9,25},{17,1},{25,9},{2,18},{10... | collective-permute-start | bytes 1081352 | tf_op jit(solution)/shard_map/ppermute | solution.py:764
  184.1 13.6 %collective-permute-start.28 = (bf16[1024,1024]{1,0:T(8,128)(2,1)}, bf16[1024,1024]{1,0:T(8,128)(2,1)S(1)}, u32[]{:S(2)}, u32[]{:S(2)}) collective-permute-start(bf16[1024,1024]{1,0:T(8,128)(2,1)} %get-tuple-element.248.so), channel_id=1, source_target_pairs={{0,8},{8,0},{16,24},{24,16},{1,9},{9,1},{17,25},{25,17},{2,10},{10... | collective-permute-start | bytes 6291464 | tf_op jit(solution)/shard_map/ppermute | solution.py:764
  197.1 43.8 %collective-permute-start.31 = (bf16[2,4,128,768]{3,2,1,0:T(8,128)(2,1)}, bf16[2,4,128,768]{3,2,1,0:T(8,128)(2,1)S(1)}, u32[]{:S(2)}, u32[]{:S(2)}) collective-permute-start(bf16[2,4,128,768]{3,2,1,0:T(8,128)(2,1)} %get-tuple-element.265), channel_id=1, source_target_pairs={{0,1},{1,0},{2,3},{3,2},{4,5},{5,4},{6,7},{7,6},{8,9},{9,8},{10,11... | collective-permute-start | bytes 4718600 | tf_op jit(solution)/shard_map/ppermute | solution.py:764
  197.7 44.6 %collective-permute-start.32 = (bf16[8,128,640]{2,1,0:T(8,128)(2,1)}, bf16[8,128,640]{2,1,0:T(8,128)(2,1)}, u32[]{:S(2)}, u32[]{:S(2)}) collective-permute-start(bf16[8,128,640]{2,1,0:T(8,128)(2,1)} %get-tuple-element.266), channel_id=1, source_target_pairs={{0,16},{8,24},{16,0},{24,8},{1,17},{9,25},{17,1},{25,9},{2,18},{10... | collective-permute-start | bytes 3932168 | tf_op jit(solution)/shard_map/ppermute | solution.py:764
  223.3 19.0 %collective-permute-start.30 = (bf16[512,1024]{1,0:T(8,128)(2,1)}, bf16[512,1024]{1,0:T(8,128)(2,1)S(1)}, u32[]{:S(2)}, u32[]{:S(2)}) collective-permute-start(bf16[512,1024]{1,0:T(8,128)(2,1)} %get-tuple-element.264), channel_id=1, source_target_pairs={{0,8},{8,0},{16,24},{24,16},{1,9},{9,1},{17,25},{25,17},{2,10},{10... | collective-permute-start | bytes 3145736 | tf_op jit(solution)/shard_map/ppermute | solution.py:764
  223.4 54.5 %collective-permute-start.34 = (bf16[2,4,656,128]{3,2,1,0:T(8,128)(2,1)}, bf16[2,4,656,128]{3,2,1,0:T(8,128)(2,1)}, u32[]{:S(2)}, u32[]{:S(2)}) collective-permute-start(bf16[2,4,656,128]{3,2,1,0:T(8,128)(2,1)} %get-tuple-element.281), channel_id=1, source_target_pairs={{0,1},{1,0},{2,3},{3,2},{4,5},{5,4},{6,7},{7,6},{8,9},{9,8},{10,11... | collective-permute-start | bytes 4030472 | tf_op jit(solution)/shard_map/ppermute | solution.py:764
  224.9 17.4 %collective-permute-start.29 = (bf16[1024,256]{1,0:T(8,128)(2,1)S(1)}, bf16[1024,256]{1,0:T(8,128)(2,1)S(1)}, u32[]{:S(2)}, u32[]{:S(2)}) collective-permute-start(bf16[1024,256]{1,0:T(8,128)(2,1)S(1)} %copy-done.53), channel_id=1, source_target_pairs={{0,16},{8,24},{16,0},{24,8},{1,17},{9,25},{17,1},{25,9},{2,18},{10... | collective-permute-start | bytes 1572872 | tf_op jit(solution)/shard_map/ppermute | solution.py:764
  240.9 37.0 %collective-permute-start.33 = (bf16[8,256,128]{2,1,0:T(8,128)(2,1)}, bf16[8,256,128]{2,1,0:T(8,128)(2,1)S(1)}, u32[]{:S(2)}, u32[]{:S(2)}) collective-permute-start(bf16[8,256,128]{2,1,0:T(8,128)(2,1)} %get-tuple-element.280), channel_id=1, source_target_pairs={{0,16},{8,24},{16,0},{24,8},{1,17},{9,25},{17,1},{25,9},{2,18},{10... | collective-permute-start | bytes 1572872 | tf_op jit(solution)/shard_map/ppermute | solution.py:764
  243.7 45.2 %collective-permute-start.35 = (bf16[4,128,768]{2,1,0:T(8,128)(2,1)}, bf16[4,128,768]{2,1,0:T(8,128)(2,1)S(1)}, u32[]{:S(2)}, u32[]{:S(2)}) collective-permute-start(bf16[4,128,768]{2,1,0:T(8,128)(2,1)} %get-tuple-element.361), channel_id=1, source_target_pairs={{0,16},{8,24},{16,0},{24,8},{1,17},{9,25},{17,1},{25,9},{2,18},{10... | collective-permute-start | bytes 2359304 | tf_op jit(solution)/shard_map/ppermute | solution.py:764
  246.1 42.8 %collective-permute-start.36 = (bf16[4,128,640]{2,1,0:T(8,128)(2,1)S(1)}, bf16[4,128,640]{2,1,0:T(8,128)(2,1)S(1)}, u32[]{:S(2)}, u32[]{:S(2)}) collective-permute-start(bf16[4,128,640]{2,1,0:T(8,128)(2,1)S(1)} %get-tuple-element.365), channel_id=1, source_target_pairs={{0,1},{1,0},{2,3},{3,2},{4,5},{5,4},{6,7},{7,6},{8,9},{9,8},{10,11... | collective-permute-start | bytes 1966088 | tf_op jit(solution)/shard_map/ppermute | solution.py:764
  280.6 39.3 %collective-permute-start.39 = (bf16[4,656,128]{2,1,0:T(8,128)(2,1)}, bf16[4,656,128]{2,1,0:T(8,128)(2,1)}, u32[]{:S(2)}, u32[]{:S(2)}) collective-permute-start(bf16[4,656,128]{2,1,0:T(8,128)(2,1)} %get-tuple-element.363), channel_id=1, source_target_pairs={{0,16},{8,24},{16,0},{24,8},{1,17},{9,25},{17,1},{25,9},{2,18},{10... | collective-permute-start | bytes 2015240 | tf_op jit(solution)/shard_map/ppermute | solution.py:764
  291.7 28.2 %collective-permute-start.37 = (bf16[2,128,1408]{2,1,0:T(8,128)(2,1)}, bf16[2,128,1408]{2,1,0:T(8,128)(2,1)S(1)}, u32[]{:S(2)}, u32[]{:S(2)}) collective-permute-start(bf16[2,128,1408]{2,1,0:T(8,128)(2,1)} %pad_maximum_fusion.5), channel_id=1, source_target_pairs={{0,2},{1,3},{2,0},{3,1},{4,6},{5,7},{6,4},{7,5},{8,10},{9,11},{10,... | collective-permute-start | bytes 2162696 | tf_op jit(solution)/shard_map/ppermute | solution.py:764
  293.0 26.9 %collective-permute-start.38 = (bf16[4,640,128]{2,1,0:T(8,128)(2,1)}, bf16[4,640,128]{2,1,0:T(8,128)(2,1)}, u32[]{:S(2)}, u32[]{:S(2)}) collective-permute-start(bf16[4,640,128]{2,1,0:T(8,128)(2,1)} %pad_maximum_fusion.8), channel_id=1, source_target_pairs={{0,1},{1,0},{2,3},{3,2},{4,5},{5,4},{6,7},{7,6},{8,9},{9,8},{10,11... | collective-permute-start | bytes 1966088 | tf_op jit(solution)/shard_map/ppermute | solution.py:764
  316.1 20.9 %collective-permute-start.40 = (bf16[2,512,1024]{2,1,0:T(8,128)(2,1)}, bf16[2,512,1024]{2,1,0:T(8,128)(2,1)}, u32[]{:S(2)}, u32[]{:S(2)}) collective-permute-start(bf16[2,512,1024]{2,1,0:T(8,128)(2,1)} %back_project.2), channel_id=1, source_target_pairs={{0,8},{8,0},{16,24},{24,16},{1,9},{9,1},{17,25},{25,17},{2,10},{10... | collective-permute-start | bytes 6291464 | tf_op jit(solution)/shard_map/ppermute | solution.py:764
  328.5 21.2 %collective-permute-start.43 = (bf16[128,1408]{1,0:T(8,128)(2,1)}, bf16[128,1408]{1,0:T(8,128)(2,1)S(1)}, u32[]{:S(2)}, u32[]{:S(2)}) collective-permute-start(bf16[128,1408]{1,0:T(8,128)(2,1)} %get-tuple-element.369), channel_id=1, source_target_pairs={{0,4},{1,5},{2,6},{3,7},{4,0},{5,1},{6,2},{7,3},{8,12},{9,13},{10,... | collective-permute-start | bytes 1081352 | tf_op jit(solution)/shard_map/ppermute | solution.py:764
  336.1 24.7 %collective-permute-start.44 = (bf16[2,1296,128]{2,1,0:T(8,128)(2,1)S(1)}, bf16[2,1296,128]{2,1,0:T(8,128)(2,1)S(1)}, u32[]{:S(2)}, u32[]{:S(2)}) collective-permute-start(bf16[2,1296,128]{2,1,0:T(8,128)(2,1)S(1)} %pad_maximum_fusion.6), channel_id=1, source_target_pairs={{0,2},{1,3},{2,0},{3,1},{4,6},{5,7},{6,4},{7,5},{8,10},{9,11},{10,... | collective-permute-start | bytes 1990664 | tf_op jit(solution)/shard_map/ppermute | solution.py:764
  337.3 12.4 %collective-permute-start.42 = (bf16[4,384,128]{2,1,0:T(8,128)(2,1)}, bf16[4,384,128]{2,1,0:T(8,128)(2,1)S(1)}, u32[]{:S(2)}, u32[]{:S(2)}) collective-permute-start(bf16[4,384,128]{2,1,0:T(8,128)(2,1)} %get-tuple-element.317), channel_id=1, source_target_pairs={{0,1},{1,0},{2,3},{3,2},{4,5},{5,4},{6,7},{7,6},{8,9},{9,8},{10,11... | collective-permute-start | bytes 1179656 | tf_op jit(solution)/shard_map/ppermute | solution.py:764
  343.1 17.8 %collective-permute-start.45 = (f32[2,1024]{1,0:T(2,128)S(1)}, f32[2,1024]{1,0:T(2,128)S(1)}, u32[]{:S(2)}, u32[]{:S(2)}) collective-permute-start(f32[2,1024]{1,0:T(2,128)S(1)} %add.246), channel_id=1, source_target_pairs={{0,1},{1,0},{2,3},{3,2},{4,5},{5,4},{6,7},{7,6},{8,9},{9,8},{10,11... | collective-permute-start | bytes 24584 | tf_op jit(solution)/shard_map/ppermute | solution.py:764
  346.6 41.5 %collective-permute-start.46 = (bf16[512,1024]{1,0:T(8,128)(2,1)S(1)}, bf16[512,1024]{1,0:T(8,128)(2,1)S(1)}, u32[]{:S(2)}, u32[]{:S(2)}) collective-permute-start(bf16[512,1024]{1,0:T(8,128)(2,1)S(1)} %fusion.2), channel_id=1, source_target_pairs={{0,16},{8,24},{16,0},{24,8},{1,17},{9,25},{17,1},{25,9},{2,18},{10... | collective-permute-start | bytes 3145736 | tf_op jit(solution)/shard_map/ppermute | solution.py:764
  361.8 7.7 %collective-permute-start.47 = (bf16[2,384,128]{2,1,0:T(8,128)(2,1)}, bf16[2,384,128]{2,1,0:T(8,128)(2,1)}, u32[]{:S(2)}, u32[]{:S(2)}) collective-permute-start(bf16[2,384,128]{2,1,0:T(8,128)(2,1)} %get-tuple-element.381), channel_id=1, source_target_pairs={{0,2},{1,3},{2,0},{3,1},{4,6},{5,7},{6,4},{7,5},{8,10},{9,11},{10,... | collective-permute-start | bytes 589832 | tf_op jit(solution)/shard_map/ppermute | solution.py:764
  364.6 19.0 %collective-permute-start.51 = (bf16[1296,128]{1,0:T(8,128)(2,1)}, bf16[1296,128]{1,0:T(8,128)(2,1)}, u32[]{:S(2)}, u32[]{:S(2)}) collective-permute-start(bf16[1296,128]{1,0:T(8,128)(2,1)} %fusion.14), channel_id=1, source_target_pairs={{0,4},{1,5},{2,6},{3,7},{4,0},{5,1},{6,2},{7,3},{8,12},{9,13},{10,... | collective-permute-start | bytes 995336 | tf_op jit(solution)/shard_map/ppermute | solution.py:764
  369.5 18.6 %collective-permute-start.49 = (f32[2,1024]{1,0:T(2,128)S(1)}, f32[2,1024]{1,0:T(2,128)S(1)}, u32[]{:S(2)}, u32[]{:S(2)}) collective-permute-start(f32[2,1024]{1,0:T(2,128)S(1)} %add.250), channel_id=1, source_target_pairs={{0,4},{1,5},{2,6},{3,7},{4,0},{5,1},{6,2},{7,3},{8,12},{9,13},{10,... | collective-permute-start | bytes 24584 | tf_op jit(solution)/shard_map/ppermute | solution.py:764
  370.5 15.2 %collective-permute-start.52 = (bf16[384,128]{1,0:T(8,128)(2,1)S(1)}, bf16[384,128]{1,0:T(8,128)(2,1)S(1)}, u32[]{:S(2)}, u32[]{:S(2)}) collective-permute-start(bf16[384,128]{1,0:T(8,128)(2,1)S(1)} %fusion.17), channel_id=1, source_target_pairs={{0,4},{1,5},{2,6},{3,7},{4,0},{5,1},{6,2},{7,3},{8,12},{9,13},{10,... | collective-permute-start | bytes 294920 | tf_op jit(solution)/shard_map/ppermute | solution.py:764
  388.1 9.1 %collective-permute-start.50 = (f32[2,1024]{1,0:T(2,128)S(1)}, f32[2,1024]{1,0:T(2,128)S(1)}, u32[]{:S(2)}, u32[]{:S(2)}) collective-permute-start(f32[2,1024]{1,0:T(2,128)S(1)} %add.251), channel_id=1, source_target_pairs={{0,16},{8,24},{16,0},{24,8},{1,17},{9,25},{17,1},{25,9},{2,18},{10... | collective-permute-start | bytes 24584 | tf_op jit(solution)/shard_map/ppermute | solution.py:764
  (60 other events, 502.1 us)

commit v4 on v3

--- a/solution.py
+++ b/solution.py
@@ -344,7 +344,7 @@
     )(q, do, *contexts, *lses, k, v, cosine, sine, *((*earlier, cosine, sine) if last else ()), *after)
 
 
-def out_kernel(count, places, idx, ma_ref, mb_ref, other_ref, *refs):
+def out_kernel(count, places, idx, ma_ref, mb_ref, oa_ref, ob_ref, *refs):
     w_refs, (o_ref, wsel_ref, w_s, sem) = refs[:-4], refs[-4:]
     copies = fetch_rows(count, idx, w_refs, places, WIDTH, w_s, sem)
     for copy in copies:
@@ -355,8 +355,8 @@
     wsel_ref[0:COLS] = w_s[aligned(seq, COLS)]
     wsel_ref[COLS:] = w_s[aligned(jnp.bitwise_xor(seq, 2), COLS)]
     rows = ma_ref.shape[0]
-    for r, mine in enumerate((ma_ref, mb_ref)):
-        both = jnp.concatenate([mine[...], other_ref[r * rows : (r + 1) * rows]], axis=1)
+    for r, (mine, other) in enumerate(((ma_ref, oa_ref), (mb_ref, ob_ref))):
+        both = jnp.concatenate([mine[...], other[...]], axis=1)
         value = jnp.dot(both, wsel_ref[...], preferred_element_type=f32)
         o_ref[r * rows : (r + 1) * rows] = value.astype(bf16)
 
@@ -366,14 +366,14 @@
     arrays, where = pieces
     return pl.pallas_call(
         partial(out_kernel, count, where),
-        in_specs=[SMEM] + [vmem] * 3 + [ANY] * len(arrays),
+        in_specs=[SMEM] + [vmem] * 4 + [ANY] * len(arrays),
         out_specs=[vmem, vmem],
         out_shape=[sds((2 * mine[0].shape[0], WIDTH)), sds((2 * COLS, WIDTH))],
         scratch_shapes=[pltpu.VMEM((WIDTH, WIDTH), bf16), pltpu.SemaphoreType.DMA((count,))],
         compiler_params=params(),
         cost_estimate=cost(5),
         name="out_project",
-    )(idx, *mine, other, *arrays)
+    )(idx, *mine, *other, *arrays)
 
 
 def mlp_kernel(count, n_arrays, mine, other, down, idx, *refs):
@@ -476,7 +476,7 @@
     )(idx, x0, x1, po, pr, c0, c1, gains, *arrays)
 
 
-def down_kernel(count, idx, hid_ref, wd_ref, c0, c1, ma, mb, other, low, res_other, res_mine, *refs):
+def down_kernel(count, idx, hid_ref, wd_ref, c0, c1, ma, mb, oa, ob, low, res_other, res_mine, *refs):
     outs, downs, acc = refs[:2], refs[2:-1], refs[-1]
     shard, x_place = idx[0], idx[2]
     rows = c0.shape[0]
@@ -492,7 +492,8 @@
         for r in range(count):
             downs[r // 4][part, r % 4] = acc[here, places[r]].astype(bf16)
     mine = jnp.concatenate([ma[...], mb[...]], axis=0)
-    for part, context in enumerate((mine, other[...])):
+    other = jnp.concatenate([oa[...], ob[...]], axis=0)
+    for part, context in enumerate((mine, other)):
         acc[0:COLS] = lax.dot_general(context, low[...], ROWS_BY_COLS, preferred_element_type=f32)
         for r in range(count):
             outs[part][r] = acc[0:COLS, places[r]].astype(bf16)
@@ -508,7 +509,7 @@
     vmem = pl.BlockSpec(memory_space=pltpu.VMEM)
     return pl.pallas_call(
         partial(down_kernel, count),
-        in_specs=[SMEM] + [vmem] * 8,
+        in_specs=[SMEM] + [vmem] * 9,
         out_specs=[vmem] * (4 + split),
         out_shape=[sds((rows, WIDTH))] * 2
         + [sds((count, COLS, WIDTH // count))] * 2
@@ -517,7 +518,7 @@
         compiler_params=params(),
         cost_estimate=cost(15),
         name="down_project",
-    )(idx, hidden, wd, c0, c1, *mine, other, low)
+    )(idx, hidden, wd, c0, c1, *mine, *other, low)
 
 
 def norm_two_kernel(x0, x1, po, pr, so, sr, c0, c1, g_ref, wsel, res_o, low_o, mine_o, other_o, gain_o):
@@ -812,22 +813,22 @@
         gain_rows = jnp.concatenate([attn_gain, mlp_gain, jnp.zeros(3 * COLS - 2 * piece, bf16)])[None]
         a0 = jnp.concatenate([w_qkv, jnp.pad(gain_rows, ((0, EXTRA - 1), (0, 0)))], axis=0)
         f0 = jnp.concatenate([w_mine, out_weight, w_down], axis=1)
-        g0, h0 = f0[:, : PADDED + WIDTH], f0[:, PADDED + WIDTH :]
         narrow = lambda value: value[..., :PADDED]
         ring = lambda value: lax.ppermute(
             value, "shard", [(place, (place + 2) % 8) for place in range(8)]
         )
         a4, a2, a1 = by_zz(a0), by_z(a0), by_y(a0)
-        a4, a2, a1, x0, cosine, sine, idx, f0, g0, h0, w_other = together(
-            a4, a2, a1, x0, cosine, sine, idx, f0, g0, h0, w_other
+        a4, a2, a1, x0, cosine, sine, idx, f0, w_other = together(
+            a4, a2, a1, x0, cosine, sine, idx, f0, w_other
         )
         a6, a35 = by_z(a4), by_y(jnp.stack([a2, a4]))
         x1 = by_core(x0)
         a6, a35, x2 = together(a6, a35, x2)
         a7 = by_y(a6)
         x3 = by_core(x2)
-        x3, x1, a7, f0, g0, h0 = together(x3, x1, a7, f0, g0, h0)
-        g1, h1, f4 = ring(g0), ring(h0), by_y(f0)
+        x3, x1, a7, f0 = together(x3, x1, a7, f0)
+        f1, f4 = ring(f0), by_y(f0)
+        c1 = by_core(c0)
         first_low, q, k, v, w_full, gains = qkv_call(
             count,
             idx,
@@ -841,41 +842,32 @@
             cosine,
             sine,
         )
-        q, g1, h1, f4 = together(q, g1, h1, f4)
-        g2, g5, h2, h5 = ring(g1), by_y(g1), ring(h1), by_y(h1)
-        e14 = by_x(jnp.stack([narrow(g1), narrow(f4)]))
+        q, f1, f4, c1 = together(q, f1, f4, c1)
+        f2, f5 = ring(f1), by_y(f1)
+        e14 = by_x(jnp.stack([narrow(f1), narrow(f4)]))
         ctx_fa, lse_fa = attend(q, k, v, 2)
         ctx_fa, q = together(ctx_fa, q)
+        oth_a = by_x(ctx_fa)
         ctx_fb, lse_fb = attend(q, k, v, 3)
-        ctx_fa, ctx_fb, q, g2, g5, h2, h5, e14 = together(ctx_fa, ctx_fb, q, g2, g5, h2, h5, e14)
-        other = by_x(jnp.concatenate([ctx_fa, ctx_fb], axis=0))
-        g3, g6 = ring(g2), by_y(g2)
-        e25 = by_x(jnp.stack([narrow(g2), narrow(g5)]))
+        ctx_fb, q, f2, f5, e14, oth_a = together(ctx_fb, q, f2, f5, e14, oth_a)
+        oth_b = by_x(ctx_fb)
+        f3, f6 = ring(f2), by_y(f2)
+        e25 = by_x(jnp.stack([narrow(f2), narrow(f5)]))
         ctx_na, lse_na = attend(q, k, v, 0)
         ctx_na, q = together(ctx_na, q)
         ctx_nb, lse_nb = attend(q, k, v, 1)
-        ctx_nb, g3, g6, e25, h2, h5 = together(ctx_nb, g3, g6, e25, h2, h5)
-        g7 = by_y(g3)
-        h3 = ring(h2)
-        e36 = by_x(jnp.stack([narrow(g3), narrow(g6)]))
-        ctx_nb, h3, g7, other = together(ctx_nb, h3, g7, other)
-        h67 = by_y(jnp.stack([h2, h3]))
-        e7 = by_x(narrow(g7))
-        arrays = (f0, g1, g2, g3, f4, g5, g6, g7, h1, h2, h3, h5, h67, w_other, e14, e25, e36, e7)
-        wide_at = tuple((array, None) for array in range(8))
-        mine_at = tuple((array, lead, 0) for array, lead in wide_at)
-        out_pieces = (arrays[:8], tuple((array, lead, PADDED) for array, lead in wide_at))
-        late = PADDED + WIDTH
-        down_at = tuple(
-            (array, lead, column)
-            for array, lead, column in
-            ((0, None, late), (8, None, 0), (9, None, 0), (10, None, 0))
-            + ((4, None, late), (11, None, 0), (12, 0, 0), (12, 1, 0))
-        )
+        ctx_nb, f3, f6, e25, oth_b = together(ctx_nb, f3, f6, e25, oth_b)
+        f7 = by_y(f3)
+        e36 = by_x(jnp.stack([narrow(f3), narrow(f6)]))
+        ctx_nb, f7 = together(ctx_nb, f7)
+        e7 = by_x(narrow(f7))
+        arrays = (f0, f1, f2, f3, f4, f5, f6, f7, w_other, e14, e25, e36, e7)
+        mine_at = tuple((array, None, 0) for array in range(8))
+        out_pieces = (arrays[:8], tuple((array, None, PADDED) for array in range(8)))
+        down_at = tuple((array, None, PADDED + WIDTH) for array in range(8))
         other_at = tuple(
             (array, lead, 0)
-            for array, lead in
-            ((13, None), (14, 0), (15, 0), (16, 0), (14, 1), (15, 1), (16, 1), (17, None))
+            for array, lead in ((8, None), (9, 0), (10, 0), (11, 0), (9, 1), (10, 1), (11, 1), (12, None))
         )
     else:
         x1, x3 = by_core(x0), by_core(x2)
@@ -895,11 +887,11 @@
         out_pieces = ((gather(out_weight),), alone)
         mine_at, down_at, other_at = alone, ((1, None, 0),), ((2, None, 0),)
         (ctx_fa, lse_fa), (ctx_fb, lse_fb) = attend(q, k, v, 2), attend(q, k, v, 3)
-        other = by_x(jnp.concatenate([ctx_fa, ctx_fb], axis=0))
+        oth_a, oth_b = by_x(ctx_fa), by_x(ctx_fb)
+        c1 = by_core(c0)
         (ctx_na, lse_na), (ctx_nb, lse_nb) = attend(q, k, v, 0), attend(q, k, v, 1)
-    c1 = by_core(c0)
-
-    near, far = (ctx_na, ctx_nb), (ctx_fa, ctx_fb)
+
+    near, far, other = (ctx_na, ctx_nb), (ctx_fa, ctx_fb), (oth_a, oth_b)
     lse_near, lse_far = (lse_na, lse_nb), (lse_fa, lse_fb)
     out_own, w_sel = out_call(count, idx, near, other, out_pieces)
     if eight:
@@ -941,29 +933,46 @@
     q_n1, grad_far = together(q_n1, grad_far)
     q_f0, k0, v0 = part(1, 0, grad_far, (dk0, dv0))
     if eight:
-        q_f0, out_got, down_got, grad_far = together(q_f0, out_got, down_got, grad_far)
+        q_f0, out_got, down_got, a_got, b_got, grad_far = together(
+            q_f0, out_got, down_got, a_got, b_got, grad_far
+        )
+        both = lambda lo, hi: jnp.concatenate(
+            [plus(a_keep[lo:hi], a_got[lo:hi]), plus(b_keep[lo:hi], b_got[lo:hi])], axis=-1
+        )
+        wide_next, wide_keep = by_z(both(2, 4)), both(0, 2)
         down_keep, down_got = plus(down[0][0], down_got[0]), by_x(plus(down[0][1], down_got[1]))
     raw0 = (q_n0, q_f0, k0, v0)
     *terms0, gain_a = qkv_grad_call(count, idx, first_low, raw0, w_full, gains, 0)
     if eight:
-        terms0[0], terms0[1], a_got, b_got, grad_far = together(
-            terms0[0], terms0[1], a_got, b_got, grad_far
-        )
-        both = lambda lo, hi: jnp.concatenate(
-            [plus(a_keep[lo:hi], a_got[lo:hi]), plus(b_keep[lo:hi], b_got[lo:hi])], axis=-1
-        )
-        wide_next, wide_keep = by_z(both(2, 4)), both(0, 2)
+        terms0[0], terms0[1], grad_far = together(terms0[0], terms0[1], grad_far)
         out_next = by_y(jnp.concatenate([plus(out_keep[4:], out_got[4:]), terms0[1]], axis=1))
         out_keep = plus(out_keep[:4], out_got[:4])
     q_f1, k1, v1 = part(1, 1, grad_far, (dk1, dv1))
+    if eight:
+        q_f1, wide_next, out_next = together(q_f1, wide_next, out_next)
+        wide_last, wide_keep = by_zz(plus(wide_keep[1], wide_next[1])), plus(wide_keep[0], wide_next[0])
     raw1 = (q_n1, q_f1, k1, v1)
     first_core = back_project((raw0, raw1), w_full, 1)
     first_got = by_core(first_core)
     if eight:
-        first_core, q_f1, wide_next, out_next, down_got = together(
-            first_core, q_f1, wide_next, out_next, down_got
-        )
-        wide_last, wide_keep = by_zz(plus(wide_keep[1], wide_next[1])), plus(wide_keep[0], wide_next[0])
+        first_core, q_f1 = together(first_core, q_f1)
+    raw1 = (q_n1, q_f1, k1, v1)
+    *terms1, gain_b = qkv_grad_call(count, idx, first_low, raw1, w_full, gains, 1)
+    if eight:
+        terms1[0], terms1[1], first_got, q_f1 = together(terms1[0], terms1[1], first_got, q_f1)
+        terms1_got = by_y(terms1[1])
+    raw1 = (q_n1, q_f1, k1, v1)
+    first_own = back_project((raw0, raw1), w_full, 0)
+    if eight:
+        first_own, first_got = together(first_own, first_got)
+    far_sum = plus(first_own[1], first_got[1])
+    first_far = by_x(far_sum)
+    gain_terms = jnp.concatenate([gain_a[:1] + gain_b[:1], gain_two[:1]], axis=0)
+    final = lambda mine, got: mine.astype(f32) + got.astype(f32)
+    crossed = (seq == 1) | (seq == 2)
+    cross = [(1, 2), (2, 1)]
+    if eight:
+        first_own, far_sum, down_got, gain_terms = together(first_own, far_sum, down_got, gain_terms)
         rest = lambda lo, hi: jnp.concatenate(
             [
                 plus(down_keep[lo:hi], down_got[lo:hi]),
@@ -973,65 +982,62 @@
             axis=1,
         )
         rest_next, rest_keep = by_z(rest(2, 4)), rest(0, 2)
-    raw1 = (q_n1, q_f1, k1, v1)
-    *terms1, gain_b = qkv_grad_call(count, idx, first_low, raw1, w_full, gains, 1)
-    gain_terms = jnp.concatenate([gain_a[:1] + gain_b[:1], gain_two[:1]], axis=0)
-    if eight:
-        terms1[0], terms1[1], gain_terms, first_got, q_f1 = together(
-            terms1[0], terms1[1], gain_terms, first_got, q_f1
-        )
-        terms1_got = by_y(terms1[1])
         gain_got = by_core(gain_terms)
-        raw1 = (q_n1, q_f1, k1, v1)
-    first_own = back_project((raw0, raw1), w_full, 0)
-    final = lambda mine, got: mine.astype(f32) + got.astype(f32)
-    if eight:
-        first_own, first_got, gain_got = together(first_own, first_got, gain_got)
-        first_far = by_x(plus(first_own[1], first_got[1]))
+        terms1_got, gain_got, down_core = together(terms1_got, gain_got, down_core)
+        terms1_next = by_z(plus(terms1[0][2:], terms1_got[2:]))
+        terms1_keep = plus(terms1[0][:2], terms1_got[:2])
         gain_terms = gain_terms + gain_got
         gain_got = by_y(gain_terms)
-        first_own, terms1_got, wide_last = together(first_own, terms1_got, wide_last)
-        terms1_next = by_z(plus(terms1[0][2:], terms1_got[2:]))
-        terms1_keep = plus(terms1[0][:2], terms1_got[:2])
-        first_own, rest_next, gain_got = together(first_own, rest_next, gain_got)
-        rest_last, rest_keep = by_zz(plus(rest_keep[1], rest_next[1])), plus(rest_keep[0], rest_next[0])
+        result = (
+            x0.astype(f32)
+            + out_own[:rows].astype(f32)
+            + out_core[rows:].astype(f32)
+            + down_mine.astype(f32)
+            + down_core.astype(f32)
+        ).astype(bf16)[None]
+        rest_next, wide_last, gain_got, result = together(rest_next, wide_last, gain_got, result)
+        rest_last, rest_keep = plus(rest_keep[1], rest_next[1]), plus(rest_keep[0], rest_next[0])
+        down_last, down_keep = rest_last[:BLOCK], rest_keep[:BLOCK]
+        down_last = lax.ppermute(
+            down_last,
+            ("seq", "shard"),
+            [(8 * j + i, 8 * (0, 2, 1, 3)[j] + (i ^ 4)) for j in range(4) for i in range(8)],
+        )
+        down_moved = lax.ppermute(down_keep, "seq", cross)
+        rest_last, rest_keep = by_zz(rest_last[BLOCK:]), rest_keep[BLOCK:]
         gain_terms = gain_terms + gain_got
         gain_got = by_z(gain_terms)
-        terms1_next, gain_got = together(terms1_next, gain_got)
+        terms1_next, gain_got, first_far = together(terms1_next, gain_got, first_far)
         terms1_last = by_zz(plus(terms1_keep[1], terms1_next[1]))
         terms1_keep = plus(terms1_keep[0], terms1_next[0])
         gain_terms = gain_terms + gain_got
-        gain_got = by_zz(gain_terms)
-        first_far, gain_got = together(first_far, gain_got)
-        gain_terms = gain_terms + gain_got
+        gain_terms = gain_terms + by_zz(gain_terms)
         gain_terms = gain_terms + by_x(gain_terms)
         wide_total = final(wide_keep, wide_last)
         rest_total = final(rest_keep, rest_last)
-        down_total, out_total = rest_total[:BLOCK], rest_total[BLOCK : BLOCK + COLS]
-        totals = [rest_total[BLOCK + COLS :], final(terms1_keep, terms1_last)]
+        down_total = final(jnp.where(crossed, down_moved, down_keep), down_last)
+        out_total = rest_total[:COLS]
+        totals = [rest_total[COLS:], final(terms1_keep, terms1_last)]
     else:
-        first_far = by_x(plus(first_own[1], first_got[1]))
         wide_sum = plus(wide[0][0, 0], by_x(wide[0][1, 0]))
         scatter = lambda value, dim: lax.psum_scatter(
             value, "shard", scatter_dimension=dim, tiled=True
         ).astype(f32)
         wide_total = scatter(wide_sum, 0)
         down_total = scatter(plus(down[0][0, 0], by_x(down[0][1, 0])), 1)
+        moved = lax.ppermute(down_total.astype(bf16), "seq", cross).astype(f32)
+        down_total = jnp.where(crossed, moved, down_total)
         out_total = scatter(plus(out_keep, by_x(out_send))[0], 1)
         totals = [scatter(terms[0].reshape(3, width, 128), 1) for terms in (terms0, terms1)]
         gain_terms = lax.psum(gain_terms, ("seq", "shard"))
-    result = (
-        x0.astype(f32)
-        + out_own[:rows].astype(f32)
-        + out_core[rows:].astype(f32)
-        + down_mine.astype(f32)
-        + down_core.astype(f32)
-    ).astype(bf16)[None]
+        result = (
+            x0.astype(f32)
+            + out_own[:rows].astype(f32)
+            + out_core[rows:].astype(f32)
+            + down_mine.astype(f32)
+            + down_core.astype(f32)
+        ).astype(bf16)[None]
     input_grad = norm_one_call(x0, res, first_own, first_got, first_far, gains)[None]
-    if eight:
-        down_total, first_own = together(down_total, first_own)
-    moved = lax.ppermute(down_total.astype(bf16), "seq", [(1, 2), (2, 1)]).astype(f32)
-    down_total = jnp.where((seq == 1) | (seq == 2), moved, down_total)
     take = width // (4 * shards)
     gain_out = lax.dynamic_slice_in_dim(gain_terms, (seq * shards + shard) * take, take, 1)
     qkv_out = jnp.concatenate([total.reshape(3, piece, 128) for total in totals], axis=2)

time: 404 us -> 387 us (0.958)
  other arithmetic: 41 us -> 31.6 us
  waiting for transfers between devices: 88.8 us -> 80.8 us
    ppermute x6 -> x3, waiting for transfers between devices: 15.2 us -> 3.48 us  [per_device(): lax.ppermute(value, 'shard', [(place, (place + 2) % 8) for place in range...]
    ppermute x1 -> x2, waiting for transfers between devices: 0.01 us -> 4.44 us  [the longest x1 4.43 us: per_device(): lax.ppermute(down_last, ('seq', 'shard'), [(8 * j + i, 8 * (0, 2, 1, 3)[j...]
    ppermute x47 -> x46, waiting for transfers between devices: 73.7 us -> 72.9 us  [swap(): lax.ppermute(value, axis, [(place, place ^ bits) for place in range(size)])]
    ppermute x47 -> x46, starting transfers between devices: 45.3 us -> 45.2 us  [swap(): lax.ppermute(value, axis, [(place, place ^ bits) for place in range(size)])]
  transfers between devices with their start and end apart: 54 -> 51, of which waited for: 16 -> 17; matrix products, arithmetic and copies ran while one was open for 11% -> 10% of each run, Pallas kernels for 45% -> 46%
where the time goes in v4:
time: 387 us; the launch traced here: 382 us
  Pallas kernels  207 us (53%)
  waiting for transfers between devices  80.8 us (21%)
  starting transfers between devices  46.5 us (12%)
  other arithmetic  31.6 us (8%)
  local copies, waits for them, and re-layouts  13.8 us (4%)
    ppermute x46, waiting for transfers between devices, swap(): lax.ppermute(value, axis, [(place, place ^ bits) for place in range(size)])  72.9 us
    pallas_call x4, Pallas kernels, attend_back(): pl.pallas_call(lambda *refs: attend_back_kernel(last, pair, *refs[:n_in],...  62.2 us
    ppermute x46, starting transfers between devices, swap(): lax.ppermute(value, axis, [(place, place ^ bits) for place in range(size)])  45.2 us
    pallas_call x4, Pallas kernels, attend(): pl.pallas_call(lambda *refs: attend_kernel(*refs[:3], *refs[3 + len(after...  35.2 us
    pallas_call x1, Pallas kernels, mlp_call(): pl.pallas_call(partial(mlp_kernel, count, len(arrays), mine, other, down)...  26.3 us
    pallas_call x1, Pallas kernels, down_call(): pl.pallas_call(partial(down_kernel, count), in_specs=[SMEM] + [vmem] * 9,...  13.8 us
    pallas_call x1, Pallas kernels, wide_call(): pl.pallas_call(partial(wide_kernel, count), grid_spec=grid_spec, out_shap...  12.7 us
    convert_element_type x13, other arithmetic, plus(): return (left.astype(f32) + right.astype(f32)).astype(bf16)  12.5 us
  transfers between devices with their start and end apart: 51, of which 17 were waited for; matrix products, arithmetic and copies ran while one was open for 10% of the time, Pallas kernels for 46%

profile of v4, /device:TPU:0, one launch (start us, length us, event | category | flops | bytes accessed | tf_op | source)
XLA Modules:
  0.0 381.8 jit_solution(4444280349123337052)
XLA Ops:
  2.9 3.0 collective-permute-start.2
  5.8 1.6 collective-permute-start.1
  7.4 2.6 collective-permute-start
  11.7 2.0 copy.27
  13.9 5.6 %fusion.1 = (f32[2048,128]{1,0:T(8,128)}, f32[2048,128]{1,0:T(8,128)}) fusion(f32[128]{0:T(128)S(1)} %compare_select_fusion, f32[128]{0:T(128)S(1)} %mul.49, f32[2048]{0:T(1024)S(1)} %bitcast.120), kind=kLoop, calls=%fused_computation.12 | loop fusion | flops 524288 | bytes 2106368 | tf_op jit(solution)/shard_map/mul | solution.py:792
  19.9 2.1 fusion.4.refs_0_.refs_7_
  25.6 5.7 %collective-permute-done.3.refs_9_ = bf16[144,768]{1,0:T(8,128)(2,1)S(1)} collective-permute-done((bf16[144,768]{1,0:T(8,128)(2,1)}, bf16[144,768]{1,0:T(8,128)(2,1)S(1)}, u32[]{:S(2)}, u32[]{:S(2)}) %collective-permute-start.3) | collective-permute-done | bytes 221216 | tf_op jit(solution)/shard_map/ppermute | solution.py:765
  31.3 4.1 %collective-permute-done.4.refs_8_ = bf16[2,144,768]{2,1,0:T(8,128)(2,1)S(1)} collective-permute-done((bf16[2,144,768]{2,1,0:T(8,128)(2,1)S(1)}, bf16[2,144,768]{2,1,0:T(8,128)(2,1)S(1)}, u32[]{:S(2)}, u32[]{:S(2)}) %collective-permute-start.4) | collective-permute-done | bytes 442400 | tf_op jit(solution)/shard_map/ppermute | solution.py:765
  36.2 7.1 %collective-permute-done.8.refs_10_ = bf16[144,768]{1,0:T(8,128)(2,1)S(1)} collective-permute-done((bf16[144,768]{1,0:T(8,128)(2,1)S(1)}, bf16[144,768]{1,0:T(8,128)(2,1)S(1)}, u32[]{:S(2)}, u32[]{:S(2)}) %collective-permute-start.8) | collective-permute-done | bytes 221216 | tf_op jit(solution)/shard_map/ppermute | solution.py:765
  44.4 11.6 %project.1 = (bf16[2048,1024]{1,0:T(8,128)(2,1)}, bf16[2048,256]{1,0:T(8,128)(2,1)}, bf16[2048,256]{1,0:T(8,128)(2,1)}, bf16[2048,256]{1,0:T(8,128)(2,1)}, bf16[1024,768]{1,0:T(8,128)(2,1)}, /*index=5*/f32[8,1024]{1,0:T(8,128)}) custom-call(s32[12]{0:T(128)} %stack.87.idx, bf16[512,1024]{1,0:T(8,128)(2,1)} %bitcast.100, bf16[512,1024]{1,0:T(8,128)(2,1)} %copy-done.7, ...), custom_call_target="tpu_custom_call" | custom-call | flops 11 | bytes 11 | tf_op jit(solution)/shard_map/project/pallas_call | solution.py:171
  56.0 10.9 %collective-permute-done.10.refs_4_.refs_11_ = bf16[128,3840]{1,0:T(8,128)(2,1)S(1)} collective-permute-done((bf16[128,3840]{1,0:T(8,128)(2,1)}, bf16[128,3840]{1,0:T(8,128)(2,1)S(1)}, u32[]{:S(2)}, u32[]{:S(2)}) %collective-permute-start.10) | collective-permute-done | bytes 983072 | tf_op jit(solution)/shard_map/ppermute | solution.py:765
  66.9 2.1 collective-permute-done.9.refs_1_.refs_8_
  72.5 8.7 %attend.4 = (bf16[512,256]{1,0:T(8,128)(2,1)}, f32[8,512]{1,0:T(8,128)}) custom-call(bf16[2048,256]{1,0:T(8,128)(2,1)} %get-tuple-element.186.refs_0_, bf16[2048,256]{1,0:T(8,128)(2,1)} %get-tuple-element.175.refs_1_.refs_6_, bf16[2048,256]{1,0:T(8,128)(2,1)} %get-tuple-element.176.refs_2_.refs_7_), custom_call_target="tpu_custom_call" | custom-call | flops 8 | bytes 8 | tf_op jit(solution)/shard_map/attend/pallas_call | solution.py:234
  81.2 1.6 collective-permute-start.15
  82.7 9.1 %attend.5 = (bf16[512,256]{1,0:T(8,128)(2,1)}, f32[8,512]{1,0:T(8,128)}) custom-call(bf16[2048,256]{1,0:T(8,128)(2,1)} %get-tuple-element.186.refs_0_, bf16[2048,256]{1,0:T(8,128)(2,1)} %get-tuple-element.175.refs_1_.refs_6_, bf16[2048,256]{1,0:T(8,128)(2,1)} %get-tuple-element.176.refs_2_.refs_7_), custom_call_target="tpu_custom_call" | custom-call | flops 8 | bytes 8 | tf_op jit(solution)/shard_map/attend/pallas_call | solution.py:234
  91.8 2.0 collective-permute-done.15.oa_ref.oa
  98.3 8.7 %attend.6 = (bf16[512,256]{1,0:T(8,128)(2,1)}, f32[8,512]{1,0:T(8,128)}) custom-call(bf16[2048,256]{1,0:T(8,128)(2,1)} %get-tuple-element.186.refs_0_, bf16[2048,256]{1,0:T(8,128)(2,1)} %get-tuple-element.175.refs_1_.refs_6_, bf16[2048,256]{1,0:T(8,128)(2,1)} %get-tuple-element.176.refs_2_.refs_7_), custom_call_target="tpu_custom_call" | custom-call | flops 8 | bytes 8 | tf_op jit(solution)/shard_map/attend/pallas_call | solution.py:234
  107.0 8.8 %attend.7 = (bf16[512,256]{1,0:T(8,128)(2,1)}, f32[8,512]{1,0:T(8,128)}) custom-call(bf16[2048,256]{1,0:T(8,128)(2,1)} %get-tuple-element.186.refs_0_, bf16[2048,256]{1,0:T(8,128)(2,1)} %get-tuple-element.175.refs_1_.refs_6_, bf16[2048,256]{1,0:T(8,128)(2,1)} %get-tuple-element.176.refs_2_.refs_7_), custom_call_target="tpu_custom_call" | custom-call | flops 8 | bytes 8 | tf_op jit(solution)/shard_map/attend/pallas_call | solution.py:234
  118.1 1.6 collective-permute-start.20
  120.4 17.5 %collective-permute-done.20.refs_7_.refs_14_ = bf16[128,3840]{1,0:T(8,128)(2,1)S(1)} collective-permute-done((bf16[128,3840]{1,0:T(8,128)(2,1)S(1)}, bf16[128,3840]{1,0:T(8,128)(2,1)S(1)}, u32[]{:S(2)}, u32[]{:S(2)}) %collective-permute-start.20) | collective-permute-done | bytes 983072 | tf_op jit(solution)/shard_map/ppermute | solution.py:765
  138.8 5.4 %out_project.1 = (bf16[1024,1024]{1,0:T(8,128)(2,1)}, bf16[512,1024]{1,0:T(8,128)(2,1)}) custom-call(s32[12]{0:T(128)} %stack.87.idx, bf16[512,256]{1,0:T(8,128)(2,1)} %get-tuple-element.185.ma_ref.ma.refs_2_, bf16[512,256]{1,0:T(8,128)(2,1)} %get-tuple-element.193.mb_ref.mb.refs_3_, bf16[512,256]{1,0:T(8,128)(2,1)} %copy-done.24, ...), custom_call_target="tpu_custom_call" | custom-call | flops 5 | bytes 5 | tf_op jit(solution)/shard_map/out_project/pallas_call | solution.py:367
  145.4 4.4 %collective-permute-done.23.refs_3_.pr = bf16[1024,1024]{1,0:T(8,128)(2,1)S(1)} collective-permute-done((bf16[1024,1024]{1,0:T(8,128)(2,1)}, bf16[1024,1024]{1,0:T(8,128)(2,1)S(1)}, u32[]{:S(2)}, u32[]{:S(2)}) %collective-permute-start.23) | collective-permute-done | bytes 2097184 | tf_op jit(solution)/shard_map/ppermute | solution.py:765
  151.1 26.3 %feed_forward.1 = (bf16[1024,1024]{1,0:T(8,128)(2,1)}, bf16[1024,1408]{1,0:T(8,128)(2,1)}, bf16[2,1024,1408]{2,1,0:T(8,128)(2,1)}, bf16[1024,1024]{1,0:T(8,128)(2,1)}, bf16[1024,1408]{1,0:T(8,128)(2,1)}) custom-call(s32[12]{0:T(128)} %stack.87.idx, bf16[512,1024]{1,0:T(8,128)(2,1)} %bitcast.101, bf16[512,1024]{1,0:T(8,128)(2,1)} %copy-done.7, ...), custom_call_target="tpu_custom_call" | custom-call | flops 25 | bytes 25 | tf_op jit(solution)/shard_map/feed_forward/pallas_call | solution.py:445
  177.6 12.7 %wide_grad.1 = (bf16[2,4,128,768]{3,2,1,0:T(8,128)(2,1)}, bf16[2,4,128,768]{3,2,1,0:T(8,128)(2,1)}, bf16[8,128,640]{2,1,0:T(8,128)(2,1)}, bf16[8,128,640]{2,1,0:T(8,128)(2,1)}) custom-call(s32[12]{0:T(128)} %stack.87.idx, bf16[1024,1024]{1,0:T(8,128)(2,1)} %get-tuple-element.221.sn_ref, bf16[2,1024,1408]{2,1,0:T(8,128)(2,1)} %get-tuple-element.222.gug_ref), custom_call_target="tpu_custom_call" | custom-call | flops 12 | bytes 12 | tf_op jit(solution)/shard_map/wide_grad/pallas_call | solution.py:643
  190.3 1.6 collective-permute-start.27
  193.3 10.4 %norm_two_back.1 = (f32[512,1024]{1,0:T(8,128)}, bf16[1024,1024]{1,0:T(8,128)(2,1)}, bf16[1024,256]{1,0:T(8,128)(2,1)}, bf16[1024,256]{1,0:T(8,128)(2,1)}, f32[8,1024]{1,0:T(8,128)}) custom-call(bf16[512,1024]{1,0:T(8,128)(2,1)} %bitcast.102, bf16[512,1024]{1,0:T(8,128)(2,1)} %copy-done.7, bf16[1024,1024]{1,0:T(8,128)(2,1)} %get-tuple-element.202.refs_2_.po, ...), custom_call_target="tpu_custom_call" | custom-call | flops 8 | bytes 8 | tf_op jit(solution)/shard_map/norm_two_back/pallas_call | solution.py:561
  203.7 13.8 %down_project.1 = (bf16[512,1024]{1,0:T(8,128)(2,1)}, bf16[512,1024]{1,0:T(8,128)(2,1)}, bf16[8,256,128]{2,1,0:T(8,128)(2,1)}, bf16[8,256,128]{2,1,0:T(8,128)(2,...) custom-call(s32[12]{0:T(128)} %stack.87.idx, bf16[1024,1408]{1,0:T(8,128)(2,1)} %get-tuple-element.218.hid_ref, ...), custom_call_target="tpu_custom_call" | custom-call | flops 15 | bytes 15 | tf_op jit(solution)/shard_map/down_project/pallas_call | solution.py:510
  218.8 15.3 %attend_back.4 = (bf16[1024,128]{1,0:T(8,128)(2,1)}, f32[2048,128]{1,0:T(8,128)}, f32[2048,128]{1,0:T(8,128)}) custom-call(bf16[2048,256]{1,0:T(8,128)(2,1)} %get-tuple-element.186.refs_0_, bf16[1024,256]{1,0:T(8,128)(2,1)} %get-tuple-element.239.refs_1_, bf16[512,256]{1,0:T(8,128)(2,1)} %get-tuple-element.185.ma_ref.ma.refs_2_, ...), custom_call_target="tpu_custom_call" | custom-call | flops 15 | bytes 15 | tf_op jit(solution)/shard_map/attend_back/pallas_call | solution.py:316
  236.9 1.7 add_convert_fusion.6
  238.6 1.6 collective-permute-start.32
  241.0 15.0 %attend_back.5 = (bf16[1024,128]{1,0:T(8,128)(2,1)}, f32[2048,128]{1,0:T(8,128)}, f32[2048,128]{1,0:T(8,128)}) custom-call(bf16[2048,256]{1,0:T(8,128)(2,1)} %get-tuple-element.186.refs_0_, bf16[1024,256]{1,0:T(8,128)(2,1)} %get-tuple-element.239.refs_1_, bf16[512,256]{1,0:T(8,128)(2,1)} %get-tuple-element.185.ma_ref.ma.refs_2_, ...), custom_call_target="tpu_custom_call" | custom-call | flops 15 | bytes 15 | tf_op jit(solution)/shard_map/attend_back/pallas_call | solution.py:316
  256.0 15.9 %attend_back.6 = (bf16[1024,128]{1,0:T(8,128)(2,1)}, bf16[2048,128]{1,0:T(8,128)(2,1)}, bf16[2048,128]{1,0:T(8,128)(2,1)}) custom-call(bf16[2048,256]{1,0:T(8,128)(2,1)} %get-tuple-element.186.refs_0_, bf16[1024,256]{1,0:T(8,128)(2,1)} %copy-done.17, bf16[512,256]{1,0:T(8,128)(2,1)} %get-tuple-element.182.refs_2_, ...), custom_call_target="tpu_custom_call" | custom-call | flops 15 | bytes 15 | tf_op jit(solution)/shard_map/attend_back/pallas_call | solution.py:316
  273.2 6.2 %project_grad.2 = (bf16[4,384,128]{2,1,0:T(8,128)(2,1)}, bf16[4,384,128]{2,1,0:T(8,128)(2,1)}, f32[8,1024]{1,0:T(8,128)}) custom-call(s32[12]{0:T(128)} %stack.87.idx, bf16[2048,1024]{1,0:T(8,128)(2,1)} %get-tuple-element.258.fn_ref, bf16[1024,128]{1,0:T(8,128)(2,1)} %get-tuple-element.255.qn.q0, bf16[1024,128]{1,0:T(8,128)(2,1)} %get-tuple-element.257.qf.f0, ...), custom_call_target="tpu_custom_call" | custom-call | flops 6 | bytes 6 | tf_op jit(solution)/shard_map/project_grad/pallas_call | solution.py:720
  281.0 16.0 %attend_back.7 = (bf16[1024,128]{1,0:T(8,128)(2,1)}, bf16[2048,128]{1,0:T(8,128)(2,1)}, bf16[2048,128]{1,0:T(8,128)(2,1)}) custom-call(bf16[2048,256]{1,0:T(8,128)(2,1)} %get-tuple-element.186.refs_0_, bf16[1024,256]{1,0:T(8,128)(2,1)} %copy-done.17, bf16[512,256]{1,0:T(8,128)(2,1)} %get-tuple-element.182.refs_2_, ...), custom_call_target="tpu_custom_call" | custom-call | flops 15 | bytes 15 | tf_op jit(solution)/shard_map/attend_back/pallas_call | solution.py:316
  297.1 5.6 %back_project.2 = bf16[2,512,1024]{2,1,0:T(8,128)(2,1)} custom-call(bf16[1024,128]{1,0:T(8,128)(2,1)} %get-tuple-element.255.qn.q0, bf16[1024,128]{1,0:T(8,128)(2,1)} %get-tuple-element.256.q1.qn, bf16[1024,128]{1,0:T(8,128)(2,1)} %get-tuple-element.257.qf.f0, bf16[1024,128]{1,0:T(8,128)(2,1)} %get-tuple-element.280.f1.qf, ...), custom_call_target="tpu_custom_call" | custom-call | flops 5 | bytes 5 | tf_op jit(solution)/shard_map/back_project/pallas_call | solution.py:669
  303.5 3.0 fusion.8
  308.7 3.8 collective-permute-start.38
  312.5 6.2 %project_grad.3 = (bf16[4,384,128]{2,1,0:T(8,128)(2,1)}, bf16[4,384,128]{2,1,0:T(8,128)(2,1)}, f32[8,1024]{1,0:T(8,128)}) custom-call(s32[12]{0:T(128)} %stack.87.idx, bf16[2048,1024]{1,0:T(8,128)(2,1)} %get-tuple-element.258.fn_ref, bf16[1024,128]{1,0:T(8,128)(2,1)} %get-tuple-element.256.q1.qn, bf16[1024,128]{1,0:T(8,128)(2,1)} %get-tuple-element.280.f1.qf, ...), custom_call_target="tpu_custom_call" | custom-call | flops 6 | bytes 6 | tf_op jit(solution)/shard_map/project_grad/pallas_call | solution.py:720
  320.4 5.9 %back_project.3.own = bf16[2,512,1024]{2,1,0:T(8,128)(2,1)} custom-call(bf16[1024,128]{1,0:T(8,128)(2,1)} %get-tuple-element.255.qn.q0, bf16[1024,128]{1,0:T(8,128)(2,1)} %get-tuple-element.256.q1.qn, bf16[1024,128]{1,0:T(8,128)(2,1)} %get-tuple-element.257.qf.f0, bf16[1024,128]{1,0:T(8,128)(2,1)} %get-tuple-element.280.f1.qf, ...), custom_call_target="tpu_custom_call" | custom-call | flops 5 | bytes 5 | tf_op jit(solution)/shard_map/back_project/pallas_call | solution.py:669
  327.8 2.8 fusion.2
  334.1 3.3 collective-permute-done.39
  340.3 2.1 fusion.3
  342.4 8.2 %collective-permute-done.37 = bf16[2,1296,128]{2,1,0:T(8,128)(2,1)S(1)} collective-permute-done((bf16[2,1296,128]{2,1,0:T(8,128)(2,1)S(1)}, bf16[2,1296,128]{2,1,0:T(8,128)(2,1)S(1)}, u32[]{:S(2)}, u32[]{:S(2)}) %collective-permute-start.37) | collective-permute-done | bytes 663584 | tf_op jit(solution)/shard_map/ppermute | solution.py:765
  355.6 7.0 %collective-permute-done.47 = bf16[640,128]{1,0:T(8,128)(2,1)} collective-permute-done((bf16[640,128]{1,0:T(8,128)(2,1)}, bf16[640,128]{1,0:T(8,128)(2,1)}, u32[]{:S(2)}, u32[]{:S(2)}) %collective-permute-start.47) | collective-permute-done | bytes 163872 | tf_op jit(solution)/shard_map/ppermute | solution.py:765
  364.3 3.0 collective-permute-start.45
  367.3 4.4 %collective-permute-done.50 = bf16[656,128]{1,0:T(8,128)(2,1)S(1)} collective-permute-done((bf16[656,128]{1,0:T(8,128)(2,1)S(1)}, bf16[656,128]{1,0:T(8,128)(2,1)S(1)}, u32[]{:S(2)}, u32[]{:S(2)}) %collective-permute-start.50) | collective-permute-done | bytes 167968 | tf_op jit(solution)/shard_map/ppermute | solution.py:1001
  372.5 1.5 collective-permute-start.46
  374.2 5.6 %norm_one_back.1 = f32[512,1024]{1,0:T(8,128)} custom-call(bf16[512,1024]{1,0:T(8,128)(2,1)} %bitcast.103, f32[512,1024]{1,0:T(8,128)} %get-tuple-element.298.res_ref, bf16[2,512,1024]{2,1,0:T(8,128)(2,1)} %back_project.3.own, bf16[2,512,1024]{2,1,0:T(8,128)(2,1)} %copy-done.16, bf16[512,1024]{1,0:T(8,128)(2,1)} %copy-done.22, ...), custom_call_target="tpu_custom_call" | custom-call | flops 3 | bytes 3 | tf_op jit(solution)/shard_map/norm_one_back/pallas_call | solution.py:744
  (244 shorter events, 55.1 us)
Async XLA Ops:
  2.9 20.7 %collective-permute-start.2 = (bf16[144,768]{1,0:T(8,128)(2,1)}, bf16[144,768]{1,0:T(8,128)(2,1)}, u32[]{:S(2)}, u32[]{:S(2)}) collective-permute-start(bf16[144,768]{1,0:T(8,128)(2,1)} %fusion.15.refs_4_), channel_id=1, source_target_pairs={{0,1},{1,0},{2,3},{3,2},{4,5},{5,4},{6,7},{7,6},{8,9},{9,8},{10,11... | collective-permute-start | bytes 663560 | tf_op jit(solution)/shard_map/ppermute | solution.py:765
  5.8 17.7 %collective-permute-start.1 = (bf16[144,768]{1,0:T(8,128)(2,1)}, bf16[144,768]{1,0:T(8,128)(2,1)S(1)}, u32[]{:S(2)}, u32[]{:S(2)}) collective-permute-start(bf16[144,768]{1,0:T(8,128)(2,1)} %fusion.15.refs_4_), channel_id=1, source_target_pairs={{0,2},{1,3},{2,0},{3,1},{4,6},{5,7},{6,4},{7,5},{8,10},{9,11},{10,... | collective-permute-start | bytes 663560 | tf_op jit(solution)/shard_map/ppermute | solution.py:765
  7.4 16.1 %collective-permute-start = (bf16[144,768]{1,0:T(8,128)(2,1)}, bf16[144,768]{1,0:T(8,128)(2,1)}, u32[]{:S(2)}, u32[]{:S(2)}) collective-permute-start(bf16[144,768]{1,0:T(8,128)(2,1)} %fusion.15.refs_4_), channel_id=1, source_target_pairs={{0,4},{1,5},{2,6},{3,7},{4,0},{5,1},{6,2},{7,3},{8,12},{9,13},{10,... | collective-permute-start | bytes 663560 | tf_op jit(solution)/shard_map/ppermute | solution.py:765
  10.0 25.5 %collective-permute-start.5 = (bf16[512,1024]{1,0:T(8,128)(2,1)S(1)}, bf16[512,1024]{1,0:T(8,128)(2,1)}, u32[]{:S(2)}, u32[]{:S(2)}) collective-permute-start(bf16[512,1024]{1,0:T(8,128)(2,1)S(1)} %bitcast.104), channel_id=1, source_target_pairs={{0,16},{8,24},{16,0},{24,8},{1,17},{9,25},{17,1},{25,9},{2,18},{10... | collective-permute-start | bytes 3145736 | tf_op jit(solution)/shard_map/ppermute | solution.py:765
  24.6 10.9 %collective-permute-start.4 = (bf16[2,144,768]{2,1,0:T(8,128)(2,1)S(1)}, bf16[2,144,768]{2,1,0:T(8,128)(2,1)S(1)}, u32[]{:S(2)}, u32[]{:S(2)}) collective-permute-start(bf16[2,144,768]{2,1,0:T(8,128)(2,1)S(1)} %pad_maximum_fusion.7), channel_id=1, source_target_pairs={{0,1},{1,0},{2,3},{3,2},{4,5},{5,4},{6,7},{7,6},{8,9},{9,8},{10,11... | collective-permute-start | bytes 1327112 | tf_op jit(solution)/shard_map/ppermute | solution.py:765
  25.2 6.1 %collective-permute-start.3 = (bf16[144,768]{1,0:T(8,128)(2,1)}, bf16[144,768]{1,0:T(8,128)(2,1)S(1)}, u32[]{:S(2)}, u32[]{:S(2)}) collective-permute-start(bf16[144,768]{1,0:T(8,128)(2,1)} %collective-permute-done.refs_7_), channel_id=1, source_target_pairs={{0,2},{1,3},{2,0},{3,1},{4,6},{5,7},{6,4},{7,5},{8,10},{9,11},{10,... | collective-permute-start | bytes 663560 | tf_op jit(solution)/shard_map/ppermute | solution.py:765
  25.6 17.7 %collective-permute-start.7 = (bf16[512,1024]{1,0:T(8,128)(2,1)S(1)}, bf16[512,1024]{1,0:T(8,128)(2,1)S(1)}, u32[]{:S(2)}, u32[]{:S(2)}) collective-permute-start(bf16[512,1024]{1,0:T(8,128)(2,1)S(1)} %bitcast.105), channel_id=1, source_target_pairs={{0,8},{8,0},{16,24},{24,16},{1,9},{9,1},{17,25},{25,17},{2,10},{10... | collective-permute-start | bytes 3145736 | tf_op jit(solution)/shard_map/ppermute | solution.py:765
  35.5 7.9 %collective-permute-start.6 = (bf16[512,1024]{1,0:T(8,128)(2,1)}, bf16[512,1024]{1,0:T(8,128)(2,1)}, u32[]{:S(2)}, u32[]{:S(2)}) collective-permute-start(bf16[512,1024]{1,0:T(8,128)(2,1)} %collective-permute-done.5.refs_2_), channel_id=1, source_target_pairs={{0,8},{8,0},{16,24},{24,16},{1,9},{9,1},{17,25},{25,17},{2,10},{10... | collective-permute-start | bytes 3145736 | tf_op jit(solution)/shard_map/ppermute | solution.py:765
  35.5 7.8 %collective-permute-start.8 = (bf16[144,768]{1,0:T(8,128)(2,1)S(1)}, bf16[144,768]{1,0:T(8,128)(2,1)S(1)}, u32[]{:S(2)}, u32[]{:S(2)}) collective-permute-start(bf16[144,768]{1,0:T(8,128)(2,1)S(1)} %collective-permute-done.3.refs_9_), channel_id=1, source_target_pairs={{0,1},{1,0},{2,3},{3,2},{4,5},{5,4},{6,7},{7,6},{8,9},{9,8},{10,11... | collective-permute-start | bytes 663560 | tf_op jit(solution)/shard_map/ppermute | solution.py:765
  36.0 20.0 %collective-permute-start.11 = (bf16[512,1024]{1,0:T(8,128)(2,1)S(1)}, bf16[512,1024]{1,0:T(8,128)(2,1)S(1)}, u32[]{:S(2)}, u32[]{:S(2)}) collective-permute-start(bf16[512,1024]{1,0:T(8,128)(2,1)S(1)} %bitcast.110), channel_id=1, source_target_pairs={{0,8},{8,0},{16,24},{24,16},{1,9},{9,1},{17,25},{25,17},{2,10},{10... | collective-permute-start | bytes 3145736 | tf_op jit(solution)/shard_map/ppermute | solution.py:765
  43.3 23.6 %collective-permute-start.10 = (bf16[128,3840]{1,0:T(8,128)(2,1)}, bf16[128,3840]{1,0:T(8,128)(2,1)S(1)}, u32[]{:S(2)}, u32[]{:S(2)}) collective-permute-start(bf16[128,3840]{1,0:T(8,128)(2,1)} %fusion.4.refs_0_.refs_7_), channel_id=1, source_target_pairs={{0,1},{1,0},{2,3},{3,2},{4,5},{5,4},{6,7},{7,6},{8,9},{9,8},{10,11... | collective-permute-start | bytes 2949128 | tf_op jit(solution)/shard_map/ppermute | solution.py:765
  43.9 25.1 %collective-permute-start.9 = (bf16[128,3840]{1,0:T(8,128)(2,1)}, bf16[128,3840]{1,0:T(8,128)(2,1)}, u32[]{:S(2)}, u32[]{:S(2)}) collective-permute-start(bf16[128,3840]{1,0:T(8,128)(2,1)} %fusion.4.refs_0_.refs_7_), channel_id=1, source_target_pairs={{0,2},{1,3},{2,4},{3,5},{4,6},{5,7},{6,0},{7,1},{8,10},{9,11},{10,... | collective-permute-start | bytes 2949128 | tf_op jit(solution)/shard_map/ppermute | solution.py:817
  69.0 24.7 %collective-permute-start.13 = (bf16[128,3840]{1,0:T(8,128)(2,1)}, bf16[128,3840]{1,0:T(8,128)(2,1)S(1)}, u32[]{:S(2)}, u32[]{:S(2)}) collective-permute-start(bf16[128,3840]{1,0:T(8,128)(2,1)} %collective-permute-done.9.refs_1_.refs_8_), channel_id=1, source_target_pairs={{0,1},{1,0},{2,3},{3,2},{4,5},{5,4},{6,7},{7,6},{8,9},{9,8},{10,11... | collective-permute-start | bytes 2949128 | tf_op jit(solution)/shard_map/ppermute | solution.py:765
  70.6 24.0 %collective-permute-start.12 = (bf16[128,3840]{1,0:T(8,128)(2,1)}, bf16[128,3840]{1,0:T(8,128)(2,1)S(1)}, u32[]{:S(2)}, u32[]{:S(2)}) collective-permute-start(bf16[128,3840]{1,0:T(8,128)(2,1)} %collective-permute-done.9.refs_1_.refs_8_), channel_id=1, source_target_pairs={{0,2},{1,3},{2,4},{3,5},{4,6},{5,7},{6,0},{7,1},{8,10},{9,11},{10,... | collective-permute-start | bytes 2949128 | tf_op jit(solution)/shard_map/ppermute | solution.py:817
  71.9 21.9 %collective-permute-start.14 = (bf16[2,128,1408]{2,1,0:T(8,128)(2,1)S(1)}, bf16[2,128,1408]{2,1,0:T(8,128)(2,1)S(1)}, u32[]{:S(2)}, u32[]{:S(2)}) collective-permute-start(bf16[2,128,1408]{2,1,0:T(8,128)(2,1)S(1)} %pad_maximum_fusion), channel_id=1, source_target_pairs={{0,16},{8,24},{16,0},{24,8},{1,17},{9,25},{17,1},{25,9},{2,18},{10... | collective-permute-start | bytes 2162696 | tf_op jit(solution)/shard_map/ppermute | solution.py:765
  81.2 12.6 %collective-permute-start.15 = (bf16[512,256]{1,0:T(8,128)(2,1)}, bf16[512,256]{1,0:T(8,128)(2,1)S(1)}, u32[]{:S(2)}, u32[]{:S(2)}) collective-permute-start(bf16[512,256]{1,0:T(8,128)(2,1)} %get-tuple-element.182.refs_2_), channel_id=1, source_target_pairs={{0,16},{8,24},{16,0},{24,8},{1,17},{9,25},{17,1},{25,9},{2,18},{10... | collective-permute-start | bytes 786440 | tf_op jit(solution)/shard_map/ppermute | solution.py:765
  94.7 22.4 %collective-permute-start.17 = (bf16[128,3840]{1,0:T(8,128)(2,1)S(1)}, bf16[128,3840]{1,0:T(8,128)(2,1)S(1)}, u32[]{:S(2)}, u32[]{:S(2)}) collective-permute-start(bf16[128,3840]{1,0:T(8,128)(2,1)S(1)} %collective-permute-done.12.refs_2_.refs_9_), channel_id=1, source_target_pairs={{0,1},{1,0},{2,3},{3,2},{4,5},{5,4},{6,7},{7,6},{8,9},{9,8},{10,11... | collective-permute-start | bytes 2949128 | tf_op jit(solution)/shard_map/ppermute | solution.py:765
  95.3 22.4 %collective-permute-start.16 = (bf16[128,3840]{1,0:T(8,128)(2,1)S(1)}, bf16[128,3840]{1,0:T(8,128)(2,1)S(1)}, u32[]{:S(2)}, u32[]{:S(2)}) collective-permute-start(bf16[128,3840]{1,0:T(8,128)(2,1)S(1)} %collective-permute-done.12.refs_2_.refs_9_), channel_id=1, source_target_pairs={{0,2},{1,3},{2,4},{3,5},{4,6},{5,7},{6,0},{7,1},{8,10},{9,11},{10,... | collective-permute-start | bytes 2949128 | tf_op jit(solution)/shard_map/ppermute | solution.py:817
  96.3 20.8 %collective-permute-start.18 = (bf16[2,128,1408]{2,1,0:T(8,128)(2,1)}, bf16[2,128,1408]{2,1,0:T(8,128)(2,1)S(1)}, u32[]{:S(2)}, u32[]{:S(2)}) collective-permute-start(bf16[2,128,1408]{2,1,0:T(8,128)(2,1)} %pad_maximum_fusion.1), channel_id=1, source_target_pairs={{0,16},{8,24},{16,0},{24,8},{1,17},{9,25},{17,1},{25,9},{2,18},{10... | collective-permute-start | bytes 2162696 | tf_op jit(solution)/shard_map/ppermute | solution.py:765
  96.8 20.3 %collective-permute-start.19 = (bf16[512,256]{1,0:T(8,128)(2,1)S(1)}, bf16[512,256]{1,0:T(8,128)(2,1)S(1)}, u32[]{:S(2)}, u32[]{:S(2)}) collective-permute-start(bf16[512,256]{1,0:T(8,128)(2,1)S(1)} %copy-done.23), channel_id=1, source_target_pairs={{0,16},{8,24},{16,0},{24,8},{1,17},{9,25},{17,1},{25,9},{2,18},{10... | collective-permute-start | bytes 786440 | tf_op jit(solution)/shard_map/ppermute | solution.py:765
  118.1 19.8 %collective-permute-start.20 = (bf16[128,3840]{1,0:T(8,128)(2,1)S(1)}, bf16[128,3840]{1,0:T(8,128)(2,1)S(1)}, u32[]{:S(2)}, u32[]{:S(2)}) collective-permute-start(bf16[128,3840]{1,0:T(8,128)(2,1)S(1)} %collective-permute-done.16.refs_3_.refs_10_), channel_id=1, source_target_pairs={{0,1},{1,0},{2,3},{3,2},{4,5},{5,4},{6,7},{7,6},{8,9},{9,8},{10,11... | collective-permute-start | bytes 2949128 | tf_op jit(solution)/shard_map/ppermute | solution.py:765
  119.8 24.4 %collective-permute-start.21 = (bf16[2,128,1408]{2,1,0:T(8,128)(2,1)S(1)}, bf16[2,128,1408]{2,1,0:T(8,128)(2,1)S(1)}, u32[]{:S(2)}, u32[]{:S(2)}) collective-permute-start(bf16[2,128,1408]{2,1,0:T(8,128)(2,1)S(1)} %pad_maximum_fusion.2), channel_id=1, source_target_pairs={{0,16},{8,24},{16,0},{24,8},{1,17},{9,25},{17,1},{25,9},{2,18},{10... | collective-permute-start | bytes 2162696 | tf_op jit(solution)/shard_map/ppermute | solution.py:765
  137.9 7.5 %collective-permute-start.22 = (bf16[128,1408]{1,0:T(8,128)(2,1)S(1)}, bf16[128,1408]{1,0:T(8,128)(2,1)S(1)}, u32[]{:S(2)}, u32[]{:S(2)}) collective-permute-start(bf16[128,1408]{1,0:T(8,128)(2,1)S(1)} %slice.245), channel_id=1, source_target_pairs={{0,16},{8,24},{16,0},{24,8},{1,17},{9,25},{17,1},{25,9},{2,18},{10... | collective-permute-start | bytes 1081352 | tf_op jit(solution)/shard_map/ppermute | solution.py:765
  177.4 14.5 %collective-permute-start.24 = (bf16[1024,1024]{1,0:T(8,128)(2,1)}, bf16[1024,1024]{1,0:T(8,128)(2,1)S(1)}, u32[]{:S(2)}, u32[]{:S(2)}) collective-permute-start(bf16[1024,1024]{1,0:T(8,128)(2,1)} %get-tuple-element.220.so), channel_id=1, source_target_pairs={{0,8},{8,0},{16,24},{24,16},{1,9},{9,1},{17,25},{25,17},{2,10},{10... | collective-permute-start | bytes 6291464 | tf_op jit(solution)/shard_map/ppermute | solution.py:765
  190.3 43.8 %collective-permute-start.27 = (bf16[2,4,128,768]{3,2,1,0:T(8,128)(2,1)}, bf16[2,4,128,768]{3,2,1,0:T(8,128)(2,1)S(1)}, u32[]{:S(2)}, u32[]{:S(2)}) collective-permute-start(bf16[2,4,128,768]{3,2,1,0:T(8,128)(2,1)} %get-tuple-element.237), channel_id=1, source_target_pairs={{0,1},{1,0},{2,3},{3,2},{4,5},{5,4},{6,7},{7,6},{8,9},{9,8},{10,11... | collective-permute-start | bytes 4718600 | tf_op jit(solution)/shard_map/ppermute | solution.py:765
  192.0 42.2 %collective-permute-start.28 = (bf16[8,128,640]{2,1,0:T(8,128)(2,1)}, bf16[8,128,640]{2,1,0:T(8,128)(2,1)}, u32[]{:S(2)}, u32[]{:S(2)}) collective-permute-start(bf16[8,128,640]{2,1,0:T(8,128)(2,1)} %get-tuple-element.238), channel_id=1, source_target_pairs={{0,16},{8,24},{16,0},{24,8},{1,17},{9,25},{17,1},{25,9},{2,18},{10... | collective-permute-start | bytes 3932168 | tf_op jit(solution)/shard_map/ppermute | solution.py:765
  217.6 16.6 %collective-permute-start.26 = (bf16[512,1024]{1,0:T(8,128)(2,1)}, bf16[512,1024]{1,0:T(8,128)(2,1)S(1)}, u32[]{:S(2)}, u32[]{:S(2)}) collective-permute-start(bf16[512,1024]{1,0:T(8,128)(2,1)} %get-tuple-element.236), channel_id=1, source_target_pairs={{0,8},{8,0},{16,24},{24,16},{1,9},{9,1},{17,25},{25,17},{2,10},{10... | collective-permute-start | bytes 3145736 | tf_op jit(solution)/shard_map/ppermute | solution.py:765
  217.7 16.5 %collective-permute-start.25 = (bf16[1024,256]{1,0:T(8,128)(2,1)S(1)}, bf16[1024,256]{1,0:T(8,128)(2,1)S(1)}, u32[]{:S(2)}, u32[]{:S(2)}) collective-permute-start(bf16[1024,256]{1,0:T(8,128)(2,1)S(1)} %copy-done.48), channel_id=1, source_target_pairs={{0,16},{8,24},{16,0},{24,8},{1,17},{9,25},{17,1},{25,9},{2,18},{10... | collective-permute-start | bytes 1572872 | tf_op jit(solution)/shard_map/ppermute | solution.py:765
  218.3 53.6 %collective-permute-start.30 = (bf16[2,4,656,128]{3,2,1,0:T(8,128)(2,1)}, bf16[2,4,656,128]{3,2,1,0:T(8,128)(2,1)}, u32[]{:S(2)}, u32[]{:S(2)}) collective-permute-start(bf16[2,4,656,128]{3,2,1,0:T(8,128)(2,1)} %get-tuple-element.249), channel_id=1, source_target_pairs={{0,1},{1,0},{2,3},{3,2},{4,5},{5,4},{6,7},{7,6},{8,9},{9,8},{10,11... | collective-permute-start | bytes 4030472 | tf_op jit(solution)/shard_map/ppermute | solution.py:765
  235.6 36.4 %collective-permute-start.31 = (bf16[4,128,768]{2,1,0:T(8,128)(2,1)}, bf16[4,128,768]{2,1,0:T(8,128)(2,1)S(1)}, u32[]{:S(2)}, u32[]{:S(2)}) collective-permute-start(bf16[4,128,768]{2,1,0:T(8,128)(2,1)} %get-tuple-element.333), channel_id=1, source_target_pairs={{0,16},{8,24},{16,0},{24,8},{1,17},{9,25},{17,1},{25,9},{2,18},{10... | collective-permute-start | bytes 2359304 | tf_op jit(solution)/shard_map/ppermute | solution.py:765
  238.6 33.4 %collective-permute-start.32 = (bf16[4,128,640]{2,1,0:T(8,128)(2,1)S(1)}, bf16[4,128,640]{2,1,0:T(8,128)(2,1)S(1)}, u32[]{:S(2)}, u32[]{:S(2)}) collective-permute-start(bf16[4,128,640]{2,1,0:T(8,128)(2,1)S(1)} %get-tuple-element.337), channel_id=1, source_target_pairs={{0,1},{1,0},{2,3},{3,2},{4,5},{5,4},{6,7},{7,6},{8,9},{9,8},{10,11... | collective-permute-start | bytes 1966088 | tf_op jit(solution)/shard_map/ppermute | solution.py:765
  240.2 31.7 %collective-permute-start.29 = (bf16[8,256,128]{2,1,0:T(8,128)(2,1)S(1)}, bf16[8,256,128]{2,1,0:T(8,128)(2,1)S(1)}, u32[]{:S(2)}, u32[]{:S(2)}) collective-permute-start(bf16[8,256,128]{2,1,0:T(8,128)(2,1)S(1)} %copy-done.47), channel_id=1, source_target_pairs={{0,16},{8,24},{16,0},{24,8},{1,17},{9,25},{17,1},{25,9},{2,18},{10... | collective-permute-start | bytes 1572872 | tf_op jit(solution)/shard_map/ppermute | solution.py:765
  273.1 24.0 %collective-permute-start.33 = (bf16[2,128,1408]{2,1,0:T(8,128)(2,1)S(1)}, bf16[2,128,1408]{2,1,0:T(8,128)(2,1)S(1)}, u32[]{:S(2)}, u32[]{:S(2)}) collective-permute-start(bf16[2,128,1408]{2,1,0:T(8,128)(2,1)S(1)} %pad_maximum_fusion.3), channel_id=1, source_target_pairs={{0,2},{1,3},{2,0},{3,1},{4,6},{5,7},{6,4},{7,5},{8,10},{9,11},{10,... | collective-permute-start | bytes 2162696 | tf_op jit(solution)/shard_map/ppermute | solution.py:765
  280.5 16.6 %collective-permute-start.34 = (bf16[4,640,128]{2,1,0:T(8,128)(2,1)S(1)}, bf16[4,640,128]{2,1,0:T(8,128)(2,1)S(1)}, u32[]{:S(2)}, u32[]{:S(2)}) collective-permute-start(bf16[4,640,128]{2,1,0:T(8,128)(2,1)S(1)} %pad_maximum_fusion.6), channel_id=1, source_target_pairs={{0,1},{1,0},{2,3},{3,2},{4,5},{5,4},{6,7},{7,6},{8,9},{9,8},{10,11... | collective-permute-start | bytes 1966088 | tf_op jit(solution)/shard_map/ppermute | solution.py:765
  302.7 17.7 %collective-permute-start.35 = (bf16[2,512,1024]{2,1,0:T(8,128)(2,1)}, bf16[2,512,1024]{2,1,0:T(8,128)(2,1)S(1)}, u32[]{:S(2)}, u32[]{:S(2)}) collective-permute-start(bf16[2,512,1024]{2,1,0:T(8,128)(2,1)} %back_project.2), channel_id=1, source_target_pairs={{0,8},{8,0},{16,24},{24,16},{1,9},{9,1},{17,25},{25,17},{2,10},{10... | collective-permute-start | bytes 6291464 | tf_op jit(solution)/shard_map/ppermute | solution.py:765
  306.5 24.8 %collective-permute-start.36 = (bf16[4,656,128]{2,1,0:T(8,128)(2,1)}, bf16[4,656,128]{2,1,0:T(8,128)(2,1)}, u32[]{:S(2)}, u32[]{:S(2)}) collective-permute-start(bf16[4,656,128]{2,1,0:T(8,128)(2,1)} %get-tuple-element.334), channel_id=1, source_target_pairs={{0,16},{8,24},{16,0},{24,8},{1,17},{9,25},{17,1},{25,9},{2,18},{10... | collective-permute-start | bytes 2015240 | tf_op jit(solution)/shard_map/ppermute | solution.py:765
  308.7 33.7 %collective-permute-start.38 = (bf16[128,1408]{1,0:T(8,128)(2,1)}, bf16[128,1408]{1,0:T(8,128)(2,1)}, u32[]{:S(2)}, u32[]{:S(2)}) collective-permute-start(bf16[128,1408]{1,0:T(8,128)(2,1)} %get-tuple-element.341), channel_id=1, source_target_pairs={{0,4},{1,5},{2,6},{3,7},{4,0},{5,1},{6,2},{7,3},{8,12},{9,13},{10,... | collective-permute-start | bytes 1081352 | tf_op jit(solution)/shard_map/ppermute | solution.py:765
  326.2 11.2 %collective-permute-start.39 = (bf16[4,384,128]{2,1,0:T(8,128)(2,1)}, bf16[4,384,128]{2,1,0:T(8,128)(2,1)S(1)}, u32[]{:S(2)}, u32[]{:S(2)}) collective-permute-start(bf16[4,384,128]{2,1,0:T(8,128)(2,1)} %get-tuple-element.292), channel_id=1, source_target_pairs={{0,1},{1,0},{2,3},{3,2},{4,5},{5,4},{6,7},{7,6},{8,9},{9,8},{10,11... | collective-permute-start | bytes 1179656 | tf_op jit(solution)/shard_map/ppermute | solution.py:765
  330.5 33.7 %collective-permute-start.44 = (bf16[512,1024]{1,0:T(8,128)(2,1)}, bf16[512,1024]{1,0:T(8,128)(2,1)S(1)}, u32[]{:S(2)}, u32[]{:S(2)}) collective-permute-start(bf16[512,1024]{1,0:T(8,128)(2,1)} %fusion.2), channel_id=1, source_target_pairs={{0,16},{8,24},{16,0},{24,8},{1,17},{9,25},{17,1},{25,9},{2,18},{10... | collective-permute-start | bytes 3145736 | tf_op jit(solution)/shard_map/ppermute | solution.py:765
  332.8 17.8 %collective-permute-start.37 = (bf16[2,1296,128]{2,1,0:T(8,128)(2,1)S(1)}, bf16[2,1296,128]{2,1,0:T(8,128)(2,1)S(1)}, u32[]{:S(2)}, u32[]{:S(2)}) collective-permute-start(bf16[2,1296,128]{2,1,0:T(8,128)(2,1)S(1)} %pad_maximum_fusion.4), channel_id=1, source_target_pairs={{0,2},{1,3},{2,0},{3,1},{4,6},{5,7},{6,4},{7,5},{8,10},{9,11},{10,... | collective-permute-start | bytes 1990664 | tf_op jit(solution)/shard_map/ppermute | solution.py:765
  339.0 25.2 %collective-permute-start.42 = (bf16[2,384,128]{2,1,0:T(8,128)(2,1)S(1)}, bf16[2,384,128]{2,1,0:T(8,128)(2,1)S(1)}, u32[]{:S(2)}, u32[]{:S(2)}) collective-permute-start(bf16[2,384,128]{2,1,0:T(8,128)(2,1)S(1)} %get-tuple-element.355), channel_id=1, source_target_pairs={{0,2},{1,3},{2,0},{3,1},{4,6},{5,7},{6,4},{7,5},{8,10},{9,11},{10,... | collective-permute-start | bytes 589832 | tf_op jit(solution)/shard_map/ppermute | solution.py:765
  350.6 13.6 %collective-permute-start.43 = (f32[2,1024]{1,0:T(2,128)S(1)}, f32[2,1024]{1,0:T(2,128)S(1)}, u32[]{:S(2)}, u32[]{:S(2)}) collective-permute-start(f32[2,1024]{1,0:T(2,128)S(1)} %add.252), channel_id=1, source_target_pairs={{0,2},{1,3},{2,0},{3,1},{4,6},{5,7},{6,4},{7,5},{8,10},{9,11},{10,... | collective-permute-start | bytes 24584 | tf_op jit(solution)/shard_map/ppermute | solution.py:765
  352.7 9.9 %collective-permute-start.47 = (bf16[640,128]{1,0:T(8,128)(2,1)}, bf16[640,128]{1,0:T(8,128)(2,1)}, u32[]{:S(2)}, u32[]{:S(2)}) collective-permute-start(bf16[640,128]{1,0:T(8,128)(2,1)} %slice_bitcast_fusion.12), channel_id=1, source_target_pairs={{0,4},{1,5},{2,6},{3,7},{4,0},{5,1},{6,2},{7,3},{8,12},{9,13},{10,... | collective-permute-start | bytes 491528 | tf_op jit(solution)/shard_map/ppermute | solution.py:765
  352.8 14.5 %collective-permute-start.49 = (bf16[656,128]{1,0:T(8,128)(2,1)S(1)}, bf16[656,128]{1,0:T(8,128)(2,1)S(1)}, u32[]{:S(2)}, u32[]{:S(2)}) collective-permute-start(bf16[656,128]{1,0:T(8,128)(2,1)S(1)} %slice_bitcast_fusion.11), channel_id=1, source_target_pairs={{8,16},{16,8},{9,17},{17,9},{10,18},{18,10},{11,19},{19,11},{12,20... | collective-permute-start | bytes 503816 | tf_op jit(solution)/shard_map/ppermute | solution.py:1006
  362.6 9.1 %collective-permute-start.50 = (bf16[656,128]{1,0:T(8,128)(2,1)S(1)}, bf16[656,128]{1,0:T(8,128)(2,1)S(1)}, u32[]{:S(2)}, u32[]{:S(2)}) collective-permute-start(bf16[656,128]{1,0:T(8,128)(2,1)S(1)} %slice_bitcast_fusion.10), channel_id=1, source_target_pairs={{0,4},{1,5},{2,6},{3,7},{4,0},{5,1},{6,2},{7,3},{8,20},{9,21},{10,... | collective-permute-start | bytes 503816 | tf_op jit(solution)/shard_map/ppermute | solution.py:1001
  364.3 8.2 %collective-permute-start.45 = (f32[2,1024]{1,0:T(2,128)S(1)}, f32[2,1024]{1,0:T(2,128)S(1)}, u32[]{:S(2)}, u32[]{:S(2)}) collective-permute-start(f32[2,1024]{1,0:T(2,128)S(1)} %add.253), channel_id=1, source_target_pairs={{0,4},{1,5},{2,6},{3,7},{4,0},{5,1},{6,2},{7,3},{8,12},{9,13},{10,... | collective-permute-start | bytes 24584 | tf_op jit(solution)/shard_map/ppermute | solution.py:765
  372.5 7.3 %collective-permute-start.46 = (f32[2,1024]{1,0:T(2,128)S(1)}, f32[2,1024]{1,0:T(2,128)S(1)}, u32[]{:S(2)}, u32[]{:S(2)}) collective-permute-start(f32[2,1024]{1,0:T(2,128)S(1)} %add.254), channel_id=1, source_target_pairs={{0,16},{8,24},{16,0},{24,8},{1,17},{9,25},{17,1},{25,9},{2,18},{10... | collective-permute-start | bytes 24584 | tf_op jit(solution)/shard_map/ppermute | solution.py:765
  374.1 6.6 %collective-permute-start.48 = (bf16[384,128]{1,0:T(8,128)(2,1)S(1)}, bf16[384,128]{1,0:T(8,128)(2,1)S(1)}, u32[]{:S(2)}, u32[]{:S(2)}) collective-permute-start(bf16[384,128]{1,0:T(8,128)(2,1)S(1)} %fusion.17), channel_id=1, source_target_pairs={{0,4},{1,5},{2,6},{3,7},{4,0},{5,1},{6,2},{7,3},{8,12},{9,13},{10,... | collective-permute-start | bytes 294920 | tf_op jit(solution)/shard_map/ppermute | solution.py:765
  (52 other events, 417.7 us)

commit v5 on v4

--- a/solution.py
+++ b/solution.py
@@ -379,9 +379,11 @@
 def mlp_kernel(count, n_arrays, mine, other, down, idx, *refs):
     x0, x1, po, pr, c0, c1, g_ref, refs = *refs[:7], refs[7:]
     w_refs, refs = refs[:n_arrays], refs[n_arrays:]
-    sn_o, hid_o, gug_o, sgp_o, wd_o, refs = *refs[:5], refs[5:]
-    xs, pos, prs, cs, wi, wd, sn_s, hid_s, gug_s, sgp_s, sem_a, sem_m, sem_i, sem_d, sem_o = refs
-    x_place = idx[2]
+    hid_o, sgp_o, wd_o, refs = *refs[:3], refs[3:]
+    grads, refs = (refs[:4], refs[4:]) if count > 1 else (refs[:1], refs[1:])
+    xs, pos, prs, cs, wi, wd, sn_s, hid_s, gug_s, sgp_s, turned_s, acc, refs = *refs[:12], refs[12:]
+    sem_a, sem_m, sem_i, sem_d, sem_o = refs
+    shard, x_place = idx[0], idx[2]
     rows = xs.shape[1]
     loads = [
         pltpu.make_async_copy(x0, xs.at[0], sem_a.at[0]),
@@ -407,15 +409,15 @@
         sn_s[here] = (xhat * g_ref[1:2]).astype(bf16)
     stores = []
 
-    def store(source, target, k):
-        copy = pltpu.make_async_copy(source, target, sem_o.at[k])
+    def store(source, target):
+        copy = pltpu.make_async_copy(source, target, sem_o.at[len(stores)])
         copy.start()
         stores.append(copy)
 
-    store(sn_s, sn_o, 0)
+    turned_s[...] = sn_s[...].T
     for copy in wi_loads + loads[4:] + wd_loads:
         copy.wait()
-    store(wd, wd_o, 1)
+    store(wd, wd_o)
     start = 0
     while start < PADDED:
         size = min(256, PADDED - start)
@@ -430,29 +432,38 @@
         gug_s[0, :, here] = (back * up * (below + gate * density)).astype(bf16)
         gug_s[1, :, here] = (back * unit).astype(bf16)
         start += size
-    store(hid_s, hid_o, 2)
-    store(gug_s, gug_o, 3)
+    store(hid_s, hid_o)
     value = lax.dot_general(gug_s[0], wi[:, :PADDED], COLS_BY_COLS, preferred_element_type=f32)
     value = value + lax.dot_general(gug_s[1], wi[:, PADDED:], COLS_BY_COLS, preferred_element_type=f32)
     sgp_s[...] = value.astype(bf16)
-    store(sgp_s, sgp_o, 4)
+    store(sgp_s, sgp_o)
+    size = WIDTH // count
+    for part in range(2):
+        terms = gug_s[jnp.bitwise_xor(x_place, part)]
+        acc[part] = jnp.dot(turned_s[...], terms, preferred_element_type=f32).astype(bf16)
+        if count == 1:
+            store(acc.at[part], grads[0].at[part, 0])
+            continue
+        keep_a, send_a, keep_b, send_b = grads
+        for k, r in enumerate(CHUNKS):
+            place = aligned(jnp.bitwise_xor(shard, r), size)
+            store(acc.at[part, place, pl.ds(0, SPLIT)], (keep_a, send_a)[k // 4].at[part, k % 4])
+            store(acc.at[part, place, pl.ds(SPLIT, PADDED - SPLIT)], (keep_b, send_b)[part].at[k])
     for copy in stores:
         copy.wait()
 
 
 def mlp_call(count, idx, x0, x1, po, pr, c0, c1, gains, arrays, mine, other, down):
     rows = x0.shape[0]
+    size = WIDTH // count
+    grads = [sds((2, 4, size, SPLIT))] * 2 + [sds((8, size, PADDED - SPLIT))] * 2
+    if count == 1:
+        grads = [sds((2, 1, WIDTH, PADDED))]
     return pl.pallas_call(
         partial(mlp_kernel, count, len(arrays), mine, other, down),
         in_specs=[SMEM] + [ANY] * 6 + [pl.BlockSpec(memory_space=pltpu.VMEM)] + [ANY] * len(arrays),
-        out_specs=[ANY] * 5,
-        out_shape=[
-            sds((2 * rows, WIDTH)),
-            sds((2 * rows, PADDED)),
-            sds((2, 2 * rows, PADDED)),
-            sds((2 * rows, WIDTH)),
-            sds((WIDTH, PADDED)),
-        ],
+        out_specs=[ANY] * (3 + len(grads)),
+        out_shape=[sds((2 * rows, PADDED)), sds((2 * rows, WIDTH)), sds((WIDTH, PADDED))] + grads,
         scratch_shapes=[
             pltpu.VMEM((2, rows, WIDTH), bf16),
             pltpu.VMEM((2 * rows, WIDTH), bf16),
@@ -464,11 +475,13 @@
             pltpu.VMEM((2 * rows, PADDED), bf16),
             pltpu.VMEM((2, 2 * rows, PADDED), bf16),
             pltpu.VMEM((2 * rows, WIDTH), bf16),
+            pltpu.VMEM((WIDTH, 2 * rows), bf16),
+            pltpu.VMEM((2, WIDTH, PADDED), bf16),
             pltpu.SemaphoreType.DMA((6,)),
             pltpu.SemaphoreType.DMA((count,)),
             pltpu.SemaphoreType.DMA((count,)),
             pltpu.SemaphoreType.DMA((count,)),
-            pltpu.SemaphoreType.DMA((5,)),
+            pltpu.SemaphoreType.DMA((40,)),
         ],
         compiler_params=params(),
         cost_estimate=cost(25),
@@ -476,49 +489,67 @@
     )(idx, x0, x1, po, pr, c0, c1, gains, *arrays)
 
 
-def down_kernel(count, idx, hid_ref, wd_ref, c0, c1, ma, mb, oa, ob, low, res_other, res_mine, *refs):
-    outs, downs, acc = refs[:2], refs[2:-1], refs[-1]
+def down_kernel(count, idx, *refs):
+    sources, refs = refs[:4], refs[4:]
+    res_other, res_mine, refs = *refs[:2], refs[2:]
+    downs, refs = refs[: 2 if count > 1 else 1], refs[2 if count > 1 else 1 :]
+    hid, wd, cs, acc, res, sem_i, sem_o = refs
     shard, x_place = idx[0], idx[2]
-    rows = c0.shape[0]
+    rows = cs.shape[0] // 2
     width = WIDTH // count
+    targets = [hid, wd, cs.at[pl.ds(0, rows)], cs.at[pl.ds(rows, rows)]]
+    loads = [pltpu.make_async_copy(*pair, sem_i.at[k]) for k, pair in enumerate(zip(sources, targets))]
+    for k in (0, 2, 3, 1):
+        loads[k].start()
     places = [
         aligned(jnp.bitwise_xor(shard, r), width) if count > 1 else pl.ds(0, width) for r in CHUNKS[:count]
     ]
-    acc[...] = lax.dot_general(
-        hid_ref[0:rows], c0[...], ROWS_BY_COLS, preferred_element_type=f32
-    ) + lax.dot_general(hid_ref[rows:], c1[...], ROWS_BY_COLS, preferred_element_type=f32)
+    stores = []
+
+    def store(source, target):
+        copy = pltpu.make_async_copy(source, target, sem_o.at[len(stores)])
+        copy.start()
+        stores.append(copy)
+
+    for k in (0, 2, 3):
+        loads[k].wait()
+    acc[...] = lax.dot_general(hid[...], cs[...], ROWS_BY_COLS, preferred_element_type=f32).astype(bf16)
     for part in range(2):
-        here = pl.ds(pl.multiple_of(jnp.bitwise_xor(x_place, part) * BLOCK, 8), BLOCK)
+        here = pl.ds(pl.multiple_of(jnp.bitwise_xor(x_place, part) * BLOCK, 16), BLOCK)
         for r in range(count):
-            downs[r // 4][part, r % 4] = acc[here, places[r]].astype(bf16)
-    mine = jnp.concatenate([ma[...], mb[...]], axis=0)
-    other = jnp.concatenate([oa[...], ob[...]], axis=0)
-    for part, context in enumerate((mine, other)):
-        acc[0:COLS] = lax.dot_general(context, low[...], ROWS_BY_COLS, preferred_element_type=f32)
-        for r in range(count):
-            outs[part][r] = acc[0:COLS, places[r]].astype(bf16)
+            store(acc.at[here, places[r]], downs[r // 4].at[part, r % 4])
+    loads[1].wait()
     for r, target in ((1, res_other), (0, res_mine)):
-        target[...] = lax.dot_general(
-            hid_ref[r * rows : (r + 1) * rows], wd_ref[...], COLS_BY_COLS, preferred_element_type=f32
+        res[r] = lax.dot_general(
+            hid[r * rows : (r + 1) * rows], wd[...], COLS_BY_COLS, preferred_element_type=f32
         ).astype(bf16)
-
-
-def down_call(count, idx, hidden, wd, c0, c1, mine, other, low):
+        store(res.at[r], target)
+    for copy in stores:
+        copy.wait()
+
+
+def down_call(count, idx, hidden, wd, c0, c1):
     rows = c0.shape[0]
     split = 2 if count > 1 else 1
-    vmem = pl.BlockSpec(memory_space=pltpu.VMEM)
     return pl.pallas_call(
         partial(down_kernel, count),
-        in_specs=[SMEM] + [vmem] * 9,
-        out_specs=[vmem] * (4 + split),
+        in_specs=[SMEM] + [ANY] * 4,
+        out_specs=[ANY] * (2 + split),
         out_shape=[sds((rows, WIDTH))] * 2
-        + [sds((count, COLS, WIDTH // count))] * 2
         + [sds((2, count // split, BLOCK, WIDTH // count))] * split,
-        scratch_shapes=[pltpu.VMEM((PADDED, WIDTH), f32)],
+        scratch_shapes=[
+            pltpu.VMEM((2 * rows, PADDED), bf16),
+            pltpu.VMEM((WIDTH, PADDED), bf16),
+            pltpu.VMEM((2 * rows, WIDTH), bf16),
+            pltpu.VMEM((PADDED, WIDTH), bf16),
+            pltpu.VMEM((2, rows, WIDTH), bf16),
+            pltpu.SemaphoreType.DMA((4,)),
+            pltpu.SemaphoreType.DMA((2 * count + 2,)),
+        ],
         compiler_params=params(),
         cost_estimate=cost(15),
         name="down_project",
-    )(idx, hidden, wd, c0, c1, *mine, *other, low)
+    )(idx, hidden, wd, c0, c1)
 
 
 def norm_two_kernel(x0, x1, po, pr, so, sr, c0, c1, g_ref, wsel, res_o, low_o, mine_o, other_o, gain_o):
@@ -593,61 +624,29 @@
     )(x0, x1, po, pr, so, sr, c0, c1, gains, wsel)
 
 
-def wide_kernel(count, idx, sn_ref, gug_ref, *refs):
+def out_grad_kernel(count, idx, ma, mb, oa, ob, low, keep_o, send_o, acc):
     shard = idx[0]
-    part = pl.program_id(0)
-    size = WIDTH // count
-    if count == 1:
-        out, acc = refs
-        acc[...] = lax.dot_general(sn_ref[...], gug_ref[0], ROWS_BY_COLS, preferred_element_type=f32)
-        out[0, 0] = acc[...].astype(bf16)
-        return
-    keep_a, send_a, keep_b, send_b, acc = refs
-    acc[...] = lax.dot_general(sn_ref[...], gug_ref[0], ROWS_BY_COLS, preferred_element_type=f32)
-    for k, r in enumerate(CHUNKS):
-        place = aligned(jnp.bitwise_xor(shard, r), size)
-        (keep_a, send_a)[k // 4][0, k % 4] = acc[place, :SPLIT].astype(bf16)
-
-    def store(target):
-        for k, r in enumerate(CHUNKS):
-            place = aligned(jnp.bitwise_xor(shard, r), size)
-            target[k] = acc[place, SPLIT:].astype(bf16)
-
-    @pl.when(part == 0)
-    def _():
-        store(keep_b)
-
-    @pl.when(part == 1)
-    def _():
-        store(send_b)
-
-
-def wide_call(count, idx, sn, gug):
-    tokens = sn.shape[0]
-    size = WIDTH // count
-    spec = lambda shape, at: pl.BlockSpec(shape, at)
-    whole = lambda shape: pl.BlockSpec(shape, lambda p, s: (0,) * len(shape))
-    by_part = lambda shape: pl.BlockSpec((1, *shape[1:]), lambda p, s: (p, 0, 0, 0))
-    first, second = (2, 4, size, SPLIT), (8, size, PADDED - SPLIT)
-    alone = (2, 1, WIDTH, PADDED)
-    grid_spec = pltpu.PrefetchScalarGridSpec(
-        num_scalar_prefetch=1,
-        grid=(2,),
-        in_specs=[
-            spec((tokens, WIDTH), lambda p, s: (0, 0)),
-            spec((1, tokens, PADDED), lambda p, s: (jnp.bitwise_xor(p, s[2]), 0, 0)),
-        ],
-        out_specs=[by_part(first)] * 2 + [whole(second)] * 2 if count > 1 else [by_part(alone)],
-        scratch_shapes=[pltpu.VMEM((WIDTH, PADDED), f32)],
-    )
+    width = WIDTH // count
+    for (first, second), target in (((oa, ob), send_o), ((ma, mb), keep_o)):
+        context = jnp.concatenate([first[...], second[...]], axis=0)
+        acc[...] = lax.dot_general(context, low[...], ROWS_BY_COLS, preferred_element_type=f32)
+        for k, r in enumerate(CHUNKS[:count]):
+            place = aligned(jnp.bitwise_xor(shard, r), width) if count > 1 else pl.ds(0, width)
+            target[k] = acc[:, place].astype(bf16)
+
+
+def out_grad_call(count, idx, mine, other, low):
+    vmem = pl.BlockSpec(memory_space=pltpu.VMEM)
     return pl.pallas_call(
-        partial(wide_kernel, count),
-        grid_spec=grid_spec,
-        out_shape=[sds(first)] * 2 + [sds(second)] * 2 if count > 1 else [sds(alone)],
+        partial(out_grad_kernel, count),
+        in_specs=[SMEM] + [vmem] * 5,
+        out_specs=[vmem] * 2,
+        out_shape=[sds((count, COLS, WIDTH // count))] * 2,
+        scratch_shapes=[pltpu.VMEM((COLS, WIDTH), f32)],
         compiler_params=params(),
-        cost_estimate=cost(12),
-        name="wide_grad",
-    )(idx, sn, gug)
+        cost_estimate=cost(4),
+        name="out_grad",
+    )(idx, *mine, *other, low)
 
 
 def back_project_kernel(q0, q1, f0, f1, k0n, k1n, k0f, k1f, v0n, v1n, v0f, v1f, w_ref, both_o):
@@ -738,7 +737,7 @@
     o_ref[...] = res_ref[...] + norm_back(first * g_ref[0:1], xhat, inv_scale)
 
 
-def norm_one_call(x, res, own, core, far, gains, steps=4):
+def norm_one_call(x, res, own, core, far, gains, steps=2):
     rows = x.shape[0]
     block = pl.BlockSpec((rows // steps, WIDTH), lambda i: (i, 0))
     return pl.pallas_call(
@@ -898,27 +897,26 @@
         out_own, *last = together(out_own, *arrays)
         arrays = tuple(last)
     out_core = by_core(out_own)
-    second_low, hidden, gate_up_grad, second_own, w_down_full = mlp_call(
+    hidden, second_own, w_down_full, *wide = mlp_call(
         count, idx, x0, x1, out_own, out_core, c0, c1, gains, arrays, mine_at, other_at, down_at
     )
     second_core = by_core(second_own)
-    wide = list(wide_call(count, idx, second_low, gate_up_grad))
-    wide[-1], second_core = together(wide[-1], second_core)
+    down_other, down_mine, *down = down_call(count, idx, hidden, w_down_full, c0, c1)
+    down_mine, second_core = together(down_mine, second_core)
     res, res_low, grad_near, grad_other, gain_two = norm_two_call(
         x0, x1, out_own, out_core, second_own, second_core, c0, c1, gains, w_sel
     )
     grad_far = by_x(grad_other)
-    down_other, down_mine, out_keep, out_send, *down = down_call(
-        count, idx, hidden, w_down_full, c0, c1, near, other, res_low
-    )
+    out_keep, out_send = out_grad_call(count, idx, near, other, res_low)
     part = lambda half, pair, grads, earlier=None: attend_back(
         half, pair, q, grads, (near, far)[half], (lse_near, lse_far)[half], k, v, cosine, sine, earlier
     )
     if eight:
         a_keep, a_send, b_keep, b_send = wide
         a_got, b_got = by_y(a_send), by_x(b_send)
-        out_send, grad_near, down[1] = together(out_send, grad_near, down[1])
-        out_got, down_got = by_x(out_send), by_y(down[1])
+        down_got = by_y(down[1])
+        out_send, grad_near = together(out_send, grad_near)
+        out_got = by_x(out_send)
         down_core = by_core(down_other)
     else:
         down_core = by_core(down_other)

time: 387 us -> 384 us (level)
  Pallas kernels: 207 us -> 203 us
    pallas_call x2, Pallas kernels: 26.6 us -> 15.5 us  [the longest x1 11.3 us: down_call(): pl.pallas_call(partial(down_kernel, count), in_specs=[SMEM] + [ANY] * 4,...]
    pallas_call x1, Pallas kernels: 26.3 us -> 33.3 us  [mlp_call(): pl.pallas_call(partial(mlp_kernel, count, len(arrays), mine, other, down)...]
    unnamed x103 -> x101, local copies, waits for them, and re-layouts: 7.87 us -> 8.64 us
  transfers between devices with their start and end apart: 51 -> 51, of which waited for: 17 -> 17; matrix products, arithmetic and copies ran while one was open for 10% -> 10% of each run, Pallas kernels for 46% -> 43%
where the time goes in v5:
time: 384 us; the launch traced here: 379 us
  Pallas kernels  203 us (53%)
  waiting for transfers between devices  80.9 us (21%)
  starting transfers between devices  46.9 us (12%)
  other arithmetic  31.7 us (8%)
  local copies, waits for them, and re-layouts  14.7 us (4%)
    ppermute x46, waiting for transfers between devices, swap(): lax.ppermute(value, axis, [(place, place ^ bits) for place in range(size)])  73.4 us
    pallas_call x4, Pallas kernels, attend_back(): pl.pallas_call(lambda *refs: attend_back_kernel(last, pair, *refs[:n_in],...  62.1 us
    ppermute x46, starting transfers between devices, swap(): lax.ppermute(value, axis, [(place, place ^ bits) for place in range(size)])  45.6 us
    pallas_call x4, Pallas kernels, attend(): pl.pallas_call(lambda *refs: attend_kernel(*refs[:3], *refs[3 + len(after...  35.3 us
    pallas_call x1, Pallas kernels, mlp_call(): pl.pallas_call(partial(mlp_kernel, count, len(arrays), mine, other, down)...  33.3 us
    convert_element_type x13, other arithmetic, plus(): return (left.astype(f32) + right.astype(f32)).astype(bf16)  12.5 us
    pallas_call x2, Pallas kernels, qkv_grad_call(): pl.pallas_call(partial(qkv_grad_kernel, count), grid=(1,), in_specs=[SMEM...  12.5 us
    pallas_call x1, Pallas kernels, qkv_call(): pl.pallas_call(partial(qkv_kernel, count, where), grid=(4,), in_specs=[SM...  11.6 us
  transfers between devices with their start and end apart: 51, of which 17 were waited for; matrix products, arithmetic and copies ran while one was open for 10% of the time, Pallas kernels for 43%

profile of v5, /device:TPU:0, one launch (start us, length us, event | category | flops | bytes accessed | tf_op | source)
XLA Modules:
  0.0 378.7 jit_solution(15702669396206120275)
XLA Ops:
  2.9 3.0 collective-permute-start.2
  5.8 1.6 collective-permute-start.1
  7.4 2.6 collective-permute-start
  11.7 2.0 copy.27
  13.9 5.6 %fusion.1 = (f32[2048,128]{1,0:T(8,128)}, f32[2048,128]{1,0:T(8,128)}) fusion(f32[128]{0:T(128)S(1)} %compare_select_fusion, f32[128]{0:T(128)S(1)} %mul.49, f32[2048]{0:T(1024)S(1)} %bitcast.120), kind=kLoop, calls=%fused_computation.12 | loop fusion | flops 524288 | bytes 2106368 | tf_op jit(solution)/shard_map/mul | solution.py:791
  20.0 2.1 fusion.4.refs_0_.refs_7_
  25.8 5.7 %collective-permute-done.3.refs_9_ = bf16[144,768]{1,0:T(8,128)(2,1)S(1)} collective-permute-done((bf16[144,768]{1,0:T(8,128)(2,1)}, bf16[144,768]{1,0:T(8,128)(2,1)S(1)}, u32[]{:S(2)}, u32[]{:S(2)}) %collective-permute-start.3) | collective-permute-done | bytes 221216 | tf_op jit(solution)/shard_map/ppermute | solution.py:764
  31.5 4.1 %collective-permute-done.4.refs_8_ = bf16[2,144,768]{2,1,0:T(8,128)(2,1)S(1)} collective-permute-done((bf16[2,144,768]{2,1,0:T(8,128)(2,1)S(1)}, bf16[2,144,768]{2,1,0:T(8,128)(2,1)S(1)}, u32[]{:S(2)}, u32[]{:S(2)}) %collective-permute-start.4) | collective-permute-done | bytes 442400 | tf_op jit(solution)/shard_map/ppermute | solution.py:764
  36.3 7.1 %collective-permute-done.8.refs_10_ = bf16[144,768]{1,0:T(8,128)(2,1)S(1)} collective-permute-done((bf16[144,768]{1,0:T(8,128)(2,1)S(1)}, bf16[144,768]{1,0:T(8,128)(2,1)S(1)}, u32[]{:S(2)}, u32[]{:S(2)}) %collective-permute-start.8) | collective-permute-done | bytes 221216 | tf_op jit(solution)/shard_map/ppermute | solution.py:764
  44.5 11.6 %project.1 = (bf16[2048,1024]{1,0:T(8,128)(2,1)}, bf16[2048,256]{1,0:T(8,128)(2,1)}, bf16[2048,256]{1,0:T(8,128)(2,1)}, bf16[2048,256]{1,0:T(8,128)(2,1)}, bf16[1024,768]{1,0:T(8,128)(2,1)}, /*index=5*/f32[8,1024]{1,0:T(8,128)}) custom-call(s32[12]{0:T(128)} %stack.87.idx, bf16[512,1024]{1,0:T(8,128)(2,1)} %bitcast.100, bf16[512,1024]{1,0:T(8,128)(2,1)} %copy-done.8, ...), custom_call_target="tpu_custom_call" | custom-call | flops 11 | bytes 11 | tf_op jit(solution)/shard_map/project/pallas_call | solution.py:171
  56.2 10.9 %collective-permute-done.10.refs_4_.refs_11_ = bf16[128,3840]{1,0:T(8,128)(2,1)S(1)} collective-permute-done((bf16[128,3840]{1,0:T(8,128)(2,1)}, bf16[128,3840]{1,0:T(8,128)(2,1)S(1)}, u32[]{:S(2)}, u32[]{:S(2)}) %collective-permute-start.10) | collective-permute-done | bytes 983072 | tf_op jit(solution)/shard_map/ppermute | solution.py:764
  67.1 2.1 collective-permute-done.9.refs_1_.refs_8_
  72.6 8.7 %attend.4 = (bf16[512,256]{1,0:T(8,128)(2,1)}, f32[8,512]{1,0:T(8,128)}) custom-call(bf16[2048,256]{1,0:T(8,128)(2,1)} %get-tuple-element.183.refs_0_, bf16[2048,256]{1,0:T(8,128)(2,1)} %get-tuple-element.172.refs_1_.refs_6_, bf16[2048,256]{1,0:T(8,128)(2,1)} %get-tuple-element.173.refs_2_.refs_7_), custom_call_target="tpu_custom_call" | custom-call | flops 8 | bytes 8 | tf_op jit(solution)/shard_map/attend/pallas_call | solution.py:234
  81.3 1.6 collective-permute-start.15
  82.8 9.1 %attend.5 = (bf16[512,256]{1,0:T(8,128)(2,1)}, f32[8,512]{1,0:T(8,128)}) custom-call(bf16[2048,256]{1,0:T(8,128)(2,1)} %get-tuple-element.183.refs_0_, bf16[2048,256]{1,0:T(8,128)(2,1)} %get-tuple-element.172.refs_1_.refs_6_, bf16[2048,256]{1,0:T(8,128)(2,1)} %get-tuple-element.173.refs_2_.refs_7_), custom_call_target="tpu_custom_call" | custom-call | flops 8 | bytes 8 | tf_op jit(solution)/shard_map/attend/pallas_call | solution.py:234
  91.9 2.0 collective-permute-done.15.oa_ref.oa
  98.5 8.7 %attend.6 = (bf16[512,256]{1,0:T(8,128)(2,1)}, f32[8,512]{1,0:T(8,128)}) custom-call(bf16[2048,256]{1,0:T(8,128)(2,1)} %get-tuple-element.183.refs_0_, bf16[2048,256]{1,0:T(8,128)(2,1)} %get-tuple-element.172.refs_1_.refs_6_, bf16[2048,256]{1,0:T(8,128)(2,1)} %get-tuple-element.173.refs_2_.refs_7_), custom_call_target="tpu_custom_call" | custom-call | flops 8 | bytes 8 | tf_op jit(solution)/shard_map/attend/pallas_call | solution.py:234
  107.2 8.9 %attend.7 = (bf16[512,256]{1,0:T(8,128)(2,1)}, f32[8,512]{1,0:T(8,128)}) custom-call(bf16[2048,256]{1,0:T(8,128)(2,1)} %get-tuple-element.183.refs_0_, bf16[2048,256]{1,0:T(8,128)(2,1)} %get-tuple-element.172.refs_1_.refs_6_, bf16[2048,256]{1,0:T(8,128)(2,1)} %get-tuple-element.173.refs_2_.refs_7_), custom_call_target="tpu_custom_call" | custom-call | flops 8 | bytes 8 | tf_op jit(solution)/shard_map/attend/pallas_call | solution.py:234
  118.3 1.6 collective-permute-start.20
  120.6 17.5 %collective-permute-done.20.refs_7_.refs_14_ = bf16[128,3840]{1,0:T(8,128)(2,1)S(1)} collective-permute-done((bf16[128,3840]{1,0:T(8,128)(2,1)S(1)}, bf16[128,3840]{1,0:T(8,128)(2,1)S(1)}, u32[]{:S(2)}, u32[]{:S(2)}) %collective-permute-start.20) | collective-permute-done | bytes 983072 | tf_op jit(solution)/shard_map/ppermute | solution.py:764
  139.0 5.4 %out_project.1 = (bf16[1024,1024]{1,0:T(8,128)(2,1)}, bf16[512,1024]{1,0:T(8,128)(2,1)}) custom-call(s32[12]{0:T(128)} %stack.87.idx, bf16[512,256]{1,0:T(8,128)(2,1)} %get-tuple-element.182.ma_ref.ma.refs_2_, bf16[512,256]{1,0:T(8,128)(2,1)} %get-tuple-element.190.mb_ref.mb.refs_3_, bf16[512,256]{1,0:T(8,128)(2,1)} %copy-done.27, ...), custom_call_target="tpu_custom_call" | custom-call | flops 5 | bytes 5 | tf_op jit(solution)/shard_map/out_project/pallas_call | solution.py:367
  145.6 4.4 %collective-permute-done.23.refs_3_.pr = bf16[1024,1024]{1,0:T(8,128)(2,1)S(1)} collective-permute-done((bf16[1024,1024]{1,0:T(8,128)(2,1)}, bf16[1024,1024]{1,0:T(8,128)(2,1)S(1)}, u32[]{:S(2)}, u32[]{:S(2)}) %collective-permute-start.23) | collective-permute-done | bytes 2097184 | tf_op jit(solution)/shard_map/ppermute | solution.py:764
  151.4 33.3 %feed_forward.1 = (bf16[1024,1408]{1,0:T(8,128)(2,1)}, bf16[1024,1024]{1,0:T(8,128)(2,1)}, bf16[1024,1408]{1,0:T(8,128)(2,1)}, bf16[2,4,128,768]{3,2,1,0:T(8,128...) custom-call(s32[12]{0:T(128)} %stack.87.idx, ...), custom_call_target="tpu_custom_call" | custom-call | flops 25 | bytes 25 | tf_op jit(solution)/shard_map/feed_forward/pallas_call | solution.py:462
  184.9 1.5 collective-permute-start.27
  186.9 11.3 %down_project.1 = (bf16[512,1024]{1,0:T(8,128)(2,1)}, bf16[512,1024]{1,0:T(8,128)(2,1)}, bf16[2,4,656,128]{3,2,1,0:T(8,128)(2,1)}, bf16[2,4,656,128]{3,2,1,0:T(8,128)(2,1)}) custom-call(s32[12]{0:T(128)} %stack.87.idx, bf16[1024,1408]{1,0:T(8,128)(2,1)} %get-tuple-element.215.refs_0_, bf16[1024,1408]{1,0:T(8,128)(2,1)} %get-tuple-element.216.refs_1_, ...), custom_call_target="tpu_custom_call" | custom-call | flops 15 | bytes 15 | tf_op jit(solution)/shard_map/down_project/pallas_call | solution.py:534
  199.6 10.4 %norm_two_back.1 = (f32[512,1024]{1,0:T(8,128)}, bf16[1024,1024]{1,0:T(8,128)(2,1)}, bf16[1024,256]{1,0:T(8,128)(2,1)}, bf16[1024,256]{1,0:T(8,128)(2,1)}, f32[8,1024]{1,0:T(8,128)}) custom-call(bf16[512,1024]{1,0:T(8,128)(2,1)} %bitcast.102, bf16[512,1024]{1,0:T(8,128)(2,1)} %copy-done.8, bf16[1024,1024]{1,0:T(8,128)(2,1)} %get-tuple-element.199.refs_2_.po, ...), custom_call_target="tpu_custom_call" | custom-call | flops 8 | bytes 8 | tf_op jit(solution)/shard_map/norm_two_back/pallas_call | solution.py:592
  210.0 1.6 collective-permute-start.25
  212.1 4.2 %out_grad.1 = (bf16[8,256,128]{2,1,0:T(8,128)(2,1)}, bf16[8,256,128]{2,1,0:T(8,128)(2,1)}) custom-call(s32[12]{0:T(128)} %stack.87.idx, bf16[512,256]{1,0:T(8,128)(2,1)} %get-tuple-element.182.ma_ref.ma.refs_2_, bf16[512,256]{1,0:T(8,128)(2,1)} %get-tuple-element.190.mb_ref.mb.refs_3_, bf16[512,256]{1,0:T(8,128)(2,1)} %copy-done.27, ...), custom_call_target="tpu_custom_call" | custom-call | flops 4 | bytes 4 | tf_op jit(solution)/shard_map/out_grad/pallas_call | solution.py:640
  216.4 15.2 %attend_back.4 = (bf16[1024,128]{1,0:T(8,128)(2,1)}, f32[2048,128]{1,0:T(8,128)}, f32[2048,128]{1,0:T(8,128)}) custom-call(bf16[2048,256]{1,0:T(8,128)(2,1)} %get-tuple-element.183.refs_0_, bf16[1024,256]{1,0:T(8,128)(2,1)} %get-tuple-element.233.refs_1_, bf16[512,256]{1,0:T(8,128)(2,1)} %get-tuple-element.182.ma_ref.ma.refs_2_, ...), custom_call_target="tpu_custom_call" | custom-call | flops 15 | bytes 15 | tf_op jit(solution)/shard_map/attend_back/pallas_call | solution.py:316
  233.7 1.7 add_convert_fusion.6
  235.4 1.6 collective-permute-start.32
  238.2 15.1 %attend_back.5 = (bf16[1024,128]{1,0:T(8,128)(2,1)}, f32[2048,128]{1,0:T(8,128)}, f32[2048,128]{1,0:T(8,128)}) custom-call(bf16[2048,256]{1,0:T(8,128)(2,1)} %get-tuple-element.183.refs_0_, bf16[1024,256]{1,0:T(8,128)(2,1)} %get-tuple-element.233.refs_1_, bf16[512,256]{1,0:T(8,128)(2,1)} %get-tuple-element.182.ma_ref.ma.refs_2_, ...), custom_call_target="tpu_custom_call" | custom-call | flops 15 | bytes 15 | tf_op jit(solution)/shard_map/attend_back/pallas_call | solution.py:316
  253.3 15.9 %attend_back.6 = (bf16[1024,128]{1,0:T(8,128)(2,1)}, bf16[2048,128]{1,0:T(8,128)(2,1)}, bf16[2048,128]{1,0:T(8,128)(2,1)}) custom-call(bf16[2048,256]{1,0:T(8,128)(2,1)} %get-tuple-element.183.refs_0_, bf16[1024,256]{1,0:T(8,128)(2,1)} %copy-done.17, bf16[512,256]{1,0:T(8,128)(2,1)} %get-tuple-element.179.refs_2_, ...), custom_call_target="tpu_custom_call" | custom-call | flops 15 | bytes 15 | tf_op jit(solution)/shard_map/attend_back/pallas_call | solution.py:316
  270.5 6.3 %project_grad.2 = (bf16[4,384,128]{2,1,0:T(8,128)(2,1)}, bf16[4,384,128]{2,1,0:T(8,128)(2,1)}, f32[8,1024]{1,0:T(8,128)}) custom-call(s32[12]{0:T(128)} %stack.87.idx, bf16[2048,1024]{1,0:T(8,128)(2,1)} %get-tuple-element.252.fn_ref, bf16[1024,128]{1,0:T(8,128)(2,1)} %get-tuple-element.249.qn.q0, bf16[1024,128]{1,0:T(8,128)(2,1)} %get-tuple-element.251.qf.f0, ...), custom_call_target="tpu_custom_call" | custom-call | flops 6 | bytes 6 | tf_op jit(solution)/shard_map/project_grad/pallas_call | solution.py:719
  278.4 16.0 %attend_back.7 = (bf16[1024,128]{1,0:T(8,128)(2,1)}, bf16[2048,128]{1,0:T(8,128)(2,1)}, bf16[2048,128]{1,0:T(8,128)(2,1)}) custom-call(bf16[2048,256]{1,0:T(8,128)(2,1)} %get-tuple-element.183.refs_0_, bf16[1024,256]{1,0:T(8,128)(2,1)} %copy-done.17, bf16[512,256]{1,0:T(8,128)(2,1)} %get-tuple-element.179.refs_2_, ...), custom_call_target="tpu_custom_call" | custom-call | flops 15 | bytes 15 | tf_op jit(solution)/shard_map/attend_back/pallas_call | solution.py:316
  294.4 5.7 %back_project.2 = bf16[2,512,1024]{2,1,0:T(8,128)(2,1)} custom-call(bf16[1024,128]{1,0:T(8,128)(2,1)} %get-tuple-element.249.qn.q0, bf16[1024,128]{1,0:T(8,128)(2,1)} %get-tuple-element.250.q1.qn, bf16[1024,128]{1,0:T(8,128)(2,1)} %get-tuple-element.251.qf.f0, bf16[1024,128]{1,0:T(8,128)(2,1)} %get-tuple-element.274.f1.qf, ...), custom_call_target="tpu_custom_call" | custom-call | flops 5 | bytes 5 | tf_op jit(solution)/shard_map/back_project/pallas_call | solution.py:668
  300.9 3.0 fusion.8
  305.6 3.8 %collective-permute-start.38 = (bf16[128,1408]{1,0:T(8,128)(2,1)}, bf16[128,1408]{1,0:T(8,128)(2,1)}, u32[]{:S(2)}, u32[]{:S(2)}) collective-permute-start(bf16[128,1408]{1,0:T(8,128)(2,1)} %get-tuple-element.335), channel_id=1, source_target_pairs={{0,4},{1,5},{2,6},{3,7},{4,0},{5,1},{6,2},{7,3},{8,12},{9,13},{10,... | collective-permute-start | bytes 1081352 | tf_op jit(solution)/shard_map/ppermute | solution.py:764
  309.4 6.2 %project_grad.3 = (bf16[4,384,128]{2,1,0:T(8,128)(2,1)}, bf16[4,384,128]{2,1,0:T(8,128)(2,1)}, f32[8,1024]{1,0:T(8,128)}) custom-call(s32[12]{0:T(128)} %stack.87.idx, bf16[2048,1024]{1,0:T(8,128)(2,1)} %get-tuple-element.252.fn_ref, bf16[1024,128]{1,0:T(8,128)(2,1)} %get-tuple-element.250.q1.qn, bf16[1024,128]{1,0:T(8,128)(2,1)} %get-tuple-element.274.f1.qf, ...), custom_call_target="tpu_custom_call" | custom-call | flops 6 | bytes 6 | tf_op jit(solution)/shard_map/project_grad/pallas_call | solution.py:719
  317.3 5.9 %back_project.3.own = bf16[2,512,1024]{2,1,0:T(8,128)(2,1)} custom-call(bf16[1024,128]{1,0:T(8,128)(2,1)} %get-tuple-element.249.qn.q0, bf16[1024,128]{1,0:T(8,128)(2,1)} %get-tuple-element.250.q1.qn, bf16[1024,128]{1,0:T(8,128)(2,1)} %get-tuple-element.251.qf.f0, bf16[1024,128]{1,0:T(8,128)(2,1)} %get-tuple-element.274.f1.qf, ...), custom_call_target="tpu_custom_call" | custom-call | flops 5 | bytes 5 | tf_op jit(solution)/shard_map/back_project/pallas_call | solution.py:668
  324.7 2.7 fusion.2
  331.5 2.8 collective-permute-done.39
  337.3 2.1 fusion.3
  339.4 8.6 %collective-permute-done.37 = bf16[2,1296,128]{2,1,0:T(8,128)(2,1)S(1)} collective-permute-done((bf16[2,1296,128]{2,1,0:T(8,128)(2,1)S(1)}, bf16[2,1296,128]{2,1,0:T(8,128)(2,1)S(1)}, u32[]{:S(2)}, u32[]{:S(2)}) %collective-permute-start.37) | collective-permute-done | bytes 663584 | tf_op jit(solution)/shard_map/ppermute | solution.py:764
  353.0 7.0 %collective-permute-done.47 = bf16[640,128]{1,0:T(8,128)(2,1)} collective-permute-done((bf16[640,128]{1,0:T(8,128)(2,1)}, bf16[640,128]{1,0:T(8,128)(2,1)}, u32[]{:S(2)}, u32[]{:S(2)}) %collective-permute-start.47) | collective-permute-done | bytes 163872 | tf_op jit(solution)/shard_map/ppermute | solution.py:764
  361.7 3.0 collective-permute-start.45
  364.7 4.0 %collective-permute-done.50 = bf16[656,128]{1,0:T(8,128)(2,1)S(1)} collective-permute-done((bf16[656,128]{1,0:T(8,128)(2,1)S(1)}, bf16[656,128]{1,0:T(8,128)(2,1)S(1)}, u32[]{:S(2)}, u32[]{:S(2)}) %collective-permute-start.50) | collective-permute-done | bytes 167968 | tf_op jit(solution)/shard_map/ppermute | solution.py:999
  371.1 5.1 %norm_one_back.1 = f32[512,1024]{1,0:T(8,128)} custom-call(bf16[512,1024]{1,0:T(8,128)(2,1)} %bitcast.103, f32[512,1024]{1,0:T(8,128)} %get-tuple-element.292.res_ref, bf16[2,512,1024]{2,1,0:T(8,128)(2,1)} %back_project.3.own, bf16[2,512,1024]{2,1,0:T(8,128)(2,1)} %copy-done.16, bf16[512,1024]{1,0:T(8,128)(2,1)} %copy-done.22, ...), custom_call_target="tpu_custom_call" | custom-call | flops 3 | bytes 3 | tf_op jit(solution)/shard_map/norm_one_back/pallas_call | solution.py:743
  (242 shorter events, 57.0 us)
Async XLA Ops:
  2.9 20.8 %collective-permute-start.2 = (bf16[144,768]{1,0:T(8,128)(2,1)}, bf16[144,768]{1,0:T(8,128)(2,1)}, u32[]{:S(2)}, u32[]{:S(2)}) collective-permute-start(bf16[144,768]{1,0:T(8,128)(2,1)} %fusion.15.refs_4_), channel_id=1, source_target_pairs={{0,1},{1,0},{2,3},{3,2},{4,5},{5,4},{6,7},{7,6},{8,9},{9,8},{10,11... | collective-permute-start | bytes 663560 | tf_op jit(solution)/shard_map/ppermute | solution.py:764
  5.8 17.8 %collective-permute-start.1 = (bf16[144,768]{1,0:T(8,128)(2,1)}, bf16[144,768]{1,0:T(8,128)(2,1)S(1)}, u32[]{:S(2)}, u32[]{:S(2)}) collective-permute-start(bf16[144,768]{1,0:T(8,128)(2,1)} %fusion.15.refs_4_), channel_id=1, source_target_pairs={{0,2},{1,3},{2,0},{3,1},{4,6},{5,7},{6,4},{7,5},{8,10},{9,11},{10,... | collective-permute-start | bytes 663560 | tf_op jit(solution)/shard_map/ppermute | solution.py:764
  7.4 16.3 %collective-permute-start = (bf16[144,768]{1,0:T(8,128)(2,1)}, bf16[144,768]{1,0:T(8,128)(2,1)}, u32[]{:S(2)}, u32[]{:S(2)}) collective-permute-start(bf16[144,768]{1,0:T(8,128)(2,1)} %fusion.15.refs_4_), channel_id=1, source_target_pairs={{0,4},{1,5},{2,6},{3,7},{4,0},{5,1},{6,2},{7,3},{8,12},{9,13},{10,... | collective-permute-start | bytes 663560 | tf_op jit(solution)/shard_map/ppermute | solution.py:764
  10.0 25.6 %collective-permute-start.5 = (bf16[512,1024]{1,0:T(8,128)(2,1)S(1)}, bf16[512,1024]{1,0:T(8,128)(2,1)}, u32[]{:S(2)}, u32[]{:S(2)}) collective-permute-start(bf16[512,1024]{1,0:T(8,128)(2,1)S(1)} %bitcast.104), channel_id=1, source_target_pairs={{0,16},{8,24},{16,0},{24,8},{1,17},{9,25},{17,1},{25,9},{2,18},{10... | collective-permute-start | bytes 3145736 | tf_op jit(solution)/shard_map/ppermute | solution.py:764
  24.7 10.9 %collective-permute-start.4 = (bf16[2,144,768]{2,1,0:T(8,128)(2,1)S(1)}, bf16[2,144,768]{2,1,0:T(8,128)(2,1)S(1)}, u32[]{:S(2)}, u32[]{:S(2)}) collective-permute-start(bf16[2,144,768]{2,1,0:T(8,128)(2,1)S(1)} %pad_maximum_fusion.7), channel_id=1, source_target_pairs={{0,1},{1,0},{2,3},{3,2},{4,5},{5,4},{6,7},{7,6},{8,9},{9,8},{10,11... | collective-permute-start | bytes 1327112 | tf_op jit(solution)/shard_map/ppermute | solution.py:764
  25.3 6.1 %collective-permute-start.3 = (bf16[144,768]{1,0:T(8,128)(2,1)}, bf16[144,768]{1,0:T(8,128)(2,1)S(1)}, u32[]{:S(2)}, u32[]{:S(2)}) collective-permute-start(bf16[144,768]{1,0:T(8,128)(2,1)} %collective-permute-done.refs_7_), channel_id=1, source_target_pairs={{0,2},{1,3},{2,0},{3,1},{4,6},{5,7},{6,4},{7,5},{8,10},{9,11},{10,... | collective-permute-start | bytes 663560 | tf_op jit(solution)/shard_map/ppermute | solution.py:764
  25.8 17.7 %collective-permute-start.7 = (bf16[512,1024]{1,0:T(8,128)(2,1)S(1)}, bf16[512,1024]{1,0:T(8,128)(2,1)S(1)}, u32[]{:S(2)}, u32[]{:S(2)}) collective-permute-start(bf16[512,1024]{1,0:T(8,128)(2,1)S(1)} %bitcast.105), channel_id=1, source_target_pairs={{0,8},{8,0},{16,24},{24,16},{1,9},{9,1},{17,25},{25,17},{2,10},{10... | collective-permute-start | bytes 3145736 | tf_op jit(solution)/shard_map/ppermute | solution.py:764
  35.6 7.9 %collective-permute-start.6 = (bf16[512,1024]{1,0:T(8,128)(2,1)}, bf16[512,1024]{1,0:T(8,128)(2,1)}, u32[]{:S(2)}, u32[]{:S(2)}) collective-permute-start(bf16[512,1024]{1,0:T(8,128)(2,1)} %collective-permute-done.5.refs_2_), channel_id=1, source_target_pairs={{0,8},{8,0},{16,24},{24,16},{1,9},{9,1},{17,25},{25,17},{2,10},{10... | collective-permute-start | bytes 3145736 | tf_op jit(solution)/shard_map/ppermute | solution.py:764
  35.6 7.8 %collective-permute-start.8 = (bf16[144,768]{1,0:T(8,128)(2,1)S(1)}, bf16[144,768]{1,0:T(8,128)(2,1)S(1)}, u32[]{:S(2)}, u32[]{:S(2)}) collective-permute-start(bf16[144,768]{1,0:T(8,128)(2,1)S(1)} %collective-permute-done.3.refs_9_), channel_id=1, source_target_pairs={{0,1},{1,0},{2,3},{3,2},{4,5},{5,4},{6,7},{7,6},{8,9},{9,8},{10,11... | collective-permute-start | bytes 663560 | tf_op jit(solution)/shard_map/ppermute | solution.py:764
  36.2 20.0 %collective-permute-start.11 = (bf16[512,1024]{1,0:T(8,128)(2,1)S(1)}, bf16[512,1024]{1,0:T(8,128)(2,1)S(1)}, u32[]{:S(2)}, u32[]{:S(2)}) collective-permute-start(bf16[512,1024]{1,0:T(8,128)(2,1)S(1)} %bitcast.110), channel_id=1, source_target_pairs={{0,8},{8,0},{16,24},{24,16},{1,9},{9,1},{17,25},{25,17},{2,10},{10... | collective-permute-start | bytes 3145736 | tf_op jit(solution)/shard_map/ppermute | solution.py:764
  43.5 23.6 %collective-permute-start.10 = (bf16[128,3840]{1,0:T(8,128)(2,1)}, bf16[128,3840]{1,0:T(8,128)(2,1)S(1)}, u32[]{:S(2)}, u32[]{:S(2)}) collective-permute-start(bf16[128,3840]{1,0:T(8,128)(2,1)} %fusion.4.refs_0_.refs_7_), channel_id=1, source_target_pairs={{0,1},{1,0},{2,3},{3,2},{4,5},{5,4},{6,7},{7,6},{8,9},{9,8},{10,11... | collective-permute-start | bytes 2949128 | tf_op jit(solution)/shard_map/ppermute | solution.py:764
  44.0 25.1 %collective-permute-start.9 = (bf16[128,3840]{1,0:T(8,128)(2,1)}, bf16[128,3840]{1,0:T(8,128)(2,1)}, u32[]{:S(2)}, u32[]{:S(2)}) collective-permute-start(bf16[128,3840]{1,0:T(8,128)(2,1)} %fusion.4.refs_0_.refs_7_), channel_id=1, source_target_pairs={{0,2},{1,3},{2,4},{3,5},{4,6},{5,7},{6,0},{7,1},{8,10},{9,11},{10,... | collective-permute-start | bytes 2949128 | tf_op jit(solution)/shard_map/ppermute | solution.py:816
  69.2 24.7 %collective-permute-start.13 = (bf16[128,3840]{1,0:T(8,128)(2,1)}, bf16[128,3840]{1,0:T(8,128)(2,1)S(1)}, u32[]{:S(2)}, u32[]{:S(2)}) collective-permute-start(bf16[128,3840]{1,0:T(8,128)(2,1)} %collective-permute-done.9.refs_1_.refs_8_), channel_id=1, source_target_pairs={{0,1},{1,0},{2,3},{3,2},{4,5},{5,4},{6,7},{7,6},{8,9},{9,8},{10,11... | collective-permute-start | bytes 2949128 | tf_op jit(solution)/shard_map/ppermute | solution.py:764
  70.7 24.0 %collective-permute-start.12 = (bf16[128,3840]{1,0:T(8,128)(2,1)}, bf16[128,3840]{1,0:T(8,128)(2,1)S(1)}, u32[]{:S(2)}, u32[]{:S(2)}) collective-permute-start(bf16[128,3840]{1,0:T(8,128)(2,1)} %collective-permute-done.9.refs_1_.refs_8_), channel_id=1, source_target_pairs={{0,2},{1,3},{2,4},{3,5},{4,6},{5,7},{6,0},{7,1},{8,10},{9,11},{10,... | collective-permute-start | bytes 2949128 | tf_op jit(solution)/shard_map/ppermute | solution.py:816
  72.0 21.9 %collective-permute-start.14 = (bf16[2,128,1408]{2,1,0:T(8,128)(2,1)S(1)}, bf16[2,128,1408]{2,1,0:T(8,128)(2,1)S(1)}, u32[]{:S(2)}, u32[]{:S(2)}) collective-permute-start(bf16[2,128,1408]{2,1,0:T(8,128)(2,1)S(1)} %pad_maximum_fusion), channel_id=1, source_target_pairs={{0,16},{8,24},{16,0},{24,8},{1,17},{9,25},{17,1},{25,9},{2,18},{10... | collective-permute-start | bytes 2162696 | tf_op jit(solution)/shard_map/ppermute | solution.py:764
  81.3 12.6 %collective-permute-start.15 = (bf16[512,256]{1,0:T(8,128)(2,1)}, bf16[512,256]{1,0:T(8,128)(2,1)S(1)}, u32[]{:S(2)}, u32[]{:S(2)}) collective-permute-start(bf16[512,256]{1,0:T(8,128)(2,1)} %get-tuple-element.179.refs_2_), channel_id=1, source_target_pairs={{0,16},{8,24},{16,0},{24,8},{1,17},{9,25},{17,1},{25,9},{2,18},{10... | collective-permute-start | bytes 786440 | tf_op jit(solution)/shard_map/ppermute | solution.py:764
  94.9 22.4 %collective-permute-start.17 = (bf16[128,3840]{1,0:T(8,128)(2,1)S(1)}, bf16[128,3840]{1,0:T(8,128)(2,1)S(1)}, u32[]{:S(2)}, u32[]{:S(2)}) collective-permute-start(bf16[128,3840]{1,0:T(8,128)(2,1)S(1)} %collective-permute-done.12.refs_2_.refs_9_), channel_id=1, source_target_pairs={{0,1},{1,0},{2,3},{3,2},{4,5},{5,4},{6,7},{7,6},{8,9},{9,8},{10,11... | collective-permute-start | bytes 2949128 | tf_op jit(solution)/shard_map/ppermute | solution.py:764
  95.5 22.4 %collective-permute-start.16 = (bf16[128,3840]{1,0:T(8,128)(2,1)S(1)}, bf16[128,3840]{1,0:T(8,128)(2,1)S(1)}, u32[]{:S(2)}, u32[]{:S(2)}) collective-permute-start(bf16[128,3840]{1,0:T(8,128)(2,1)S(1)} %collective-permute-done.12.refs_2_.refs_9_), channel_id=1, source_target_pairs={{0,2},{1,3},{2,4},{3,5},{4,6},{5,7},{6,0},{7,1},{8,10},{9,11},{10,... | collective-permute-start | bytes 2949128 | tf_op jit(solution)/shard_map/ppermute | solution.py:816
  96.4 20.8 %collective-permute-start.18 = (bf16[2,128,1408]{2,1,0:T(8,128)(2,1)}, bf16[2,128,1408]{2,1,0:T(8,128)(2,1)S(1)}, u32[]{:S(2)}, u32[]{:S(2)}) collective-permute-start(bf16[2,128,1408]{2,1,0:T(8,128)(2,1)} %pad_maximum_fusion.1), channel_id=1, source_target_pairs={{0,16},{8,24},{16,0},{24,8},{1,17},{9,25},{17,1},{25,9},{2,18},{10... | collective-permute-start | bytes 2162696 | tf_op jit(solution)/shard_map/ppermute | solution.py:764
  97.0 20.3 %collective-permute-start.19 = (bf16[512,256]{1,0:T(8,128)(2,1)S(1)}, bf16[512,256]{1,0:T(8,128)(2,1)S(1)}, u32[]{:S(2)}, u32[]{:S(2)}) collective-permute-start(bf16[512,256]{1,0:T(8,128)(2,1)S(1)} %copy-done.23), channel_id=1, source_target_pairs={{0,16},{8,24},{16,0},{24,8},{1,17},{9,25},{17,1},{25,9},{2,18},{10... | collective-permute-start | bytes 786440 | tf_op jit(solution)/shard_map/ppermute | solution.py:764
  118.3 19.8 %collective-permute-start.20 = (bf16[128,3840]{1,0:T(8,128)(2,1)S(1)}, bf16[128,3840]{1,0:T(8,128)(2,1)S(1)}, u32[]{:S(2)}, u32[]{:S(2)}) collective-permute-start(bf16[128,3840]{1,0:T(8,128)(2,1)S(1)} %collective-permute-done.16.refs_3_.refs_10_), channel_id=1, source_target_pairs={{0,1},{1,0},{2,3},{3,2},{4,5},{5,4},{6,7},{7,6},{8,9},{9,8},{10,11... | collective-permute-start | bytes 2949128 | tf_op jit(solution)/shard_map/ppermute | solution.py:764
  120.0 24.4 %collective-permute-start.21 = (bf16[2,128,1408]{2,1,0:T(8,128)(2,1)S(1)}, bf16[2,128,1408]{2,1,0:T(8,128)(2,1)S(1)}, u32[]{:S(2)}, u32[]{:S(2)}) collective-permute-start(bf16[2,128,1408]{2,1,0:T(8,128)(2,1)S(1)} %pad_maximum_fusion.2), channel_id=1, source_target_pairs={{0,16},{8,24},{16,0},{24,8},{1,17},{9,25},{17,1},{25,9},{2,18},{10... | collective-permute-start | bytes 2162696 | tf_op jit(solution)/shard_map/ppermute | solution.py:764
  138.1 7.5 %collective-permute-start.22 = (bf16[128,1408]{1,0:T(8,128)(2,1)S(1)}, bf16[128,1408]{1,0:T(8,128)(2,1)S(1)}, u32[]{:S(2)}, u32[]{:S(2)}) collective-permute-start(bf16[128,1408]{1,0:T(8,128)(2,1)S(1)} %slice.245), channel_id=1, source_target_pairs={{0,16},{8,24},{16,0},{24,8},{1,17},{9,25},{17,1},{25,9},{2,18},{10... | collective-permute-start | bytes 1081352 | tf_op jit(solution)/shard_map/ppermute | solution.py:764
  184.7 13.6 %collective-permute-start.24 = (bf16[1024,1024]{1,0:T(8,128)(2,1)}, bf16[1024,1024]{1,0:T(8,128)(2,1)S(1)}, u32[]{:S(2)}, u32[]{:S(2)}) collective-permute-start(bf16[1024,1024]{1,0:T(8,128)(2,1)} %get-tuple-element.218.so), channel_id=1, source_target_pairs={{0,8},{8,0},{16,24},{24,16},{1,9},{9,1},{17,25},{25,17},{2,10},{10... | collective-permute-start | bytes 6291464 | tf_op jit(solution)/shard_map/ppermute | solution.py:764
  184.9 46.7 %collective-permute-start.27 = (bf16[2,4,128,768]{3,2,1,0:T(8,128)(2,1)}, bf16[2,4,128,768]{3,2,1,0:T(8,128)(2,1)S(1)}, u32[]{:S(2)}, u32[]{:S(2)}) collective-permute-start(bf16[2,4,128,768]{3,2,1,0:T(8,128)(2,1)} %get-tuple-element.231), channel_id=1, source_target_pairs={{0,1},{1,0},{2,3},{3,2},{4,5},{5,4},{6,7},{7,6},{8,9},{9,8},{10,11... | collective-permute-start | bytes 4718600 | tf_op jit(solution)/shard_map/ppermute | solution.py:764
  186.4 45.2 %collective-permute-start.28 = (bf16[8,128,640]{2,1,0:T(8,128)(2,1)}, bf16[8,128,640]{2,1,0:T(8,128)(2,1)}, u32[]{:S(2)}, u32[]{:S(2)}) collective-permute-start(bf16[8,128,640]{2,1,0:T(8,128)(2,1)} %get-tuple-element.232), channel_id=1, source_target_pairs={{0,16},{8,24},{16,0},{24,8},{1,17},{9,25},{17,1},{25,9},{2,18},{10... | collective-permute-start | bytes 3932168 | tf_op jit(solution)/shard_map/ppermute | solution.py:764
  198.2 33.3 %collective-permute-start.26 = (bf16[512,1024]{1,0:T(8,128)(2,1)}, bf16[512,1024]{1,0:T(8,128)(2,1)S(1)}, u32[]{:S(2)}, u32[]{:S(2)}) collective-permute-start(bf16[512,1024]{1,0:T(8,128)(2,1)} %get-tuple-element.230), channel_id=1, source_target_pairs={{0,8},{8,0},{16,24},{24,16},{1,9},{9,1},{17,25},{25,17},{2,10},{10... | collective-permute-start | bytes 3145736 | tf_op jit(solution)/shard_map/ppermute | solution.py:764
  210.0 21.5 %collective-permute-start.25 = (bf16[1024,256]{1,0:T(8,128)(2,1)}, bf16[1024,256]{1,0:T(8,128)(2,1)S(1)}, u32[]{:S(2)}, u32[]{:S(2)}) collective-permute-start(bf16[1024,256]{1,0:T(8,128)(2,1)} %get-tuple-element.229), channel_id=1, source_target_pairs={{0,16},{8,24},{16,0},{24,8},{1,17},{9,25},{17,1},{25,9},{2,18},{10... | collective-permute-start | bytes 1572872 | tf_op jit(solution)/shard_map/ppermute | solution.py:764
  211.6 57.6 %collective-permute-start.30 = (bf16[2,4,656,128]{3,2,1,0:T(8,128)(2,1)}, bf16[2,4,656,128]{3,2,1,0:T(8,128)(2,1)}, u32[]{:S(2)}, u32[]{:S(2)}) collective-permute-start(bf16[2,4,656,128]{3,2,1,0:T(8,128)(2,1)} %get-tuple-element.243), channel_id=1, source_target_pairs={{0,1},{1,0},{2,3},{3,2},{4,5},{5,4},{6,7},{7,6},{8,9},{9,8},{10,11... | collective-permute-start | bytes 4030472 | tf_op jit(solution)/shard_map/ppermute | solution.py:764
  232.9 36.3 %collective-permute-start.31 = (bf16[4,128,768]{2,1,0:T(8,128)(2,1)}, bf16[4,128,768]{2,1,0:T(8,128)(2,1)S(1)}, u32[]{:S(2)}, u32[]{:S(2)}) collective-permute-start(bf16[4,128,768]{2,1,0:T(8,128)(2,1)} %get-tuple-element.327), channel_id=1, source_target_pairs={{0,16},{8,24},{16,0},{24,8},{1,17},{9,25},{17,1},{25,9},{2,18},{10... | collective-permute-start | bytes 2359304 | tf_op jit(solution)/shard_map/ppermute | solution.py:764
  235.4 33.8 %collective-permute-start.32 = (bf16[4,128,640]{2,1,0:T(8,128)(2,1)S(1)}, bf16[4,128,640]{2,1,0:T(8,128)(2,1)S(1)}, u32[]{:S(2)}, u32[]{:S(2)}) collective-permute-start(bf16[4,128,640]{2,1,0:T(8,128)(2,1)S(1)} %get-tuple-element.331), channel_id=1, source_target_pairs={{0,1},{1,0},{2,3},{3,2},{4,5},{5,4},{6,7},{7,6},{8,9},{9,8},{10,11... | collective-permute-start | bytes 1966088 | tf_op jit(solution)/shard_map/ppermute | solution.py:764
  237.0 32.3 %collective-permute-start.29 = (bf16[8,256,128]{2,1,0:T(8,128)(2,1)S(1)}, bf16[8,256,128]{2,1,0:T(8,128)(2,1)S(1)}, u32[]{:S(2)}, u32[]{:S(2)}) collective-permute-start(bf16[8,256,128]{2,1,0:T(8,128)(2,1)S(1)} %copy-done.47), channel_id=1, source_target_pairs={{0,16},{8,24},{16,0},{24,8},{1,17},{9,25},{17,1},{25,9},{2,18},{10... | collective-permute-start | bytes 1572872 | tf_op jit(solution)/shard_map/ppermute | solution.py:764
  270.4 24.0 %collective-permute-start.33 = (bf16[2,128,1408]{2,1,0:T(8,128)(2,1)S(1)}, bf16[2,128,1408]{2,1,0:T(8,128)(2,1)S(1)}, u32[]{:S(2)}, u32[]{:S(2)}) collective-permute-start(bf16[2,128,1408]{2,1,0:T(8,128)(2,1)S(1)} %pad_maximum_fusion.3), channel_id=1, source_target_pairs={{0,2},{1,3},{2,0},{3,1},{4,6},{5,7},{6,4},{7,5},{8,10},{9,11},{10,... | collective-permute-start | bytes 2162696 | tf_op jit(solution)/shard_map/ppermute | solution.py:764
  277.8 16.6 %collective-permute-start.34 = (bf16[4,640,128]{2,1,0:T(8,128)(2,1)S(1)}, bf16[4,640,128]{2,1,0:T(8,128)(2,1)S(1)}, u32[]{:S(2)}, u32[]{:S(2)}) collective-permute-start(bf16[4,640,128]{2,1,0:T(8,128)(2,1)S(1)} %pad_maximum_fusion.6), channel_id=1, source_target_pairs={{0,1},{1,0},{2,3},{3,2},{4,5},{5,4},{6,7},{7,6},{8,9},{9,8},{10,11... | collective-permute-start | bytes 1966088 | tf_op jit(solution)/shard_map/ppermute | solution.py:764
  300.1 17.2 %collective-permute-start.35 = (bf16[2,512,1024]{2,1,0:T(8,128)(2,1)}, bf16[2,512,1024]{2,1,0:T(8,128)(2,1)S(1)}, u32[]{:S(2)}, u32[]{:S(2)}) collective-permute-start(bf16[2,512,1024]{2,1,0:T(8,128)(2,1)} %back_project.2), channel_id=1, source_target_pairs={{0,8},{8,0},{16,24},{24,16},{1,9},{9,1},{17,25},{25,17},{2,10},{10... | collective-permute-start | bytes 6291464 | tf_op jit(solution)/shard_map/ppermute | solution.py:764
  303.9 24.8 %collective-permute-start.36 = (bf16[4,656,128]{2,1,0:T(8,128)(2,1)}, bf16[4,656,128]{2,1,0:T(8,128)(2,1)}, u32[]{:S(2)}, u32[]{:S(2)}) collective-permute-start(bf16[4,656,128]{2,1,0:T(8,128)(2,1)} %get-tuple-element.328), channel_id=1, source_target_pairs={{0,16},{8,24},{16,0},{24,8},{1,17},{9,25},{17,1},{25,9},{2,18},{10... | collective-permute-start | bytes 2015240 | tf_op jit(solution)/shard_map/ppermute | solution.py:764
  305.6 33.8 %collective-permute-start.38 = (bf16[128,1408]{1,0:T(8,128)(2,1)}, bf16[128,1408]{1,0:T(8,128)(2,1)}, u32[]{:S(2)}, u32[]{:S(2)}) collective-permute-start(bf16[128,1408]{1,0:T(8,128)(2,1)} %get-tuple-element.335), channel_id=1, source_target_pairs={{0,4},{1,5},{2,6},{3,7},{4,0},{5,1},{6,2},{7,3},{8,12},{9,13},{10,... | collective-permute-start | bytes 1081352 | tf_op jit(solution)/shard_map/ppermute | solution.py:764
  323.2 11.2 %collective-permute-start.39 = (bf16[4,384,128]{2,1,0:T(8,128)(2,1)}, bf16[4,384,128]{2,1,0:T(8,128)(2,1)S(1)}, u32[]{:S(2)}, u32[]{:S(2)}) collective-permute-start(bf16[4,384,128]{2,1,0:T(8,128)(2,1)} %get-tuple-element.286), channel_id=1, source_target_pairs={{0,1},{1,0},{2,3},{3,2},{4,5},{5,4},{6,7},{7,6},{8,9},{9,8},{10,11... | collective-permute-start | bytes 1179656 | tf_op jit(solution)/shard_map/ppermute | solution.py:764
  327.5 34.2 %collective-permute-start.44 = (bf16[512,1024]{1,0:T(8,128)(2,1)}, bf16[512,1024]{1,0:T(8,128)(2,1)S(1)}, u32[]{:S(2)}, u32[]{:S(2)}) collective-permute-start(bf16[512,1024]{1,0:T(8,128)(2,1)} %fusion.2), channel_id=1, source_target_pairs={{0,16},{8,24},{16,0},{24,8},{1,17},{9,25},{17,1},{25,9},{2,18},{10... | collective-permute-start | bytes 3145736 | tf_op jit(solution)/shard_map/ppermute | solution.py:764
  330.2 17.8 %collective-permute-start.37 = (bf16[2,1296,128]{2,1,0:T(8,128)(2,1)S(1)}, bf16[2,1296,128]{2,1,0:T(8,128)(2,1)S(1)}, u32[]{:S(2)}, u32[]{:S(2)}) collective-permute-start(bf16[2,1296,128]{2,1,0:T(8,128)(2,1)S(1)} %pad_maximum_fusion.4), channel_id=1, source_target_pairs={{0,2},{1,3},{2,0},{3,1},{4,6},{5,7},{6,4},{7,5},{8,10},{9,11},{10,... | collective-permute-start | bytes 1990664 | tf_op jit(solution)/shard_map/ppermute | solution.py:764
  336.0 25.6 %collective-permute-start.42 = (bf16[2,384,128]{2,1,0:T(8,128)(2,1)S(1)}, bf16[2,384,128]{2,1,0:T(8,128)(2,1)S(1)}, u32[]{:S(2)}, u32[]{:S(2)}) collective-permute-start(bf16[2,384,128]{2,1,0:T(8,128)(2,1)S(1)} %get-tuple-element.349), channel_id=1, source_target_pairs={{0,2},{1,3},{2,0},{3,1},{4,6},{5,7},{6,4},{7,5},{8,10},{9,11},{10,... | collective-permute-start | bytes 589832 | tf_op jit(solution)/shard_map/ppermute | solution.py:764
  348.0 13.6 %collective-permute-start.43 = (f32[2,1024]{1,0:T(2,128)S(1)}, f32[2,1024]{1,0:T(2,128)S(1)}, u32[]{:S(2)}, u32[]{:S(2)}) collective-permute-start(f32[2,1024]{1,0:T(2,128)S(1)} %add.252), channel_id=1, source_target_pairs={{0,2},{1,3},{2,0},{3,1},{4,6},{5,7},{6,4},{7,5},{8,10},{9,11},{10,... | collective-permute-start | bytes 24584 | tf_op jit(solution)/shard_map/ppermute | solution.py:764
  350.1 9.9 %collective-permute-start.47 = (bf16[640,128]{1,0:T(8,128)(2,1)}, bf16[640,128]{1,0:T(8,128)(2,1)}, u32[]{:S(2)}, u32[]{:S(2)}) collective-permute-start(bf16[640,128]{1,0:T(8,128)(2,1)} %slice_bitcast_fusion.12), channel_id=1, source_target_pairs={{0,4},{1,5},{2,6},{3,7},{4,0},{5,1},{6,2},{7,3},{8,12},{9,13},{10,... | collective-permute-start | bytes 491528 | tf_op jit(solution)/shard_map/ppermute | solution.py:764
  350.2 14.5 %collective-permute-start.49 = (bf16[656,128]{1,0:T(8,128)(2,1)S(1)}, bf16[656,128]{1,0:T(8,128)(2,1)S(1)}, u32[]{:S(2)}, u32[]{:S(2)}) collective-permute-start(bf16[656,128]{1,0:T(8,128)(2,1)S(1)} %slice_bitcast_fusion.11), channel_id=1, source_target_pairs={{8,16},{16,8},{9,17},{17,9},{10,18},{18,10},{11,19},{19,11},{12,20... | collective-permute-start | bytes 503816 | tf_op jit(solution)/shard_map/ppermute | solution.py:1004
  360.0 8.7 %collective-permute-start.50 = (bf16[656,128]{1,0:T(8,128)(2,1)S(1)}, bf16[656,128]{1,0:T(8,128)(2,1)S(1)}, u32[]{:S(2)}, u32[]{:S(2)}) collective-permute-start(bf16[656,128]{1,0:T(8,128)(2,1)S(1)} %slice_bitcast_fusion.10), channel_id=1, source_target_pairs={{0,4},{1,5},{2,6},{3,7},{4,0},{5,1},{6,2},{7,3},{8,20},{9,21},{10,... | collective-permute-start | bytes 503816 | tf_op jit(solution)/shard_map/ppermute | solution.py:999
  361.7 7.8 %collective-permute-start.45 = (f32[2,1024]{1,0:T(2,128)S(1)}, f32[2,1024]{1,0:T(2,128)S(1)}, u32[]{:S(2)}, u32[]{:S(2)}) collective-permute-start(f32[2,1024]{1,0:T(2,128)S(1)} %add.253), channel_id=1, source_target_pairs={{0,4},{1,5},{2,6},{3,7},{4,0},{5,1},{6,2},{7,3},{8,12},{9,13},{10,... | collective-permute-start | bytes 24584 | tf_op jit(solution)/shard_map/ppermute | solution.py:764
  369.5 6.7 %collective-permute-start.46 = (f32[2,1024]{1,0:T(2,128)S(1)}, f32[2,1024]{1,0:T(2,128)S(1)}, u32[]{:S(2)}, u32[]{:S(2)}) collective-permute-start(f32[2,1024]{1,0:T(2,128)S(1)} %add.254), channel_id=1, source_target_pairs={{0,16},{8,24},{16,0},{24,8},{1,17},{9,25},{17,1},{25,9},{2,18},{10... | collective-permute-start | bytes 24584 | tf_op jit(solution)/shard_map/ppermute | solution.py:764
  371.0 6.6 %collective-permute-start.48 = (bf16[384,128]{1,0:T(8,128)(2,1)S(1)}, bf16[384,128]{1,0:T(8,128)(2,1)S(1)}, u32[]{:S(2)}, u32[]{:S(2)}) collective-permute-start(bf16[384,128]{1,0:T(8,128)(2,1)S(1)} %fusion.17), channel_id=1, source_target_pairs={{0,4},{1,5},{2,6},{3,7},{4,0},{5,1},{6,2},{7,3},{8,12},{9,13},{10,... | collective-permute-start | bytes 294920 | tf_op jit(solution)/shard_map/ppermute | solution.py:764
  (51 other events, 401.0 us)

commit v6 on v5

--- a/solution.py
+++ b/solution.py
@@ -1005,7 +1005,8 @@
         rest_last, rest_keep = by_zz(rest_last[BLOCK:]), rest_keep[BLOCK:]
         gain_terms = gain_terms + gain_got
         gain_got = by_z(gain_terms)
-        terms1_next, gain_got, first_far = together(terms1_next, gain_got, first_far)
+        input_grad = norm_one_call(x0, res, first_own, first_got, first_far, gains)[None]
+        terms1_next, gain_got, input_grad = together(terms1_next, gain_got, input_grad)
         terms1_last = by_zz(plus(terms1_keep[1], terms1_next[1]))
         terms1_keep = plus(terms1_keep[0], terms1_next[0])
         gain_terms = gain_terms + gain_got
@@ -1017,6 +1018,7 @@
         out_total = rest_total[:COLS]
         totals = [rest_total[COLS:], final(terms1_keep, terms1_last)]
     else:
+        input_grad = norm_one_call(x0, res, first_own, first_got, first_far, gains)[None]
         wide_sum = plus(wide[0][0, 0], by_x(wide[0][1, 0]))
         scatter = lambda value, dim: lax.psum_scatter(
             value, "shard", scatter_dimension=dim, tiled=True
@@ -1035,7 +1037,6 @@
             + down_mine.astype(f32)
             + down_core.astype(f32)
         ).astype(bf16)[None]
-    input_grad = norm_one_call(x0, res, first_own, first_got, first_far, gains)[None]
     take = width // (4 * shards)
     gain_out = lax.dynamic_slice_in_dim(gain_terms, (seq * shards + shard) * take, take, 1)
     qkv_out = jnp.concatenate([total.reshape(3, piece, 128) for total in totals], axis=2)

time: 384 us -> 386 us (level)
    ppermute x1, waiting for transfers between devices: 4.03 us -> 0.01 us  [per_device(): lax.ppermute(down_last, ('seq', 'shard'), [(8 * j + i, 8 * (0, 2, 1, 3)[j...]
    unnamed x101 -> x103, local copies, waits for them, and re-layouts: 8.64 us -> 9.6 us
where the time goes in v6:
time: 386 us; the launch traced here: 381 us
  Pallas kernels  203 us (53%)
  waiting for transfers between devices  79.9 us (21%)
  starting transfers between devices  49.1 us (13%)
  other arithmetic  31.6 us (8%)
  local copies, waits for them, and re-layouts  15.7 us (4%)
    ppermute x46, waiting for transfers between devices, swap(): lax.ppermute(value, axis, [(place, place ^ bits) for place in range(size)])  76.5 us
    pallas_call x4, Pallas kernels, attend_back(): pl.pallas_call(lambda *refs: attend_back_kernel(last, pair, *refs[:n_in],...  62.1 us
    ppermute x46, starting transfers between devices, swap(): lax.ppermute(value, axis, [(place, place ^ bits) for place in range(size)])  47.8 us
    pallas_call x4, Pallas kernels, attend(): pl.pallas_call(lambda *refs: attend_kernel(*refs[:3], *refs[3 + len(after...  35.2 us
    pallas_call x1, Pallas kernels, mlp_call(): pl.pallas_call(partial(mlp_kernel, count, len(arrays), mine, other, down)...  33.2 us
    convert_element_type x13, other arithmetic, plus(): return (left.astype(f32) + right.astype(f32)).astype(bf16)  12.5 us
    pallas_call x2, Pallas kernels, qkv_grad_call(): pl.pallas_call(partial(qkv_grad_kernel, count), grid=(1,), in_specs=[SMEM...  12.4 us
    pallas_call x1, Pallas kernels, qkv_call(): pl.pallas_call(partial(qkv_kernel, count, where), grid=(4,), in_specs=[SM...  11.6 us
  transfers between devices with their start and end apart: 51, of which 17 were waited for; matrix products, arithmetic and copies ran while one was open for 10% of the time, Pallas kernels for 43%

profile of v6, /device:TPU:0, one launch (start us, length us, event | category | flops | bytes accessed | tf_op | source)
XLA Modules:
  0.0 380.5 jit_solution(14506464409023249527)
XLA Ops:
  2.9 3.0 collective-permute-start.2
  5.8 1.6 collective-permute-start.1
  7.4 2.6 collective-permute-start
  11.7 2.0 copy.27
  13.9 5.6 %fusion.1 = (f32[2048,128]{1,0:T(8,128)}, f32[2048,128]{1,0:T(8,128)}) fusion(f32[128]{0:T(128)S(1)} %compare_select_fusion, f32[128]{0:T(128)S(1)} %mul.49, f32[2048]{0:T(1024)S(1)} %bitcast.120), kind=kLoop, calls=%fused_computation.12 | loop fusion | flops 524288 | bytes 2106368 | tf_op jit(solution)/shard_map/mul | solution.py:791
  19.9 2.1 fusion.4.refs_0_.refs_7_
  25.6 5.7 %collective-permute-done.3.refs_9_ = bf16[144,768]{1,0:T(8,128)(2,1)S(1)} collective-permute-done((bf16[144,768]{1,0:T(8,128)(2,1)}, bf16[144,768]{1,0:T(8,128)(2,1)S(1)}, u32[]{:S(2)}, u32[]{:S(2)}) %collective-permute-start.3) | collective-permute-done | bytes 221216 | tf_op jit(solution)/shard_map/ppermute | solution.py:764
  31.3 4.1 %collective-permute-done.4.refs_8_ = bf16[2,144,768]{2,1,0:T(8,128)(2,1)S(1)} collective-permute-done((bf16[2,144,768]{2,1,0:T(8,128)(2,1)S(1)}, bf16[2,144,768]{2,1,0:T(8,128)(2,1)S(1)}, u32[]{:S(2)}, u32[]{:S(2)}) %collective-permute-start.4) | collective-permute-done | bytes 442400 | tf_op jit(solution)/shard_map/ppermute | solution.py:764
  36.2 7.1 %collective-permute-done.8.refs_10_ = bf16[144,768]{1,0:T(8,128)(2,1)S(1)} collective-permute-done((bf16[144,768]{1,0:T(8,128)(2,1)S(1)}, bf16[144,768]{1,0:T(8,128)(2,1)S(1)}, u32[]{:S(2)}, u32[]{:S(2)}) %collective-permute-start.8) | collective-permute-done | bytes 221216 | tf_op jit(solution)/shard_map/ppermute | solution.py:764
  44.4 11.6 %project.1 = (bf16[2048,1024]{1,0:T(8,128)(2,1)}, bf16[2048,256]{1,0:T(8,128)(2,1)}, bf16[2048,256]{1,0:T(8,128)(2,1)}, bf16[2048,256]{1,0:T(8,128)(2,1)}, bf16[1024,768]{1,0:T(8,128)(2,1)}, /*index=5*/f32[8,1024]{1,0:T(8,128)}) custom-call(s32[12]{0:T(128)} %stack.87.idx, bf16[512,1024]{1,0:T(8,128)(2,1)} %bitcast.100, bf16[512,1024]{1,0:T(8,128)(2,1)} %copy-done.8, ...), custom_call_target="tpu_custom_call" | custom-call | flops 11 | bytes 11 | tf_op jit(solution)/shard_map/project/pallas_call | solution.py:171
  56.0 10.9 %collective-permute-done.10.refs_4_.refs_11_ = bf16[128,3840]{1,0:T(8,128)(2,1)S(1)} collective-permute-done((bf16[128,3840]{1,0:T(8,128)(2,1)}, bf16[128,3840]{1,0:T(8,128)(2,1)S(1)}, u32[]{:S(2)}, u32[]{:S(2)}) %collective-permute-start.10) | collective-permute-done | bytes 983072 | tf_op jit(solution)/shard_map/ppermute | solution.py:764
  66.9 2.1 collective-permute-done.9.refs_1_.refs_8_
  72.5 8.7 %attend.4 = (bf16[512,256]{1,0:T(8,128)(2,1)}, f32[8,512]{1,0:T(8,128)}) custom-call(bf16[2048,256]{1,0:T(8,128)(2,1)} %get-tuple-element.183.refs_0_, bf16[2048,256]{1,0:T(8,128)(2,1)} %get-tuple-element.172.refs_1_.refs_6_, bf16[2048,256]{1,0:T(8,128)(2,1)} %get-tuple-element.173.refs_2_.refs_7_), custom_call_target="tpu_custom_call" | custom-call | flops 8 | bytes 8 | tf_op jit(solution)/shard_map/attend/pallas_call | solution.py:234
  81.1 1.6 collective-permute-start.15
  82.7 9.1 %attend.5 = (bf16[512,256]{1,0:T(8,128)(2,1)}, f32[8,512]{1,0:T(8,128)}) custom-call(bf16[2048,256]{1,0:T(8,128)(2,1)} %get-tuple-element.183.refs_0_, bf16[2048,256]{1,0:T(8,128)(2,1)} %get-tuple-element.172.refs_1_.refs_6_, bf16[2048,256]{1,0:T(8,128)(2,1)} %get-tuple-element.173.refs_2_.refs_7_), custom_call_target="tpu_custom_call" | custom-call | flops 8 | bytes 8 | tf_op jit(solution)/shard_map/attend/pallas_call | solution.py:234
  91.8 2.0 collective-permute-done.15.oa_ref.oa
  98.4 8.7 %attend.6 = (bf16[512,256]{1,0:T(8,128)(2,1)}, f32[8,512]{1,0:T(8,128)}) custom-call(bf16[2048,256]{1,0:T(8,128)(2,1)} %get-tuple-element.183.refs_0_, bf16[2048,256]{1,0:T(8,128)(2,1)} %get-tuple-element.172.refs_1_.refs_6_, bf16[2048,256]{1,0:T(8,128)(2,1)} %get-tuple-element.173.refs_2_.refs_7_), custom_call_target="tpu_custom_call" | custom-call | flops 8 | bytes 8 | tf_op jit(solution)/shard_map/attend/pallas_call | solution.py:234
  107.0 8.9 %attend.7 = (bf16[512,256]{1,0:T(8,128)(2,1)}, f32[8,512]{1,0:T(8,128)}) custom-call(bf16[2048,256]{1,0:T(8,128)(2,1)} %get-tuple-element.183.refs_0_, bf16[2048,256]{1,0:T(8,128)(2,1)} %get-tuple-element.172.refs_1_.refs_6_, bf16[2048,256]{1,0:T(8,128)(2,1)} %get-tuple-element.173.refs_2_.refs_7_), custom_call_target="tpu_custom_call" | custom-call | flops 8 | bytes 8 | tf_op jit(solution)/shard_map/attend/pallas_call | solution.py:234
  118.1 1.6 collective-permute-start.20
  120.4 17.5 %collective-permute-done.20.refs_7_.refs_14_ = bf16[128,3840]{1,0:T(8,128)(2,1)S(1)} collective-permute-done((bf16[128,3840]{1,0:T(8,128)(2,1)S(1)}, bf16[128,3840]{1,0:T(8,128)(2,1)S(1)}, u32[]{:S(2)}, u32[]{:S(2)}) %collective-permute-start.20) | collective-permute-done | bytes 983072 | tf_op jit(solution)/shard_map/ppermute | solution.py:764
  138.8 5.4 %out_project.1 = (bf16[1024,1024]{1,0:T(8,128)(2,1)}, bf16[512,1024]{1,0:T(8,128)(2,1)}) custom-call(s32[12]{0:T(128)} %stack.87.idx, bf16[512,256]{1,0:T(8,128)(2,1)} %get-tuple-element.182.ma_ref.ma.refs_2_, bf16[512,256]{1,0:T(8,128)(2,1)} %get-tuple-element.190.mb_ref.mb.refs_3_, bf16[512,256]{1,0:T(8,128)(2,1)} %copy-done.28, ...), custom_call_target="tpu_custom_call" | custom-call | flops 5 | bytes 5 | tf_op jit(solution)/shard_map/out_project/pallas_call | solution.py:367
  145.5 4.4 %collective-permute-done.23.refs_3_.pr = bf16[1024,1024]{1,0:T(8,128)(2,1)S(1)} collective-permute-done((bf16[1024,1024]{1,0:T(8,128)(2,1)}, bf16[1024,1024]{1,0:T(8,128)(2,1)S(1)}, u32[]{:S(2)}, u32[]{:S(2)}) %collective-permute-start.23) | collective-permute-done | bytes 2097184 | tf_op jit(solution)/shard_map/ppermute | solution.py:764
  151.2 33.2 %feed_forward.1 = (bf16[1024,1408]{1,0:T(8,128)(2,1)}, bf16[1024,1024]{1,0:T(8,128)(2,1)}, bf16[1024,1408]{1,0:T(8,128)(2,1)}, bf16[2,4,128,768]{3,2,1,0:T(8,128...) custom-call(s32[12]{0:T(128)} %stack.87.idx, ...), custom_call_target="tpu_custom_call" | custom-call | flops 25 | bytes 25 | tf_op jit(solution)/shard_map/feed_forward/pallas_call | solution.py:462
  186.8 11.3 %down_project.1 = (bf16[512,1024]{1,0:T(8,128)(2,1)}, bf16[512,1024]{1,0:T(8,128)(2,1)}, bf16[2,4,656,128]{3,2,1,0:T(8,128)(2,1)}, bf16[2,4,656,128]{3,2,1,0:T(8,128)(2,1)}) custom-call(s32[12]{0:T(128)} %stack.87.idx, bf16[1024,1408]{1,0:T(8,128)(2,1)} %get-tuple-element.215.refs_0_, bf16[1024,1408]{1,0:T(8,128)(2,1)} %get-tuple-element.216.refs_1_, ...), custom_call_target="tpu_custom_call" | custom-call | flops 15 | bytes 15 | tf_op jit(solution)/shard_map/down_project/pallas_call | solution.py:534
  199.5 10.4 %norm_two_back.1 = (f32[512,1024]{1,0:T(8,128)}, bf16[1024,1024]{1,0:T(8,128)(2,1)}, bf16[1024,256]{1,0:T(8,128)(2,1)}, bf16[1024,256]{1,0:T(8,128)(2,1)}, f32[8,1024]{1,0:T(8,128)}) custom-call(bf16[512,1024]{1,0:T(8,128)(2,1)} %bitcast.102, bf16[512,1024]{1,0:T(8,128)(2,1)} %copy-done.8, bf16[1024,1024]{1,0:T(8,128)(2,1)} %get-tuple-element.199.refs_2_.po, ...), custom_call_target="tpu_custom_call" | custom-call | flops 8 | bytes 8 | tf_op jit(solution)/shard_map/norm_two_back/pallas_call | solution.py:592
  209.9 1.6 collective-permute-start.25
  211.9 4.2 %out_grad.1 = (bf16[8,256,128]{2,1,0:T(8,128)(2,1)}, bf16[8,256,128]{2,1,0:T(8,128)(2,1)}) custom-call(s32[12]{0:T(128)} %stack.87.idx, bf16[512,256]{1,0:T(8,128)(2,1)} %get-tuple-element.182.ma_ref.ma.refs_2_, bf16[512,256]{1,0:T(8,128)(2,1)} %get-tuple-element.190.mb_ref.mb.refs_3_, bf16[512,256]{1,0:T(8,128)(2,1)} %copy-done.28, ...), custom_call_target="tpu_custom_call" | custom-call | flops 4 | bytes 4 | tf_op jit(solution)/shard_map/out_grad/pallas_call | solution.py:640
  216.2 15.2 %attend_back.4 = (bf16[1024,128]{1,0:T(8,128)(2,1)}, f32[2048,128]{1,0:T(8,128)}, f32[2048,128]{1,0:T(8,128)}) custom-call(bf16[2048,256]{1,0:T(8,128)(2,1)} %get-tuple-element.183.refs_0_, bf16[1024,256]{1,0:T(8,128)(2,1)} %get-tuple-element.233.refs_1_, bf16[512,256]{1,0:T(8,128)(2,1)} %get-tuple-element.182.ma_ref.ma.refs_2_, ...), custom_call_target="tpu_custom_call" | custom-call | flops 15 | bytes 15 | tf_op jit(solution)/shard_map/attend_back/pallas_call | solution.py:316
  233.5 1.7 add_convert_fusion.6
  235.2 1.6 collective-permute-start.32
  238.0 15.0 %attend_back.5 = (bf16[1024,128]{1,0:T(8,128)(2,1)}, f32[2048,128]{1,0:T(8,128)}, f32[2048,128]{1,0:T(8,128)}) custom-call(bf16[2048,256]{1,0:T(8,128)(2,1)} %get-tuple-element.183.refs_0_, bf16[1024,256]{1,0:T(8,128)(2,1)} %get-tuple-element.233.refs_1_, bf16[512,256]{1,0:T(8,128)(2,1)} %get-tuple-element.182.ma_ref.ma.refs_2_, ...), custom_call_target="tpu_custom_call" | custom-call | flops 15 | bytes 15 | tf_op jit(solution)/shard_map/attend_back/pallas_call | solution.py:316
  253.1 16.0 %attend_back.6 = (bf16[1024,128]{1,0:T(8,128)(2,1)}, bf16[2048,128]{1,0:T(8,128)(2,1)}, bf16[2048,128]{1,0:T(8,128)(2,1)}) custom-call(bf16[2048,256]{1,0:T(8,128)(2,1)} %get-tuple-element.183.refs_0_, bf16[1024,256]{1,0:T(8,128)(2,1)} %copy-done.17, bf16[512,256]{1,0:T(8,128)(2,1)} %get-tuple-element.179.refs_2_, ...), custom_call_target="tpu_custom_call" | custom-call | flops 15 | bytes 15 | tf_op jit(solution)/shard_map/attend_back/pallas_call | solution.py:316
  270.3 6.2 %project_grad.2 = (bf16[4,384,128]{2,1,0:T(8,128)(2,1)}, bf16[4,384,128]{2,1,0:T(8,128)(2,1)}, f32[8,1024]{1,0:T(8,128)}) custom-call(s32[12]{0:T(128)} %stack.87.idx, bf16[2048,1024]{1,0:T(8,128)(2,1)} %get-tuple-element.252.fn_ref, bf16[1024,128]{1,0:T(8,128)(2,1)} %get-tuple-element.249.qn.q0, bf16[1024,128]{1,0:T(8,128)(2,1)} %get-tuple-element.251.qf.f0, ...), custom_call_target="tpu_custom_call" | custom-call | flops 6 | bytes 6 | tf_op jit(solution)/shard_map/project_grad/pallas_call | solution.py:719
  278.2 16.0 %attend_back.7 = (bf16[1024,128]{1,0:T(8,128)(2,1)}, bf16[2048,128]{1,0:T(8,128)(2,1)}, bf16[2048,128]{1,0:T(8,128)(2,1)}) custom-call(bf16[2048,256]{1,0:T(8,128)(2,1)} %get-tuple-element.183.refs_0_, bf16[1024,256]{1,0:T(8,128)(2,1)} %copy-done.17, bf16[512,256]{1,0:T(8,128)(2,1)} %get-tuple-element.179.refs_2_, ...), custom_call_target="tpu_custom_call" | custom-call | flops 15 | bytes 15 | tf_op jit(solution)/shard_map/attend_back/pallas_call | solution.py:316
  294.2 5.6 %back_project.2 = bf16[2,512,1024]{2,1,0:T(8,128)(2,1)} custom-call(bf16[1024,128]{1,0:T(8,128)(2,1)} %get-tuple-element.249.qn.q0, bf16[1024,128]{1,0:T(8,128)(2,1)} %get-tuple-element.250.q1.qn, bf16[1024,128]{1,0:T(8,128)(2,1)} %get-tuple-element.251.qf.f0, bf16[1024,128]{1,0:T(8,128)(2,1)} %get-tuple-element.274.f1.qf, ...), custom_call_target="tpu_custom_call" | custom-call | flops 5 | bytes 5 | tf_op jit(solution)/shard_map/back_project/pallas_call | solution.py:668
  300.7 3.0 fusion.8
  305.4 3.8 collective-permute-start.38
  309.2 6.2 %project_grad.3 = (bf16[4,384,128]{2,1,0:T(8,128)(2,1)}, bf16[4,384,128]{2,1,0:T(8,128)(2,1)}, f32[8,1024]{1,0:T(8,128)}) custom-call(s32[12]{0:T(128)} %stack.87.idx, bf16[2048,1024]{1,0:T(8,128)(2,1)} %get-tuple-element.252.fn_ref, bf16[1024,128]{1,0:T(8,128)(2,1)} %get-tuple-element.250.q1.qn, bf16[1024,128]{1,0:T(8,128)(2,1)} %get-tuple-element.274.f1.qf, ...), custom_call_target="tpu_custom_call" | custom-call | flops 6 | bytes 6 | tf_op jit(solution)/shard_map/project_grad/pallas_call | solution.py:719
  317.0 5.9 %back_project.3.own = bf16[2,512,1024]{2,1,0:T(8,128)(2,1)} custom-call(bf16[1024,128]{1,0:T(8,128)(2,1)} %get-tuple-element.249.qn.q0, bf16[1024,128]{1,0:T(8,128)(2,1)} %get-tuple-element.250.q1.qn, bf16[1024,128]{1,0:T(8,128)(2,1)} %get-tuple-element.251.qf.f0, bf16[1024,128]{1,0:T(8,128)(2,1)} %get-tuple-element.274.f1.qf, ...), custom_call_target="tpu_custom_call" | custom-call | flops 5 | bytes 5 | tf_op jit(solution)/shard_map/back_project/pallas_call | solution.py:668
  324.5 2.7 fusion.2
  331.3 2.8 collective-permute-done.39
  337.0 2.1 fusion.3
  339.2 8.6 %collective-permute-done.37 = bf16[2,1296,128]{2,1,0:T(8,128)(2,1)S(1)} collective-permute-done((bf16[2,1296,128]{2,1,0:T(8,128)(2,1)S(1)}, bf16[2,1296,128]{2,1,0:T(8,128)(2,1)S(1)}, u32[]{:S(2)}, u32[]{:S(2)}) %collective-permute-start.37) | collective-permute-done | bytes 663584 | tf_op jit(solution)/shard_map/ppermute | solution.py:764
  352.8 7.0 %collective-permute-done.47 = bf16[640,128]{1,0:T(8,128)(2,1)} collective-permute-done((bf16[640,128]{1,0:T(8,128)(2,1)}, bf16[640,128]{1,0:T(8,128)(2,1)}, u32[]{:S(2)}, u32[]{:S(2)}) %collective-permute-start.47) | collective-permute-done | bytes 163872 | tf_op jit(solution)/shard_map/ppermute | solution.py:764
  362.4 5.1 %norm_one_back.1 = f32[512,1024]{1,0:T(8,128)} custom-call(bf16[512,1024]{1,0:T(8,128)(2,1)} %bitcast.103, f32[512,1024]{1,0:T(8,128)} %get-tuple-element.295.res_ref, bf16[2,512,1024]{2,1,0:T(8,128)(2,1)} %back_project.3.own, bf16[2,512,1024]{2,1,0:T(8,128)(2,1)} %copy-done.16, bf16[512,1024]{1,0:T(8,128)(2,1)} %copy-done.23, ...), custom_call_target="tpu_custom_call" | custom-call | flops 3 | bytes 3 | tf_op jit(solution)/shard_map/norm_one_back/pallas_call | solution.py:743
  367.5 3.0 collective-permute-start.45
  373.0 2.9 collective-permute-start.48
  376.5 2.9 collective-permute-done.48
  (245 shorter events, 58.8 us)
Async XLA Ops:
  2.9 20.7 %collective-permute-start.2 = (bf16[144,768]{1,0:T(8,128)(2,1)}, bf16[144,768]{1,0:T(8,128)(2,1)}, u32[]{:S(2)}, u32[]{:S(2)}) collective-permute-start(bf16[144,768]{1,0:T(8,128)(2,1)} %fusion.15.refs_4_), channel_id=1, source_target_pairs={{0,1},{1,0},{2,3},{3,2},{4,5},{5,4},{6,7},{7,6},{8,9},{9,8},{10,11... | collective-permute-start | bytes 663560 | tf_op jit(solution)/shard_map/ppermute | solution.py:764
  5.8 17.7 %collective-permute-start.1 = (bf16[144,768]{1,0:T(8,128)(2,1)}, bf16[144,768]{1,0:T(8,128)(2,1)S(1)}, u32[]{:S(2)}, u32[]{:S(2)}) collective-permute-start(bf16[144,768]{1,0:T(8,128)(2,1)} %fusion.15.refs_4_), channel_id=1, source_target_pairs={{0,2},{1,3},{2,0},{3,1},{4,6},{5,7},{6,4},{7,5},{8,10},{9,11},{10,... | collective-permute-start | bytes 663560 | tf_op jit(solution)/shard_map/ppermute | solution.py:764
  7.4 16.1 %collective-permute-start = (bf16[144,768]{1,0:T(8,128)(2,1)}, bf16[144,768]{1,0:T(8,128)(2,1)}, u32[]{:S(2)}, u32[]{:S(2)}) collective-permute-start(bf16[144,768]{1,0:T(8,128)(2,1)} %fusion.15.refs_4_), channel_id=1, source_target_pairs={{0,4},{1,5},{2,6},{3,7},{4,0},{5,1},{6,2},{7,3},{8,12},{9,13},{10,... | collective-permute-start | bytes 663560 | tf_op jit(solution)/shard_map/ppermute | solution.py:764
  10.0 25.5 %collective-permute-start.5 = (bf16[512,1024]{1,0:T(8,128)(2,1)S(1)}, bf16[512,1024]{1,0:T(8,128)(2,1)}, u32[]{:S(2)}, u32[]{:S(2)}) collective-permute-start(bf16[512,1024]{1,0:T(8,128)(2,1)S(1)} %bitcast.104), channel_id=1, source_target_pairs={{0,16},{8,24},{16,0},{24,8},{1,17},{9,25},{17,1},{25,9},{2,18},{10... | collective-permute-start | bytes 3145736 | tf_op jit(solution)/shard_map/ppermute | solution.py:764
  24.6 10.9 %collective-permute-start.4 = (bf16[2,144,768]{2,1,0:T(8,128)(2,1)S(1)}, bf16[2,144,768]{2,1,0:T(8,128)(2,1)S(1)}, u32[]{:S(2)}, u32[]{:S(2)}) collective-permute-start(bf16[2,144,768]{2,1,0:T(8,128)(2,1)S(1)} %pad_maximum_fusion.7), channel_id=1, source_target_pairs={{0,1},{1,0},{2,3},{3,2},{4,5},{5,4},{6,7},{7,6},{8,9},{9,8},{10,11... | collective-permute-start | bytes 1327112 | tf_op jit(solution)/shard_map/ppermute | solution.py:764
  25.2 6.1 %collective-permute-start.3 = (bf16[144,768]{1,0:T(8,128)(2,1)}, bf16[144,768]{1,0:T(8,128)(2,1)S(1)}, u32[]{:S(2)}, u32[]{:S(2)}) collective-permute-start(bf16[144,768]{1,0:T(8,128)(2,1)} %collective-permute-done.refs_7_), channel_id=1, source_target_pairs={{0,2},{1,3},{2,0},{3,1},{4,6},{5,7},{6,4},{7,5},{8,10},{9,11},{10,... | collective-permute-start | bytes 663560 | tf_op jit(solution)/shard_map/ppermute | solution.py:764
  25.6 17.7 %collective-permute-start.7 = (bf16[512,1024]{1,0:T(8,128)(2,1)S(1)}, bf16[512,1024]{1,0:T(8,128)(2,1)S(1)}, u32[]{:S(2)}, u32[]{:S(2)}) collective-permute-start(bf16[512,1024]{1,0:T(8,128)(2,1)S(1)} %bitcast.105), channel_id=1, source_target_pairs={{0,8},{8,0},{16,24},{24,16},{1,9},{9,1},{17,25},{25,17},{2,10},{10... | collective-permute-start | bytes 3145736 | tf_op jit(solution)/shard_map/ppermute | solution.py:764
  35.5 7.9 %collective-permute-start.6 = (bf16[512,1024]{1,0:T(8,128)(2,1)}, bf16[512,1024]{1,0:T(8,128)(2,1)}, u32[]{:S(2)}, u32[]{:S(2)}) collective-permute-start(bf16[512,1024]{1,0:T(8,128)(2,1)} %collective-permute-done.5.refs_2_), channel_id=1, source_target_pairs={{0,8},{8,0},{16,24},{24,16},{1,9},{9,1},{17,25},{25,17},{2,10},{10... | collective-permute-start | bytes 3145736 | tf_op jit(solution)/shard_map/ppermute | solution.py:764
  35.5 7.8 %collective-permute-start.8 = (bf16[144,768]{1,0:T(8,128)(2,1)S(1)}, bf16[144,768]{1,0:T(8,128)(2,1)S(1)}, u32[]{:S(2)}, u32[]{:S(2)}) collective-permute-start(bf16[144,768]{1,0:T(8,128)(2,1)S(1)} %collective-permute-done.3.refs_9_), channel_id=1, source_target_pairs={{0,1},{1,0},{2,3},{3,2},{4,5},{5,4},{6,7},{7,6},{8,9},{9,8},{10,11... | collective-permute-start | bytes 663560 | tf_op jit(solution)/shard_map/ppermute | solution.py:764
  36.1 19.9 %collective-permute-start.11 = (bf16[512,1024]{1,0:T(8,128)(2,1)S(1)}, bf16[512,1024]{1,0:T(8,128)(2,1)S(1)}, u32[]{:S(2)}, u32[]{:S(2)}) collective-permute-start(bf16[512,1024]{1,0:T(8,128)(2,1)S(1)} %bitcast.110), channel_id=1, source_target_pairs={{0,8},{8,0},{16,24},{24,16},{1,9},{9,1},{17,25},{25,17},{2,10},{10... | collective-permute-start | bytes 3145736 | tf_op jit(solution)/shard_map/ppermute | solution.py:764
  43.3 23.6 %collective-permute-start.10 = (bf16[128,3840]{1,0:T(8,128)(2,1)}, bf16[128,3840]{1,0:T(8,128)(2,1)S(1)}, u32[]{:S(2)}, u32[]{:S(2)}) collective-permute-start(bf16[128,3840]{1,0:T(8,128)(2,1)} %fusion.4.refs_0_.refs_7_), channel_id=1, source_target_pairs={{0,1},{1,0},{2,3},{3,2},{4,5},{5,4},{6,7},{7,6},{8,9},{9,8},{10,11... | collective-permute-start | bytes 2949128 | tf_op jit(solution)/shard_map/ppermute | solution.py:764
  43.9 25.1 %collective-permute-start.9 = (bf16[128,3840]{1,0:T(8,128)(2,1)}, bf16[128,3840]{1,0:T(8,128)(2,1)}, u32[]{:S(2)}, u32[]{:S(2)}) collective-permute-start(bf16[128,3840]{1,0:T(8,128)(2,1)} %fusion.4.refs_0_.refs_7_), channel_id=1, source_target_pairs={{0,2},{1,3},{2,4},{3,5},{4,6},{5,7},{6,0},{7,1},{8,10},{9,11},{10,... | collective-permute-start | bytes 2949128 | tf_op jit(solution)/shard_map/ppermute | solution.py:816
  69.0 24.7 %collective-permute-start.13 = (bf16[128,3840]{1,0:T(8,128)(2,1)}, bf16[128,3840]{1,0:T(8,128)(2,1)S(1)}, u32[]{:S(2)}, u32[]{:S(2)}) collective-permute-start(bf16[128,3840]{1,0:T(8,128)(2,1)} %collective-permute-done.9.refs_1_.refs_8_), channel_id=1, source_target_pairs={{0,1},{1,0},{2,3},{3,2},{4,5},{5,4},{6,7},{7,6},{8,9},{9,8},{10,11... | collective-permute-start | bytes 2949128 | tf_op jit(solution)/shard_map/ppermute | solution.py:764
  70.6 24.0 %collective-permute-start.12 = (bf16[128,3840]{1,0:T(8,128)(2,1)}, bf16[128,3840]{1,0:T(8,128)(2,1)S(1)}, u32[]{:S(2)}, u32[]{:S(2)}) collective-permute-start(bf16[128,3840]{1,0:T(8,128)(2,1)} %collective-permute-done.9.refs_1_.refs_8_), channel_id=1, source_target_pairs={{0,2},{1,3},{2,4},{3,5},{4,6},{5,7},{6,0},{7,1},{8,10},{9,11},{10,... | collective-permute-start | bytes 2949128 | tf_op jit(solution)/shard_map/ppermute | solution.py:816
  71.9 21.9 %collective-permute-start.14 = (bf16[2,128,1408]{2,1,0:T(8,128)(2,1)S(1)}, bf16[2,128,1408]{2,1,0:T(8,128)(2,1)S(1)}, u32[]{:S(2)}, u32[]{:S(2)}) collective-permute-start(bf16[2,128,1408]{2,1,0:T(8,128)(2,1)S(1)} %pad_maximum_fusion), channel_id=1, source_target_pairs={{0,16},{8,24},{16,0},{24,8},{1,17},{9,25},{17,1},{25,9},{2,18},{10... | collective-permute-start | bytes 2162696 | tf_op jit(solution)/shard_map/ppermute | solution.py:764
  81.1 12.6 %collective-permute-start.15 = (bf16[512,256]{1,0:T(8,128)(2,1)}, bf16[512,256]{1,0:T(8,128)(2,1)S(1)}, u32[]{:S(2)}, u32[]{:S(2)}) collective-permute-start(bf16[512,256]{1,0:T(8,128)(2,1)} %get-tuple-element.179.refs_2_), channel_id=1, source_target_pairs={{0,16},{8,24},{16,0},{24,8},{1,17},{9,25},{17,1},{25,9},{2,18},{10... | collective-permute-start | bytes 786440 | tf_op jit(solution)/shard_map/ppermute | solution.py:764
  94.8 22.4 %collective-permute-start.17 = (bf16[128,3840]{1,0:T(8,128)(2,1)S(1)}, bf16[128,3840]{1,0:T(8,128)(2,1)S(1)}, u32[]{:S(2)}, u32[]{:S(2)}) collective-permute-start(bf16[128,3840]{1,0:T(8,128)(2,1)S(1)} %collective-permute-done.12.refs_2_.refs_9_), channel_id=1, source_target_pairs={{0,1},{1,0},{2,3},{3,2},{4,5},{5,4},{6,7},{7,6},{8,9},{9,8},{10,11... | collective-permute-start | bytes 2949128 | tf_op jit(solution)/shard_map/ppermute | solution.py:764
  95.4 22.4 %collective-permute-start.16 = (bf16[128,3840]{1,0:T(8,128)(2,1)S(1)}, bf16[128,3840]{1,0:T(8,128)(2,1)S(1)}, u32[]{:S(2)}, u32[]{:S(2)}) collective-permute-start(bf16[128,3840]{1,0:T(8,128)(2,1)S(1)} %collective-permute-done.12.refs_2_.refs_9_), channel_id=1, source_target_pairs={{0,2},{1,3},{2,4},{3,5},{4,6},{5,7},{6,0},{7,1},{8,10},{9,11},{10,... | collective-permute-start | bytes 2949128 | tf_op jit(solution)/shard_map/ppermute | solution.py:816
  96.3 20.8 %collective-permute-start.18 = (bf16[2,128,1408]{2,1,0:T(8,128)(2,1)}, bf16[2,128,1408]{2,1,0:T(8,128)(2,1)S(1)}, u32[]{:S(2)}, u32[]{:S(2)}) collective-permute-start(bf16[2,128,1408]{2,1,0:T(8,128)(2,1)} %pad_maximum_fusion.1), channel_id=1, source_target_pairs={{0,16},{8,24},{16,0},{24,8},{1,17},{9,25},{17,1},{25,9},{2,18},{10... | collective-permute-start | bytes 2162696 | tf_op jit(solution)/shard_map/ppermute | solution.py:764
  96.9 20.3 %collective-permute-start.19 = (bf16[512,256]{1,0:T(8,128)(2,1)S(1)}, bf16[512,256]{1,0:T(8,128)(2,1)S(1)}, u32[]{:S(2)}, u32[]{:S(2)}) collective-permute-start(bf16[512,256]{1,0:T(8,128)(2,1)S(1)} %copy-done.24), channel_id=1, source_target_pairs={{0,16},{8,24},{16,0},{24,8},{1,17},{9,25},{17,1},{25,9},{2,18},{10... | collective-permute-start | bytes 786440 | tf_op jit(solution)/shard_map/ppermute | solution.py:764
  118.1 19.8 %collective-permute-start.20 = (bf16[128,3840]{1,0:T(8,128)(2,1)S(1)}, bf16[128,3840]{1,0:T(8,128)(2,1)S(1)}, u32[]{:S(2)}, u32[]{:S(2)}) collective-permute-start(bf16[128,3840]{1,0:T(8,128)(2,1)S(1)} %collective-permute-done.16.refs_3_.refs_10_), channel_id=1, source_target_pairs={{0,1},{1,0},{2,3},{3,2},{4,5},{5,4},{6,7},{7,6},{8,9},{9,8},{10,11... | collective-permute-start | bytes 2949128 | tf_op jit(solution)/shard_map/ppermute | solution.py:764
  119.8 24.4 %collective-permute-start.21 = (bf16[2,128,1408]{2,1,0:T(8,128)(2,1)S(1)}, bf16[2,128,1408]{2,1,0:T(8,128)(2,1)S(1)}, u32[]{:S(2)}, u32[]{:S(2)}) collective-permute-start(bf16[2,128,1408]{2,1,0:T(8,128)(2,1)S(1)} %pad_maximum_fusion.2), channel_id=1, source_target_pairs={{0,16},{8,24},{16,0},{24,8},{1,17},{9,25},{17,1},{25,9},{2,18},{10... | collective-permute-start | bytes 2162696 | tf_op jit(solution)/shard_map/ppermute | solution.py:764
  138.0 7.5 %collective-permute-start.22 = (bf16[128,1408]{1,0:T(8,128)(2,1)S(1)}, bf16[128,1408]{1,0:T(8,128)(2,1)S(1)}, u32[]{:S(2)}, u32[]{:S(2)}) collective-permute-start(bf16[128,1408]{1,0:T(8,128)(2,1)S(1)} %slice.245), channel_id=1, source_target_pairs={{0,16},{8,24},{16,0},{24,8},{1,17},{9,25},{17,1},{25,9},{2,18},{10... | collective-permute-start | bytes 1081352 | tf_op jit(solution)/shard_map/ppermute | solution.py:764
  184.5 13.6 %collective-permute-start.24 = (bf16[1024,1024]{1,0:T(8,128)(2,1)}, bf16[1024,1024]{1,0:T(8,128)(2,1)S(1)}, u32[]{:S(2)}, u32[]{:S(2)}) collective-permute-start(bf16[1024,1024]{1,0:T(8,128)(2,1)} %get-tuple-element.218.so), channel_id=1, source_target_pairs={{0,8},{8,0},{16,24},{24,16},{1,9},{9,1},{17,25},{25,17},{2,10},{10... | collective-permute-start | bytes 6291464 | tf_op jit(solution)/shard_map/ppermute | solution.py:764
  184.7 46.7 %collective-permute-start.27 = (bf16[2,4,128,768]{3,2,1,0:T(8,128)(2,1)}, bf16[2,4,128,768]{3,2,1,0:T(8,128)(2,1)S(1)}, u32[]{:S(2)}, u32[]{:S(2)}) collective-permute-start(bf16[2,4,128,768]{3,2,1,0:T(8,128)(2,1)} %get-tuple-element.231), channel_id=1, source_target_pairs={{0,1},{1,0},{2,3},{3,2},{4,5},{5,4},{6,7},{7,6},{8,9},{9,8},{10,11... | collective-permute-start | bytes 4718600 | tf_op jit(solution)/shard_map/ppermute | solution.py:764
  186.2 45.2 %collective-permute-start.28 = (bf16[8,128,640]{2,1,0:T(8,128)(2,1)}, bf16[8,128,640]{2,1,0:T(8,128)(2,1)}, u32[]{:S(2)}, u32[]{:S(2)}) collective-permute-start(bf16[8,128,640]{2,1,0:T(8,128)(2,1)} %get-tuple-element.232), channel_id=1, source_target_pairs={{0,16},{8,24},{16,0},{24,8},{1,17},{9,25},{17,1},{25,9},{2,18},{10... | collective-permute-start | bytes 3932168 | tf_op jit(solution)/shard_map/ppermute | solution.py:764
  198.0 33.3 %collective-permute-start.26 = (bf16[512,1024]{1,0:T(8,128)(2,1)}, bf16[512,1024]{1,0:T(8,128)(2,1)S(1)}, u32[]{:S(2)}, u32[]{:S(2)}) collective-permute-start(bf16[512,1024]{1,0:T(8,128)(2,1)} %get-tuple-element.230), channel_id=1, source_target_pairs={{0,8},{8,0},{16,24},{24,16},{1,9},{9,1},{17,25},{25,17},{2,10},{10... | collective-permute-start | bytes 3145736 | tf_op jit(solution)/shard_map/ppermute | solution.py:764
  209.9 21.5 %collective-permute-start.25 = (bf16[1024,256]{1,0:T(8,128)(2,1)}, bf16[1024,256]{1,0:T(8,128)(2,1)S(1)}, u32[]{:S(2)}, u32[]{:S(2)}) collective-permute-start(bf16[1024,256]{1,0:T(8,128)(2,1)} %get-tuple-element.229), channel_id=1, source_target_pairs={{0,16},{8,24},{16,0},{24,8},{1,17},{9,25},{17,1},{25,9},{2,18},{10... | collective-permute-start | bytes 1572872 | tf_op jit(solution)/shard_map/ppermute | solution.py:764
  211.4 57.6 %collective-permute-start.30 = (bf16[2,4,656,128]{3,2,1,0:T(8,128)(2,1)}, bf16[2,4,656,128]{3,2,1,0:T(8,128)(2,1)}, u32[]{:S(2)}, u32[]{:S(2)}) collective-permute-start(bf16[2,4,656,128]{3,2,1,0:T(8,128)(2,1)} %get-tuple-element.243), channel_id=1, source_target_pairs={{0,1},{1,0},{2,3},{3,2},{4,5},{5,4},{6,7},{7,6},{8,9},{9,8},{10,11... | collective-permute-start | bytes 4030472 | tf_op jit(solution)/shard_map/ppermute | solution.py:764
  232.7 36.3 %collective-permute-start.31 = (bf16[4,128,768]{2,1,0:T(8,128)(2,1)}, bf16[4,128,768]{2,1,0:T(8,128)(2,1)S(1)}, u32[]{:S(2)}, u32[]{:S(2)}) collective-permute-start(bf16[4,128,768]{2,1,0:T(8,128)(2,1)} %get-tuple-element.327), channel_id=1, source_target_pairs={{0,16},{8,24},{16,0},{24,8},{1,17},{9,25},{17,1},{25,9},{2,18},{10... | collective-permute-start | bytes 2359304 | tf_op jit(solution)/shard_map/ppermute | solution.py:764
  235.2 33.8 %collective-permute-start.32 = (bf16[4,128,640]{2,1,0:T(8,128)(2,1)S(1)}, bf16[4,128,640]{2,1,0:T(8,128)(2,1)S(1)}, u32[]{:S(2)}, u32[]{:S(2)}) collective-permute-start(bf16[4,128,640]{2,1,0:T(8,128)(2,1)S(1)} %get-tuple-element.331), channel_id=1, source_target_pairs={{0,1},{1,0},{2,3},{3,2},{4,5},{5,4},{6,7},{7,6},{8,9},{9,8},{10,11... | collective-permute-start | bytes 1966088 | tf_op jit(solution)/shard_map/ppermute | solution.py:764
  236.8 32.2 %collective-permute-start.29 = (bf16[8,256,128]{2,1,0:T(8,128)(2,1)S(1)}, bf16[8,256,128]{2,1,0:T(8,128)(2,1)S(1)}, u32[]{:S(2)}, u32[]{:S(2)}) collective-permute-start(bf16[8,256,128]{2,1,0:T(8,128)(2,1)S(1)} %copy-done.48), channel_id=1, source_target_pairs={{0,16},{8,24},{16,0},{24,8},{1,17},{9,25},{17,1},{25,9},{2,18},{10... | collective-permute-start | bytes 1572872 | tf_op jit(solution)/shard_map/ppermute | solution.py:764
  270.2 24.0 %collective-permute-start.33 = (bf16[2,128,1408]{2,1,0:T(8,128)(2,1)S(1)}, bf16[2,128,1408]{2,1,0:T(8,128)(2,1)S(1)}, u32[]{:S(2)}, u32[]{:S(2)}) collective-permute-start(bf16[2,128,1408]{2,1,0:T(8,128)(2,1)S(1)} %pad_maximum_fusion.3), channel_id=1, source_target_pairs={{0,2},{1,3},{2,0},{3,1},{4,6},{5,7},{6,4},{7,5},{8,10},{9,11},{10,... | collective-permute-start | bytes 2162696 | tf_op jit(solution)/shard_map/ppermute | solution.py:764
  277.6 16.6 %collective-permute-start.34 = (bf16[4,640,128]{2,1,0:T(8,128)(2,1)S(1)}, bf16[4,640,128]{2,1,0:T(8,128)(2,1)S(1)}, u32[]{:S(2)}, u32[]{:S(2)}) collective-permute-start(bf16[4,640,128]{2,1,0:T(8,128)(2,1)S(1)} %pad_maximum_fusion.6), channel_id=1, source_target_pairs={{0,1},{1,0},{2,3},{3,2},{4,5},{5,4},{6,7},{7,6},{8,9},{9,8},{10,11... | collective-permute-start | bytes 1966088 | tf_op jit(solution)/shard_map/ppermute | solution.py:764
  299.8 17.2 %collective-permute-start.35 = (bf16[2,512,1024]{2,1,0:T(8,128)(2,1)}, bf16[2,512,1024]{2,1,0:T(8,128)(2,1)S(1)}, u32[]{:S(2)}, u32[]{:S(2)}) collective-permute-start(bf16[2,512,1024]{2,1,0:T(8,128)(2,1)} %back_project.2), channel_id=1, source_target_pairs={{0,8},{8,0},{16,24},{24,16},{1,9},{9,1},{17,25},{25,17},{2,10},{10... | collective-permute-start | bytes 6291464 | tf_op jit(solution)/shard_map/ppermute | solution.py:764
  303.7 24.8 %collective-permute-start.36 = (bf16[4,656,128]{2,1,0:T(8,128)(2,1)}, bf16[4,656,128]{2,1,0:T(8,128)(2,1)}, u32[]{:S(2)}, u32[]{:S(2)}) collective-permute-start(bf16[4,656,128]{2,1,0:T(8,128)(2,1)} %get-tuple-element.328), channel_id=1, source_target_pairs={{0,16},{8,24},{16,0},{24,8},{1,17},{9,25},{17,1},{25,9},{2,18},{10... | collective-permute-start | bytes 2015240 | tf_op jit(solution)/shard_map/ppermute | solution.py:764
  305.4 33.8 %collective-permute-start.38 = (bf16[128,1408]{1,0:T(8,128)(2,1)}, bf16[128,1408]{1,0:T(8,128)(2,1)}, u32[]{:S(2)}, u32[]{:S(2)}) collective-permute-start(bf16[128,1408]{1,0:T(8,128)(2,1)} %get-tuple-element.335), channel_id=1, source_target_pairs={{0,4},{1,5},{2,6},{3,7},{4,0},{5,1},{6,2},{7,3},{8,12},{9,13},{10,... | collective-permute-start | bytes 1081352 | tf_op jit(solution)/shard_map/ppermute | solution.py:764
  323.0 11.2 %collective-permute-start.39 = (bf16[4,384,128]{2,1,0:T(8,128)(2,1)}, bf16[4,384,128]{2,1,0:T(8,128)(2,1)S(1)}, u32[]{:S(2)}, u32[]{:S(2)}) collective-permute-start(bf16[4,384,128]{2,1,0:T(8,128)(2,1)} %get-tuple-element.286), channel_id=1, source_target_pairs={{0,1},{1,0},{2,3},{3,2},{4,5},{5,4},{6,7},{7,6},{8,9},{9,8},{10,11... | collective-permute-start | bytes 1179656 | tf_op jit(solution)/shard_map/ppermute | solution.py:764
  327.2 34.2 %collective-permute-start.44 = (bf16[512,1024]{1,0:T(8,128)(2,1)}, bf16[512,1024]{1,0:T(8,128)(2,1)S(1)}, u32[]{:S(2)}, u32[]{:S(2)}) collective-permute-start(bf16[512,1024]{1,0:T(8,128)(2,1)} %fusion.2), channel_id=1, source_target_pairs={{0,16},{8,24},{16,0},{24,8},{1,17},{9,25},{17,1},{25,9},{2,18},{10... | collective-permute-start | bytes 3145736 | tf_op jit(solution)/shard_map/ppermute | solution.py:764
  330.0 17.8 %collective-permute-start.37 = (bf16[2,1296,128]{2,1,0:T(8,128)(2,1)S(1)}, bf16[2,1296,128]{2,1,0:T(8,128)(2,1)S(1)}, u32[]{:S(2)}, u32[]{:S(2)}) collective-permute-start(bf16[2,1296,128]{2,1,0:T(8,128)(2,1)S(1)} %pad_maximum_fusion.4), channel_id=1, source_target_pairs={{0,2},{1,3},{2,0},{3,1},{4,6},{5,7},{6,4},{7,5},{8,10},{9,11},{10,... | collective-permute-start | bytes 1990664 | tf_op jit(solution)/shard_map/ppermute | solution.py:764
  334.1 5.0 %collective-permute-start.41 = (f32[2,1024]{1,0:T(2,128)S(1)}, f32[2,1024]{1,0:T(2,128)S(1)}, u32[]{:S(2)}, u32[]{:S(2)}) collective-permute-start(f32[2,1024]{1,0:T(2,128)S(1)} %add.246), channel_id=1, source_target_pairs={{0,1},{1,0},{2,3},{3,2},{4,5},{5,4},{6,7},{7,6},{8,9},{9,8},{10,11... | collective-permute-start | bytes 24584 | tf_op jit(solution)/shard_map/ppermute | solution.py:764
  335.8 31.7 %collective-permute-start.42 = (bf16[2,384,128]{2,1,0:T(8,128)(2,1)S(1)}, bf16[2,384,128]{2,1,0:T(8,128)(2,1)S(1)}, u32[]{:S(2)}, u32[]{:S(2)}) collective-permute-start(bf16[2,384,128]{2,1,0:T(8,128)(2,1)S(1)} %get-tuple-element.349), channel_id=1, source_target_pairs={{0,2},{1,3},{2,0},{3,1},{4,6},{5,7},{6,4},{7,5},{8,10},{9,11},{10,... | collective-permute-start | bytes 589832 | tf_op jit(solution)/shard_map/ppermute | solution.py:764
  347.8 19.8 %collective-permute-start.43 = (f32[2,1024]{1,0:T(2,128)S(1)}, f32[2,1024]{1,0:T(2,128)S(1)}, u32[]{:S(2)}, u32[]{:S(2)}) collective-permute-start(f32[2,1024]{1,0:T(2,128)S(1)} %add.252), channel_id=1, source_target_pairs={{0,2},{1,3},{2,0},{3,1},{4,6},{5,7},{6,4},{7,5},{8,10},{9,11},{10,... | collective-permute-start | bytes 24584 | tf_op jit(solution)/shard_map/ppermute | solution.py:764
  349.9 9.9 %collective-permute-start.47 = (bf16[640,128]{1,0:T(8,128)(2,1)}, bf16[640,128]{1,0:T(8,128)(2,1)}, u32[]{:S(2)}, u32[]{:S(2)}) collective-permute-start(bf16[640,128]{1,0:T(8,128)(2,1)} %slice_bitcast_fusion.12), channel_id=1, source_target_pairs={{0,4},{1,5},{2,6},{3,7},{4,0},{5,1},{6,2},{7,3},{8,12},{9,13},{10,... | collective-permute-start | bytes 491528 | tf_op jit(solution)/shard_map/ppermute | solution.py:764
  350.0 20.6 %collective-permute-start.49 = (bf16[656,128]{1,0:T(8,128)(2,1)S(1)}, bf16[656,128]{1,0:T(8,128)(2,1)S(1)}, u32[]{:S(2)}, u32[]{:S(2)}) collective-permute-start(bf16[656,128]{1,0:T(8,128)(2,1)S(1)} %slice_bitcast_fusion.11), channel_id=1, source_target_pairs={{8,16},{16,8},{9,17},{17,9},{10,18},{18,10},{11,19},{19,11},{12,20... | collective-permute-start | bytes 503816 | tf_op jit(solution)/shard_map/ppermute | solution.py:1004
  359.8 10.8 %collective-permute-start.50 = (bf16[656,128]{1,0:T(8,128)(2,1)S(1)}, bf16[656,128]{1,0:T(8,128)(2,1)S(1)}, u32[]{:S(2)}, u32[]{:S(2)}) collective-permute-start(bf16[656,128]{1,0:T(8,128)(2,1)S(1)} %slice_bitcast_fusion.10), channel_id=1, source_target_pairs={{0,4},{1,5},{2,6},{3,7},{4,0},{5,1},{6,2},{7,3},{8,20},{9,21},{10,... | collective-permute-start | bytes 503816 | tf_op jit(solution)/shard_map/ppermute | solution.py:999
  367.5 4.6 %collective-permute-start.45 = (f32[2,1024]{1,0:T(2,128)S(1)}, f32[2,1024]{1,0:T(2,128)S(1)}, u32[]{:S(2)}, u32[]{:S(2)}) collective-permute-start(f32[2,1024]{1,0:T(2,128)S(1)} %add.253), channel_id=1, source_target_pairs={{0,4},{1,5},{2,6},{3,7},{4,0},{5,1},{6,2},{7,3},{8,12},{9,13},{10,... | collective-permute-start | bytes 24584 | tf_op jit(solution)/shard_map/ppermute | solution.py:764
  373.0 6.5 %collective-permute-start.48 = (bf16[384,128]{1,0:T(8,128)(2,1)S(1)}, bf16[384,128]{1,0:T(8,128)(2,1)S(1)}, u32[]{:S(2)}, u32[]{:S(2)}) collective-permute-start(bf16[384,128]{1,0:T(8,128)(2,1)S(1)} %fusion.17), channel_id=1, source_target_pairs={{0,4},{1,5},{2,6},{3,7},{4,0},{5,1},{6,2},{7,3},{8,12},{9,13},{10,... | collective-permute-start | bytes 294920 | tf_op jit(solution)/shard_map/ppermute | solution.py:764
  (53 other events, 420.5 us)
